TPU v7x, 128 devices: a whole 4x4x4 slice. The times are simulated.
128 devices in a mesh: row: 16 (over z, y_hi, core), col: 8 (over y_lo, x).
Axes of the slice: x: 4, y: 4 (y_hi: 2, y_lo: 2; y = y_hi * 2 + y_lo), z: 4, core: 2. Of those that a mesh axis runs over, the one named last changes fastest.
Arguments:
- features: bfloat16 [65536, 256], P(('row', 'col')), may hold values from -6 to 6
- blocks: bfloat16 [16, 8, 192, 64, 64], P('row', 'col'), may hold values from -0.3125 to 0.3125
- block_rows: int32 [16, 8, 192], P('row', 'col'), may hold values from 0 to 63
- block_cols: int32 [16, 8, 192], P('row', 'col'), may hold values from 0 to 127
- block_count: int32 [16, 8], P('row', 'col'), may hold values from 1 to 192, as said below
- w_in: bfloat16 [512, 1024], replicated, may hold values from -0.25 to 0.25
- w_mid: bfloat16 [1024, 1024], replicated, may hold values from -0.1875 to 0.1875
- w_out: bfloat16 [1024, 256], replicated, may hold values from -0.1875 to 0.1875
- cotangent: bfloat16 [65536, 256], P(('row', 'col')), may hold values from -6 to 6
Outputs:
- updated: bfloat16 [65536, 256], P(('row', 'col'))
- grad_nodes: bfloat16 [65536, 256], P(('row', 'col'))
- grad_in: float32 [512, 1024], replicated
- grad_mid: float32 [1024, 1024], replicated
- grad_out: float32 [1024, 256], replicated
Inputs may be any that keep to these rules, and one draw needn't show every extreme that they name: Only slots below a cell's block_count are used; the busiest cell uses all 192 slots.
All inputs are finite; a program needn't handle non-finite values.
Results may differ from a plain program's by a relative error of at most 0.015.
Values may be sent and summed in bfloat16 or wider, within the bound.
No kernel may reach another device: no remote copies, remote signals or barrier semaphores. Data moves between devices by JAX's collectives and lax.ppermute only.
A program may use at most 128 MiB of HBM per device.

v0:
```python
import math

import jax
import jax.numpy as jnp
from jax import lax
from jax.sharding import PartitionSpec as P


def silu_grad(value):
    sig = jax.nn.sigmoid(value)
    return sig * (1.0 + value * (1.0 - sig))


def cell_term(cell_blocks, gather_idx, add_idx, count, source, n_dst, transposed):
    slots = cell_blocks.shape[0]
    side = cell_blocks.shape[1]
    n_src = source.shape[0]
    feats = source.shape[2]
    width = slots // 8
    form = "sba,sbf->saf" if transposed else "sab,sbf->saf"
    flat_source = source.reshape(n_src, side * feats)
    src_ids = jnp.arange(n_src, dtype=jnp.int32)
    dst_ids = jnp.arange(n_dst, dtype=jnp.int32)

    def one_group(step, total):
        start = step * width
        part_blocks = lax.dynamic_slice_in_dim(cell_blocks, start, width, 0)
        part_gather = lax.dynamic_slice_in_dim(gather_idx, start, width, 0)
        part_add = lax.dynamic_slice_in_dim(add_idx, start, width, 0)
        pick_table = (part_gather[:, None] == src_ids[None, :]).astype(jnp.bfloat16)
        picked = jnp.dot(pick_table, flat_source, preferred_element_type=jnp.float32).astype(
            jnp.bfloat16
        )
        picked = picked.reshape(width, side, feats)
        prod = jnp.einsum(form, part_blocks, picked, preferred_element_type=jnp.float32)
        prod = prod.reshape(width, side * feats)
        upper = prod.astype(jnp.bfloat16)
        lower = (prod - upper.astype(jnp.float32)).astype(jnp.bfloat16)
        live = start + jnp.arange(width, dtype=jnp.int32) < count
        add_table = ((part_add[:, None] == dst_ids[None, :]) & live[:, None]).astype(jnp.bfloat16)
        total = total + jnp.einsum(
            "sn,sk->nk", add_table, upper, preferred_element_type=jnp.float32
        )
        return total + jnp.einsum("sn,sk->nk", add_table, lower, preferred_element_type=jnp.float32)

    steps = 8
    total = lax.fori_loop(0, steps, one_group, jnp.zeros((n_dst, side * feats), jnp.float32))
    return total.reshape(n_dst * side, feats)


def shards(features, blocks, block_rows, block_cols, block_count, w_in, w_mid, w_out, cotangent):
    side = blocks.shape[-1]
    feats = features.shape[1]
    node_dev = features.shape[0]
    cell_blocks = blocks[0, 0]
    rows_here = block_rows[0, 0]
    cols_here = block_cols[0, 0]
    count = block_count[0, 0]
    row_blocks = node_dev * lax.axis_size("col") // side
    column_feats = lax.all_gather(features, "row", axis=0, tiled=True)
    col_blocks = column_feats.shape[0] // side
    partial_value = cell_term(
        cell_blocks,
        cols_here,
        rows_here,
        count,
        column_feats.reshape(col_blocks, side, feats),
        row_blocks,
        False,
    )
    aggregated = lax.psum_scatter(
        partial_value.astype(jnp.bfloat16), "col", scatter_dimension=0, tiled=True
    )
    joined = jnp.concatenate([features, aggregated], axis=1)
    pre_one = jnp.dot(joined, w_in, preferred_element_type=jnp.float32)
    act_one = jax.nn.silu(pre_one).astype(jnp.bfloat16)
    pre_two = jnp.dot(act_one, w_mid, preferred_element_type=jnp.float32)
    act_two = jax.nn.silu(pre_two).astype(jnp.bfloat16)
    updated = (
        features.astype(jnp.float32) + jnp.dot(act_two, w_out, preferred_element_type=jnp.float32)
    ).astype(jnp.bfloat16)
    ratio = 1.0 / math.sqrt(node_dev * lax.axis_size("row") * lax.axis_size("col"))
    local_out = jnp.einsum("nh,nf->hf", act_two, cotangent, preferred_element_type=jnp.float32)
    grad_pre_two = (
        jnp.dot(cotangent, w_out.T, preferred_element_type=jnp.float32) * silu_grad(pre_two)
    ).astype(jnp.bfloat16)
    local_mid = jnp.einsum("nh,nk->hk", act_one, grad_pre_two, preferred_element_type=jnp.float32)
    grad_pre_one = (
        jnp.dot(grad_pre_two, w_mid.T, preferred_element_type=jnp.float32) * silu_grad(pre_one)
    ).astype(jnp.bfloat16)
    local_in = jnp.einsum("nd,nh->dh", joined, grad_pre_one, preferred_element_type=jnp.float32)
    grad_joined = jnp.dot(grad_pre_one, w_in.T, preferred_element_type=jnp.float32)
    direct = cotangent.astype(jnp.float32) + grad_joined[:, :feats]
    grad_agg = grad_joined[:, feats:].astype(jnp.bfloat16)
    row_grads = lax.all_gather(grad_agg, "col", axis=0, tiled=True)
    back = cell_term(
        cell_blocks,
        rows_here,
        cols_here,
        count,
        row_grads.reshape(row_blocks, side, feats),
        col_blocks,
        True,
    )
    relaid = lax.psum_scatter(
        back.astype(jnp.bfloat16), "row", scatter_dimension=0, tiled=True
    ).astype(jnp.float32)
    grad_nodes = (direct + relaid).astype(jnp.bfloat16)
    summed_in, summed_mid, summed_out = lax.psum((local_in, local_mid, local_out), ("row", "col"))
    return (updated, grad_nodes, summed_in * ratio, summed_mid * ratio, summed_out * ratio)


def solution(mesh):
    placed = (
        P(("row", "col"), None),
        P("row", "col", None, None, None),
        P("row", "col", None),
        P("row", "col", None),
        P("row", "col"),
        P(),
        P(),
        P(),
        P(("row", "col"), None),
    )
    return jax.shard_map(
        shards,
        mesh=mesh,
        in_specs=placed,
        out_specs=(P(("row", "col"), None), P(("row", "col"), None), P(), P(), P()),
        check_vma=False,
    )
```

profile of v0, /device:TPU:0, one launch (start us, length us, event | category | flops | bytes accessed | tf_op | source)
XLA Modules:
  0.0 512.8 jit_solution(10486671452108770741)
XLA Ops:
  8.0 5.2 %copy.15 = bf16[192,64,64]{2,1,0:T(8,128)(2,1)} copy(bf16[192,64,64]{0,2,1:T(8,128)(2,1)} %bitcast.67) | data formatting | bytes 3145728
  13.2 54.9 %all-gather.3.cloned.1.call-done = bf16[8192,256]{1,0:T(8,128)(2,1)} async-done(((bf16[512,256]{1,0:T(8,128)(2,1)}), bf16[8192,256]{1,0:T(8,128)(2,1)}) %all-gather.3.cloned.1.call-update) | async-done | bytes 4194320 | tf_op jit(solution)/shard_map/all_gather | solution.py:60
  68.0 7.4 %reshape_reshape.6 = bf16[128,16384]{1,0:T(8,128)(2,1)} reshape(bf16[8192,256]{1,0:T(8,128)(2,1)} %all-gather.3.cloned.1.call-done) | data formatting | bytes 8388608 | tf_op jit(solution)/shard_map/reshape;reshape | solution.py:21
  75.5 80.3 %while.28 = (s32[]{:T(128)}, f32[64,16384]{1,0:T(8,128)}, s32[192]{0:T(256)S(1)}, s32[]{:T(128)}, bf16[192,64,64]{2,1,0:T(8,128)(2,1)}, /*index=5*/s32[192]{0:T(...) while((s32[]{:T(128)}, f32[64,16384]{1,0:T(8,128)}, ...), condition=%wide.region_1.0_spmd.clone, body=%wide.region_0.0_spmd.clone.sunk | while | flops 257172528 | bytes 49152960 | solution.py:47
  75.5 2.9 convolution_convert_fusion.4
  85.6 2.9 convolution_convert_fusion.4
  95.6 2.9 convolution_convert_fusion.4
  105.7 2.9 convolution_convert_fusion.4
  115.7 2.9 convolution_convert_fusion.4
  125.7 2.9 convolution_convert_fusion.4
  135.8 2.9 convolution_convert_fusion.4
  145.8 2.9 convolution_convert_fusion.4
  155.8 3.7 convert_element_type.109
  159.5 4.2 convert_element_type.110
  164.7 39.8 %reduce-scatter.3.cloned.1.call-done = bf16[512,256]{1,0:T(8,128)(2,1)} async-done(((bf16[4096,256]{1,0:T(8,128)(2,1)}), bf16[512,256]{1,0:T(8,128)(2,1)}) %reduce-scatter.3.cloned.1.call-update) | async-done | bytes 262160 | tf_op jit(solution)/shard_map/reduce_scatter | solution.py:71
  215.6 5.1 copy.14
  225.9 3.3 fusion.37
  229.2 26.3 %all-gather.5.cloned.1.call-done = bf16[4096,256]{1,0:T(8,128)(2,1)} async-done(((bf16[512,256]{1,0:T(8,128)(2,1)}), bf16[4096,256]{1,0:T(8,128)(2,1)}) %all-gather.5.cloned.1.call-update) | async-done | bytes 2097168 | tf_op jit(solution)/shard_map/all_gather | solution.py:95
  255.5 4.2 reshape_reshape.7
  259.7 97.8 %while.29 = (s32[]{:T(128)}, f32[128,16384]{1,0:T(8,128)}, s32[192]{0:T(256)S(1)}, s32[]{:T(128)}, bf16[192,64,64]{1,2,0:T(8,128)(2,1)}, /*index=5*/s32[192]{0:T...) while((s32[]{:T(128)}, f32[128,16384]{1,0:T(8,128)}, ...), condition=%wide.region_4.5_spmd.clone, body=%wide.region_3.4_spmd.clone.sunk | while | flops 310654528 | bytes 80610240 | solution.py:47
  267.1 4.7 convolution_add_fusion.12
  279.5 4.7 convolution_add_fusion.12
  291.9 4.7 convolution_add_fusion.12
  304.2 4.7 convolution_add_fusion.12
  316.4 4.7 convolution_add_fusion.12
  328.5 4.7 convolution_add_fusion.12
  340.6 4.7 convolution_add_fusion.12
  352.8 4.7 convolution_add_fusion.12
  357.5 5.9 %convert_element_type.117 = bf16[128,16384]{1,0:T(8,128)(2,1)} convert(f32[128,16384]{1,0:T(8,128)} %get-tuple-element.314) | non-fusion elementwise | flops 2097152 | bytes 12582912 | tf_op jit(solution)/shard_map/convert_element_type | solution.py:106
  363.4 7.4 %convert_element_type.118 = bf16[8192,256]{1,0:T(8,128)(2,1)} reshape(bf16[128,16384]{1,0:T(8,128)(2,1)} %convert_element_type.117) | data formatting | bytes 8388608 | tf_op jit(solution)/shard_map/convert_element_type | solution.py:106
  373.3 48.0 %all-reduce.3.cloned.1.call-done = (f32[512,1024]{1,0:T(8,128)}, f32[1024,1024]{1,0:T(8,128)}, f32[1024,256]{1,0:T(8,128)}) async-done(((f32[512,1024]{1,0:T(8,128)}, f32[1024,1024]{1,0:T(8,128)}, f32[1024,256]{1,0:T(8,128)}), (f32[512,1024]{1,0:T(8,128)}, f32[1024,1024]{1,0:T(8,128)}, f32[1024,256]{1,0:T(8,128)})) %all-reduce.3.cloned.1.call-update) | async-done | bytes 7340048 | tf_op jit(solution)/shard_map/psum | solution.py:109
  429.0 75.3 %reduce-scatter.5.cloned.1.call-done = bf16[512,256]{1,0:T(8,128)(2,1)} async-done(((bf16[8192,256]{1,0:T(8,128)(2,1)}), bf16[512,256]{1,0:T(8,128)(2,1)}) %reduce-scatter.5.cloned.1.call-update) | async-done | bytes 262160 | tf_op jit(solution)/shard_map/reduce_scatter | solution.py:105
  (227 shorter events, 146.9 us)
Async XLA Ops:
  7.2 200.2 %copy-start = (bf16[1024,1024]{1,0:T(8,128)(2,1)S(1)}, bf16[1024,1024]{1,0:T(8,128)(2,1)}, u32[]{:S(2)}) copy-start(bf16[1024,1024]{1,0:T(8,128)(2,1)} %param.19) | copy-start | bytes 6291460
  7.2 60.8 %all-gather.3.cloned.1.call-start = ((), (), s32[]{:S(2)}) async-start(), calls=%async_computation.2 | async-start | bytes 4456448 | tf_op jit(solution)/shard_map/all_gather | solution.py:60
  7.9 196.5 %reduce-scatter.3.cloned.1.call-start = ((), (), s32[]{:S(2)}) async-start(), calls=%async_computation.3 | async-start | bytes 2359296 | tf_op jit(solution)/shard_map/reduce_scatter | solution.py:71
  13.2 62.3 %copy-start.18 = (s32[1,1,192]{2,1,0:T(1,128)S(1)}, s32[1,1,192]{2,1,0:T(1,128)}, u32[]{:S(2)}) copy-start(s32[1,1,192]{2,1,0:T(1,128)} %param.15) | copy-start | bytes 2308
  13.2 62.3 %copy-start.19 = (s32[1,1,192]{2,1,0:T(1,128)S(1)}, s32[1,1,192]{2,1,0:T(1,128)}, u32[]{:S(2)}) copy-start(s32[1,1,192]{2,1,0:T(1,128)} %param.16) | copy-start | bytes 2308
  78.6 3.2 copy-start.3
  88.7 3.2 copy-start.3
  98.7 3.2 copy-start.3
  108.8 3.2 copy-start.3
  118.8 3.2 copy-start.3
  128.8 3.2 copy-start.3
  138.9 3.2 copy-start.3
  148.9 3.2 copy-start.3
  163.7 91.8 %all-gather.5.cloned.1.call-start = ((), (), s32[]{:S(2)}) async-start(), calls=%async_computation.4 | async-start | bytes 2359296 | tf_op jit(solution)/shard_map/all_gather | solution.py:95
  207.4 3.5 copy-start.6
  207.4 2.6 copy-start.12
  207.4 2.6 copy-start.16
  212.7 2.9 copy-start.4
  215.3 205.9 %all-reduce.3.cloned.1.call-start = ((), (), s32[]{:S(2)}) async-start(), calls=%async_computation.6 | async-start | bytes 14680064 | tf_op jit(solution)/shard_map/psum | solution.py:109
  220.7 2.9 copy-start.11
  229.2 275.2 %reduce-scatter.5.cloned.1.call-start = ((), (), s32[]{:S(2)}) async-start(), calls=%async_computation.5 | async-start | bytes 4456448 | tf_op jit(solution)/shard_map/reduce_scatter | solution.py:105
  259.8 5.9 %copy-start.2 = (f32[128,16384]{1,0:T(8,128)S(1)}, f32[128,16384]{1,0:T(8,128)}, u32[]{:S(2)}) copy-start(f32[128,16384]{1,0:T(8,128)} %get-tuple-element.542) | copy-start | bytes 25165828 | tf_op jit(solution)/shard_map/while
  271.9 6.2 %copy-start.2 = (f32[128,16384]{1,0:T(8,128)S(1)}, f32[128,16384]{1,0:T(8,128)}, u32[]{:S(2)}) copy-start(f32[128,16384]{1,0:T(8,128)} %get-tuple-element.542) | copy-start | bytes 25165828 | tf_op jit(solution)/shard_map/while
  284.2 6.2 %copy-start.2 = (f32[128,16384]{1,0:T(8,128)S(1)}, f32[128,16384]{1,0:T(8,128)}, u32[]{:S(2)}) copy-start(f32[128,16384]{1,0:T(8,128)} %get-tuple-element.542) | copy-start | bytes 25165828 | tf_op jit(solution)/shard_map/while
  296.6 6.2 %copy-start.2 = (f32[128,16384]{1,0:T(8,128)S(1)}, f32[128,16384]{1,0:T(8,128)}, u32[]{:S(2)}) copy-start(f32[128,16384]{1,0:T(8,128)} %get-tuple-element.542) | copy-start | bytes 25165828 | tf_op jit(solution)/shard_map/while
  309.0 6.0 %copy-start.2 = (f32[128,16384]{1,0:T(8,128)S(1)}, f32[128,16384]{1,0:T(8,128)}, u32[]{:S(2)}) copy-start(f32[128,16384]{1,0:T(8,128)} %get-tuple-element.542) | copy-start | bytes 25165828 | tf_op jit(solution)/shard_map/while
  321.2 5.9 %copy-start.2 = (f32[128,16384]{1,0:T(8,128)S(1)}, f32[128,16384]{1,0:T(8,128)}, u32[]{:S(2)}) copy-start(f32[128,16384]{1,0:T(8,128)} %get-tuple-element.542) | copy-start | bytes 25165828 | tf_op jit(solution)/shard_map/while
  333.2 5.9 %copy-start.2 = (f32[128,16384]{1,0:T(8,128)S(1)}, f32[128,16384]{1,0:T(8,128)}, u32[]{:S(2)}) copy-start(f32[128,16384]{1,0:T(8,128)} %get-tuple-element.542) | copy-start | bytes 25165828 | tf_op jit(solution)/shard_map/while
  345.4 6.0 %copy-start.2 = (f32[128,16384]{1,0:T(8,128)S(1)}, f32[128,16384]{1,0:T(8,128)}, u32[]{:S(2)}) copy-start(f32[128,16384]{1,0:T(8,128)} %get-tuple-element.542) | copy-start | bytes 25165828 | tf_op jit(solution)/shard_map/while
  421.2 2.4 copy-start.8
  423.6 2.9 copy-start.5
  426.6 79.7 %copy-start.1 = (bf16[1024,1024]{1,0:T(8,128)(2,1)S(1)}, bf16[1024,1024]{1,0:T(8,128)(2,1)}, u32[]{:S(2)}) copy-start(bf16[1024,1024]{1,0:T(8,128)(2,1)} %param.19) | copy-start | bytes 6291460
  (9 other events, 13.3 us)
Sparse Core Ops, SparseCore 0:
  10.5 57.5 all-gather.2
  163.8 40.5 reduce-scatter.2
  215.5 40.0 all-gather.4
  260.9 160.2 all-reduce.2
  425.1 79.2 reduce-scatter.4
where the time goes:
time: 514 us; the launch traced here: 513 us
  waiting for transfers between devices  245 us (48%)
  matrix products  164 us (32%)
  local copies, waits for them, and re-layouts  60.2 us (12%)
  other arithmetic  28.4 us (6%)
  between operations  13.9 us (3%)
    reduce_scatter x1, waiting for transfers between devices, shards(): lax.psum_scatter(back.astype(jnp.bfloat16), 'row', scatter_dimension=0, t...  75.3 us
    dot_general x16, matrix products, one_group(): jnp.einsum('sn,sk->nk', add_table, lower, preferred_element_type=jnp.floa...  60.3 us
    all_gather x1, waiting for transfers between devices, shards(): column_feats = lax.all_gather(features, 'row', axis=0, tiled=True)  54.9 us
    psum x1, waiting for transfers between devices, shards(): lax.psum((local_in, local_mid, local_out), ('row', 'col'))  48 us
    dot_general x16, matrix products, one_group(): jnp.dot(pick_table, flat_source, preferred_element_type=jnp.float32)  40.8 us
    reduce_scatter x1, waiting for transfers between devices, shards(): lax.psum_scatter(partial_value.astype(jnp.bfloat16), 'col', scatter_dimen...  39.8 us
    dot_general x16, matrix products, one_group(): jnp.einsum(form, part_blocks, picked, preferred_element_type=jnp.float32)  27.7 us
    all_gather x1, waiting for transfers between devices, shards(): row_grads = lax.all_gather(grad_agg, 'col', axis=0, tiled=True)  26.3 us
  transfers between devices with their start and end apart: 5, of which 5 were waited for; matrix products, arithmetic and copies ran while one was open for 27% of the time, Pallas kernels for 0%

commit v1 on v0

v1 whole, which is shorter than its diff:
```python
import functools
import math

import jax
import jax.numpy as jnp
from jax import lax
from jax.experimental import pallas as pl
from jax.experimental.pallas import tpu as pltpu
from jax.sharding import Mesh, PartitionSpec as P

BF = jnp.bfloat16
F32 = jnp.float32
ROW = ("z", "yh", "core")
COL = ("yl", "x")
SLOTS = 192
SIDE = 64
CHUNK = 32
UNROLL = 8
VMEM_LIMIT = 60 * 1024 * 1024


def silu_grad(value):
    sig = jax.nn.sigmoid(value)
    return sig * (1.0 + value * (1.0 - sig))


def cells_kernel(transposed, off_ref, cnt_ref, blk0, blk1, *rest):
    pieces = rest[:8]
    out_ref, src, held, acc, blk_sem, src_sem = rest[8:]
    n_chunks = SLOTS // CHUNK
    blocks = (blk0, blk1)

    def copy_of(j, ch):
        at = pl.multiple_of(ch * CHUNK, CHUNK)
        return pltpu.make_async_copy(
            blocks[j].at[pl.ds(at, CHUNK)],
            held.at[j, pl.ds(at, CHUNK)],
            blk_sem.at[j * n_chunks + ch],
        )

    moves = [
        pltpu.make_async_copy(piece, src.at[pl.ds(p * 1024, 1024)], src_sem.at[p])
        for p, piece in enumerate(pieces)
    ]
    for move in moves:
        move.start()
    used = [lax.div(cnt_ref[j] + (CHUNK - 1), CHUNK) for j in range(2)]
    for j in range(2):

        @pl.loop(0, used[j])
        def _(ch):
            copy_of(j, ch).start()

    acc[...] = jnp.zeros_like(acc)
    for move in moves:
        move.wait()
    dims = (((0,), (0,)), ((), ())) if transposed else (((1,), (0,)), ((), ()))
    for j in range(2):
        count = cnt_ref[j]

        @pl.loop(0, used[j])
        def _(ch):
            copy_of(j, ch).wait()
            left = jnp.minimum(count - ch * CHUNK, CHUNK)

            @pl.loop(0, lax.div(left + (UNROLL - 1), UNROLL))
            def _(step):
                base = ch * CHUNK + step * UNROLL
                for u in range(UNROLL):
                    slot = base + u
                    take = pl.multiple_of(off_ref[j * SLOTS + slot], SIDE)
                    put = pl.multiple_of(off_ref[(2 + j) * SLOTS + slot], SIDE)
                    term = lax.dot_general(
                        held[j, slot],
                        src[pl.ds(take, SIDE), :],
                        dims,
                        preferred_element_type=F32,
                    )
                    acc[pl.ds(put, SIDE), :] += term

    out_ref[...] = acc[: 16 * 512, :].astype(BF).reshape(out_ref.shape)


def cell_products(transposed, offsets, counts, blk_own, blk_other, pieces):
    any_spec = pl.BlockSpec(memory_space=pl.ANY)
    smem = pl.BlockSpec(memory_space=pltpu.SMEM)
    n_chunks = SLOTS // CHUNK
    return pl.pallas_call(
        functools.partial(cells_kernel, transposed),
        out_shape=jax.ShapeDtypeStruct((16, 512, 128), BF),
        in_specs=[smem, smem] + [any_spec] * 10,
        out_specs=pl.BlockSpec(memory_space=pltpu.VMEM),
        scratch_shapes=[
            pltpu.VMEM((8192, 128), BF),
            pltpu.VMEM((2, SLOTS, SIDE, SIDE), BF),
            pltpu.VMEM((8192 + SIDE, 128), F32),
            pltpu.SemaphoreType.DMA((2 * n_chunks,)),
            pltpu.SemaphoreType.DMA((8,)),
        ],
        compiler_params=pltpu.CompilerParams(vmem_limit_bytes=VMEM_LIMIT),
        cost_estimate=pl.CostEstimate(
            flops=2 * 2 * SLOTS * SIDE * SIDE * 128, bytes_accessed=10 << 20, transcendentals=0
        ),
        name="cells_back" if transposed else "cells_forward",
    )(offsets, counts, blk_own, blk_other, *pieces)


def grads_kernel(core_ref, joined, act_one, cot, gp_one, gp_two, act_two, own_ref, other_ref):
    core = core_ref[0]
    sides = ((joined, gp_one, 0, 512), (act_one, gp_two, 512, 1024), (cot, act_two, 1536, 256))
    for ref, half in ((own_ref, core), (other_ref, 1 - core)):
        at = pl.multiple_of(half * 512, 512)
        for left, right, row, size in sides:
            for part in range(0, size, 256):
                ref[row + part : row + part + 256, :] = lax.dot_general(
                    left[:, part : part + 256],
                    right[:, pl.ds(at, 512)],
                    (((0,), (0,)), ((), ())),
                    preferred_element_type=F32,
                ).astype(BF)


def local_grads(core, joined, act_one, cot, gp_one, gp_two, act_two):
    vm = pl.BlockSpec(memory_space=pltpu.VMEM)
    return pl.pallas_call(
        grads_kernel,
        out_shape=(jax.ShapeDtypeStruct((1792, 512), BF),) * 2,
        in_specs=[pl.BlockSpec(memory_space=pltpu.SMEM)] + [vm] * 6,
        out_specs=(vm, vm),
        compiler_params=pltpu.CompilerParams(vmem_limit_bytes=VMEM_LIMIT),
        cost_estimate=pl.CostEstimate(
            flops=2 * 512 * 1792 * 1024, bytes_accessed=8 << 20, transcendentals=0
        ),
        name="local_grads",
    )(core.reshape(1), joined, act_one, cot, gp_one, gp_two, act_two)


def gather_steps(value, axes):
    pieces = []
    for p in range(8):
        big, small = p >> 1, p & 1
        if p == 0:
            pieces.append(value)
            continue
        perm = []
        for i in range(8):
            if axes == ("z", "yh"):
                to = (((i >> 1) + big) % 4) * 2 + ((i & 1) ^ small)
            else:
                to = ((i >> 2) ^ small) * 4 + ((i & 3) + big) % 4
            perm.append((i, to))
        pieces.append(lax.ppermute(value, axes, perm))
    return pieces


def halves(value, core):
    left, right = value[:, :128], value[:, 128:]
    first = core == 0
    mine = jnp.where(first, left, right)
    yours = jnp.where(first, right, left)
    got = lax.ppermute(yours, "core", [(0, 1), (1, 0)])
    return jnp.concatenate([mine, got], axis=0)


def finish_kernel(core_ref, pos_ref, *rest):
    own, other = rest[:4], rest[4:8]
    in_ref, mid_ref, out_ref = rest[8:]
    ratio = 1.0 / 256.0
    core, x = core_ref[0], pos_ref[0]
    for group, half in ((own, core), (other, 1 - core)):
        for k, piece in enumerate(group):
            src_x = lax.rem(x + (4 - k), 4)
            lane = pl.multiple_of(half * 512 + src_x * 128, 128)
            full = piece[...].astype(F32) * ratio
            in_ref[:, pl.ds(lane, 128)] = full[:512]
            mid_ref[:, pl.ds(lane, 128)] = full[512:1536]
            out_ref[pl.ds(lane, 128), :] = full[1536:].T


def finish_grads(core, x, own, other):
    vm = pl.BlockSpec(memory_space=pltpu.VMEM)
    sm = pl.BlockSpec(memory_space=pltpu.SMEM)
    return pl.pallas_call(
        finish_kernel,
        out_shape=(
            jax.ShapeDtypeStruct((512, 1024), F32),
            jax.ShapeDtypeStruct((1024, 1024), F32),
            jax.ShapeDtypeStruct((1024, 256), F32),
        ),
        in_specs=[sm, sm] + [vm] * 8,
        out_specs=(vm, vm, vm),
        compiler_params=pltpu.CompilerParams(vmem_limit_bytes=VMEM_LIMIT),
        cost_estimate=pl.CostEstimate(flops=1 << 20, bytes_accessed=11 << 20, transcendentals=0),
        name="finish_grads",
    )(core.reshape(1), x.reshape(1), *own, *other)


def sum_grads(core, own, other):
    x = lax.axis_index("x")
    got = lax.ppermute(other, "core", [(0, 1), (1, 0)])
    chip = (own.astype(F32) + got.astype(F32)).astype(BF)
    part = lax.all_to_all(chip.reshape(4, 448, 512), "z", 0, 0, tiled=True)
    part = jnp.sum(part.astype(F32), axis=0).astype(BF)
    part = part.reshape(4, 112, 4, 128).transpose(0, 2, 1, 3).reshape(16, 112, 128)
    part = lax.all_to_all(part, ("yh", "yl", "x"), 0, 0, tiled=True)
    part = jnp.sum(part.astype(F32), axis=0).astype(BF)
    lanes = jnp.broadcast_to(part[None], (16, 112, 128))
    lanes = lax.all_to_all(lanes, ("z", "yh", "yl"), 0, 0, tiled=True).reshape(1792, 128)
    mine = [lanes] + [
        lax.ppermute(lanes, "x", [(i, (i + k) % 4) for i in range(4)]) for k in range(1, 4)
    ]
    yours = [lax.ppermute(piece, "core", [(0, 1), (1, 0)]) for piece in mine]
    return finish_grads(core, x, mine, yours)


def shards(features, blocks, block_rows, block_cols, block_count, w_in, w_mid, w_out, cotangent):
    core = lax.axis_index("core")
    z, yh = lax.axis_index("z"), lax.axis_index("yh")
    yl, x = lax.axis_index("yl"), lax.axis_index("x")
    swap = [(0, 1), (1, 0)]
    blk_own = blocks[0, 0]
    meta = jnp.concatenate(
        [block_rows[0, 0], block_cols[0, 0], jnp.broadcast_to(block_count[0, 0], (128,))]
    )
    meta_other = lax.ppermute(meta, "core", swap)
    blk_other = lax.ppermute(blk_own, "core", swap)

    both = jnp.stack([meta, meta_other])
    rows, cols, count = both[:, :SLOTS], both[:, SLOTS : 2 * SLOTS], both[:, 2 * SLOTS]
    live = jnp.arange(SLOTS, dtype=jnp.int32)[None, :] < count[:, None]
    cell_core = jnp.stack([core, 1 - core])[:, None]
    spare = 16 * 512
    grp = cols >> 3
    step = (((z - (grp >> 2)) & 3) * 2) + (((grp >> 1) & 1) ^ yh)
    col_at = step * 1024 + ((grp & 1) ^ core) * 512 + (cols & 7) * SIDE
    row_to = jnp.where(live, cell_core * 4096 + rows * SIDE, spare)
    fwd_off = jnp.concatenate([col_at, row_to]).reshape(4 * SLOTS)
    own8 = rows >> 3
    step = (((x - own8) & 3) * 2) + ((own8 >> 2) ^ yl)
    row_at = step * 1024 + jnp.arange(2, dtype=jnp.int32)[:, None] * 512 + (rows & 7) * SIDE
    col_to = jnp.where(live, cols * SIDE, spare)
    bwd_off = jnp.concatenate([row_at, col_to]).reshape(4 * SLOTS)

    pieces = gather_steps(halves(features, core), ("z", "yh"))
    cells = cell_products(False, fwd_off, count, blk_own, blk_other, pieces)
    cells = lax.all_to_all(cells, ("core", "yl", "x"), 0, 0, tiled=True)
    sums = jnp.sum(cells.reshape(2, 8, 512, 128).astype(F32), axis=1).astype(BF)
    aggregated = jnp.concatenate([sums[0], sums[1]], axis=1)

    joined = jnp.concatenate([features, aggregated], axis=1)
    pre_one = jnp.dot(joined, w_in, preferred_element_type=F32)
    act_one = jax.nn.silu(pre_one).astype(BF)
    pre_two = jnp.dot(act_one, w_mid, preferred_element_type=F32)
    act_two = jax.nn.silu(pre_two).astype(BF)
    updated = (
        features.astype(F32) + jnp.dot(act_two, w_out, preferred_element_type=F32)
    ).astype(BF)
    grad_pre_two = (
        jnp.dot(cotangent, w_out.T, preferred_element_type=F32) * silu_grad(pre_two)
    ).astype(BF)
    grad_pre_one = (
        jnp.dot(grad_pre_two, w_mid.T, preferred_element_type=F32) * silu_grad(pre_one)
    ).astype(BF)
    grad_joined = jnp.dot(grad_pre_one, w_in.T, preferred_element_type=F32)
    direct = cotangent.astype(F32) + grad_joined[:, :256]
    grad_agg = grad_joined[:, 256:].astype(BF)

    pieces = gather_steps(halves(grad_agg, core), COL)
    own, other = local_grads(core, joined, act_one, cotangent, grad_pre_one, grad_pre_two, act_two)
    back = cell_products(True, bwd_off, count, blk_own, blk_other, pieces)
    back = lax.all_to_all(back, ROW, 0, 0, tiled=True)
    sums = jnp.sum(back.reshape(8, 2, 512, 128).astype(F32), axis=0)
    relaid = jnp.concatenate([sums[0], sums[1]], axis=1)
    grad_nodes = (direct + relaid).astype(BF)
    grad_in, grad_mid, grad_out = sum_grads(core, own, other)
    return updated, grad_nodes, grad_in, grad_mid, grad_out


def solution(mesh):
    fine = Mesh(mesh.devices.reshape(4, 2, 2, 2, 4), ROW + COL)
    nodes = P(ROW + COL, None)
    placed = (
        nodes,
        P(ROW, COL, None, None, None),
        P(ROW, COL, None),
        P(ROW, COL, None),
        P(ROW, COL),
        P(),
        P(),
        P(),
        nodes,
    )
    return jax.shard_map(
        shards,
        mesh=fine,
        in_specs=placed,
        out_specs=(nodes, nodes, P(), P(), P()),
        check_vma=False,
    )
```

time: 514 us -> 250 us (0.49)
  waiting for transfers between devices: 245 us -> 89.6 us
  matrix products: 164 us -> 12.6 us
  starting transfers between devices: 0.38 us -> 49.1 us
  local copies, waits for them, and re-layouts: 60.2 us -> 17 us
  Pallas kernels: 0 us -> 32.4 us
  blocking collectives: 0 us -> 31.4 us
  other arithmetic: 28.4 us -> 14.2 us
  between operations: 13.9 us -> 1.62 us
    dot_general x73 -> x6, matrix products: 164 us -> 12.6 us  [the longest x1 3.09 us: shards(): grad_joined = jnp.dot(grad_pre_one, w_in.T, preferred_element_type=F32)]
    reduce_scatter x2 -> x0, waiting for transfers between devices: 115 us -> none  [the longest x1 75.3 us: shards(): lax.psum_scatter(back.astype(jnp.bfloat16), 'row', scatter_dimension=0, t...]
    all_gather x2 -> x0, waiting for transfers between devices: 81.1 us -> none  [the longest x1 54.9 us: shards(): column_feats = lax.all_gather(features, 'row', axis=0, tiled=True)]
    all_to_all x0 -> x4, waiting for transfers between devices: none -> 49 us  [the longest x1 24.7 us: shards(): back = lax.all_to_all(back, ROW, 0, 0, tiled=True)]
    psum x1 -> x0, waiting for transfers between devices: 48 us -> none  [shards(): lax.psum((local_in, local_mid, local_out), ('row', 'col'))]
    ppermute x0 -> x26, waiting for transfers between devices: none -> 40.6 us  [the longest x14 32 us: gather_steps(): pieces.append(lax.ppermute(value, axes, perm))]
    pallas_call x0 -> x4, Pallas kernels: none -> 32.4 us  [the longest x2 20.7 us: cell_products(): pl.pallas_call(functools.partial(cells_kernel, transposed), out_shape=jax...]
    all_to_all x0 -> x1, blocking collectives: none -> 31.4 us  [shards(): cells = lax.all_to_all(cells, ('core', 'yl', 'x'), 0, 0, tiled=True)]
  transfers between devices with their start and end apart: 5 -> 30, of which waited for: 5 -> 16; matrix products, arithmetic and copies ran while one was open for 27% -> 10% of each run, Pallas kernels for 0% -> 4%
where the time goes in v1:
time: 250 us; the launch traced here: 248 us
  waiting for transfers between devices  89.6 us (36%)
  starting transfers between devices  49.1 us (20%)
  Pallas kernels  32.4 us (13%)
  blocking collectives  31.4 us (13%)
  local copies, waits for them, and re-layouts  17 us (7%)
  other arithmetic  14.2 us (6%)
  matrix products  12.6 us (5%)
    ppermute x14, waiting for transfers between devices, gather_steps(): pieces.append(lax.ppermute(value, axes, perm))  32 us
    all_to_all x1, blocking collectives, shards(): cells = lax.all_to_all(cells, ('core', 'yl', 'x'), 0, 0, tiled=True)  31.4 us
    ppermute x14, starting transfers between devices, gather_steps(): pieces.append(lax.ppermute(value, axes, perm))  26.5 us
    all_to_all x1, waiting for transfers between devices, shards(): back = lax.all_to_all(back, ROW, 0, 0, tiled=True)  24.7 us
    all_to_all x1, waiting for transfers between devices, sum_grads(): part = lax.all_to_all(chip.reshape(4, 448, 512), 'z', 0, 0, tiled=True)  21.2 us
    pallas_call x2, Pallas kernels, cell_products(): pl.pallas_call(functools.partial(cells_kernel, transposed), out_shape=jax...  20.7 us
    pallas_call x1, Pallas kernels, finish_grads(): pl.pallas_call(finish_kernel, out_shape=(jax.ShapeDtypeStruct((512, 1024)...  5.89 us
    unnamed x35, local copies, waits for them, and re-layouts  5.81 us
  transfers between devices with their start and end apart: 30, of which 16 were waited for; matrix products, arithmetic and copies ran while one was open for 10% of the time, Pallas kernels for 4%

profile of v1, /device:TPU:0, one launch (start us, length us, event | category | flops | bytes accessed | tf_op | source)
XLA Modules:
  0.0 248.0 jit_solution(2401331028335590881)
XLA Ops:
  5.3 6.8 %collective-permute-start.9 = (bf16[1024,128]{1,0:T(8,128)(2,1)S(1)}, bf16[1024,128]{1,0:T(8,128)(2,1)S(1)}, u32[]{:S(2)}, u32[]{:S(2)}) collective-permute-start(bf16[1024,128]{1,0:T(8,128)(2,1)S(1)} %pad_maximum_fusion.1.rest_0_), channel_id=1, source_target_pairs={{0,112},{16,96},{32,16},{48,0},{64,48},{80,32},{96,80},{112,64},{1... | collective-permute-start | bytes 786440 | tf_op jit(solution)/shard_map/ppermute | solution.py:152
  12.6 5.1 %copy.18 = bf16[1,1,192,64,64]{4,3,2,1,0:T(8,128)(2,1)} copy(bf16[1,1,192,64,64]{2,4,3,1,0:T(8,128)(2,1)} %param.10) | data formatting | bytes 3145728 | tf_op args[1]
  18.0 3.3 %collective-permute-start.6 = (bf16[1024,128]{1,0:T(8,128)(2,1)S(1)}, bf16[1024,128]{1,0:T(8,128)(2,1)S(1)}, u32[]{:S(2)}, u32[]{:S(2)}) collective-permute-start(bf16[1024,128]{1,0:T(8,128)(2,1)S(1)} %pad_maximum_fusion.1.rest_0_), channel_id=1, source_target_pairs={{0,64},{16,80},{32,96},{48,112},{64,0},{80,16},{96,32},{112,48},{1... | collective-permute-start | bytes 786440 | tf_op jit(solution)/shard_map/ppermute | solution.py:152
  21.3 4.3 %collective-permute-start.5 = (bf16[1024,128]{1,0:T(8,128)(2,1)S(1)}, bf16[1024,128]{1,0:T(8,128)(2,1)}, u32[]{:S(2)}, u32[]{:S(2)}) collective-permute-start(bf16[1024,128]{1,0:T(8,128)(2,1)S(1)} %pad_maximum_fusion.1.rest_0_), channel_id=1, source_target_pairs={{0,48},{16,32},{32,80},{48,64},{64,112},{80,96},{96,16},{112,0},{1... | collective-permute-start | bytes 786440 | tf_op jit(solution)/shard_map/ppermute | solution.py:152
  25.5 9.1 %collective-permute-done.8.rest_6_ = bf16[1024,128]{1,0:T(8,128)(2,1)S(1)} collective-permute-done((bf16[1024,128]{1,0:T(8,128)(2,1)S(1)}, bf16[1024,128]{1,0:T(8,128)(2,1)S(1)}, u32[]{:S(2)}, u32[]{:S(2)}) %collective-permute-start.8) | collective-permute-done | bytes 262176 | tf_op jit(solution)/shard_map/ppermute | solution.py:152
  36.4 5.2 %copy.20.blk1 = bf16[192,64,64]{2,1,0:T(8,128)(2,1)} copy(bf16[192,64,64]{0,2,1:T(8,128)(2,1)} %collective-permute-done.1) | data formatting | bytes 3145728 | tf_op jit(solution)/shard_map/ppermute | solution.py:226
  41.6 3.4 %collective-permute-done.4.rest_2_ = bf16[1024,128]{1,0:T(8,128)(2,1)} collective-permute-done((bf16[1024,128]{1,0:T(8,128)(2,1)S(1)}, bf16[1024,128]{1,0:T(8,128)(2,1)}, u32[]{:S(2)}, u32[]{:S(2)}) %collective-permute-start.4) | collective-permute-done | bytes 262176 | tf_op jit(solution)/shard_map/ppermute | solution.py:152
  45.0 9.7 %cells_forward.1 = bf16[16,512,128]{2,1,0:T(8,128)(2,1)} custom-call(s32[768]{0:T(1024)} %reshape.63.off_ref, s32[2]{0:T(128)} %copy-done.13, bf16[192,64,64]{2,1,0:T(8,128)(2,1)} %bitcast.38, bf16[192,64,64]{2,1,0:T(8,128)(2,1)} %copy.20.blk1, bf16[1024,128]{1,0:T(8,128)(2,1)} %copy-done.2, bf16[1024,128]{1,0:T(8,128)(2,1)} %collective-permute-done.3.rest_1_, ...), custom_call_target="tpu_custom_call" | custom-call | flops 402653184 | bytes 10485760 | tf_op jit(solution)/shard_map/cells_forward/pallas_call | solution.py:88
  54.8 31.4 %all_to_all.25 = bf16[16,512,128]{2,1,0:T(8,128)(2,1)S(1)} all-to-all(bf16[16,512,128]{2,1,0:T(8,128)(2,1)} %cells_forward.1), channel_id=1, replica_groups=mesh['z'=4,'yh'=2,'core'=2,'yl'=2,'x'=4] {'core','yl','x'}, dimensions={0} | all-to-all | bytes 4194304 | tf_op jit(solution)/shard_map/all_to_all | solution.py:246
  89.1 2.5 multiply_convert_fusion.2
  92.5 2.6 %multiply_convert_fusion.gp_one = bf16[512,1024]{1,0:T(8,128)(2,1)} fusion(f32[512,1024]{1,0:T(8,128)S(1)} %get-tuple-element.28, bf16[512,1024]{1,0:T(8,128)(2,1)S(1)} %multiply_convert_fusion.1.gp_two, bf16[1024,1024]{1,0:T(8,128)(2,1)S(1)} %copy-done), kind=kOutput, calls=%fused_computation.3 | convolution fusion | flops 1078460416 | bytes 6291456 | tf_op jit(solution)/shard_map/dot_general | solution.py:262
  95.1 5.8 %local_grads.1 = (bf16[1792,512]{1,0:T(8,128)(2,1)}, bf16[1792,512]{1,0:T(8,128)(2,1)}) custom-call(s32[1]{0:T(128)} %bitcast.5.core_ref, bf16[512,512]{1,0:T(8,128)(2,1)} %pad_maximum_fusion.joined, bf16[512,1024]{1,0:T(8,128)(2,1)} %copy-done.15, bf16[512,256]{1,0:T(8,128)(2,1)} %cot.1, bf16[512,1024]{1,0:T(8,128)(2,1)} %multiply_convert_fusion.gp_one, ...), custom_call_target="tpu_custom_call" | custom-call | flops 1879048192 | bytes 8388608 | tf_op jit(solution)/shard_map/local_grads/pallas_call | solution.py:125
  101.3 3.6 %collective-permute-done.18 = bf16[1792,512]{1,0:T(8,128)(2,1)S(1)} collective-permute-done((bf16[1792,512]{1,0:T(8,128)(2,1)}, bf16[1792,512]{1,0:T(8,128)(2,1)S(1)}, u32[]{:S(2)}, u32[]{:S(2)}) %collective-permute-start.18) | collective-permute-done | bytes 1835040 | tf_op jit(solution)/shard_map/ppermute | solution.py:200
  104.9 3.3 %add_convert_fusion = bf16[1792,512]{1,0:T(8,128)(2,1)} fusion(bf16[1792,512]{1,0:T(8,128)(2,1)S(1)} %collective-permute-done.18, bf16[1792,512]{1,0:T(8,128)(2,1)} %get-tuple-element.10), kind=kLoop, calls=%fused_computation.1 | loop fusion | flops 3670016 | bytes 5505024 | tf_op jit(solution)/shard_map/convert_element_type | solution.py:201
  108.2 5.1 %all-to-all-start.2 = ((bf16[4,448,512]{2,1,0:T(8,128)(2,1)}), bf16[4,448,512]{2,1,0:T(8,128)(2,1)}, u32[]{:S(2)}, u32[]{:S(2)}) async-start(bf16[4,448,512]{2,1,0:T(8,128)(2,1)} %bitcast.40), calls=%async_computation.2 | async-start | bytes 3670016 | tf_op jit(solution)/shard_map/all_to_all | solution.py:202
  113.2 3.1 %fusion.11 = (bf16[512,512]{1,0:T(8,128)(2,1)}, f32[512,512]{1,0:T(8,128)S(1)}) fusion(bf16[512,1024]{1,0:T(8,128)(2,1)} %multiply_convert_fusion.gp_one, bf16[512,1024]{1,0:T(8,128)(2,1)} %param.14), kind=kOutput, calls=%fused_computation.48 | convolution fusion | flops 537133056 | bytes 3670016 | tf_op jit(solution)/shard_map/dot_general | solution.py:264
  116.3 21.2 %all-to-all-done.2 = bf16[4,448,512]{2,1,0:T(8,128)(2,1)} async-done(((bf16[4,448,512]{2,1,0:T(8,128)(2,1)}), bf16[4,448,512]{2,1,0:T(8,128)(2,1)}, u32[]{:S(2)}, u32[]{:S(2)}) %all-to-all-start.2) | async-done | bytes 1835040 | tf_op jit(solution)/shard_map/all_to_all | solution.py:202
  137.6 2.7 %reduce_sum.47 = bf16[448,512]{1,0:T(8,128)(2,1)} reduce(bf16[4,448,512]{2,1,0:T(8,128)(2,1)} %all-to-all-done.2, bf16[]{:T(256)} %constant.49.clone.1), dimensions={0}, to_apply=%region_2.3 | reduce | flops 688128 | bytes 2293762 | tf_op jit(solution)/shard_map/reduce_sum | solution.py:203
  144.0 4.4 %all-to-all-start.3 = ((bf16[16,112,128]{2,1,0:T(8,128)(2,1)}), bf16[16,112,128]{2,1,0:T(8,128)(2,1)}, u32[]{:S(2)}, u32[]{:S(2)}) async-start(bf16[16,112,128]{2,1,0:T(8,128)(2,1)} %bitcast.42), calls=%async_computation.3 | async-start | bytes 917504 | tf_op jit(solution)/shard_map/all_to_all | solution.py:205
  150.8 4.1 %collective-permute-start.17 = (bf16[1024,128]{1,0:T(8,128)(2,1)S(1)}, bf16[1024,128]{1,0:T(8,128)(2,1)}, u32[]{:S(2)}, u32[]{:S(2)}) collective-permute-start(bf16[1024,128]{1,0:T(8,128)(2,1)S(1)} %pad_maximum_fusion.2.rest_0_), channel_id=1, source_target_pairs={{0,7},{1,4},{2,5},{3,6},{4,3},{5,0},{6,1},{7,2},{8,15},{9,12},{10,... | collective-permute-start | bytes 786440 | tf_op jit(solution)/shard_map/ppermute | solution.py:152
  155.7 3.1 %all-to-all-done.3 = bf16[16,112,128]{2,1,0:T(8,128)(2,1)} async-done(((bf16[16,112,128]{2,1,0:T(8,128)(2,1)}), bf16[16,112,128]{2,1,0:T(8,128)(2,1)}, u32[]{:S(2)}, u32[]{:S(2)}) %all-to-all-start.3) | async-done | bytes 458784 | tf_op jit(solution)/shard_map/all_to_all | solution.py:205
  160.8 4.2 %all-to-all-start.4 = ((bf16[16,112,128]{2,1,0:T(8,128)(2,1)}), bf16[16,112,128]{2,1,0:T(8,128)(2,1)}, u32[]{:S(2)}, u32[]{:S(2)}) async-start(bf16[16,112,128]{2,1,0:T(8,128)(2,1)} %broadcast_in_dim.19), calls=%async_computation.4 | async-start | bytes 917504 | tf_op jit(solution)/shard_map/all_to_all | solution.py:208
  167.0 2.7 %collective-permute-start.14 = (bf16[1024,128]{1,0:T(8,128)(2,1)S(1)}, bf16[1024,128]{1,0:T(8,128)(2,1)}, u32[]{:S(2)}, u32[]{:S(2)}) collective-permute-start(bf16[1024,128]{1,0:T(8,128)(2,1)S(1)} %pad_maximum_fusion.2.rest_0_), channel_id=1, source_target_pairs={{0,2},{1,3},{2,0},{3,1},{4,6},{5,7},{6,4},{7,5},{8,10},{9,11},{10,... | collective-permute-start | bytes 786440 | tf_op jit(solution)/shard_map/ppermute | solution.py:152
  170.8 6.8 %collective-permute-done.16.rest_6_ = bf16[1024,128]{1,0:T(8,128)(2,1)} collective-permute-done((bf16[1024,128]{1,0:T(8,128)(2,1)S(1)}, bf16[1024,128]{1,0:T(8,128)(2,1)}, u32[]{:S(2)}, u32[]{:S(2)}) %collective-permute-start.16) | collective-permute-done | bytes 262176 | tf_op jit(solution)/shard_map/ppermute | solution.py:152
  178.3 4.4 %collective-permute-done.14.rest_4_ = bf16[1024,128]{1,0:T(8,128)(2,1)} collective-permute-done((bf16[1024,128]{1,0:T(8,128)(2,1)S(1)}, bf16[1024,128]{1,0:T(8,128)(2,1)}, u32[]{:S(2)}, u32[]{:S(2)}) %collective-permute-start.14) | collective-permute-done | bytes 262176 | tf_op jit(solution)/shard_map/ppermute | solution.py:152
  182.7 2.9 %collective-permute-done.13.rest_3_ = bf16[1024,128]{1,0:T(8,128)(2,1)} collective-permute-done((bf16[1024,128]{1,0:T(8,128)(2,1)S(1)}, bf16[1024,128]{1,0:T(8,128)(2,1)}, u32[]{:S(2)}, u32[]{:S(2)}) %collective-permute-start.13) | collective-permute-done | bytes 262176 | tf_op jit(solution)/shard_map/ppermute | solution.py:152
  185.6 5.4 %collective-permute-done.12.rest_2_ = bf16[1024,128]{1,0:T(8,128)(2,1)} collective-permute-done((bf16[1024,128]{1,0:T(8,128)(2,1)S(1)}, bf16[1024,128]{1,0:T(8,128)(2,1)}, u32[]{:S(2)}, u32[]{:S(2)}) %collective-permute-start.12) | collective-permute-done | bytes 262176 | tf_op jit(solution)/shard_map/ppermute | solution.py:152
  191.0 11.0 %cells_back.1 = bf16[16,512,128]{2,1,0:T(8,128)(2,1)} custom-call(s32[768]{0:T(1024)} %reshape.65.off_ref, s32[2]{0:T(128)} %copy-done.13, bf16[192,64,64]{2,1,0:T(8,128)(2,1)} %bitcast.39, bf16[192,64,64]{2,1,0:T(8,128)(2,1)} %copy.20.blk1, bf16[1024,128]{1,0:T(8,128)(2,1)} %copy-done.3, bf16[1024,128]{1,0:T(8,128)(2,1)} %collective-permute-done.11.rest_1_, ...), custom_call_target="tpu_custom_call" | custom-call | flops 402653184 | bytes 10485760 | tf_op jit(solution)/shard_map/cells_back/pallas_call | solution.py:88
  202.1 4.6 %all-to-all-start.1 = ((bf16[16,512,128]{2,1,0:T(8,128)(2,1)}), bf16[16,512,128]{2,1,0:T(8,128)(2,1)}, u32[]{:S(2)}, u32[]{:S(2)}) async-start(bf16[16,512,128]{2,1,0:T(8,128)(2,1)} %cells_back.1), calls=%async_computation.1 | async-start | bytes 4194304 | tf_op jit(solution)/shard_map/all_to_all | solution.py:271
  208.7 2.5 %fusion = bf16[512,256]{1,0:T(8,128)(2,1)} fusion(bf16[512,1024]{1,0:T(8,128)(2,1)} %get-tuple-element.29.act_two, bf16[1024,256]{1,0:T(8,128)(2,1)} %param.16, bf16[512,256]{1,0:T(8,128)(2,1)S(1)} %copy-done.5), kind=kOutput, calls=%fused_computation.10 | convolution fusion | flops 268828672 | bytes 2097152 | tf_op jit(solution)/shard_map/dot_general | solution.py:256
  211.3 24.7 %all-to-all-done.1 = bf16[16,512,128]{2,1,0:T(8,128)(2,1)} async-done(((bf16[16,512,128]{2,1,0:T(8,128)(2,1)}), bf16[16,512,128]{2,1,0:T(8,128)(2,1)}, u32[]{:S(2)}, u32[]{:S(2)}) %all-to-all-start.1) | async-done | bytes 2097184 | tf_op jit(solution)/shard_map/all_to_all | solution.py:271
  242.1 5.9 %finish_grads.1 = (f32[512,1024]{1,0:T(8,128)}, f32[1024,1024]{1,0:T(8,128)}, f32[1024,256]{1,0:T(8,128)}) custom-call(s32[1]{0:T(128)} %bitcast.5.core_ref, s32[1]{0:T(128)} %bitcast.15.pos_ref, bf16[1792,128]{1,0:T(8,128)(2,1)} %bitcast.19.rest_0_, bf16[1792,128]{1,0:T(8,128)(2,1)} %collective-permute-done.19.rest_1_, ...), custom_call_target="tpu_custom_call" | custom-call | flops 1048576 | bytes 11534336 | tf_op jit(solution)/shard_map/finish_grads/pallas_call | solution.py:183
  (102 shorter events, 31.6 us)
Async XLA Ops:
  0.6 88.4 %copy-start = (bf16[1024,1024]{1,0:T(8,128)(2,1)S(1)}, bf16[1024,1024]{1,0:T(8,128)(2,1)}, u32[]{:S(2)}) copy-start(bf16[1024,1024]{1,0:T(8,128)(2,1)} %param.15) | copy-start | bytes 6291460
  0.6 34.0 %collective-permute-start.1 = (bf16[192,64,64]{0,2,1:T(8,128)(2,1)}, bf16[192,64,64]{0,2,1:T(8,128)(2,1)}, u32[]{:S(2)}, u32[]{:S(2)}) collective-permute-start(bf16[192,64,64]{0,2,1:T(8,128)(2,1)} %bitcast.41), channel_id=1, source_target_pairs={{0,8},{8,0},{1,9},{9,1},{2,10},{10,2},{3,11},{11,3},{4,12},{12,4},... | collective-permute-start | bytes 4718600 | tf_op jit(solution)/shard_map/ppermute | solution.py:226
  1.9 3.4 %collective-permute-start.2 = (bf16[512,128]{1,0:T(8,128)(2,1)S(1)}, bf16[512,128]{1,0:T(8,128)(2,1)S(1)}, u32[]{:S(2)}, u32[]{:S(2)}) collective-permute-start(bf16[512,128]{1,0:T(8,128)(2,1)S(1)} %get-tuple-element.24), channel_id=1, source_target_pairs={{0,8},{8,0},{1,9},{9,1},{2,10},{10,2},{3,11},{11,3},{4,12},{12,4},... | collective-permute-start | bytes 393224 | tf_op jit(solution)/shard_map/ppermute | solution.py:161
  3.7 14.0 %collective-permute-start = (s32[512]{0:T(512)S(1)}, s32[512]{0:T(512)S(1)}, u32[]{:S(2)}, u32[]{:S(2)}) collective-permute-start(s32[512]{0:T(512)S(1)} %pad_add_fusion.3), channel_id=1, source_target_pairs={{0,8},{8,0},{1,9},{9,1},{2,10},{10,2},{3,11},{11,3},{4,12},{12,4},... | collective-permute-start | bytes 6152 | tf_op jit(solution)/shard_map/ppermute | solution.py:225
  5.3 16.0 %collective-permute-start.9 = (bf16[1024,128]{1,0:T(8,128)(2,1)S(1)}, bf16[1024,128]{1,0:T(8,128)(2,1)S(1)}, u32[]{:S(2)}, u32[]{:S(2)}) collective-permute-start(bf16[1024,128]{1,0:T(8,128)(2,1)S(1)} %pad_maximum_fusion.1.rest_0_), channel_id=1, source_target_pairs={{0,112},{16,96},{32,16},{48,0},{64,48},{80,32},{96,80},{112,64},{1... | collective-permute-start | bytes 786440 | tf_op jit(solution)/shard_map/ppermute | solution.py:152
  12.2 22.5 %collective-permute-start.8 = (bf16[1024,128]{1,0:T(8,128)(2,1)S(1)}, bf16[1024,128]{1,0:T(8,128)(2,1)S(1)}, u32[]{:S(2)}, u32[]{:S(2)}) collective-permute-start(bf16[1024,128]{1,0:T(8,128)(2,1)S(1)} %pad_maximum_fusion.1.rest_0_), channel_id=1, source_target_pairs={{0,96},{16,112},{32,0},{48,16},{64,32},{80,48},{96,64},{112,80},{1... | collective-permute-start | bytes 786440 | tf_op jit(solution)/shard_map/ppermute | solution.py:152
  17.9 23.6 %collective-permute-start.7 = (bf16[1024,128]{1,0:T(8,128)(2,1)S(1)}, bf16[1024,128]{1,0:T(8,128)(2,1)S(1)}, u32[]{:S(2)}, u32[]{:S(2)}) collective-permute-start(bf16[1024,128]{1,0:T(8,128)(2,1)S(1)} %pad_maximum_fusion.1.rest_0_), channel_id=1, source_target_pairs={{0,80},{16,64},{32,112},{48,96},{64,16},{80,0},{96,48},{112,32},{1... | collective-permute-start | bytes 786440 | tf_op jit(solution)/shard_map/ppermute | solution.py:152
  18.0 23.6 %collective-permute-start.6 = (bf16[1024,128]{1,0:T(8,128)(2,1)S(1)}, bf16[1024,128]{1,0:T(8,128)(2,1)S(1)}, u32[]{:S(2)}, u32[]{:S(2)}) collective-permute-start(bf16[1024,128]{1,0:T(8,128)(2,1)S(1)} %pad_maximum_fusion.1.rest_0_), channel_id=1, source_target_pairs={{0,64},{16,80},{32,96},{48,112},{64,0},{80,16},{96,32},{112,48},{1... | collective-permute-start | bytes 786440 | tf_op jit(solution)/shard_map/ppermute | solution.py:152
  21.3 20.3 %collective-permute-start.5 = (bf16[1024,128]{1,0:T(8,128)(2,1)S(1)}, bf16[1024,128]{1,0:T(8,128)(2,1)}, u32[]{:S(2)}, u32[]{:S(2)}) collective-permute-start(bf16[1024,128]{1,0:T(8,128)(2,1)S(1)} %pad_maximum_fusion.1.rest_0_), channel_id=1, source_target_pairs={{0,48},{16,32},{32,80},{48,64},{64,112},{80,96},{96,16},{112,0},{1... | collective-permute-start | bytes 786440 | tf_op jit(solution)/shard_map/ppermute | solution.py:152
  34.7 10.4 %collective-permute-start.4 = (bf16[1024,128]{1,0:T(8,128)(2,1)S(1)}, bf16[1024,128]{1,0:T(8,128)(2,1)}, u32[]{:S(2)}, u32[]{:S(2)}) collective-permute-start(bf16[1024,128]{1,0:T(8,128)(2,1)S(1)} %pad_maximum_fusion.1.rest_0_), channel_id=1, source_target_pairs={{0,32},{16,48},{32,64},{48,80},{64,96},{80,112},{96,0},{112,16},{1... | collective-permute-start | bytes 786440 | tf_op jit(solution)/shard_map/ppermute | solution.py:152
  34.7 10.4 %collective-permute-start.3 = (bf16[1024,128]{1,0:T(8,128)(2,1)S(1)}, bf16[1024,128]{1,0:T(8,128)(2,1)}, u32[]{:S(2)}, u32[]{:S(2)}) collective-permute-start(bf16[1024,128]{1,0:T(8,128)(2,1)S(1)} %pad_maximum_fusion.1.rest_0_), channel_id=1, source_target_pairs={{0,16},{16,0},{32,48},{48,32},{64,80},{80,64},{96,112},{112,96},{1... | collective-permute-start | bytes 786440 | tf_op jit(solution)/shard_map/ppermute | solution.py:152
  100.9 4.0 %collective-permute-start.18 = (bf16[1792,512]{1,0:T(8,128)(2,1)}, bf16[1792,512]{1,0:T(8,128)(2,1)S(1)}, u32[]{:S(2)}, u32[]{:S(2)}) collective-permute-start(bf16[1792,512]{1,0:T(8,128)(2,1)} %get-tuple-element.11), channel_id=1, source_target_pairs={{0,8},{8,0},{1,9},{9,1},{2,10},{10,2},{3,11},{11,3},{4,12},{12,4},... | collective-permute-start | bytes 5505032 | tf_op jit(solution)/shard_map/ppermute | solution.py:200
  108.2 29.4 %all-to-all-start.2 = ((bf16[4,448,512]{2,1,0:T(8,128)(2,1)}), bf16[4,448,512]{2,1,0:T(8,128)(2,1)}, u32[]{:S(2)}, u32[]{:S(2)}) async-start(bf16[4,448,512]{2,1,0:T(8,128)(2,1)} %bitcast.40), calls=%async_computation.2 | async-start | bytes 3670016 | tf_op jit(solution)/shard_map/all_to_all | solution.py:202
  144.0 14.9 %all-to-all-start.3 = ((bf16[16,112,128]{2,1,0:T(8,128)(2,1)}), bf16[16,112,128]{2,1,0:T(8,128)(2,1)}, u32[]{:S(2)}, u32[]{:S(2)}) async-start(bf16[16,112,128]{2,1,0:T(8,128)(2,1)} %bitcast.42), calls=%async_computation.3 | async-start | bytes 917504 | tf_op jit(solution)/shard_map/all_to_all | solution.py:205
  149.3 1.4 collective-permute-start.10
  150.8 40.2 %copy-start.3 = (bf16[1024,128]{1,0:T(8,128)(2,1)}, bf16[1024,128]{1,0:T(8,128)(2,1)S(1)}, u32[]{:S(2)}) copy-start(bf16[1024,128]{1,0:T(8,128)(2,1)S(1)} %pad_maximum_fusion.2.rest_0_) | copy-start | bytes 786436
  150.8 19.8 %collective-permute-start.17 = (bf16[1024,128]{1,0:T(8,128)(2,1)S(1)}, bf16[1024,128]{1,0:T(8,128)(2,1)}, u32[]{:S(2)}, u32[]{:S(2)}) collective-permute-start(bf16[1024,128]{1,0:T(8,128)(2,1)S(1)} %pad_maximum_fusion.2.rest_0_), channel_id=1, source_target_pairs={{0,7},{1,4},{2,5},{3,6},{4,3},{5,0},{6,1},{7,2},{8,15},{9,12},{10,... | collective-permute-start | bytes 786440 | tf_op jit(solution)/shard_map/ppermute | solution.py:152
  154.9 22.8 %collective-permute-start.16 = (bf16[1024,128]{1,0:T(8,128)(2,1)S(1)}, bf16[1024,128]{1,0:T(8,128)(2,1)}, u32[]{:S(2)}, u32[]{:S(2)}) collective-permute-start(bf16[1024,128]{1,0:T(8,128)(2,1)S(1)} %pad_maximum_fusion.2.rest_0_), channel_id=1, source_target_pairs={{0,3},{1,0},{2,1},{3,2},{4,7},{5,4},{6,5},{7,6},{8,11},{9,8},{10,9... | collective-permute-start | bytes 786440 | tf_op jit(solution)/shard_map/ppermute | solution.py:152
  160.8 41.3 %all-to-all-start.4 = ((bf16[16,112,128]{2,1,0:T(8,128)(2,1)}), bf16[16,112,128]{2,1,0:T(8,128)(2,1)}, u32[]{:S(2)}, u32[]{:S(2)}) async-start(bf16[16,112,128]{2,1,0:T(8,128)(2,1)} %broadcast_in_dim.19), calls=%async_computation.4 | async-start | bytes 917504 | tf_op jit(solution)/shard_map/all_to_all | solution.py:208
  165.0 13.3 %collective-permute-start.15 = (bf16[1024,128]{1,0:T(8,128)(2,1)S(1)}, bf16[1024,128]{1,0:T(8,128)(2,1)}, u32[]{:S(2)}, u32[]{:S(2)}) collective-permute-start(bf16[1024,128]{1,0:T(8,128)(2,1)S(1)} %pad_maximum_fusion.2.rest_0_), channel_id=1, source_target_pairs={{0,6},{1,7},{2,4},{3,5},{4,2},{5,3},{6,0},{7,1},{8,14},{9,15},{10,... | collective-permute-start | bytes 786440 | tf_op jit(solution)/shard_map/ppermute | solution.py:152
  167.0 15.7 %collective-permute-start.14 = (bf16[1024,128]{1,0:T(8,128)(2,1)S(1)}, bf16[1024,128]{1,0:T(8,128)(2,1)}, u32[]{:S(2)}, u32[]{:S(2)}) collective-permute-start(bf16[1024,128]{1,0:T(8,128)(2,1)S(1)} %pad_maximum_fusion.2.rest_0_), channel_id=1, source_target_pairs={{0,2},{1,3},{2,0},{3,1},{4,6},{5,7},{6,4},{7,5},{8,10},{9,11},{10,... | collective-permute-start | bytes 786440 | tf_op jit(solution)/shard_map/ppermute | solution.py:152
  169.7 15.8 %collective-permute-start.13 = (bf16[1024,128]{1,0:T(8,128)(2,1)S(1)}, bf16[1024,128]{1,0:T(8,128)(2,1)}, u32[]{:S(2)}, u32[]{:S(2)}) collective-permute-start(bf16[1024,128]{1,0:T(8,128)(2,1)S(1)} %pad_maximum_fusion.2.rest_0_), channel_id=1, source_target_pairs={{0,5},{1,6},{2,7},{3,4},{4,1},{5,2},{6,3},{7,0},{8,13},{9,14},{10,... | collective-permute-start | bytes 786440 | tf_op jit(solution)/shard_map/ppermute | solution.py:152
  170.6 20.4 %collective-permute-start.12 = (bf16[1024,128]{1,0:T(8,128)(2,1)S(1)}, bf16[1024,128]{1,0:T(8,128)(2,1)}, u32[]{:S(2)}, u32[]{:S(2)}) collective-permute-start(bf16[1024,128]{1,0:T(8,128)(2,1)S(1)} %pad_maximum_fusion.2.rest_0_), channel_id=1, source_target_pairs={{0,1},{1,2},{2,3},{3,0},{4,5},{5,6},{6,7},{7,4},{8,9},{9,10},{10,1... | collective-permute-start | bytes 786440 | tf_op jit(solution)/shard_map/ppermute | solution.py:152
  177.6 13.4 %collective-permute-start.11 = (bf16[1024,128]{1,0:T(8,128)(2,1)S(1)}, bf16[1024,128]{1,0:T(8,128)(2,1)}, u32[]{:S(2)}, u32[]{:S(2)}) collective-permute-start(bf16[1024,128]{1,0:T(8,128)(2,1)S(1)} %pad_maximum_fusion.2.rest_0_), channel_id=1, source_target_pairs={{0,4},{1,5},{2,6},{3,7},{4,0},{5,1},{6,2},{7,3},{8,12},{9,13},{10,... | collective-permute-start | bytes 786440 | tf_op jit(solution)/shard_map/ppermute | solution.py:152
  202.1 33.9 %all-to-all-start.1 = ((bf16[16,512,128]{2,1,0:T(8,128)(2,1)}), bf16[16,512,128]{2,1,0:T(8,128)(2,1)}, u32[]{:S(2)}, u32[]{:S(2)}) async-start(bf16[16,512,128]{2,1,0:T(8,128)(2,1)} %cells_back.1), calls=%async_computation.1 | async-start | bytes 4194304 | tf_op jit(solution)/shard_map/all_to_all | solution.py:271
  206.6 31.3 %collective-permute-start.21 = (bf16[1792,128]{1,0:T(8,128)(2,1)}, bf16[1792,128]{1,0:T(8,128)(2,1)}, u32[]{:S(2)}, u32[]{:S(2)}) collective-permute-start(bf16[1792,128]{1,0:T(8,128)(2,1)} %bitcast.19.rest_0_), channel_id=1, source_target_pairs={{0,3},{1,0},{2,1},{3,2},{4,7},{5,4},{6,5},{7,6},{8,11},{9,8},{10,9... | collective-permute-start | bytes 1376264 | tf_op jit(solution)/shard_map/ppermute | solution.py:210
  206.8 31.7 %collective-permute-start.20 = (bf16[1792,128]{1,0:T(8,128)(2,1)}, bf16[1792,128]{1,0:T(8,128)(2,1)}, u32[]{:S(2)}, u32[]{:S(2)}) collective-permute-start(bf16[1792,128]{1,0:T(8,128)(2,1)} %bitcast.19.rest_0_), channel_id=1, source_target_pairs={{0,2},{1,3},{2,0},{3,1},{4,6},{5,7},{6,4},{7,5},{8,10},{9,11},{10,... | collective-permute-start | bytes 1376264 | tf_op jit(solution)/shard_map/ppermute | solution.py:210
  207.4 31.2 %collective-permute-start.19 = (bf16[1792,128]{1,0:T(8,128)(2,1)}, bf16[1792,128]{1,0:T(8,128)(2,1)}, u32[]{:S(2)}, u32[]{:S(2)}) collective-permute-start(bf16[1792,128]{1,0:T(8,128)(2,1)} %bitcast.19.rest_0_), channel_id=1, source_target_pairs={{0,1},{1,2},{2,3},{3,0},{4,5},{5,6},{6,7},{7,4},{8,9},{9,10},{10,1... | collective-permute-start | bytes 1376264 | tf_op jit(solution)/shard_map/ppermute | solution.py:210
  237.9 2.1 collective-permute-start.22
  238.0 2.8 %collective-permute-start.25 = (bf16[1792,128]{1,0:T(8,128)(2,1)}, bf16[1792,128]{1,0:T(8,128)(2,1)}, u32[]{:S(2)}, u32[]{:S(2)}) collective-permute-start(bf16[1792,128]{1,0:T(8,128)(2,1)} %collective-permute-done.21.rest_3_), channel_id=1, source_target_pairs={{0,8},{8,0},{1,9},{9,1},{2,10},{10,2},{3,11},{11,3},{4,12},{12,4},... | collective-permute-start | bytes 1376264 | tf_op jit(solution)/shard_map/ppermute | solution.py:212
  238.5 3.0 %collective-permute-start.24 = (bf16[1792,128]{1,0:T(8,128)(2,1)}, bf16[1792,128]{1,0:T(8,128)(2,1)}, u32[]{:S(2)}, u32[]{:S(2)}) collective-permute-start(bf16[1792,128]{1,0:T(8,128)(2,1)} %collective-permute-done.20.rest_2_), channel_id=1, source_target_pairs={{0,8},{8,0},{1,9},{9,1},{2,10},{10,2},{3,11},{11,3},{4,12},{12,4},... | collective-permute-start | bytes 1376264 | tf_op jit(solution)/shard_map/ppermute | solution.py:212
  238.6 3.5 %collective-permute-start.23 = (bf16[1792,128]{1,0:T(8,128)(2,1)}, bf16[1792,128]{1,0:T(8,128)(2,1)}, u32[]{:S(2)}, u32[]{:S(2)}) collective-permute-start(bf16[1792,128]{1,0:T(8,128)(2,1)} %collective-permute-done.19.rest_1_), channel_id=1, source_target_pairs={{0,8},{8,0},{1,9},{9,1},{2,10},{10,2},{3,11},{11,3},{4,12},{12,4},... | collective-permute-start | bytes 1376264 | tf_op jit(solution)/shard_map/ppermute | solution.py:212
  (15 other events, 136.7 us)

commit v2 on v1

v2 whole, which is shorter than its diff:
```python
import functools

import jax
import jax.numpy as jnp
from jax import lax
from jax.experimental import pallas as pl
from jax.experimental.pallas import tpu as pltpu
from jax.sharding import Mesh, PartitionSpec as P


BF = jnp.bfloat16
F32 = jnp.float32
ROW = ("z", "yh", "core")
COL = ("yl", "x")
SLOTS = 192
SIDE = 64
CHUNK = 32
UNROLL = 8
VMEM_LIMIT = 60 * 1024 * 1024


def silu_grad(value):
    sig = jax.nn.sigmoid(value)
    return sig * (1.0 + value * (1.0 - sig))


def cells_kernel(transposed, off_ref, cnt_ref, place_ref, blk0, blk1, *rest):
    pieces = rest[:8]
    out_refs = rest[8:-5]
    src, held, acc, blk_sem, src_sem = rest[-5:]
    n_chunks = SLOTS // CHUNK
    blocks = (blk0, blk1)

    def copy_of(j, ch):
        at = pl.multiple_of(ch * CHUNK, CHUNK)
        return pltpu.make_async_copy(
            blocks[j].at[pl.ds(at, CHUNK)],
            held.at[j, pl.ds(at, CHUNK)],
            blk_sem.at[j * n_chunks + ch],
        )

    moves = [
        pltpu.make_async_copy(piece, src.at[pl.ds(p * 1024, 1024)], src_sem.at[p])
        for p, piece in enumerate(pieces)
    ]
    for move in moves:
        move.start()
    used = [lax.div(cnt_ref[j] + (CHUNK - 1), CHUNK) for j in range(2)]
    for j in range(2):

        @pl.loop(0, used[j])
        def _(ch):
            copy_of(j, ch).start()

    acc[...] = jnp.zeros_like(acc)
    for move in moves:
        move.wait()
    dims = (((0,), (0,)), ((), ())) if transposed else (((1,), (0,)), ((), ()))
    for j in range(2):
        count = cnt_ref[j]

        @pl.loop(0, used[j])
        def _(ch):
            copy_of(j, ch).wait()
            left = jnp.minimum(count - ch * CHUNK, CHUNK)

            @pl.loop(0, lax.div(left + (UNROLL - 1), UNROLL))
            def _(step):
                base = ch * CHUNK + step * UNROLL
                for u in range(UNROLL):
                    slot = base + u
                    take = pl.multiple_of(off_ref[j * SLOTS + slot], SIDE)
                    put = pl.multiple_of(off_ref[(2 + j) * SLOTS + slot], SIDE)
                    term = lax.dot_general(
                        held[j, slot],
                        src[pl.ds(take, SIDE), :],
                        dims,
                        preferred_element_type=F32,
                    )
                    acc[pl.ds(put, SIDE), :] += term

    if len(out_refs) == 1:
        out_refs[0][...] = acc[: 16 * 512, :].astype(BF).reshape(out_refs[0].shape)
    else:
        for p, out_ref in enumerate(out_refs):
            for h in range(2):
                at = pl.multiple_of(place_ref[2 * p + h], 512)
                out_ref[h * 512 : (h + 1) * 512, :] = acc[pl.ds(at, 512), :].astype(BF)


def cell_products(transposed, offsets, counts, place, blk_own, blk_other, pieces):
    any_spec = pl.BlockSpec(memory_space=pl.ANY)
    smem = pl.BlockSpec(memory_space=pltpu.SMEM)
    n_chunks = SLOTS // CHUNK
    return pl.pallas_call(
        functools.partial(cells_kernel, transposed),
        out_shape=(jax.ShapeDtypeStruct((1024, 128), BF),) * 8
        if transposed
        else jax.ShapeDtypeStruct((16, 512, 128), BF),
        in_specs=[smem] * 3 + [any_spec] * 10,
        out_specs=(pl.BlockSpec(memory_space=pltpu.VMEM),) * 8
        if transposed
        else pl.BlockSpec(memory_space=pltpu.VMEM),
        scratch_shapes=[
            pltpu.VMEM((8192, 128), BF),
            pltpu.VMEM((2, SLOTS, SIDE, SIDE), BF),
            pltpu.VMEM((8192 + SIDE, 128), F32),
            pltpu.SemaphoreType.DMA((2 * n_chunks,)),
            pltpu.SemaphoreType.DMA((8,)),
        ],
        compiler_params=pltpu.CompilerParams(vmem_limit_bytes=VMEM_LIMIT),
        cost_estimate=pl.CostEstimate(
            flops=2 * 2 * SLOTS * SIDE * SIDE * 128, bytes_accessed=10 << 20, transcendentals=0
        ),
        name="cells_back" if transposed else "cells_forward",
    )(offsets, counts, place, blk_own, blk_other, *pieces)


def grads_kernel(half_ref, joined, act_one, cot, gp_one, gp_two, act_two, sum_ref):
    at = pl.multiple_of(half_ref[0] * 512, 512)
    sides = ((joined, gp_one, 0, 512), (act_one, gp_two, 512, 1024), (cot, act_two, 1536, 256))
    for left, right, row, size in sides:
        for part in range(0, size, 256):
            sum_ref[row + part : row + part + 256, :] = lax.dot_general(
                left[:, part : part + 256],
                right[:, pl.ds(at, 512)],
                (((0,), (0,)), ((), ())),
                preferred_element_type=F32,
            ).astype(BF)


def local_grads(half, *operands):
    vm = pl.BlockSpec(memory_space=pltpu.VMEM)
    return pl.pallas_call(
        grads_kernel,
        out_shape=jax.ShapeDtypeStruct((1792, 512), BF),
        in_specs=[pl.BlockSpec(memory_space=pltpu.SMEM)] + [vm] * 6,
        out_specs=vm,
        compiler_params=pltpu.CompilerParams(vmem_limit_bytes=VMEM_LIMIT),
        cost_estimate=pl.CostEstimate(
            flops=512 * 1792 * 1024, bytes_accessed=8 << 20, transcendentals=0
        ),
    )(half.reshape(1), *operands)


def chip_kernel(z_ref, own, got, *out_refs):
    for k, out_ref in enumerate(out_refs):
        at = pl.multiple_of(lax.rem(z_ref[0] + k, 4) * 448, 64)
        rows = pl.ds(at, 448)
        out_ref[...] = (own[rows, :].astype(F32) + got[rows, :].astype(F32)).astype(BF)


def chip_sum(z, own, got):
    vm = pl.BlockSpec(memory_space=pltpu.VMEM)
    return pl.pallas_call(
        chip_kernel,
        out_shape=(jax.ShapeDtypeStruct((448, 512), BF),) * 4,
        in_specs=[pl.BlockSpec(memory_space=pltpu.SMEM), vm, vm],
        out_specs=(vm,) * 4,
        cost_estimate=pl.CostEstimate(flops=1 << 20, bytes_accessed=6 << 20, transcendentals=0),
        name="chip_sum",
    )(z.reshape(1), own, got)


def quarter_kernel(*refs):
    out_ref = refs[-1]
    total = refs[0][...].astype(F32)
    for ref in refs[1:-1]:
        total = total + ref[...].astype(F32)
    for row in range(4):
        for lane in range(4):
            out_ref[row * 4 + lane] = total[
                row * 112 : (row + 1) * 112, lane * 128 : (lane + 1) * 128
            ].astype(BF)


def quarter_sum(parts):
    vm = pl.BlockSpec(memory_space=pltpu.VMEM)
    return pl.pallas_call(
        quarter_kernel,
        out_shape=jax.ShapeDtypeStruct((16, 112, 128), BF),
        in_specs=[vm] * len(parts),
        out_specs=vm,
        cost_estimate=pl.CostEstimate(flops=1 << 20, bytes_accessed=3 << 20, transcendentals=0),
        name="quarter_sum",
    )(*parts)


def chunk_kernel(parts, out_ref):
    total = jnp.sum(parts[...].astype(F32), axis=0).astype(BF)
    for k in range(16):
        out_ref[k] = total


def chunk_sum(parts):
    vm = pl.BlockSpec(memory_space=pltpu.VMEM)
    return pl.pallas_call(
        chunk_kernel,
        out_shape=jax.ShapeDtypeStruct((16, 112, 128), BF),
        in_specs=[vm],
        out_specs=vm,
        cost_estimate=pl.CostEstimate(flops=1 << 20, bytes_accessed=1 << 20, transcendentals=0),
        name="chunk_sum",
    )(parts)


def step_perm(axes, p):
    big, small = p >> 1, p & 1
    perm = []
    for i in range(8):
        if axes == ("z", "yh"):
            to = (((i >> 1) + big) % 4) * 2 + ((i & 1) ^ small)
        else:
            to = ((i >> 2) ^ small) * 4 + ((i & 3) + big) % 4
        perm.append((i, to))
    return perm


def send_steps(pieces, axes):
    got = [pieces[0]]
    for p in range(1, 8):
        got.append(lax.ppermute(pieces[p], axes, step_perm(axes, p)))
    return got


def node_kernel(*refs):
    mine_ref, yours_ref = refs[-2:]
    for rows, out_ref in ((slice(0, 512), mine_ref), (slice(512, 1024), yours_ref)):
        total = refs[0][rows, :].astype(F32)
        for ref in refs[1:-2]:
            total = total + ref[rows, :].astype(F32)
        out_ref[...] = total.astype(out_ref.dtype)


def node_sum(parts):
    vm = pl.BlockSpec(memory_space=pltpu.VMEM)
    return pl.pallas_call(
        node_kernel,
        out_shape=(
            jax.ShapeDtypeStruct((512, 128), F32),
            jax.ShapeDtypeStruct((512, 128), BF),
        ),
        in_specs=[vm] * len(parts),
        out_specs=(vm, vm),
        cost_estimate=pl.CostEstimate(flops=1 << 20, bytes_accessed=3 << 20, transcendentals=0),
        name="node_sum",
    )(*parts)


def halves(value, core):
    left, right = value[:, :128], value[:, 128:]
    first = core == 0
    mine = jnp.where(first, left, right)
    yours = jnp.where(first, right, left)
    got = lax.ppermute(yours, "core", [(0, 1), (1, 0)])
    return jnp.concatenate([mine, got], axis=0)


def finish_kernel(lane_ref, own, other, *rest):
    outs = rest[-10:-7]
    scratch, sems = rest[-7:-1], rest[-1]
    moves = []
    for group, piece in enumerate((own, other)):
        full = piece[...].astype(F32) * (1.0 / 256.0)
        lane = pl.multiple_of(lane_ref[group], 128)
        held = scratch[group * 3 : group * 3 + 3]
        held[0][...] = full[:512]
        held[1][...] = full[512:1536]
        held[2][...] = full[1536:].T
        targets = (
            outs[0].at[:, pl.ds(lane, 128)],
            outs[1].at[:, pl.ds(lane, 128)],
            outs[2].at[pl.ds(lane, 128), :],
        )
        for k in range(3):
            move = pltpu.make_async_copy(held[k], targets[k], sems.at[group * 3 + k])
            move.start()
            moves.append(move)
    for move in moves:
        move.wait()


def finish_grads(lanes, own, other, outs):
    vm = pl.BlockSpec(memory_space=pltpu.VMEM)
    any_spec = pl.BlockSpec(memory_space=pl.ANY)
    held = [
        pltpu.VMEM((512, 128), F32),
        pltpu.VMEM((1024, 128), F32),
        pltpu.VMEM((128, 256), F32),
    ]
    return pl.pallas_call(
        finish_kernel,
        out_shape=(
            jax.ShapeDtypeStruct((512, 1024), F32),
            jax.ShapeDtypeStruct((1024, 1024), F32),
            jax.ShapeDtypeStruct((1024, 256), F32),
        ),
        in_specs=[pl.BlockSpec(memory_space=pltpu.SMEM), vm, vm] + [any_spec] * len(outs),
        out_specs=(any_spec,) * 3,
        scratch_shapes=held + held + [pltpu.SemaphoreType.DMA((6,))],
        input_output_aliases={3 + k: k for k in range(len(outs))},
        cost_estimate=pl.CostEstimate(flops=1 << 20, bytes_accessed=3 << 20, transcendentals=0),
        name="finish_grads",
    )(lanes, own, other, *outs)


def sum_grads(core, operands):
    x, z = lax.axis_index("x"), lax.axis_index("z")
    swap = [(0, 1), (1, 0)]
    other = local_grads(1 - core, *operands)
    got = lax.ppermute(other, "core", swap)
    own = local_grads(core, *operands)
    quarters = chip_sum(z, own, got)
    parts = [quarters[0]]
    for k in range(1, 4):
        parts.append(lax.ppermute(quarters[k], "z", [(i, (i + k) % 4) for i in range(4)]))
    part = quarter_sum(parts)
    part = lax.all_to_all(part, ("yh", "yl", "x"), 0, 0, tiled=True)
    lanes = lax.all_to_all(chunk_sum(part), ("z", "yh", "yl"), 0, 0, tiled=True)
    lanes = lanes.reshape(1792, 128)
    outs = ()
    for k in range(4):
        piece = lanes
        if k:
            piece = lax.ppermute(lanes, "x", [(i, (i + k) % 4) for i in range(4)])
        place = ((x - k) & 3) * 128
        at = jnp.stack([core * 512 + place, (1 - core) * 512 + place])
        outs = finish_grads(at, piece, lax.ppermute(piece, "core", swap), outs)
    return outs


def shards(features, blocks, block_rows, block_cols, block_count, w_in, w_mid, w_out, cotangent):
    core = lax.axis_index("core")
    z, yh = lax.axis_index("z"), lax.axis_index("yh")
    yl, x = lax.axis_index("yl"), lax.axis_index("x")
    swap = [(0, 1), (1, 0)]
    blk_own = blocks[0, 0]
    meta = jnp.concatenate(
        [block_rows[0, 0], block_cols[0, 0], jnp.broadcast_to(block_count[0, 0], (128,))]
    )
    meta_other = lax.ppermute(meta, "core", swap)
    blk_other = lax.ppermute(blk_own, "core", swap)

    both = jnp.stack([meta, meta_other])
    rows, cols, count = both[:, :SLOTS], both[:, SLOTS : 2 * SLOTS], both[:, 2 * SLOTS]
    live = jnp.arange(SLOTS, dtype=jnp.int32)[None, :] < count[:, None]
    cell_core = jnp.stack([core, 1 - core])[:, None]
    spare = 16 * 512
    grp = cols >> 3
    step = (((z - (grp >> 2)) & 3) * 2) + (((grp >> 1) & 1) ^ yh)
    col_at = step * 1024 + ((grp & 1) ^ core) * 512 + (cols & 7) * SIDE
    row_to = jnp.where(live, cell_core * 4096 + rows * SIDE, spare)
    fwd_off = jnp.concatenate([col_at, row_to]).reshape(4 * SLOTS)
    own8 = rows >> 3
    step = (((x - own8) & 3) * 2) + ((own8 >> 2) ^ yl)
    row_at = step * 1024 + jnp.arange(2, dtype=jnp.int32)[:, None] * 512 + (rows & 7) * SIDE
    col_to = jnp.where(live, cols * SIDE, spare)
    bwd_off = jnp.concatenate([row_at, col_to]).reshape(4 * SLOTS)

    p = jnp.arange(16, dtype=jnp.int32)
    place = (((z + (p >> 2)) & 3) * 4 + (yh ^ ((p >> 1) & 1)) * 2 + (core ^ (p & 1))) * 512
    shard = halves(features, core)
    pieces = send_steps([shard] * 8, ("z", "yh"))
    blk_own, _ = lax.optimization_barrier((blk_own, shard))
    cells = cell_products(False, fwd_off, count, place, blk_own, blk_other, pieces)
    cells = lax.all_to_all(cells, ("core", "yl", "x"), 0, 0, tiled=True)
    sums = jnp.sum(cells.reshape(2, 8, 512, 128).astype(F32), axis=1).astype(BF)
    aggregated = jnp.concatenate([sums[0], sums[1]], axis=1)

    joined = jnp.concatenate([features, aggregated], axis=1)
    pre_one = jnp.dot(joined, w_in, preferred_element_type=F32)
    act_one = jax.nn.silu(pre_one).astype(BF)
    pre_two = jnp.dot(act_one, w_mid, preferred_element_type=F32)
    act_two = jax.nn.silu(pre_two).astype(BF)
    updated = (
        features.astype(F32) + jnp.dot(act_two, w_out, preferred_element_type=F32)
    ).astype(BF)
    grad_pre_two = (
        jnp.dot(cotangent, w_out.T, preferred_element_type=F32) * silu_grad(pre_two)
    ).astype(BF)
    grad_pre_one = (
        jnp.dot(grad_pre_two, w_mid.T, preferred_element_type=F32) * silu_grad(pre_one)
    ).astype(BF)
    grad_joined = jnp.dot(grad_pre_one, w_in.T, preferred_element_type=F32)
    direct = cotangent.astype(F32) + grad_joined[:, :256]
    grad_agg = grad_joined[:, 256:].astype(BF)

    pieces = send_steps([halves(grad_agg, core)] * 8, COL)
    operands = (joined, act_one, cotangent, grad_pre_one, grad_pre_two, act_two)
    grad_in, grad_mid, grad_out = sum_grads(core, operands)
    back = cell_products(True, bwd_off, count, place, blk_own, blk_other, pieces)
    mine, yours = node_sum(send_steps(back, ("z", "yh")))
    got = lax.ppermute(yours, "core", swap).astype(F32)
    first = core == 0
    relaid = jnp.concatenate([jnp.where(first, mine, got), jnp.where(first, got, mine)], axis=1)
    grad_nodes = (direct + relaid).astype(BF)
    return updated, grad_nodes, grad_in, grad_mid, grad_out


def solution(mesh):
    fine = Mesh(mesh.devices.reshape(4, 2, 2, 2, 4), ROW + COL)
    nodes = P(ROW + COL, None)
    placed = (
        nodes,
        P(ROW, COL, None, None, None),
        P(ROW, COL, None),
        P(ROW, COL, None),
        P(ROW, COL),
        P(),
        P(),
        P(),
        nodes,
    )

    return jax.shard_map(
        shards,
        mesh=fine,
        in_specs=placed,
        out_specs=(nodes, nodes, P(), P(), P()),
        check_vma=False,
    )
```

time: 250 us -> 259 us (1.036)
  starting transfers between devices: 49.1 us -> 85.6 us
  waiting for transfers between devices: 89.6 us -> 59.2 us
  Pallas kernels: 32.4 us -> 44.3 us
  other arithmetic: 14.2 us -> 7.12 us
    all_to_all x3 -> x1, waiting for transfers between devices: 45.9 us -> 0.01 us  [sum_grads(): lanes = lax.all_to_all(chunk_sum(part), ('z', 'yh', 'yl'), 0, 0, tiled=True)]
    ppermute x22 -> x33, starting transfers between devices: 30.1 us -> 74.8 us  [the longest x21 43.3 us: send_steps(): got.append(lax.ppermute(pieces[p], axes, step_perm(axes, p)))]
    ppermute x22 -> x33, waiting for transfers between devices: 37.9 us -> 58.4 us  [the longest x21 32.9 us: send_steps(): got.append(lax.ppermute(pieces[p], axes, step_perm(axes, p)))]
    pallas_call x3 -> x8, Pallas kernels: 26.5 us -> 34.3 us  [the longest x2 14.2 us: cell_products(): pl.pallas_call(functools.partial(cells_kernel, transposed), out_shape=(ja...]
    all_to_all x3 -> x1, starting transfers between devices: 13.9 us -> 6.43 us  [sum_grads(): lanes = lax.all_to_all(chunk_sum(part), ('z', 'yh', 'yl'), 0, 0, tiled=True)]
    reduce_sum x3 -> x0, other arithmetic: 5.7 us -> none  [the longest x2 3.76 us: sum_grads(): part = jnp.sum(part.astype(F32), axis=0).astype(BF)]
    pallas_call x1 -> x4, Pallas kernels: 5.89 us -> 10.1 us  [finish_grads(): pl.pallas_call(finish_kernel, out_shape=(jax.ShapeDtypeStruct((512, 1024)...]
    convert_element_type x1 -> x0, other arithmetic: 3.27 us -> none  [sum_grads(): chip = (own.astype(F32) + got.astype(F32)).astype(BF)]
  transfers between devices with their start and end apart: 30 -> 39, of which waited for: 16 -> 10; matrix products, arithmetic and copies ran while one was open for 10% -> 9% of each run, Pallas kernels for 4% -> 10%
where the time goes in v2:
time: 259 us; the launch traced here: 257 us
  starting transfers between devices  85.6 us (33%)
  waiting for transfers between devices  59.2 us (23%)
  Pallas kernels  44.3 us (17%)
  blocking collectives  31.7 us (12%)
  local copies, waits for them, and re-layouts  14.7 us (6%)
  matrix products  12.4 us (5%)
  other arithmetic  7.12 us (3%)
    ppermute x21, starting transfers between devices, send_steps(): got.append(lax.ppermute(pieces[p], axes, step_perm(axes, p)))  43.3 us
    ppermute x21, waiting for transfers between devices, send_steps(): got.append(lax.ppermute(pieces[p], axes, step_perm(axes, p)))  32.9 us
    all_to_all x1, blocking collectives, shards(): cells = lax.all_to_all(cells, ('core', 'yl', 'x'), 0, 0, tiled=True)  31.7 us
    ppermute x3, starting transfers between devices, sum_grads(): piece = lax.ppermute(lanes, 'x', [(i, (i + k) % 4) for i in range(4)])  19.9 us
    ppermute x3, waiting for transfers between devices, sum_grads(): lax.ppermute(quarters[k], 'z', [(i, (i + k) % 4) for i in range(4)])  15.3 us
    pallas_call x2, Pallas kernels, cell_products(): pl.pallas_call(functools.partial(cells_kernel, transposed), out_shape=(ja...  14.2 us
    ppermute x3, starting transfers between devices, sum_grads(): lax.ppermute(quarters[k], 'z', [(i, (i + k) % 4) for i in range(4)])  10.6 us
    ppermute x3, waiting for transfers between devices, sum_grads(): piece = lax.ppermute(lanes, 'x', [(i, (i + k) % 4) for i in range(4)])  10.3 us
  transfers between devices with their start and end apart: 39, of which 10 were waited for; matrix products, arithmetic and copies ran while one was open for 9% of the time, Pallas kernels for 10%

profile of v2, /device:TPU:0, one launch (start us, length us, event | category | flops | bytes accessed | tf_op | source)
XLA Modules:
  0.0 257.0 jit_solution(3660576824102262326)
XLA Ops:
  5.3 6.8 %collective-permute-start.9 = (bf16[1024,128]{1,0:T(8,128)(2,1)S(1)}, bf16[1024,128]{1,0:T(8,128)(2,1)S(1)}, u32[]{:S(2)}, u32[]{:S(2)}) collective-permute-start(bf16[1024,128]{1,0:T(8,128)(2,1)S(1)} %pad_maximum_fusion.1.rest_0_), channel_id=1, source_target_pairs={{0,112},{16,96},{32,16},{48,0},{64,48},{80,32},{96,80},{112,64},{1... | collective-permute-start | bytes 786440 | tf_op jit(solution)/shard_map/ppermute | solution.py:222
  12.6 5.1 %copy.26 = bf16[1,1,192,64,64]{4,3,2,1,0:T(8,128)(2,1)} copy(bf16[1,1,192,64,64]{2,4,3,1,0:T(8,128)(2,1)} %param.10) | data formatting | bytes 3145728 | tf_op args[1]
  18.0 3.3 %collective-permute-start.6 = (bf16[1024,128]{1,0:T(8,128)(2,1)S(1)}, bf16[1024,128]{1,0:T(8,128)(2,1)S(1)}, u32[]{:S(2)}, u32[]{:S(2)}) collective-permute-start(bf16[1024,128]{1,0:T(8,128)(2,1)S(1)} %pad_maximum_fusion.1.rest_0_), channel_id=1, source_target_pairs={{0,64},{16,80},{32,96},{48,112},{64,0},{80,16},{96,32},{112,48},{1... | collective-permute-start | bytes 786440 | tf_op jit(solution)/shard_map/ppermute | solution.py:222
  21.3 4.3 %collective-permute-start.5 = (bf16[1024,128]{1,0:T(8,128)(2,1)S(1)}, bf16[1024,128]{1,0:T(8,128)(2,1)}, u32[]{:S(2)}, u32[]{:S(2)}) collective-permute-start(bf16[1024,128]{1,0:T(8,128)(2,1)S(1)} %pad_maximum_fusion.1.rest_0_), channel_id=1, source_target_pairs={{0,48},{16,32},{32,80},{48,64},{64,112},{80,96},{96,16},{112,0},{1... | collective-permute-start | bytes 786440 | tf_op jit(solution)/shard_map/ppermute | solution.py:222
  25.5 9.1 %collective-permute-done.8.rest_6_ = bf16[1024,128]{1,0:T(8,128)(2,1)S(1)} collective-permute-done((bf16[1024,128]{1,0:T(8,128)(2,1)S(1)}, bf16[1024,128]{1,0:T(8,128)(2,1)S(1)}, u32[]{:S(2)}, u32[]{:S(2)}) %collective-permute-start.8) | collective-permute-done | bytes 262176 | tf_op jit(solution)/shard_map/ppermute | solution.py:222
  36.3 5.2 %copy.28.blk1 = bf16[192,64,64]{2,1,0:T(8,128)(2,1)} copy(bf16[192,64,64]{0,2,1:T(8,128)(2,1)} %collective-permute-done.2) | data formatting | bytes 3145728 | tf_op jit(solution)/shard_map/ppermute | solution.py:342
  41.6 3.4 %collective-permute-done.4.rest_2_ = bf16[1024,128]{1,0:T(8,128)(2,1)} collective-permute-done((bf16[1024,128]{1,0:T(8,128)(2,1)S(1)}, bf16[1024,128]{1,0:T(8,128)(2,1)}, u32[]{:S(2)}, u32[]{:S(2)}) %collective-permute-start.4) | collective-permute-done | bytes 262176 | tf_op jit(solution)/shard_map/ppermute | solution.py:222
  45.0 6.7 %cells_forward.1 = bf16[16,512,128]{2,1,0:T(8,128)(2,1)} custom-call(s32[768]{0:T(1024)} %reshape.50.off_ref, s32[2]{0:T(128)} %copy-done.23, s32[16]{0:T(128)} %add_multiply_fusion.1.place_ref, bf16[192,64,64]{2,1,0:T(8,128)(2,1)} %bitcast.37, bf16[192,64,64]{2,1,0:T(8,128)(2,1)} %copy.28.blk1, bf16[1024,128]{1,0:T(8,128)(2,1)} %copy-done.10, ...), custom_call_target="tpu_custom_call" | custom-call | flops 402653184 | bytes 10485760 | tf_op jit(solution)/shard_map/cells_forward/pallas_call | solution.py:95
  51.8 31.7 %all_to_all.15 = bf16[16,512,128]{2,1,0:T(8,128)(2,1)S(1)} all-to-all(bf16[16,512,128]{2,1,0:T(8,128)(2,1)} %cells_forward.1), channel_id=1, replica_groups=mesh['z'=4,'yh'=2,'core'=2,'yl'=2,'x'=4] {'core','yl','x'}, dimensions={0} | all-to-all | bytes 4194304 | tf_op jit(solution)/shard_map/all_to_all | solution.py:366
  89.7 2.7 %multiply_convert_fusion.gp_one = bf16[512,1024]{1,0:T(8,128)(2,1)} fusion(f32[512,1024]{1,0:T(8,128)S(1)} %get-tuple-element.72, bf16[512,1024]{1,0:T(8,128)(2,1)S(1)} %multiply_convert_fusion.1.gp_two, bf16[1024,1024]{1,0:T(8,128)(2,1)S(1)} %copy-done), kind=kOutput, calls=%fused_computation.1 | convolution fusion | flops 1078460416 | bytes 6291456 | tf_op jit(solution)/shard_map/dot_general | solution.py:382
  92.4 4.8 %shard_map.129 = bf16[1792,512]{1,0:T(8,128)(2,1)} custom-call(s32[1]{0:T(128)} %bitcast.6.half_ref, bf16[512,512]{1,0:T(8,128)(2,1)} %pad_maximum_fusion.joined, bf16[512,1024]{1,0:T(8,128)(2,1)} %copy-done.3, bf16[512,256]{1,0:T(8,128)(2,1)} %cot.3, bf16[512,1024]{1,0:T(8,128)(2,1)} %multiply_convert_fusion.gp_one, bf16[512,1024]{1,0:T(8,128)(2,1)} %copy-done.4, ...), custom_call_target="tpu_custom_call" | custom-call | flops 939524096 | bytes 8388608 | tf_op jit(solution)/shard_map/pallas_call | solution.py:134
  97.7 4.8 %shard_map.128.own = bf16[1792,512]{1,0:T(8,128)(2,1)} custom-call(s32[1]{0:T(128)} %bitcast.5.half_ref, bf16[512,512]{1,0:T(8,128)(2,1)} %pad_maximum_fusion.joined, bf16[512,1024]{1,0:T(8,128)(2,1)} %copy-done.3, bf16[512,256]{1,0:T(8,128)(2,1)} %cot.3, bf16[512,1024]{1,0:T(8,128)(2,1)} %multiply_convert_fusion.gp_one, bf16[512,1024]{1,0:T(8,128)(2,1)} %copy-done.4, ...), custom_call_target="tpu_custom_call" | custom-call | flops 939524096 | bytes 8388608 | tf_op jit(solution)/shard_map/pallas_call | solution.py:134
  102.4 3.7 %chip_sum.1 = (bf16[448,512]{1,0:T(8,128)(2,1)}, bf16[448,512]{1,0:T(8,128)(2,1)}, bf16[448,512]{1,0:T(8,128)(2,1)}, bf16[448,512]{1,0:T(8,128)(2,1)}) custom-call(s32[1]{0:T(128)} %bitcast.14.z_ref, bf16[1792,512]{1,0:T(8,128)(2,1)} %shard_map.128.own, bf16[1792,512]{1,0:T(8,128)(2,1)} %collective-permute-done.26.got), custom_call_target="tpu_custom_call" | custom-call | flops 1048576 | bytes 6291456 | tf_op jit(solution)/shard_map/chip_sum/pallas_call | solution.py:155
  106.2 3.4 %collective-permute-start.27 = (bf16[448,512]{1,0:T(8,128)(2,1)}, bf16[448,512]{1,0:T(8,128)(2,1)}, u32[]{:S(2)}, u32[]{:S(2)}) collective-permute-start(bf16[448,512]{1,0:T(8,128)(2,1)} %get-tuple-element.44), channel_id=1, source_target_pairs={{0,32},{32,64},{64,96},{96,0},{1,33},{33,65},{65,97},{97,1},{2,34}... | collective-permute-start | bytes 1376264 | tf_op jit(solution)/shard_map/ppermute | solution.py:316
  109.5 4.6 %collective-permute-start.28 = (bf16[448,512]{1,0:T(8,128)(2,1)}, bf16[448,512]{1,0:T(8,128)(2,1)}, u32[]{:S(2)}, u32[]{:S(2)}) collective-permute-start(bf16[448,512]{1,0:T(8,128)(2,1)} %get-tuple-element.45), channel_id=1, source_target_pairs={{0,64},{32,96},{64,0},{96,32},{1,65},{33,97},{65,1},{97,33},{2,66}... | collective-permute-start | bytes 1376264 | tf_op jit(solution)/shard_map/ppermute | solution.py:316
  114.2 2.6 %collective-permute-start.29 = (bf16[448,512]{1,0:T(8,128)(2,1)}, bf16[448,512]{1,0:T(8,128)(2,1)}, u32[]{:S(2)}, u32[]{:S(2)}) collective-permute-start(bf16[448,512]{1,0:T(8,128)(2,1)} %get-tuple-element.46), channel_id=1, source_target_pairs={{0,96},{32,0},{64,32},{96,64},{1,97},{33,1},{65,33},{97,65},{2,98}... | collective-permute-start | bytes 1376264 | tf_op jit(solution)/shard_map/ppermute | solution.py:316
  116.8 2.9 %fusion.11 = (bf16[512,512]{1,0:T(8,128)(2,1)S(1)}, f32[512,512]{1,0:T(8,128)}) fusion(bf16[512,1024]{1,0:T(8,128)(2,1)S(1)} %copy-done.1, bf16[512,1024]{1,0:T(8,128)(2,1)} %param.14), kind=kOutput, calls=%fused_computation.51 | convolution fusion | flops 537133056 | bytes 3670016 | tf_op jit(solution)/shard_map/dot_general | solution.py:384
  121.8 13.3 %collective-permute-done.28.refs_2_ = bf16[448,512]{1,0:T(8,128)(2,1)} collective-permute-done((bf16[448,512]{1,0:T(8,128)(2,1)}, bf16[448,512]{1,0:T(8,128)(2,1)}, u32[]{:S(2)}, u32[]{:S(2)}) %collective-permute-start.28) | collective-permute-done | bytes 458784 | tf_op jit(solution)/shard_map/ppermute | solution.py:316
  137.6 3.6 %all-to-all-start.1 = ((bf16[16,112,128]{2,1,0:T(8,128)(2,1)}), bf16[16,112,128]{2,1,0:T(8,128)(2,1)S(1)}, u32[]{:S(2)}, u32[]{:S(2)}) async-start(bf16[16,112,128]{2,1,0:T(8,128)(2,1)} %quarter_sum.1), calls=%async_computation.1 | async-start | bytes 917504 | tf_op jit(solution)/shard_map/all_to_all | solution.py:318
  141.2 4.0 %collective-permute-start.17 = (bf16[1024,128]{1,0:T(8,128)(2,1)S(1)}, bf16[1024,128]{1,0:T(8,128)(2,1)S(1)}, u32[]{:S(2)}, u32[]{:S(2)}) collective-permute-start(bf16[1024,128]{1,0:T(8,128)(2,1)S(1)} %pad_maximum_fusion.2.rest_0_), channel_id=1, source_target_pairs={{0,7},{1,4},{2,5},{3,6},{4,3},{5,0},{6,1},{7,2},{8,15},{9,12},{10,... | collective-permute-start | bytes 786440 | tf_op jit(solution)/shard_map/ppermute | solution.py:222
  146.3 3.3 %collective-permute-start.14 = (bf16[1024,128]{1,0:T(8,128)(2,1)S(1)}, bf16[1024,128]{1,0:T(8,128)(2,1)}, u32[]{:S(2)}, u32[]{:S(2)}) collective-permute-start(bf16[1024,128]{1,0:T(8,128)(2,1)S(1)} %pad_maximum_fusion.2.rest_0_), channel_id=1, source_target_pairs={{0,2},{1,3},{2,0},{3,1},{4,6},{5,7},{6,4},{7,5},{8,10},{9,11},{10,... | collective-permute-start | bytes 786440 | tf_op jit(solution)/shard_map/ppermute | solution.py:222
  151.7 9.0 %collective-permute-done.17.rest_7_ = bf16[1024,128]{1,0:T(8,128)(2,1)S(1)} collective-permute-done((bf16[1024,128]{1,0:T(8,128)(2,1)S(1)}, bf16[1024,128]{1,0:T(8,128)(2,1)S(1)}, u32[]{:S(2)}, u32[]{:S(2)}) %collective-permute-start.17) | collective-permute-done | bytes 262176 | tf_op jit(solution)/shard_map/ppermute | solution.py:222
  160.7 3.4 %collective-permute-done.16.rest_6_ = bf16[1024,128]{1,0:T(8,128)(2,1)S(1)} collective-permute-done((bf16[1024,128]{1,0:T(8,128)(2,1)S(1)}, bf16[1024,128]{1,0:T(8,128)(2,1)S(1)}, u32[]{:S(2)}, u32[]{:S(2)}) %collective-permute-start.16) | collective-permute-done | bytes 262176 | tf_op jit(solution)/shard_map/ppermute | solution.py:222
  168.9 6.4 %all-to-all-start.2 = ((bf16[16,112,128]{2,1,0:T(8,128)(2,1)}), bf16[16,112,128]{2,1,0:T(8,128)(2,1)}, u32[]{:S(2)}, u32[]{:S(2)}) async-start(bf16[16,112,128]{2,1,0:T(8,128)(2,1)} %chunk_sum.1), calls=%async_computation.2 | async-start | bytes 917504 | tf_op jit(solution)/shard_map/all_to_all | solution.py:319
  176.1 7.4 %cells_back.1 = (bf16[1024,128]{1,0:T(8,128)(2,1)}, bf16[1024,128]{1,0:T(8,128)(2,1)}, bf16[1024,128]{1,0:T(8,128)(2,1)}, bf16[1024,128]{1,0:T(8,128)(2,1)}, bf1...) custom-call(s32[768]{0:T(1024)} %reshape.52.off_ref, ...), custom_call_target="tpu_custom_call" | custom-call | flops 402653184 | bytes 10485760 | tf_op jit(solution)/shard_map/cells_back/pallas_call | solution.py:95
  185.6 3.1 %collective-permute-start.19 = (bf16[1024,128]{1,0:T(8,128)(2,1)}, bf16[1024,128]{1,0:T(8,128)(2,1)}, u32[]{:S(2)}, u32[]{:S(2)}) collective-permute-start(bf16[1024,128]{1,0:T(8,128)(2,1)} %get-tuple-element.35), channel_id=1, source_target_pairs={{0,32},{16,48},{32,64},{48,80},{64,96},{80,112},{96,0},{112,16},{1... | collective-permute-start | bytes 786440 | tf_op jit(solution)/shard_map/ppermute | solution.py:222
  188.7 3.3 %collective-permute-start.20 = (bf16[1024,128]{1,0:T(8,128)(2,1)}, bf16[1024,128]{1,0:T(8,128)(2,1)}, u32[]{:S(2)}, u32[]{:S(2)}) collective-permute-start(bf16[1024,128]{1,0:T(8,128)(2,1)} %get-tuple-element.36), channel_id=1, source_target_pairs={{0,48},{16,32},{32,80},{48,64},{64,112},{80,96},{96,16},{112,0},{1... | collective-permute-start | bytes 786440 | tf_op jit(solution)/shard_map/ppermute | solution.py:222
  192.5 5.9 %collective-permute-start.22 = (bf16[1024,128]{1,0:T(8,128)(2,1)}, bf16[1024,128]{1,0:T(8,128)(2,1)}, u32[]{:S(2)}, u32[]{:S(2)}) collective-permute-start(bf16[1024,128]{1,0:T(8,128)(2,1)} %get-tuple-element.38), channel_id=1, source_target_pairs={{0,80},{16,64},{32,112},{48,96},{64,16},{80,0},{96,48},{112,32},{1... | collective-permute-start | bytes 786440 | tf_op jit(solution)/shard_map/ppermute | solution.py:222
  199.0 7.8 %collective-permute-done.19.refs_2_ = bf16[1024,128]{1,0:T(8,128)(2,1)} collective-permute-done((bf16[1024,128]{1,0:T(8,128)(2,1)}, bf16[1024,128]{1,0:T(8,128)(2,1)}, u32[]{:S(2)}, u32[]{:S(2)}) %collective-permute-start.19) | collective-permute-done | bytes 262176 | tf_op jit(solution)/shard_map/ppermute | solution.py:222
  207.5 15.7 %collective-permute-start.34 = (bf16[1792,128]{1,0:T(8,128)(2,1)}, bf16[1792,128]{1,0:T(8,128)(2,1)}, u32[]{:S(2)}, u32[]{:S(2)}) collective-permute-start(bf16[1792,128]{1,0:T(8,128)(2,1)} %bitcast.15.own), channel_id=1, source_target_pairs={{0,1},{1,2},{2,3},{3,0},{4,5},{5,6},{6,7},{7,4},{8,9},{9,10},{10,1... | collective-permute-start | bytes 1376264 | tf_op jit(solution)/shard_map/ppermute | solution.py:325
  223.2 4.2 %collective-permute-start.30 = (bf16[1792,128]{1,0:T(8,128)(2,1)}, bf16[1792,128]{1,0:T(8,128)(2,1)}, u32[]{:S(2)}, u32[]{:S(2)}) collective-permute-start(bf16[1792,128]{1,0:T(8,128)(2,1)} %bitcast.15.own), channel_id=1, source_target_pairs={{0,3},{1,0},{2,1},{3,2},{4,7},{5,4},{6,5},{7,6},{8,11},{9,8},{10,9... | collective-permute-start | bytes 1376264 | tf_op jit(solution)/shard_map/ppermute | solution.py:325
  234.0 7.9 %collective-permute-done.32.own = bf16[1792,128]{1,0:T(8,128)(2,1)} collective-permute-done((bf16[1792,128]{1,0:T(8,128)(2,1)}, bf16[1792,128]{1,0:T(8,128)(2,1)}, u32[]{:S(2)}, u32[]{:S(2)}) %collective-permute-start.32) | collective-permute-done | bytes 458784 | tf_op jit(solution)/shard_map/ppermute | solution.py:325
  (142 shorter events, 51.2 us)
Async XLA Ops:
  0.6 34.0 %collective-permute-start.2 = (bf16[192,64,64]{0,2,1:T(8,128)(2,1)}, bf16[192,64,64]{0,2,1:T(8,128)(2,1)}, u32[]{:S(2)}, u32[]{:S(2)}) collective-permute-start(bf16[192,64,64]{0,2,1:T(8,128)(2,1)} %bitcast.39), channel_id=1, source_target_pairs={{0,8},{8,0},{1,9},{9,1},{2,10},{10,2},{3,11},{11,3},{4,12},{12,4},... | collective-permute-start | bytes 4718600 | tf_op jit(solution)/shard_map/ppermute | solution.py:342
  2.3 15.4 %collective-permute-start = (s32[512]{0:T(512)S(1)}, s32[512]{0:T(512)S(1)}, u32[]{:S(2)}, u32[]{:S(2)}) collective-permute-start(s32[512]{0:T(512)S(1)} %pad_add_fusion.3), channel_id=1, source_target_pairs={{0,8},{8,0},{1,9},{9,1},{2,10},{10,2},{3,11},{11,3},{4,12},{12,4},... | collective-permute-start | bytes 6152 | tf_op jit(solution)/shard_map/ppermute | solution.py:341
  5.3 16.0 %collective-permute-start.9 = (bf16[1024,128]{1,0:T(8,128)(2,1)S(1)}, bf16[1024,128]{1,0:T(8,128)(2,1)S(1)}, u32[]{:S(2)}, u32[]{:S(2)}) collective-permute-start(bf16[1024,128]{1,0:T(8,128)(2,1)S(1)} %pad_maximum_fusion.1.rest_0_), channel_id=1, source_target_pairs={{0,112},{16,96},{32,16},{48,0},{64,48},{80,32},{96,80},{112,64},{1... | collective-permute-start | bytes 786440 | tf_op jit(solution)/shard_map/ppermute | solution.py:222
  12.2 22.5 %collective-permute-start.8 = (bf16[1024,128]{1,0:T(8,128)(2,1)S(1)}, bf16[1024,128]{1,0:T(8,128)(2,1)S(1)}, u32[]{:S(2)}, u32[]{:S(2)}) collective-permute-start(bf16[1024,128]{1,0:T(8,128)(2,1)S(1)} %pad_maximum_fusion.1.rest_0_), channel_id=1, source_target_pairs={{0,96},{16,112},{32,0},{48,16},{64,32},{80,48},{96,64},{112,80},{1... | collective-permute-start | bytes 786440 | tf_op jit(solution)/shard_map/ppermute | solution.py:222
  17.9 23.6 %collective-permute-start.7 = (bf16[1024,128]{1,0:T(8,128)(2,1)S(1)}, bf16[1024,128]{1,0:T(8,128)(2,1)S(1)}, u32[]{:S(2)}, u32[]{:S(2)}) collective-permute-start(bf16[1024,128]{1,0:T(8,128)(2,1)S(1)} %pad_maximum_fusion.1.rest_0_), channel_id=1, source_target_pairs={{0,80},{16,64},{32,112},{48,96},{64,16},{80,0},{96,48},{112,32},{1... | collective-permute-start | bytes 786440 | tf_op jit(solution)/shard_map/ppermute | solution.py:222
  18.0 23.6 %collective-permute-start.6 = (bf16[1024,128]{1,0:T(8,128)(2,1)S(1)}, bf16[1024,128]{1,0:T(8,128)(2,1)S(1)}, u32[]{:S(2)}, u32[]{:S(2)}) collective-permute-start(bf16[1024,128]{1,0:T(8,128)(2,1)S(1)} %pad_maximum_fusion.1.rest_0_), channel_id=1, source_target_pairs={{0,64},{16,80},{32,96},{48,112},{64,0},{80,16},{96,32},{112,48},{1... | collective-permute-start | bytes 786440 | tf_op jit(solution)/shard_map/ppermute | solution.py:222
  21.3 20.3 %collective-permute-start.5 = (bf16[1024,128]{1,0:T(8,128)(2,1)S(1)}, bf16[1024,128]{1,0:T(8,128)(2,1)}, u32[]{:S(2)}, u32[]{:S(2)}) collective-permute-start(bf16[1024,128]{1,0:T(8,128)(2,1)S(1)} %pad_maximum_fusion.1.rest_0_), channel_id=1, source_target_pairs={{0,48},{16,32},{32,80},{48,64},{64,112},{80,96},{96,16},{112,0},{1... | collective-permute-start | bytes 786440 | tf_op jit(solution)/shard_map/ppermute | solution.py:222
  106.2 15.6 %collective-permute-start.27 = (bf16[448,512]{1,0:T(8,128)(2,1)}, bf16[448,512]{1,0:T(8,128)(2,1)}, u32[]{:S(2)}, u32[]{:S(2)}) collective-permute-start(bf16[448,512]{1,0:T(8,128)(2,1)} %get-tuple-element.44), channel_id=1, source_target_pairs={{0,32},{32,64},{64,96},{96,0},{1,33},{33,65},{65,97},{97,1},{2,34}... | collective-permute-start | bytes 1376264 | tf_op jit(solution)/shard_map/ppermute | solution.py:316
  109.5 25.6 %collective-permute-start.28 = (bf16[448,512]{1,0:T(8,128)(2,1)}, bf16[448,512]{1,0:T(8,128)(2,1)}, u32[]{:S(2)}, u32[]{:S(2)}) collective-permute-start(bf16[448,512]{1,0:T(8,128)(2,1)} %get-tuple-element.45), channel_id=1, source_target_pairs={{0,64},{32,96},{64,0},{96,32},{1,65},{33,97},{65,1},{97,33},{2,66}... | collective-permute-start | bytes 1376264 | tf_op jit(solution)/shard_map/ppermute | solution.py:316
  114.2 21.0 %collective-permute-start.29 = (bf16[448,512]{1,0:T(8,128)(2,1)}, bf16[448,512]{1,0:T(8,128)(2,1)}, u32[]{:S(2)}, u32[]{:S(2)}) collective-permute-start(bf16[448,512]{1,0:T(8,128)(2,1)} %get-tuple-element.46), channel_id=1, source_target_pairs={{0,96},{32,0},{64,32},{96,64},{1,97},{33,1},{65,33},{97,65},{2,98}... | collective-permute-start | bytes 1376264 | tf_op jit(solution)/shard_map/ppermute | solution.py:316
  119.8 21.4 %collective-permute-start.10 = (bf16[512,128]{1,0:T(8,128)(2,1)S(1)}, bf16[512,128]{1,0:T(8,128)(2,1)S(1)}, u32[]{:S(2)}, u32[]{:S(2)}) collective-permute-start(bf16[512,128]{1,0:T(8,128)(2,1)S(1)} %get-tuple-element.62), channel_id=1, source_target_pairs={{0,8},{8,0},{1,9},{9,1},{2,10},{10,2},{3,11},{11,3},{4,12},{12,4},... | collective-permute-start | bytes 393224 | tf_op jit(solution)/shard_map/ppermute | solution.py:255
  137.6 28.7 %all-to-all-start.1 = ((bf16[16,112,128]{2,1,0:T(8,128)(2,1)}), bf16[16,112,128]{2,1,0:T(8,128)(2,1)S(1)}, u32[]{:S(2)}, u32[]{:S(2)}) async-start(bf16[16,112,128]{2,1,0:T(8,128)(2,1)} %quarter_sum.1), calls=%async_computation.1 | async-start | bytes 917504 | tf_op jit(solution)/shard_map/all_to_all | solution.py:318
  141.2 19.5 %collective-permute-start.17 = (bf16[1024,128]{1,0:T(8,128)(2,1)S(1)}, bf16[1024,128]{1,0:T(8,128)(2,1)S(1)}, u32[]{:S(2)}, u32[]{:S(2)}) collective-permute-start(bf16[1024,128]{1,0:T(8,128)(2,1)S(1)} %pad_maximum_fusion.2.rest_0_), channel_id=1, source_target_pairs={{0,7},{1,4},{2,5},{3,6},{4,3},{5,0},{6,1},{7,2},{8,15},{9,12},{10,... | collective-permute-start | bytes 786440 | tf_op jit(solution)/shard_map/ppermute | solution.py:222
  145.2 18.9 %collective-permute-start.16 = (bf16[1024,128]{1,0:T(8,128)(2,1)S(1)}, bf16[1024,128]{1,0:T(8,128)(2,1)S(1)}, u32[]{:S(2)}, u32[]{:S(2)}) collective-permute-start(bf16[1024,128]{1,0:T(8,128)(2,1)S(1)} %pad_maximum_fusion.2.rest_0_), channel_id=1, source_target_pairs={{0,3},{1,0},{2,1},{3,2},{4,7},{5,4},{6,5},{7,6},{8,11},{9,8},{10,9... | collective-permute-start | bytes 786440 | tf_op jit(solution)/shard_map/ppermute | solution.py:222
  146.1 30.0 %collective-permute-start.15 = (bf16[1024,128]{1,0:T(8,128)(2,1)S(1)}, bf16[1024,128]{1,0:T(8,128)(2,1)}, u32[]{:S(2)}, u32[]{:S(2)}) collective-permute-start(bf16[1024,128]{1,0:T(8,128)(2,1)S(1)} %pad_maximum_fusion.2.rest_0_), channel_id=1, source_target_pairs={{0,6},{1,7},{2,4},{3,5},{4,2},{5,3},{6,0},{7,1},{8,14},{9,15},{10,... | collective-permute-start | bytes 786440 | tf_op jit(solution)/shard_map/ppermute | solution.py:222
  146.3 29.8 %collective-permute-start.14 = (bf16[1024,128]{1,0:T(8,128)(2,1)S(1)}, bf16[1024,128]{1,0:T(8,128)(2,1)}, u32[]{:S(2)}, u32[]{:S(2)}) collective-permute-start(bf16[1024,128]{1,0:T(8,128)(2,1)S(1)} %pad_maximum_fusion.2.rest_0_), channel_id=1, source_target_pairs={{0,2},{1,3},{2,0},{3,1},{4,6},{5,7},{6,4},{7,5},{8,10},{9,11},{10,... | collective-permute-start | bytes 786440 | tf_op jit(solution)/shard_map/ppermute | solution.py:222
  149.6 26.5 %collective-permute-start.13 = (bf16[1024,128]{1,0:T(8,128)(2,1)S(1)}, bf16[1024,128]{1,0:T(8,128)(2,1)}, u32[]{:S(2)}, u32[]{:S(2)}) collective-permute-start(bf16[1024,128]{1,0:T(8,128)(2,1)S(1)} %pad_maximum_fusion.2.rest_0_), channel_id=1, source_target_pairs={{0,5},{1,6},{2,7},{3,4},{4,1},{5,2},{6,3},{7,0},{8,13},{9,14},{10,... | collective-permute-start | bytes 786440 | tf_op jit(solution)/shard_map/ppermute | solution.py:222
  160.7 15.4 %collective-permute-start.12 = (bf16[1024,128]{1,0:T(8,128)(2,1)S(1)}, bf16[1024,128]{1,0:T(8,128)(2,1)}, u32[]{:S(2)}, u32[]{:S(2)}) collective-permute-start(bf16[1024,128]{1,0:T(8,128)(2,1)S(1)} %pad_maximum_fusion.2.rest_0_), channel_id=1, source_target_pairs={{0,1},{1,2},{2,3},{3,0},{4,5},{5,6},{6,7},{7,4},{8,9},{9,10},{10,1... | collective-permute-start | bytes 786440 | tf_op jit(solution)/shard_map/ppermute | solution.py:222
  164.1 12.0 %collective-permute-start.11 = (bf16[1024,128]{1,0:T(8,128)(2,1)S(1)}, bf16[1024,128]{1,0:T(8,128)(2,1)}, u32[]{:S(2)}, u32[]{:S(2)}) collective-permute-start(bf16[1024,128]{1,0:T(8,128)(2,1)S(1)} %pad_maximum_fusion.2.rest_0_), channel_id=1, source_target_pairs={{0,4},{1,5},{2,6},{3,7},{4,0},{5,1},{6,2},{7,3},{8,12},{9,13},{10,... | collective-permute-start | bytes 786440 | tf_op jit(solution)/shard_map/ppermute | solution.py:222
  168.9 38.5 %all-to-all-start.2 = ((bf16[16,112,128]{2,1,0:T(8,128)(2,1)}), bf16[16,112,128]{2,1,0:T(8,128)(2,1)}, u32[]{:S(2)}, u32[]{:S(2)}) async-start(bf16[16,112,128]{2,1,0:T(8,128)(2,1)} %chunk_sum.1), calls=%async_computation.2 | async-start | bytes 917504 | tf_op jit(solution)/shard_map/all_to_all | solution.py:319
  183.5 15.5 %collective-permute-start.18 = (bf16[1024,128]{1,0:T(8,128)(2,1)}, bf16[1024,128]{1,0:T(8,128)(2,1)S(1)}, u32[]{:S(2)}, u32[]{:S(2)}) collective-permute-start(bf16[1024,128]{1,0:T(8,128)(2,1)} %get-tuple-element.34), channel_id=1, source_target_pairs={{0,16},{16,0},{32,48},{48,32},{64,80},{80,64},{96,112},{112,96},{1... | collective-permute-start | bytes 786440 | tf_op jit(solution)/shard_map/ppermute | solution.py:222
  185.6 21.3 %collective-permute-start.19 = (bf16[1024,128]{1,0:T(8,128)(2,1)}, bf16[1024,128]{1,0:T(8,128)(2,1)}, u32[]{:S(2)}, u32[]{:S(2)}) collective-permute-start(bf16[1024,128]{1,0:T(8,128)(2,1)} %get-tuple-element.35), channel_id=1, source_target_pairs={{0,32},{16,48},{32,64},{48,80},{64,96},{80,112},{96,0},{112,16},{1... | collective-permute-start | bytes 786440 | tf_op jit(solution)/shard_map/ppermute | solution.py:222
  188.7 18.8 %collective-permute-start.20 = (bf16[1024,128]{1,0:T(8,128)(2,1)}, bf16[1024,128]{1,0:T(8,128)(2,1)}, u32[]{:S(2)}, u32[]{:S(2)}) collective-permute-start(bf16[1024,128]{1,0:T(8,128)(2,1)} %get-tuple-element.36), channel_id=1, source_target_pairs={{0,48},{16,32},{32,80},{48,64},{64,112},{80,96},{96,16},{112,0},{1... | collective-permute-start | bytes 786440 | tf_op jit(solution)/shard_map/ppermute | solution.py:222
  192.0 31.2 %collective-permute-start.21 = (bf16[1024,128]{1,0:T(8,128)(2,1)}, bf16[1024,128]{1,0:T(8,128)(2,1)}, u32[]{:S(2)}, u32[]{:S(2)}) collective-permute-start(bf16[1024,128]{1,0:T(8,128)(2,1)} %get-tuple-element.37), channel_id=1, source_target_pairs={{0,64},{16,80},{32,96},{48,112},{64,0},{80,16},{96,32},{112,48},{1... | collective-permute-start | bytes 786440 | tf_op jit(solution)/shard_map/ppermute | solution.py:222
  192.5 30.7 %collective-permute-start.22 = (bf16[1024,128]{1,0:T(8,128)(2,1)}, bf16[1024,128]{1,0:T(8,128)(2,1)}, u32[]{:S(2)}, u32[]{:S(2)}) collective-permute-start(bf16[1024,128]{1,0:T(8,128)(2,1)} %get-tuple-element.38), channel_id=1, source_target_pairs={{0,80},{16,64},{32,112},{48,96},{64,16},{80,0},{96,48},{112,32},{1... | collective-permute-start | bytes 786440 | tf_op jit(solution)/shard_map/ppermute | solution.py:222
  199.0 29.6 %collective-permute-start.23 = (bf16[1024,128]{1,0:T(8,128)(2,1)}, bf16[1024,128]{1,0:T(8,128)(2,1)}, u32[]{:S(2)}, u32[]{:S(2)}) collective-permute-start(bf16[1024,128]{1,0:T(8,128)(2,1)} %get-tuple-element.39), channel_id=1, source_target_pairs={{0,96},{16,112},{32,0},{48,16},{64,32},{80,48},{96,64},{112,80},{1... | collective-permute-start | bytes 786440 | tf_op jit(solution)/shard_map/ppermute | solution.py:222
  206.8 21.8 %collective-permute-start.24 = (bf16[1024,128]{1,0:T(8,128)(2,1)}, bf16[1024,128]{1,0:T(8,128)(2,1)}, u32[]{:S(2)}, u32[]{:S(2)}) collective-permute-start(bf16[1024,128]{1,0:T(8,128)(2,1)} %get-tuple-element.40), channel_id=1, source_target_pairs={{0,112},{16,96},{32,16},{48,0},{64,48},{80,32},{96,80},{112,64},{1... | collective-permute-start | bytes 786440 | tf_op jit(solution)/shard_map/ppermute | solution.py:222
  207.5 26.5 %collective-permute-start.34 = (bf16[1792,128]{1,0:T(8,128)(2,1)}, bf16[1792,128]{1,0:T(8,128)(2,1)}, u32[]{:S(2)}, u32[]{:S(2)}) collective-permute-start(bf16[1792,128]{1,0:T(8,128)(2,1)} %bitcast.15.own), channel_id=1, source_target_pairs={{0,1},{1,2},{2,3},{3,0},{4,5},{5,6},{6,7},{7,4},{8,9},{9,10},{10,1... | collective-permute-start | bytes 1376264 | tf_op jit(solution)/shard_map/ppermute | solution.py:325
  223.2 18.8 %collective-permute-start.32 = (bf16[1792,128]{1,0:T(8,128)(2,1)}, bf16[1792,128]{1,0:T(8,128)(2,1)}, u32[]{:S(2)}, u32[]{:S(2)}) collective-permute-start(bf16[1792,128]{1,0:T(8,128)(2,1)} %bitcast.15.own), channel_id=1, source_target_pairs={{0,2},{1,3},{2,0},{3,1},{4,6},{5,7},{6,4},{7,5},{8,10},{9,11},{10,... | collective-permute-start | bytes 1376264 | tf_op jit(solution)/shard_map/ppermute | solution.py:325
  223.2 21.1 %collective-permute-start.30 = (bf16[1792,128]{1,0:T(8,128)(2,1)}, bf16[1792,128]{1,0:T(8,128)(2,1)}, u32[]{:S(2)}, u32[]{:S(2)}) collective-permute-start(bf16[1792,128]{1,0:T(8,128)(2,1)} %bitcast.15.own), channel_id=1, source_target_pairs={{0,3},{1,0},{2,1},{3,2},{4,7},{5,4},{6,5},{7,6},{8,11},{9,8},{10,9... | collective-permute-start | bytes 1376264 | tf_op jit(solution)/shard_map/ppermute | solution.py:325
  231.1 13.2 %collective-permute-start.25 = (bf16[512,128]{1,0:T(8,128)(2,1)}, bf16[512,128]{1,0:T(8,128)(2,1)S(1)}, u32[]{:S(2)}, u32[]{:S(2)}) collective-permute-start(bf16[512,128]{1,0:T(8,128)(2,1)} %get-tuple-element.42), channel_id=1, source_target_pairs={{0,8},{8,0},{1,9},{9,1},{2,10},{10,2},{3,11},{11,3},{4,12},{12,4},... | collective-permute-start | bytes 393224 | tf_op jit(solution)/shard_map/ppermute | solution.py:393
  233.9 14.6 %collective-permute-start.35 = (bf16[1792,128]{1,0:T(8,128)(2,1)}, bf16[1792,128]{1,0:T(8,128)(2,1)}, u32[]{:S(2)}, u32[]{:S(2)}) collective-permute-start(bf16[1792,128]{1,0:T(8,128)(2,1)} %collective-permute-done.34.own), channel_id=1, source_target_pairs={{0,8},{8,0},{1,9},{9,1},{2,10},{10,2},{3,11},{11,3},{4,12},{12,4},... | collective-permute-start | bytes 1376264 | tf_op jit(solution)/shard_map/ppermute | solution.py:328
  (32 other events, 441.8 us)

commit v3 on v2

--- a/solution.py
+++ b/solution.py
@@ -5,6 +5,7 @@
 from jax import lax
 from jax.experimental import pallas as pl
 from jax.experimental.pallas import tpu as pltpu
+from jax.experimental.layout import Layout, with_layout_constraint
 from jax.sharding import Mesh, PartitionSpec as P
 
 
@@ -16,6 +17,16 @@
 SIDE = 64
 CHUNK = 32
 UNROLL = 8
+FINISH = (
+    ("m", 0),
+    ("y", 0),
+    ("m", 1),
+    ("m", 3),
+    ("y", 1),
+    ("y", 3),
+    ("m", 2),
+    ("y", 2),
+)
 VMEM_LIMIT = 60 * 1024 * 1024
 
 
@@ -143,47 +154,26 @@
     )(half.reshape(1), *operands)
 
 
-def chip_kernel(z_ref, own, got, *out_refs):
-    for k, out_ref in enumerate(out_refs):
-        at = pl.multiple_of(lax.rem(z_ref[0] + k, 4) * 448, 64)
-        rows = pl.ds(at, 448)
-        out_ref[...] = (own[rows, :].astype(F32) + got[rows, :].astype(F32)).astype(BF)
-
-
-def chip_sum(z, own, got):
+def chip_kernel(own, got, out_ref):
+    for row in range(16):
+        rows = slice(row * 112, (row + 1) * 112)
+        for lane in range(4):
+            lanes = slice(lane * 128, (lane + 1) * 128)
+            out_ref[row * 4 + lane] = (
+                own[rows, lanes].astype(F32) + got[rows, lanes].astype(F32)
+            ).astype(BF)
+
+
+def chip_sum(own, got):
     vm = pl.BlockSpec(memory_space=pltpu.VMEM)
     return pl.pallas_call(
         chip_kernel,
-        out_shape=(jax.ShapeDtypeStruct((448, 512), BF),) * 4,
-        in_specs=[pl.BlockSpec(memory_space=pltpu.SMEM), vm, vm],
-        out_specs=(vm,) * 4,
+        out_shape=jax.ShapeDtypeStruct((64, 112, 128), BF),
+        in_specs=[vm, vm],
+        out_specs=vm,
         cost_estimate=pl.CostEstimate(flops=1 << 20, bytes_accessed=6 << 20, transcendentals=0),
         name="chip_sum",
-    )(z.reshape(1), own, got)
-
-
-def quarter_kernel(*refs):
-    out_ref = refs[-1]
-    total = refs[0][...].astype(F32)
-    for ref in refs[1:-1]:
-        total = total + ref[...].astype(F32)
-    for row in range(4):
-        for lane in range(4):
-            out_ref[row * 4 + lane] = total[
-                row * 112 : (row + 1) * 112, lane * 128 : (lane + 1) * 128
-            ].astype(BF)
-
-
-def quarter_sum(parts):
-    vm = pl.BlockSpec(memory_space=pltpu.VMEM)
-    return pl.pallas_call(
-        quarter_kernel,
-        out_shape=jax.ShapeDtypeStruct((16, 112, 128), BF),
-        in_specs=[vm] * len(parts),
-        out_specs=vm,
-        cost_estimate=pl.CostEstimate(flops=1 << 20, bytes_accessed=3 << 20, transcendentals=0),
-        name="quarter_sum",
-    )(*parts)
+    )(own, got)
 
 
 def chunk_kernel(parts, out_ref):
@@ -256,38 +246,28 @@
     return jnp.concatenate([mine, got], axis=0)
 
 
-def finish_kernel(lane_ref, own, other, *rest):
-    outs = rest[-10:-7]
-    scratch, sems = rest[-7:-1], rest[-1]
-    moves = []
-    for group, piece in enumerate((own, other)):
-        full = piece[...].astype(F32) * (1.0 / 256.0)
-        lane = pl.multiple_of(lane_ref[group], 128)
-        held = scratch[group * 3 : group * 3 + 3]
-        held[0][...] = full[:512]
-        held[1][...] = full[512:1536]
-        held[2][...] = full[1536:].T
-        targets = (
-            outs[0].at[:, pl.ds(lane, 128)],
-            outs[1].at[:, pl.ds(lane, 128)],
-            outs[2].at[pl.ds(lane, 128), :],
-        )
-        for k in range(3):
-            move = pltpu.make_async_copy(held[k], targets[k], sems.at[group * 3 + k])
-            move.start()
-            moves.append(move)
+def finish_kernel(lane_ref, piece, *rest):
+    outs, held, sems = rest[-7:-4], rest[-4:-1], rest[-1]
+    lane = pl.multiple_of(lane_ref[0], 128)
+    targets = (
+        outs[0].at[:, pl.ds(lane, 128)],
+        outs[1].at[:, pl.ds(lane, 128)],
+        outs[2].at[pl.ds(lane, 128), :],
+    )
+    moves = [pltpu.make_async_copy(held[k], targets[k], sems.at[k]) for k in range(3)]
+    held[0][...] = piece[:512, :].astype(F32) * (1.0 / 256.0)
+    moves[0].start()
+    held[1][...] = piece[512:1536, :].astype(F32) * (1.0 / 256.0)
+    moves[1].start()
+    held[2][...] = (piece[1536:, :].astype(F32) * (1.0 / 256.0)).T
+    moves[2].start()
     for move in moves:
         move.wait()
 
 
-def finish_grads(lanes, own, other, outs):
+def finish_grads(lane, piece, outs):
     vm = pl.BlockSpec(memory_space=pltpu.VMEM)
     any_spec = pl.BlockSpec(memory_space=pl.ANY)
-    held = [
-        pltpu.VMEM((512, 128), F32),
-        pltpu.VMEM((1024, 128), F32),
-        pltpu.VMEM((128, 256), F32),
-    ]
     return pl.pallas_call(
         finish_kernel,
         out_shape=(
@@ -295,37 +275,43 @@
             jax.ShapeDtypeStruct((1024, 1024), F32),
             jax.ShapeDtypeStruct((1024, 256), F32),
         ),
-        in_specs=[pl.BlockSpec(memory_space=pltpu.SMEM), vm, vm] + [any_spec] * len(outs),
+        in_specs=[pl.BlockSpec(memory_space=pltpu.SMEM), vm] + [any_spec] * len(outs),
         out_specs=(any_spec,) * 3,
-        scratch_shapes=held + held + [pltpu.SemaphoreType.DMA((6,))],
-        input_output_aliases={3 + k: k for k in range(len(outs))},
-        cost_estimate=pl.CostEstimate(flops=1 << 20, bytes_accessed=3 << 20, transcendentals=0),
+        scratch_shapes=[
+            pltpu.VMEM((512, 128), F32),
+            pltpu.VMEM((1024, 128), F32),
+            pltpu.VMEM((128, 256), F32),
+            pltpu.SemaphoreType.DMA((3,)),
+        ],
+        input_output_aliases={2 + k: k for k in range(len(outs))},
+        cost_estimate=pl.CostEstimate(flops=1 << 20, bytes_accessed=2 << 20, transcendentals=0),
         name="finish_grads",
-    )(lanes, own, other, *outs)
+    )(lane, piece, *outs)
 
 
 def sum_grads(core, operands):
-    x, z = lax.axis_index("x"), lax.axis_index("z")
+    x = lax.axis_index("x")
     swap = [(0, 1), (1, 0)]
     other = local_grads(1 - core, *operands)
     got = lax.ppermute(other, "core", swap)
     own = local_grads(core, *operands)
-    quarters = chip_sum(z, own, got)
-    parts = [quarters[0]]
+    parts = lax.all_to_all(chip_sum(own, got), ("z", "yh", "yl", "x"), 0, 0, tiled=True)
+    chunk = chunk_sum(parts)
+    lanes = lax.all_to_all(chunk, ("z", "yh", "yl"), 0, 0, tiled=True)
+    lanes = lanes.reshape(1792, 128)
+    mine, yours = [lanes], []
     for k in range(1, 4):
-        parts.append(lax.ppermute(quarters[k], "z", [(i, (i + k) % 4) for i in range(4)]))
-    part = quarter_sum(parts)
-    part = lax.all_to_all(part, ("yh", "yl", "x"), 0, 0, tiled=True)
-    lanes = lax.all_to_all(chunk_sum(part), ("z", "yh", "yl"), 0, 0, tiled=True)
-    lanes = lanes.reshape(1792, 128)
+        mine.append(lax.ppermute(lanes, "x", [(i, (i + k) % 4) for i in range(4)]))
+    for k in range(4):
+        yours.append(lax.ppermute(mine[k], "core", swap))
+    place = ((x - jnp.arange(4, dtype=jnp.int32)) & 3) * 128
+    at_mine, at_yours = core * 512 + place, (1 - core) * 512 + place
     outs = ()
-    for k in range(4):
-        piece = lanes
-        if k:
-            piece = lax.ppermute(lanes, "x", [(i, (i + k) % 4) for i in range(4)])
-        place = ((x - k) & 3) * 128
-        at = jnp.stack([core * 512 + place, (1 - core) * 512 + place])
-        outs = finish_grads(at, piece, lax.ppermute(piece, "core", swap), outs)
+    for side, k in FINISH:
+        if side == "m":
+            outs = finish_grads(at_mine[k : k + 1], mine[k], outs)
+        else:
+            outs = finish_grads(at_yours[k : k + 1], yours[k], outs)
     return outs
 
 
@@ -334,7 +320,7 @@
     z, yh = lax.axis_index("z"), lax.axis_index("yh")
     yl, x = lax.axis_index("yl"), lax.axis_index("x")
     swap = [(0, 1), (1, 0)]
-    blk_own = blocks[0, 0]
+    blk_own = blocks[0, 0].transpose(1, 2, 0)
     meta = jnp.concatenate(
         [block_rows[0, 0], block_cols[0, 0], jnp.broadcast_to(block_count[0, 0], (128,))]
     )
@@ -362,6 +348,8 @@
     shard = halves(features, core)
     pieces = send_steps([shard] * 8, ("z", "yh"))
     blk_own, _ = lax.optimization_barrier((blk_own, shard))
+    blk_own = with_layout_constraint(blk_own, Layout((0, 1, 2))).transpose(2, 0, 1)
+    blk_other = blk_other.transpose(2, 0, 1)
     cells = cell_products(False, fwd_off, count, place, blk_own, blk_other, pieces)
     cells = lax.all_to_all(cells, ("core", "yl", "x"), 0, 0, tiled=True)
     sums = jnp.sum(cells.reshape(2, 8, 512, 128).astype(F32), axis=1).astype(BF)

time: 259 us -> 265 us (1.023)
  Pallas kernels: 44.3 us -> 53.5 us
  starting transfers between devices: 85.6 us -> 79.3 us
    ppermute x21, waiting for transfers between devices: 32.9 us -> 48.4 us  [send_steps(): got.append(lax.ppermute(pieces[p], axes, step_perm(axes, p)))]
    ppermute x10 -> x7, waiting for transfers between devices: 25.6 us -> 10.2 us  [the longest x3 10.2 us: sum_grads(): mine.append(lax.ppermute(lanes, 'x', [(i, (i + k) % 4) for i in range(4)]))]
    ppermute x10 -> x7, starting transfers between devices: 31.1 us -> 19.8 us  [the longest x3 19.4 us: sum_grads(): mine.append(lax.ppermute(lanes, 'x', [(i, (i + k) % 4) for i in range(4)]))]
    pallas_call x4 -> x8, Pallas kernels: 10.1 us -> 21.1 us  [finish_grads(): pl.pallas_call(finish_kernel, out_shape=(jax.ShapeDtypeStruct((512, 1024)...]
    all_to_all x2, starting transfers between devices: 9.99 us -> 20 us  [the longest x1 12.9 us: sum_grads(): lax.all_to_all(chip_sum(own, got), ('z', 'yh', 'yl', 'x'), 0, 0, tiled=True)]
    ppermute x21, starting transfers between devices: 43.3 us -> 38 us  [send_steps(): got.append(lax.ppermute(pieces[p], axes, step_perm(axes, p)))]
    another operation x0 -> x1, local copies, waits for them, and re-layouts: none -> 5.09 us  [shards(): with_layout_constraint(blk_own, Layout((0, 1, 2))).transpose(2, 0, 1)]
    unnamed x51 -> x52, local copies, waits for them, and re-layouts: 8.14 us -> 3.75 us
  transfers between devices with their start and end apart: 39 -> 36, of which waited for: 10 -> 10; matrix products, arithmetic and copies ran while one was open for 9% -> 8% of each run, Pallas kernels for 10% -> 14%
where the time goes in v3:
time: 265 us; the launch traced here: 262 us
  starting transfers between devices  79.3 us (30%)
  waiting for transfers between devices  60.6 us (23%)
  Pallas kernels  53.5 us (20%)
  blocking collectives  32.7 us (12%)
  local copies, waits for them, and re-layouts  16.7 us (6%)
  matrix products  12.3 us (5%)
  other arithmetic  4.65 us (2%)
    ppermute x21, waiting for transfers between devices, send_steps(): got.append(lax.ppermute(pieces[p], axes, step_perm(axes, p)))  48.4 us
    ppermute x21, starting transfers between devices, send_steps(): got.append(lax.ppermute(pieces[p], axes, step_perm(axes, p)))  38 us
    all_to_all x1, blocking collectives, shards(): cells = lax.all_to_all(cells, ('core', 'yl', 'x'), 0, 0, tiled=True)  32.7 us
    pallas_call x8, Pallas kernels, finish_grads(): pl.pallas_call(finish_kernel, out_shape=(jax.ShapeDtypeStruct((512, 1024)...  21.1 us
    ppermute x3, starting transfers between devices, sum_grads(): mine.append(lax.ppermute(lanes, 'x', [(i, (i + k) % 4) for i in range(4)]))  19.4 us
    pallas_call x2, Pallas kernels, cell_products(): pl.pallas_call(functools.partial(cells_kernel, transposed), out_shape=(ja...  14.1 us
    all_to_all x1, starting transfers between devices, sum_grads(): lax.all_to_all(chip_sum(own, got), ('z', 'yh', 'yl', 'x'), 0, 0, tiled=True)  12.9 us
    ppermute x3, waiting for transfers between devices, sum_grads(): mine.append(lax.ppermute(lanes, 'x', [(i, (i + k) % 4) for i in range(4)]))  10.2 us
  transfers between devices with their start and end apart: 36, of which 10 were waited for; matrix products, arithmetic and copies ran while one was open for 8% of the time, Pallas kernels for 14%

profile of v3, /device:TPU:0, one launch (start us, length us, event | category | flops | bytes accessed | tf_op | source)
XLA Modules:
  0.0 261.9 jit_solution(8204706377906875705)
XLA Ops:
  5.3 6.8 %collective-permute-start.9 = (bf16[1024,128]{1,0:T(8,128)(2,1)S(1)}, bf16[1024,128]{1,0:T(8,128)(2,1)S(1)}, u32[]{:S(2)}, u32[]{:S(2)}) collective-permute-start(bf16[1024,128]{1,0:T(8,128)(2,1)S(1)} %pad_maximum_fusion.1.rest_0_), channel_id=1, source_target_pairs={{0,112},{16,96},{32,16},{48,0},{64,48},{80,32},{96,80},{112,64},{1... | collective-permute-start | bytes 786440 | tf_op jit(solution)/shard_map/ppermute | solution.py:212
  12.9 3.3 %collective-permute-start.6 = (bf16[1024,128]{1,0:T(8,128)(2,1)S(1)}, bf16[1024,128]{1,0:T(8,128)(2,1)S(1)}, u32[]{:S(2)}, u32[]{:S(2)}) collective-permute-start(bf16[1024,128]{1,0:T(8,128)(2,1)S(1)} %pad_maximum_fusion.1.rest_0_), channel_id=1, source_target_pairs={{0,64},{16,80},{32,96},{48,112},{64,0},{80,16},{96,32},{112,48},{1... | collective-permute-start | bytes 786440 | tf_op jit(solution)/shard_map/ppermute | solution.py:212
  16.2 3.7 %collective-permute-done.9.rest_7_ = bf16[1024,128]{1,0:T(8,128)(2,1)S(1)} collective-permute-done((bf16[1024,128]{1,0:T(8,128)(2,1)S(1)}, bf16[1024,128]{1,0:T(8,128)(2,1)S(1)}, u32[]{:S(2)}, u32[]{:S(2)}) %collective-permute-start.9) | collective-permute-done | bytes 262176 | tf_op jit(solution)/shard_map/ppermute | solution.py:212
  21.7 13.0 %collective-permute-done.8.rest_6_ = bf16[1024,128]{1,0:T(8,128)(2,1)S(1)} collective-permute-done((bf16[1024,128]{1,0:T(8,128)(2,1)S(1)}, bf16[1024,128]{1,0:T(8,128)(2,1)S(1)}, u32[]{:S(2)}, u32[]{:S(2)}) %collective-permute-start.8) | collective-permute-done | bytes 262176 | tf_op jit(solution)/shard_map/ppermute | solution.py:212
  35.5 5.1 %copy.44 = bf16[64,64,192]{1,0,2:T(8,128)(2,1)} copy(bf16[64,64,192]{2,1,0:T(8,128)(2,1)} %bitcast.36) | data formatting | bytes 3145728 | tf_op jit(solution)/shard_map/layout_constraint | solution.py:351
  40.6 5.2 %copy.45 = bf16[64,64,192]{1,0,2:T(8,128)(2,1)} copy(bf16[64,64,192]{2,1,0:T(8,128)(2,1)} %collective-permute-done.2) | data formatting | bytes 3145728 | tf_op jit(solution)/shard_map/ppermute | solution.py:328
  46.6 6.7 %cells_forward.1 = bf16[16,512,128]{2,1,0:T(8,128)(2,1)} custom-call(s32[768]{0:T(1024)} %reshape.47.off_ref, s32[2]{0:T(128)} %copy-done.24, s32[16]{0:T(128)} %add_multiply_fusion.1.place_ref, bf16[192,64,64]{2,1,0:T(8,128)(2,1)} %bitcast.31, bf16[192,64,64]{2,1,0:T(8,128)(2,1)} %bitcast.33, bf16[1024,128]{1,0:T(8,128)(2,1)} %copy-done.9, ...), custom_call_target="tpu_custom_call" | custom-call | flops 402653184 | bytes 10485760 | tf_op jit(solution)/shard_map/cells_forward/pallas_call | solution.py:106
  53.3 32.7 %all_to_all.15 = bf16[16,512,128]{2,1,0:T(8,128)(2,1)S(1)} all-to-all(bf16[16,512,128]{2,1,0:T(8,128)(2,1)} %cells_forward.1), channel_id=1, replica_groups=mesh['z'=4,'yh'=2,'core'=2,'yl'=2,'x'=4] {'core','yl','x'}, dimensions={0} | all-to-all | bytes 4194304 | tf_op jit(solution)/shard_map/all_to_all | solution.py:354
  92.3 2.7 %multiply_convert_fusion.gp_one = bf16[512,1024]{1,0:T(8,128)(2,1)} fusion(f32[512,1024]{1,0:T(8,128)S(1)} %get-tuple-element.96, bf16[512,1024]{1,0:T(8,128)(2,1)S(1)} %multiply_convert_fusion.1.gp_two, bf16[1024,1024]{1,0:T(8,128)(2,1)S(1)} %copy-done), kind=kOutput, calls=%fused_computation.1 | convolution fusion | flops 1078460416 | bytes 6291456 | tf_op jit(solution)/shard_map/dot_general | solution.py:370
  95.0 4.8 %shard_map.129 = bf16[1792,512]{1,0:T(8,128)(2,1)} custom-call(s32[1]{0:T(128)} %bitcast.6.half_ref, bf16[512,512]{1,0:T(8,128)(2,1)} %pad_maximum_fusion.joined, bf16[512,1024]{1,0:T(8,128)(2,1)} %copy-done.3, bf16[512,256]{1,0:T(8,128)(2,1)} %cot.3, bf16[512,1024]{1,0:T(8,128)(2,1)} %multiply_convert_fusion.gp_one, bf16[512,1024]{1,0:T(8,128)(2,1)} %copy-done.4, ...), custom_call_target="tpu_custom_call" | custom-call | flops 939524096 | bytes 8388608 | tf_op jit(solution)/shard_map/pallas_call | solution.py:145
  100.2 4.8 %shard_map.128.own = bf16[1792,512]{1,0:T(8,128)(2,1)} custom-call(s32[1]{0:T(128)} %bitcast.5.half_ref, bf16[512,512]{1,0:T(8,128)(2,1)} %pad_maximum_fusion.joined, bf16[512,1024]{1,0:T(8,128)(2,1)} %copy-done.3, bf16[512,256]{1,0:T(8,128)(2,1)} %cot.3, bf16[512,1024]{1,0:T(8,128)(2,1)} %multiply_convert_fusion.gp_one, bf16[512,1024]{1,0:T(8,128)(2,1)} %copy-done.4, ...), custom_call_target="tpu_custom_call" | custom-call | flops 939524096 | bytes 8388608 | tf_op jit(solution)/shard_map/pallas_call | solution.py:145
  105.0 3.7 %chip_sum.1 = bf16[64,112,128]{2,1,0:T(8,128)(2,1)} custom-call(bf16[1792,512]{1,0:T(8,128)(2,1)} %shard_map.128.own, bf16[1792,512]{1,0:T(8,128)(2,1)} %collective-permute-done.26.got), custom_call_target="tpu_custom_call" | custom-call | flops 1048576 | bytes 6291456 | tf_op jit(solution)/shard_map/chip_sum/pallas_call | solution.py:169
  108.7 12.9 %all-to-all-start.1 = ((bf16[64,112,128]{2,1,0:T(8,128)(2,1)}), bf16[64,112,128]{2,1,0:T(8,128)(2,1)}, u32[]{:S(2)}, u32[]{:S(2)}) async-start(bf16[64,112,128]{2,1,0:T(8,128)(2,1)} %chip_sum.1), calls=%async_computation.1 | async-start | bytes 3670016 | tf_op jit(solution)/shard_map/all_to_all | solution.py:298
  121.6 2.9 %fusion.14 = (bf16[512,512]{1,0:T(8,128)(2,1)S(1)}, f32[512,512]{1,0:T(8,128)}) fusion(bf16[512,1024]{1,0:T(8,128)(2,1)S(1)} %copy-done.1, bf16[512,1024]{1,0:T(8,128)(2,1)} %param.14), kind=kOutput, calls=%fused_computation.52 | convolution fusion | flops 537133056 | bytes 3670016 | tf_op jit(solution)/shard_map/dot_general | solution.py:372
  126.1 3.7 %collective-permute-start.17 = (bf16[1024,128]{1,0:T(8,128)(2,1)S(1)}, bf16[1024,128]{1,0:T(8,128)(2,1)S(1)}, u32[]{:S(2)}, u32[]{:S(2)}) collective-permute-start(bf16[1024,128]{1,0:T(8,128)(2,1)S(1)} %pad_maximum_fusion.2.rest_0_), channel_id=1, source_target_pairs={{0,7},{1,4},{2,5},{3,6},{4,3},{5,0},{6,1},{7,2},{8,15},{9,12},{10,... | collective-permute-start | bytes 786440 | tf_op jit(solution)/shard_map/ppermute | solution.py:212
  131.1 3.0 %collective-permute-start.14 = (bf16[1024,128]{1,0:T(8,128)(2,1)S(1)}, bf16[1024,128]{1,0:T(8,128)(2,1)S(1)}, u32[]{:S(2)}, u32[]{:S(2)}) collective-permute-start(bf16[1024,128]{1,0:T(8,128)(2,1)S(1)} %pad_maximum_fusion.2.rest_0_), channel_id=1, source_target_pairs={{0,2},{1,3},{2,0},{3,1},{4,6},{5,7},{6,4},{7,5},{8,10},{9,11},{10,... | collective-permute-start | bytes 786440 | tf_op jit(solution)/shard_map/ppermute | solution.py:212
  136.2 20.1 %collective-permute-done.17.rest_7_ = bf16[1024,128]{1,0:T(8,128)(2,1)S(1)} collective-permute-done((bf16[1024,128]{1,0:T(8,128)(2,1)S(1)}, bf16[1024,128]{1,0:T(8,128)(2,1)S(1)}, u32[]{:S(2)}, u32[]{:S(2)}) %collective-permute-start.17) | collective-permute-done | bytes 262176 | tf_op jit(solution)/shard_map/ppermute | solution.py:212
  156.3 5.2 %collective-permute-done.16.rest_6_ = bf16[1024,128]{1,0:T(8,128)(2,1)S(1)} collective-permute-done((bf16[1024,128]{1,0:T(8,128)(2,1)S(1)}, bf16[1024,128]{1,0:T(8,128)(2,1)S(1)}, u32[]{:S(2)}, u32[]{:S(2)}) %collective-permute-start.16) | collective-permute-done | bytes 262176 | tf_op jit(solution)/shard_map/ppermute | solution.py:212
  164.6 7.0 %all-to-all-start.2 = ((bf16[16,112,128]{2,1,0:T(8,128)(2,1)}), bf16[16,112,128]{2,1,0:T(8,128)(2,1)}, u32[]{:S(2)}, u32[]{:S(2)}) async-start(bf16[16,112,128]{2,1,0:T(8,128)(2,1)} %chunk_sum.1), calls=%async_computation.2 | async-start | bytes 917504 | tf_op jit(solution)/shard_map/all_to_all | solution.py:300
  173.1 7.4 %cells_back.1 = (bf16[1024,128]{1,0:T(8,128)(2,1)}, bf16[1024,128]{1,0:T(8,128)(2,1)}, bf16[1024,128]{1,0:T(8,128)(2,1)}, bf16[1024,128]{1,0:T(8,128)(2,1)}, bf1...) custom-call(s32[768]{0:T(1024)} %reshape.49.off_ref, ...), custom_call_target="tpu_custom_call" | custom-call | flops 402653184 | bytes 10485760 | tf_op jit(solution)/shard_map/cells_back/pallas_call | solution.py:106
  182.5 3.1 %collective-permute-start.19 = (bf16[1024,128]{1,0:T(8,128)(2,1)}, bf16[1024,128]{1,0:T(8,128)(2,1)}, u32[]{:S(2)}, u32[]{:S(2)}) collective-permute-start(bf16[1024,128]{1,0:T(8,128)(2,1)} %get-tuple-element.43), channel_id=1, source_target_pairs={{0,32},{16,48},{32,64},{48,80},{64,96},{80,112},{96,0},{112,16},{1... | collective-permute-start | bytes 786440 | tf_op jit(solution)/shard_map/ppermute | solution.py:212
  185.6 3.3 %collective-permute-start.20 = (bf16[1024,128]{1,0:T(8,128)(2,1)}, bf16[1024,128]{1,0:T(8,128)(2,1)}, u32[]{:S(2)}, u32[]{:S(2)}) collective-permute-start(bf16[1024,128]{1,0:T(8,128)(2,1)} %get-tuple-element.44), channel_id=1, source_target_pairs={{0,48},{16,32},{32,80},{48,64},{64,112},{80,96},{96,16},{112,0},{1... | collective-permute-start | bytes 786440 | tf_op jit(solution)/shard_map/ppermute | solution.py:212
  189.4 5.9 %collective-permute-start.22 = (bf16[1024,128]{1,0:T(8,128)(2,1)}, bf16[1024,128]{1,0:T(8,128)(2,1)}, u32[]{:S(2)}, u32[]{:S(2)}) collective-permute-start(bf16[1024,128]{1,0:T(8,128)(2,1)} %get-tuple-element.46), channel_id=1, source_target_pairs={{0,80},{16,64},{32,112},{48,96},{64,16},{80,0},{96,48},{112,32},{1... | collective-permute-start | bytes 786440 | tf_op jit(solution)/shard_map/ppermute | solution.py:212
  195.4 6.4 %collective-permute-done.19.refs_2_ = bf16[1024,128]{1,0:T(8,128)(2,1)} collective-permute-done((bf16[1024,128]{1,0:T(8,128)(2,1)}, bf16[1024,128]{1,0:T(8,128)(2,1)}, u32[]{:S(2)}, u32[]{:S(2)}) %collective-permute-start.19) | collective-permute-done | bytes 262176 | tf_op jit(solution)/shard_map/ppermute | solution.py:212
  202.5 15.9 %collective-permute-start.31 = (bf16[1792,128]{1,0:T(8,128)(2,1)}, bf16[1792,128]{1,0:T(8,128)(2,1)}, u32[]{:S(2)}, u32[]{:S(2)}) collective-permute-start(bf16[1792,128]{1,0:T(8,128)(2,1)} %bitcast.15.piece), channel_id=1, source_target_pairs={{0,1},{1,2},{2,3},{3,0},{4,5},{5,6},{6,7},{7,4},{8,9},{9,10},{10,1... | collective-permute-start | bytes 1376264 | tf_op jit(solution)/shard_map/ppermute | solution.py:304
  218.5 3.5 %collective-permute-start.27 = (bf16[1792,128]{1,0:T(8,128)(2,1)}, bf16[1792,128]{1,0:T(8,128)(2,1)}, u32[]{:S(2)}, u32[]{:S(2)}) collective-permute-start(bf16[1792,128]{1,0:T(8,128)(2,1)} %bitcast.15.piece), channel_id=1, source_target_pairs={{0,2},{1,3},{2,0},{3,1},{4,6},{5,7},{6,4},{7,5},{8,10},{9,11},{10,... | collective-permute-start | bytes 1376264 | tf_op jit(solution)/shard_map/ppermute | solution.py:304
  229.2 2.9 %collective-permute-done.29.piece = bf16[1792,128]{1,0:T(8,128)(2,1)} collective-permute-done((bf16[1792,128]{1,0:T(8,128)(2,1)}, bf16[1792,128]{1,0:T(8,128)(2,1)}, u32[]{:S(2)}, u32[]{:S(2)}) %collective-permute-start.29) | collective-permute-done | bytes 458784 | tf_op jit(solution)/shard_map/ppermute | solution.py:304
  232.2 5.9 %collective-permute-done.27.piece = bf16[1792,128]{1,0:T(8,128)(2,1)} collective-permute-done((bf16[1792,128]{1,0:T(8,128)(2,1)}, bf16[1792,128]{1,0:T(8,128)(2,1)}, u32[]{:S(2)}, u32[]{:S(2)}) %collective-permute-start.27) | collective-permute-done | bytes 458784 | tf_op jit(solution)/shard_map/ppermute | solution.py:304
  239.0 2.7 %finish_grads.8 = (f32[512,1024]{1,0:T(8,128)}, f32[1024,1024]{1,0:T(8,128)}, f32[1024,256]{1,0:T(8,128)}) custom-call(s32[1]{0:T(128)} %get-tuple-element.87.lane_ref, bf16[1792,128]{1,0:T(8,128)(2,1)} %bitcast.15.piece), custom_call_target="tpu_custom_call" | custom-call | flops 1048576 | bytes 2097152 | tf_op jit(solution)/shard_map/finish_grads/pallas_call | solution.py:271
  241.7 2.7 %finish_grads.9 = (f32[512,1024]{1,0:T(8,128)}, f32[1024,1024]{1,0:T(8,128)}, f32[1024,256]{1,0:T(8,128)}) custom-call(s32[1]{0:T(128)} %get-tuple-element.91.lane_ref, bf16[1792,128]{1,0:T(8,128)(2,1)} %collective-permute-done.33.piece, f32[512,1024]{1,0:T(8,128)} %get-tuple-element.51.rest_0_, ...), custom_call_target="tpu_custom_call", output_to_operand_aliasing={{0}: (2, {}), {1}: (3, {}), {2}: (4, {})} | custom-call | flops 1048576 | bytes 2097152 | tf_op jit(solution)/shard_map/finish_grads/pallas_call | solution.py:271
  246.9 2.7 %finish_grads.11 = (f32[512,1024]{1,0:T(8,128)}, f32[1024,1024]{1,0:T(8,128)}, f32[1024,256]{1,0:T(8,128)}) custom-call(s32[1]{0:T(128)} %get-tuple-element.89.lane_ref, bf16[1792,128]{1,0:T(8,128)(2,1)} %collective-permute-done.29.piece, f32[512,1024]{1,0:T(8,128)} %get-tuple-element.57.rest_0_, ...), custom_call_target="tpu_custom_call", output_to_operand_aliasing={{0}: (2, {}), {1}: (3, {}), {2}: (4, {})} | custom-call | flops 1048576 | bytes 2097152 | tf_op jit(solution)/shard_map/finish_grads/pallas_call | solution.py:271
  259.1 2.7 %finish_grads.15 = (f32[512,1024]{1,0:T(8,128)}, f32[1024,1024]{1,0:T(8,128)}, f32[1024,256]{1,0:T(8,128)}) custom-call(s32[1]{0:T(128)} %get-tuple-element.94.lane_ref, bf16[1792,128]{1,0:T(8,128)(2,1)} %copy-done.12, f32[512,1024]{1,0:T(8,128)} %get-tuple-element.69.rest_0_, ...), custom_call_target="tpu_custom_call", output_to_operand_aliasing={{0}: (2, {}), {1}: (3, {}), {2}: (4, {})} | custom-call | flops 1048576 | bytes 2097152 | tf_op jit(solution)/shard_map/finish_grads/pallas_call | solution.py:271
  (141 shorter events, 47.3 us)
Async XLA Ops:
  0.6 34.0 %collective-permute-start.2 = (bf16[64,64,192]{2,1,0:T(8,128)(2,1)}, bf16[64,64,192]{2,1,0:T(8,128)(2,1)}, u32[]{:S(2)}, u32[]{:S(2)}) collective-permute-start(bf16[64,64,192]{2,1,0:T(8,128)(2,1)} %bitcast.35), channel_id=1, source_target_pairs={{0,8},{8,0},{1,9},{9,1},{2,10},{10,2},{3,11},{11,3},{4,12},{12,4},... | collective-permute-start | bytes 4718600 | tf_op jit(solution)/shard_map/ppermute | solution.py:328
  5.3 14.5 %collective-permute-start.9 = (bf16[1024,128]{1,0:T(8,128)(2,1)S(1)}, bf16[1024,128]{1,0:T(8,128)(2,1)S(1)}, u32[]{:S(2)}, u32[]{:S(2)}) collective-permute-start(bf16[1024,128]{1,0:T(8,128)(2,1)S(1)} %pad_maximum_fusion.1.rest_0_), channel_id=1, source_target_pairs={{0,112},{16,96},{32,16},{48,0},{64,48},{80,32},{96,80},{112,64},{1... | collective-permute-start | bytes 786440 | tf_op jit(solution)/shard_map/ppermute | solution.py:212
  12.2 22.5 %collective-permute-start.8 = (bf16[1024,128]{1,0:T(8,128)(2,1)S(1)}, bf16[1024,128]{1,0:T(8,128)(2,1)S(1)}, u32[]{:S(2)}, u32[]{:S(2)}) collective-permute-start(bf16[1024,128]{1,0:T(8,128)(2,1)S(1)} %pad_maximum_fusion.1.rest_0_), channel_id=1, source_target_pairs={{0,96},{16,112},{32,0},{48,16},{64,32},{80,48},{96,64},{112,80},{1... | collective-permute-start | bytes 786440 | tf_op jit(solution)/shard_map/ppermute | solution.py:212
  12.9 32.9 %collective-permute-start.7 = (bf16[1024,128]{1,0:T(8,128)(2,1)S(1)}, bf16[1024,128]{1,0:T(8,128)(2,1)S(1)}, u32[]{:S(2)}, u32[]{:S(2)}) collective-permute-start(bf16[1024,128]{1,0:T(8,128)(2,1)S(1)} %pad_maximum_fusion.1.rest_0_), channel_id=1, source_target_pairs={{0,80},{16,64},{32,112},{48,96},{64,16},{80,0},{96,48},{112,32},{1... | collective-permute-start | bytes 786440 | tf_op jit(solution)/shard_map/ppermute | solution.py:212
  12.9 32.9 %collective-permute-start.6 = (bf16[1024,128]{1,0:T(8,128)(2,1)S(1)}, bf16[1024,128]{1,0:T(8,128)(2,1)S(1)}, u32[]{:S(2)}, u32[]{:S(2)}) collective-permute-start(bf16[1024,128]{1,0:T(8,128)(2,1)S(1)} %pad_maximum_fusion.1.rest_0_), channel_id=1, source_target_pairs={{0,64},{16,80},{32,96},{48,112},{64,0},{80,16},{96,32},{112,48},{1... | collective-permute-start | bytes 786440 | tf_op jit(solution)/shard_map/ppermute | solution.py:212
  19.9 25.9 %collective-permute-start.5 = (bf16[1024,128]{1,0:T(8,128)(2,1)S(1)}, bf16[1024,128]{1,0:T(8,128)(2,1)}, u32[]{:S(2)}, u32[]{:S(2)}) collective-permute-start(bf16[1024,128]{1,0:T(8,128)(2,1)S(1)} %pad_maximum_fusion.1.rest_0_), channel_id=1, source_target_pairs={{0,48},{16,32},{32,80},{48,64},{64,112},{80,96},{96,16},{112,0},{1... | collective-permute-start | bytes 786440 | tf_op jit(solution)/shard_map/ppermute | solution.py:212
  34.7 11.1 %collective-permute-start.4 = (bf16[1024,128]{1,0:T(8,128)(2,1)S(1)}, bf16[1024,128]{1,0:T(8,128)(2,1)}, u32[]{:S(2)}, u32[]{:S(2)}) collective-permute-start(bf16[1024,128]{1,0:T(8,128)(2,1)S(1)} %pad_maximum_fusion.1.rest_0_), channel_id=1, source_target_pairs={{0,32},{16,48},{32,64},{48,80},{64,96},{80,112},{96,0},{112,16},{1... | collective-permute-start | bytes 786440 | tf_op jit(solution)/shard_map/ppermute | solution.py:212
  34.7 11.2 %collective-permute-start.3 = (bf16[1024,128]{1,0:T(8,128)(2,1)S(1)}, bf16[1024,128]{1,0:T(8,128)(2,1)}, u32[]{:S(2)}, u32[]{:S(2)}) collective-permute-start(bf16[1024,128]{1,0:T(8,128)(2,1)S(1)} %pad_maximum_fusion.1.rest_0_), channel_id=1, source_target_pairs={{0,16},{16,0},{32,48},{48,32},{64,80},{80,64},{96,112},{112,96},{1... | collective-permute-start | bytes 786440 | tf_op jit(solution)/shard_map/ppermute | solution.py:212
  108.7 53.3 %all-to-all-start.1 = ((bf16[64,112,128]{2,1,0:T(8,128)(2,1)}), bf16[64,112,128]{2,1,0:T(8,128)(2,1)}, u32[]{:S(2)}, u32[]{:S(2)}) async-start(bf16[64,112,128]{2,1,0:T(8,128)(2,1)} %chip_sum.1), calls=%async_computation.1 | async-start | bytes 3670016 | tf_op jit(solution)/shard_map/all_to_all | solution.py:298
  126.1 30.2 %collective-permute-start.17 = (bf16[1024,128]{1,0:T(8,128)(2,1)S(1)}, bf16[1024,128]{1,0:T(8,128)(2,1)S(1)}, u32[]{:S(2)}, u32[]{:S(2)}) collective-permute-start(bf16[1024,128]{1,0:T(8,128)(2,1)S(1)} %pad_maximum_fusion.2.rest_0_), channel_id=1, source_target_pairs={{0,7},{1,4},{2,5},{3,6},{4,3},{5,0},{6,1},{7,2},{8,15},{9,12},{10,... | collective-permute-start | bytes 786440 | tf_op jit(solution)/shard_map/ppermute | solution.py:212
  129.7 31.8 %collective-permute-start.16 = (bf16[1024,128]{1,0:T(8,128)(2,1)S(1)}, bf16[1024,128]{1,0:T(8,128)(2,1)S(1)}, u32[]{:S(2)}, u32[]{:S(2)}) collective-permute-start(bf16[1024,128]{1,0:T(8,128)(2,1)S(1)} %pad_maximum_fusion.2.rest_0_), channel_id=1, source_target_pairs={{0,3},{1,0},{2,1},{3,2},{4,7},{5,4},{6,5},{7,6},{8,11},{9,8},{10,9... | collective-permute-start | bytes 786440 | tf_op jit(solution)/shard_map/ppermute | solution.py:212
  130.6 41.7 %collective-permute-start.15 = (bf16[1024,128]{1,0:T(8,128)(2,1)S(1)}, bf16[1024,128]{1,0:T(8,128)(2,1)S(1)}, u32[]{:S(2)}, u32[]{:S(2)}) collective-permute-start(bf16[1024,128]{1,0:T(8,128)(2,1)S(1)} %pad_maximum_fusion.2.rest_0_), channel_id=1, source_target_pairs={{0,6},{1,7},{2,4},{3,5},{4,2},{5,3},{6,0},{7,1},{8,14},{9,15},{10,... | collective-permute-start | bytes 786440 | tf_op jit(solution)/shard_map/ppermute | solution.py:212
  131.1 41.2 %collective-permute-start.14 = (bf16[1024,128]{1,0:T(8,128)(2,1)S(1)}, bf16[1024,128]{1,0:T(8,128)(2,1)S(1)}, u32[]{:S(2)}, u32[]{:S(2)}) collective-permute-start(bf16[1024,128]{1,0:T(8,128)(2,1)S(1)} %pad_maximum_fusion.2.rest_0_), channel_id=1, source_target_pairs={{0,2},{1,3},{2,0},{3,1},{4,6},{5,7},{6,4},{7,5},{8,10},{9,11},{10,... | collective-permute-start | bytes 786440 | tf_op jit(solution)/shard_map/ppermute | solution.py:212
  134.1 38.2 %collective-permute-start.13 = (bf16[1024,128]{1,0:T(8,128)(2,1)S(1)}, bf16[1024,128]{1,0:T(8,128)(2,1)}, u32[]{:S(2)}, u32[]{:S(2)}) collective-permute-start(bf16[1024,128]{1,0:T(8,128)(2,1)S(1)} %pad_maximum_fusion.2.rest_0_), channel_id=1, source_target_pairs={{0,5},{1,6},{2,7},{3,4},{4,1},{5,2},{6,3},{7,0},{8,13},{9,14},{10,... | collective-permute-start | bytes 786440 | tf_op jit(solution)/shard_map/ppermute | solution.py:212
  156.3 16.0 %collective-permute-start.12 = (bf16[1024,128]{1,0:T(8,128)(2,1)S(1)}, bf16[1024,128]{1,0:T(8,128)(2,1)}, u32[]{:S(2)}, u32[]{:S(2)}) collective-permute-start(bf16[1024,128]{1,0:T(8,128)(2,1)S(1)} %pad_maximum_fusion.2.rest_0_), channel_id=1, source_target_pairs={{0,1},{1,2},{2,3},{3,0},{4,5},{5,6},{6,7},{7,4},{8,9},{9,10},{10,1... | collective-permute-start | bytes 786440 | tf_op jit(solution)/shard_map/ppermute | solution.py:212
  161.5 10.8 %collective-permute-start.11 = (bf16[1024,128]{1,0:T(8,128)(2,1)S(1)}, bf16[1024,128]{1,0:T(8,128)(2,1)}, u32[]{:S(2)}, u32[]{:S(2)}) collective-permute-start(bf16[1024,128]{1,0:T(8,128)(2,1)S(1)} %pad_maximum_fusion.2.rest_0_), channel_id=1, source_target_pairs={{0,4},{1,5},{2,6},{3,7},{4,0},{5,1},{6,2},{7,3},{8,12},{9,13},{10,... | collective-permute-start | bytes 786440 | tf_op jit(solution)/shard_map/ppermute | solution.py:212
  164.6 37.9 %all-to-all-start.2 = ((bf16[16,112,128]{2,1,0:T(8,128)(2,1)}), bf16[16,112,128]{2,1,0:T(8,128)(2,1)}, u32[]{:S(2)}, u32[]{:S(2)}) async-start(bf16[16,112,128]{2,1,0:T(8,128)(2,1)} %chunk_sum.1), calls=%async_computation.2 | async-start | bytes 917504 | tf_op jit(solution)/shard_map/all_to_all | solution.py:300
  180.5 14.9 %collective-permute-start.18 = (bf16[1024,128]{1,0:T(8,128)(2,1)}, bf16[1024,128]{1,0:T(8,128)(2,1)S(1)}, u32[]{:S(2)}, u32[]{:S(2)}) collective-permute-start(bf16[1024,128]{1,0:T(8,128)(2,1)} %get-tuple-element.42), channel_id=1, source_target_pairs={{0,16},{16,0},{32,48},{48,32},{64,80},{80,64},{96,112},{112,96},{1... | collective-permute-start | bytes 786440 | tf_op jit(solution)/shard_map/ppermute | solution.py:212
  182.5 19.3 %collective-permute-start.19 = (bf16[1024,128]{1,0:T(8,128)(2,1)}, bf16[1024,128]{1,0:T(8,128)(2,1)}, u32[]{:S(2)}, u32[]{:S(2)}) collective-permute-start(bf16[1024,128]{1,0:T(8,128)(2,1)} %get-tuple-element.43), channel_id=1, source_target_pairs={{0,32},{16,48},{32,64},{48,80},{64,96},{80,112},{96,0},{112,16},{1... | collective-permute-start | bytes 786440 | tf_op jit(solution)/shard_map/ppermute | solution.py:212
  185.6 16.9 %collective-permute-start.20 = (bf16[1024,128]{1,0:T(8,128)(2,1)}, bf16[1024,128]{1,0:T(8,128)(2,1)}, u32[]{:S(2)}, u32[]{:S(2)}) collective-permute-start(bf16[1024,128]{1,0:T(8,128)(2,1)} %get-tuple-element.44), channel_id=1, source_target_pairs={{0,48},{16,32},{32,80},{48,64},{64,112},{80,96},{96,16},{112,0},{1... | collective-permute-start | bytes 786440 | tf_op jit(solution)/shard_map/ppermute | solution.py:212
  188.9 29.5 %collective-permute-start.21 = (bf16[1024,128]{1,0:T(8,128)(2,1)}, bf16[1024,128]{1,0:T(8,128)(2,1)}, u32[]{:S(2)}, u32[]{:S(2)}) collective-permute-start(bf16[1024,128]{1,0:T(8,128)(2,1)} %get-tuple-element.45), channel_id=1, source_target_pairs={{0,64},{16,80},{32,96},{48,112},{64,0},{80,16},{96,32},{112,48},{1... | collective-permute-start | bytes 786440 | tf_op jit(solution)/shard_map/ppermute | solution.py:212
  189.4 29.0 %collective-permute-start.22 = (bf16[1024,128]{1,0:T(8,128)(2,1)}, bf16[1024,128]{1,0:T(8,128)(2,1)}, u32[]{:S(2)}, u32[]{:S(2)}) collective-permute-start(bf16[1024,128]{1,0:T(8,128)(2,1)} %get-tuple-element.46), channel_id=1, source_target_pairs={{0,80},{16,64},{32,112},{48,96},{64,16},{80,0},{96,48},{112,32},{1... | collective-permute-start | bytes 786440 | tf_op jit(solution)/shard_map/ppermute | solution.py:212
  195.3 27.3 %collective-permute-start.23 = (bf16[1024,128]{1,0:T(8,128)(2,1)}, bf16[1024,128]{1,0:T(8,128)(2,1)}, u32[]{:S(2)}, u32[]{:S(2)}) collective-permute-start(bf16[1024,128]{1,0:T(8,128)(2,1)} %get-tuple-element.47), channel_id=1, source_target_pairs={{0,96},{16,112},{32,0},{48,16},{64,32},{80,48},{96,64},{112,80},{1... | collective-permute-start | bytes 786440 | tf_op jit(solution)/shard_map/ppermute | solution.py:212
  201.8 20.8 %collective-permute-start.24 = (bf16[1024,128]{1,0:T(8,128)(2,1)}, bf16[1024,128]{1,0:T(8,128)(2,1)}, u32[]{:S(2)}, u32[]{:S(2)}) collective-permute-start(bf16[1024,128]{1,0:T(8,128)(2,1)} %get-tuple-element.48), channel_id=1, source_target_pairs={{0,112},{16,96},{32,16},{48,0},{64,48},{80,32},{96,80},{112,64},{1... | collective-permute-start | bytes 786440 | tf_op jit(solution)/shard_map/ppermute | solution.py:212
  202.5 26.7 %collective-permute-start.31 = (bf16[1792,128]{1,0:T(8,128)(2,1)}, bf16[1792,128]{1,0:T(8,128)(2,1)}, u32[]{:S(2)}, u32[]{:S(2)}) collective-permute-start(bf16[1792,128]{1,0:T(8,128)(2,1)} %bitcast.15.piece), channel_id=1, source_target_pairs={{0,1},{1,2},{2,3},{3,0},{4,5},{5,6},{6,7},{7,4},{8,9},{9,10},{10,1... | collective-permute-start | bytes 1376264 | tf_op jit(solution)/shard_map/ppermute | solution.py:304
  218.4 13.7 %collective-permute-start.29 = (bf16[1792,128]{1,0:T(8,128)(2,1)}, bf16[1792,128]{1,0:T(8,128)(2,1)}, u32[]{:S(2)}, u32[]{:S(2)}) collective-permute-start(bf16[1792,128]{1,0:T(8,128)(2,1)} %bitcast.15.piece), channel_id=1, source_target_pairs={{0,3},{1,0},{2,1},{3,2},{4,7},{5,4},{6,5},{7,6},{8,11},{9,8},{10,9... | collective-permute-start | bytes 1376264 | tf_op jit(solution)/shard_map/ppermute | solution.py:304
  218.5 19.6 %collective-permute-start.27 = (bf16[1792,128]{1,0:T(8,128)(2,1)}, bf16[1792,128]{1,0:T(8,128)(2,1)}, u32[]{:S(2)}, u32[]{:S(2)}) collective-permute-start(bf16[1792,128]{1,0:T(8,128)(2,1)} %bitcast.15.piece), channel_id=1, source_target_pairs={{0,2},{1,3},{2,0},{3,1},{4,6},{5,7},{6,4},{7,5},{8,10},{9,11},{10,... | collective-permute-start | bytes 1376264 | tf_op jit(solution)/shard_map/ppermute | solution.py:304
  225.1 13.0 %collective-permute-start.25 = (bf16[512,128]{1,0:T(8,128)(2,1)}, bf16[512,128]{1,0:T(8,128)(2,1)S(1)}, u32[]{:S(2)}, u32[]{:S(2)}) collective-permute-start(bf16[512,128]{1,0:T(8,128)(2,1)} %get-tuple-element.50), channel_id=1, source_target_pairs={{0,8},{8,0},{1,9},{9,1},{2,10},{10,2},{3,11},{11,3},{4,12},{12,4},... | collective-permute-start | bytes 393224 | tf_op jit(solution)/shard_map/ppermute | solution.py:381
  227.5 14.2 %collective-permute-start.33 = (bf16[1792,128]{1,0:T(8,128)(2,1)}, bf16[1792,128]{1,0:T(8,128)(2,1)}, u32[]{:S(2)}, u32[]{:S(2)}) collective-permute-start(bf16[1792,128]{1,0:T(8,128)(2,1)} %bitcast.15.piece), channel_id=1, source_target_pairs={{0,8},{8,0},{1,9},{9,1},{2,10},{10,2},{3,11},{11,3},{4,12},{12,4},... | collective-permute-start | bytes 1376264 | tf_op jit(solution)/shard_map/ppermute | solution.py:306
  229.2 20.4 %collective-permute-start.32 = (bf16[1792,128]{1,0:T(8,128)(2,1)}, bf16[1792,128]{1,0:T(8,128)(2,1)}, u32[]{:S(2)}, u32[]{:S(2)}) collective-permute-start(bf16[1792,128]{1,0:T(8,128)(2,1)} %collective-permute-done.31.piece), channel_id=1, source_target_pairs={{0,8},{8,0},{1,9},{9,1},{2,10},{10,2},{3,11},{11,3},{4,12},{12,4},... | collective-permute-start | bytes 1376264 | tf_op jit(solution)/shard_map/ppermute | solution.py:306
  232.2 20.1 %collective-permute-start.30 = (bf16[1792,128]{1,0:T(8,128)(2,1)}, bf16[1792,128]{1,0:T(8,128)(2,1)S(1)}, u32[]{:S(2)}, u32[]{:S(2)}) collective-permute-start(bf16[1792,128]{1,0:T(8,128)(2,1)} %collective-permute-done.29.piece), channel_id=1, source_target_pairs={{0,8},{8,0},{1,9},{9,1},{2,10},{10,2},{3,11},{11,3},{4,12},{12,4},... | collective-permute-start | bytes 1376264 | tf_op jit(solution)/shard_map/ppermute | solution.py:306
  238.1 20.2 %collective-permute-start.28 = (bf16[1792,128]{1,0:T(8,128)(2,1)}, bf16[1792,128]{1,0:T(8,128)(2,1)S(1)}, u32[]{:S(2)}, u32[]{:S(2)}) collective-permute-start(bf16[1792,128]{1,0:T(8,128)(2,1)} %collective-permute-done.27.piece), channel_id=1, source_target_pairs={{0,8},{8,0},{1,9},{9,1},{2,10},{10,2},{3,11},{11,3},{4,12},{12,4},... | collective-permute-start | bytes 1376264 | tf_op jit(solution)/shard_map/ppermute | solution.py:306
  (30 other events, 413.7 us)

commit v4 on v3

--- a/solution.py
+++ b/solution.py
@@ -18,14 +18,8 @@
 CHUNK = 32
 UNROLL = 8
 FINISH = (
-    ("m", 0),
-    ("y", 0),
-    ("m", 1),
-    ("m", 3),
-    ("y", 1),
-    ("y", 3),
-    ("m", 2),
-    ("y", 2),
+    (("m", 0), ("y", 0), ("m", 1), ("m", 3), ("y", 1), ("y", 3)),
+    (("m", 2), ("y", 2)),
 )
 VMEM_LIMIT = 60 * 1024 * 1024
 
@@ -194,23 +188,51 @@
     )(parts)
 
 
-def step_perm(axes, p):
-    big, small = p >> 1, p & 1
-    perm = []
-    for i in range(8):
-        if axes == ("z", "yh"):
-            to = (((i >> 1) + big) % 4) * 2 + ((i & 1) ^ small)
-        else:
-            to = ((i >> 2) ^ small) * 4 + ((i & 3) + big) % 4
-        perm.append((i, to))
-    return perm
-
-
-def send_steps(pieces, axes):
-    got = [pieces[0]]
-    for p in range(1, 8):
-        got.append(lax.ppermute(pieces[p], axes, step_perm(axes, p)))
+def ring_shift(value, axis, k):
+    return lax.ppermute(value, axis, [(i, (i + k) % 4) for i in range(4)])
+
+
+def flip(value, axis):
+    return lax.ppermute(value, axis, [(0, 1), (1, 0)])
+
+
+def gather_steps(value, ring, pair):
+    got = [value] * 8
+    got[1] = flip(value, pair)
+    for small in range(2):
+        for big in (2, 1, 3):
+            p = 2 * big + small
+            got[p] = ring_shift(got[small], ring, big)
     return got
+
+
+def pair_kernel(*refs):
+    total = refs[0][...].astype(F32)
+    for ref in refs[1:-1]:
+        total = total + ref[...].astype(F32)
+    refs[-1][...] = total.astype(BF)
+
+
+def pair_sum(parts):
+    vm = pl.BlockSpec(memory_space=pltpu.VMEM)
+    return pl.pallas_call(
+        pair_kernel,
+        out_shape=jax.ShapeDtypeStruct((1024, 128), BF),
+        in_specs=[vm] * len(parts),
+        out_specs=vm,
+        cost_estimate=pl.CostEstimate(flops=1 << 19, bytes_accessed=5 << 18, transcendentals=0),
+        name="pair_sum",
+    )(*parts)
+
+
+def scatter_steps(pieces, ring, pair):
+    far, near = [pieces[1]], [pieces[0]]
+    for small, got in ((1, far), (0, near)):
+        for big in (2, 1, 3):
+            p = 2 * big + small
+            got.append(ring_shift(pieces[p], ring, big))
+    far = pair_sum(far)
+    return near + [flip(far, pair)]
 
 
 def node_kernel(*refs):
@@ -246,47 +268,63 @@
     return jnp.concatenate([mine, got], axis=0)
 
 
-def finish_kernel(lane_ref, piece, *rest):
-    outs, held, sems = rest[-7:-4], rest[-4:-1], rest[-1]
-    lane = pl.multiple_of(lane_ref[0], 128)
-    targets = (
-        outs[0].at[:, pl.ds(lane, 128)],
-        outs[1].at[:, pl.ds(lane, 128)],
-        outs[2].at[pl.ds(lane, 128), :],
-    )
-    moves = [pltpu.make_async_copy(held[k], targets[k], sems.at[k]) for k in range(3)]
-    held[0][...] = piece[:512, :].astype(F32) * (1.0 / 256.0)
-    moves[0].start()
-    held[1][...] = piece[512:1536, :].astype(F32) * (1.0 / 256.0)
-    moves[1].start()
-    held[2][...] = (piece[1536:, :].astype(F32) * (1.0 / 256.0)).T
-    moves[2].start()
-    for move in moves:
-        move.wait()
-
-
-def finish_grads(lane, piece, outs):
-    vm = pl.BlockSpec(memory_space=pltpu.VMEM)
+def finish_kernel(n, lane_ref, *rest):
+    pieces, rest = rest[:n], rest[-9:]
+    outs = rest[:3]
+    taken, first, second, third, in_sem, out_sem = rest[3:9]
+    reads = [
+        pltpu.make_async_copy(piece, taken.at[k], in_sem.at[k]) for k, piece in enumerate(pieces)
+    ]
+    for read in reads:
+        read.start()
+    writes = []
+    for k in range(n):
+        lane = pl.multiple_of(lane_ref[k], 128)
+        held = (first.at[k], second.at[k], third.at[k])
+        targets = (
+            outs[0].at[:, pl.ds(lane, 128)],
+            outs[1].at[:, pl.ds(lane, 128)],
+            outs[2].at[pl.ds(lane, 128), :],
+        )
+        moves = [
+            pltpu.make_async_copy(held[i], targets[i], out_sem.at[3 * k + i]) for i in range(3)
+        ]
+        reads[k].wait()
+        first[k] = taken[k, :512, :].astype(F32) * (1.0 / 256.0)
+        moves[0].start()
+        second[k] = taken[k, 512:1536, :].astype(F32) * (1.0 / 256.0)
+        moves[1].start()
+        third[k] = (taken[k, 1536:, :].astype(F32) * (1.0 / 256.0)).T
+        moves[2].start()
+        writes += moves
+    for write in writes:
+        write.wait()
+
+
+def finish_grads(lanes, pieces, outs):
     any_spec = pl.BlockSpec(memory_space=pl.ANY)
-    return pl.pallas_call(
-        finish_kernel,
+    n = len(pieces)
+    return pl.pallas_call(
+        functools.partial(finish_kernel, n),
         out_shape=(
             jax.ShapeDtypeStruct((512, 1024), F32),
             jax.ShapeDtypeStruct((1024, 1024), F32),
             jax.ShapeDtypeStruct((1024, 256), F32),
         ),
-        in_specs=[pl.BlockSpec(memory_space=pltpu.SMEM), vm] + [any_spec] * len(outs),
+        in_specs=[pl.BlockSpec(memory_space=pltpu.SMEM)] + [any_spec] * (n + len(outs)),
         out_specs=(any_spec,) * 3,
         scratch_shapes=[
-            pltpu.VMEM((512, 128), F32),
-            pltpu.VMEM((1024, 128), F32),
-            pltpu.VMEM((128, 256), F32),
-            pltpu.SemaphoreType.DMA((3,)),
+            pltpu.VMEM((n, 1792, 128), BF),
+            pltpu.VMEM((n, 512, 128), F32),
+            pltpu.VMEM((n, 1024, 128), F32),
+            pltpu.VMEM((n, 128, 256), F32),
+            pltpu.SemaphoreType.DMA((n,)),
+            pltpu.SemaphoreType.DMA((3 * n,)),
         ],
-        input_output_aliases={2 + k: k for k in range(len(outs))},
-        cost_estimate=pl.CostEstimate(flops=1 << 20, bytes_accessed=2 << 20, transcendentals=0),
+        input_output_aliases={1 + n + k: k for k in range(len(outs))},
+        cost_estimate=pl.CostEstimate(flops=n << 20, bytes_accessed=n << 20, transcendentals=0),
         name="finish_grads",
-    )(lane, piece, *outs)
+    )(lanes, *pieces, *outs)
 
 
 def sum_grads(core, operands):
@@ -307,11 +345,10 @@
     place = ((x - jnp.arange(4, dtype=jnp.int32)) & 3) * 128
     at_mine, at_yours = core * 512 + place, (1 - core) * 512 + place
     outs = ()
-    for side, k in FINISH:
-        if side == "m":
-            outs = finish_grads(at_mine[k : k + 1], mine[k], outs)
-        else:
-            outs = finish_grads(at_yours[k : k + 1], yours[k], outs)
+    for order in FINISH:
+        lanes = jnp.stack([(at_mine if side == "m" else at_yours)[k] for side, k in order])
+        pieces = [(mine if side == "m" else yours)[k] for side, k in order]
+        outs = finish_grads(lanes, pieces, outs)
     return outs
 
 
@@ -346,7 +383,7 @@
     p = jnp.arange(16, dtype=jnp.int32)
     place = (((z + (p >> 2)) & 3) * 4 + (yh ^ ((p >> 1) & 1)) * 2 + (core ^ (p & 1))) * 512
     shard = halves(features, core)
-    pieces = send_steps([shard] * 8, ("z", "yh"))
+    pieces = gather_steps(shard, "z", "yh")
     blk_own, _ = lax.optimization_barrier((blk_own, shard))
     blk_own = with_layout_constraint(blk_own, Layout((0, 1, 2))).transpose(2, 0, 1)
     blk_other = blk_other.transpose(2, 0, 1)
@@ -373,11 +410,11 @@
     direct = cotangent.astype(F32) + grad_joined[:, :256]
     grad_agg = grad_joined[:, 256:].astype(BF)
 
-    pieces = send_steps([halves(grad_agg, core)] * 8, COL)
+    pieces = gather_steps(halves(grad_agg, core), "x", "yl")
     operands = (joined, act_one, cotangent, grad_pre_one, grad_pre_two, act_two)
     grad_in, grad_mid, grad_out = sum_grads(core, operands)
     back = cell_products(True, bwd_off, count, place, blk_own, blk_other, pieces)
-    mine, yours = node_sum(send_steps(back, ("z", "yh")))
+    mine, yours = node_sum(scatter_steps(back, "z", "yh"))
     got = lax.ppermute(yours, "core", swap).astype(F32)
     first = core == 0
     relaid = jnp.concatenate([jnp.where(first, mine, got), jnp.where(first, got, mine)], axis=1)

time: 265 us -> 222 us (0.84)
  waiting for transfers between devices: 60.6 us -> 38.7 us
  Pallas kernels: 53.5 us -> 41.5 us
  starting transfers between devices: 79.3 us -> 68.9 us
    ppermute x21, waiting for transfers between devices: 48.4 us -> 29.8 us  [the longest x3 15.7 us: flip(): return lax.ppermute(value, axis, [(0, 1), (1, 0)])]
    ppermute x3, starting transfers between devices: 19.4 us -> 3.37 us  [sum_grads(): mine.append(lax.ppermute(lanes, 'x', [(i, (i + k) % 4) for i in range(4)]))]
    pallas_call x8 -> x3, Pallas kernels: 21.1 us -> 9.36 us  [the longest x2 7.34 us: finish_grads(): pl.pallas_call(functools.partial(finish_kernel, n), out_shape=(jax.ShapeD...]
    ppermute x21, starting transfers between devices: 38 us -> 47 us  [the longest x18 37.4 us: ring_shift(): return lax.ppermute(value, axis, [(i, (i + k) % 4) for i in range(4)])]
    ppermute x3, waiting for transfers between devices: 10.2 us -> 5.02 us  [sum_grads(): mine.append(lax.ppermute(lanes, 'x', [(i, (i + k) % 4) for i in range(4)]))]
    another operation x0 -> x1, local copies, waits for them, and re-layouts: none -> 4.38 us  [sum_grads(): jnp.stack([(at_mine if side == 'm' else at_yours)[k] for side, k in order])]
    all_to_all x1, starting transfers between devices: 12.9 us -> 9.42 us  [sum_grads(): lax.all_to_all(chip_sum(own, got), ('z', 'yh', 'yl', 'x'), 0, 0, tiled=True)]
  transfers between devices with their start and end apart: 36 -> 36, of which waited for: 10 -> 10; matrix products, arithmetic and copies ran while one was open for 8% -> 12% of each run, Pallas kernels for 14% -> 11%
where the time goes in v4:
time: 222 us; the launch traced here: 220 us
  starting transfers between devices  68.9 us (31%)
  Pallas kernels  41.5 us (19%)
  waiting for transfers between devices  38.7 us (17%)
  blocking collectives  31.4 us (14%)
  local copies, waits for them, and re-layouts  19 us (9%)
  matrix products  12.4 us (6%)
  other arithmetic  6.53 us (3%)
    ppermute x18, starting transfers between devices, ring_shift(): return lax.ppermute(value, axis, [(i, (i + k) % 4) for i in range(4)])  37.4 us
    all_to_all x1, blocking collectives, shards(): cells = lax.all_to_all(cells, ('core', 'yl', 'x'), 0, 0, tiled=True)  31.4 us
    ppermute x3, waiting for transfers between devices, flip(): return lax.ppermute(value, axis, [(0, 1), (1, 0)])  15.7 us
    pallas_call x2, Pallas kernels, cell_products(): pl.pallas_call(functools.partial(cells_kernel, transposed), out_shape=(ja...  14.2 us
    ppermute x18, waiting for transfers between devices, ring_shift(): return lax.ppermute(value, axis, [(i, (i + k) % 4) for i in range(4)])  14.1 us
    ppermute x3, starting transfers between devices, flip(): return lax.ppermute(value, axis, [(0, 1), (1, 0)])  9.61 us
    pallas_call x2, Pallas kernels, local_grads(): pl.pallas_call(grads_kernel, out_shape=jax.ShapeDtypeStruct((1792, 512),...  9.59 us
    all_to_all x1, starting transfers between devices, sum_grads(): lax.all_to_all(chip_sum(own, got), ('z', 'yh', 'yl', 'x'), 0, 0, tiled=True)  9.42 us
  transfers between devices with their start and end apart: 36, of which 10 were waited for; matrix products, arithmetic and copies ran while one was open for 12% of the time, Pallas kernels for 11%

profile of v4, /device:TPU:0, one launch (start us, length us, event | category | flops | bytes accessed | tf_op | source)
XLA Modules:
  0.0 220.5 jit_solution(4261761452438034840)
XLA Ops:
  5.3 3.4 %collective-permute-start.3 = (bf16[1024,128]{1,0:T(8,128)(2,1)S(1)}, bf16[1024,128]{1,0:T(8,128)(2,1)S(1)}, u32[]{:S(2)}, u32[]{:S(2)}) collective-permute-start(bf16[1024,128]{1,0:T(8,128)(2,1)S(1)} %pad_maximum_fusion.1.rest_0_), channel_id=1, source_target_pairs={{0,16},{16,0},{1,17},{17,1},{2,18},{18,2},{3,19},{19,3},{4,20},{20... | collective-permute-start | bytes 786440 | tf_op jit(solution)/shard_map/ppermute | solution.py:196
  11.4 3.6 %collective-permute-start.6 = (bf16[1024,128]{1,0:T(8,128)(2,1)S(1)}, bf16[1024,128]{1,0:T(8,128)(2,1)S(1)}, u32[]{:S(2)}, u32[]{:S(2)}) collective-permute-start(bf16[1024,128]{1,0:T(8,128)(2,1)S(1)} %pad_maximum_fusion.1.rest_0_), channel_id=1, source_target_pairs={{0,64},{32,96},{64,0},{96,32},{1,65},{33,97},{65,1},{97,33},{2,66}... | collective-permute-start | bytes 786440 | tf_op jit(solution)/shard_map/ppermute | solution.py:192
  19.1 7.6 %collective-permute-start.7 = (bf16[1024,128]{1,0:T(8,128)(2,1)S(1)}, bf16[1024,128]{1,0:T(8,128)(2,1)}, u32[]{:S(2)}, u32[]{:S(2)}) collective-permute-start(bf16[1024,128]{1,0:T(8,128)(2,1)S(1)} %collective-permute-done.3.rest_1_), channel_id=1, source_target_pairs={{0,64},{32,96},{64,0},{96,32},{1,65},{33,97},{65,1},{97,33},{2,66}... | collective-permute-start | bytes 786440 | tf_op jit(solution)/shard_map/ppermute | solution.py:192
  27.4 5.1 %copy.26 = bf16[64,64,192]{1,0,2:T(8,128)(2,1)} copy(bf16[64,64,192]{2,1,0:T(8,128)(2,1)} %bitcast.36) | data formatting | bytes 3145728 | tf_op jit(solution)/shard_map/layout_constraint | solution.py:388
  32.5 5.2 %copy.27 = bf16[64,64,192]{1,0,2:T(8,128)(2,1)} copy(bf16[64,64,192]{2,1,0:T(8,128)(2,1)} %collective-permute-done.2) | data formatting | bytes 3145728 | tf_op jit(solution)/shard_map/ppermute | solution.py:365
  38.5 6.7 %cells_forward.1 = bf16[16,512,128]{2,1,0:T(8,128)(2,1)} custom-call(s32[768]{0:T(1024)} %reshape.47.off_ref, s32[2]{0:T(128)} %copy-done.24, s32[16]{0:T(128)} %add_multiply_fusion.1.place_ref, bf16[192,64,64]{2,1,0:T(8,128)(2,1)} %bitcast.31, bf16[192,64,64]{2,1,0:T(8,128)(2,1)} %bitcast.33, bf16[1024,128]{1,0:T(8,128)(2,1)} %copy-done.9, ...), custom_call_target="tpu_custom_call" | custom-call | flops 402653184 | bytes 10485760 | tf_op jit(solution)/shard_map/cells_forward/pallas_call | solution.py:100
  45.2 31.4 %all_to_all.15 = bf16[16,512,128]{2,1,0:T(8,128)(2,1)S(1)} all-to-all(bf16[16,512,128]{2,1,0:T(8,128)(2,1)} %cells_forward.1), channel_id=1, replica_groups=mesh['z'=4,'yh'=2,'core'=2,'yl'=2,'x'=4] {'core','yl','x'}, dimensions={0} | all-to-all | bytes 4194304 | tf_op jit(solution)/shard_map/all_to_all | solution.py:391
  79.5 2.5 %multiply_convert_fusion.2 = (bf16[512,1024]{1,0:T(8,128)(2,1)}, f32[512,1024]{1,0:T(8,128)S(1)}) fusion(bf16[512,1024]{1,0:T(8,128)(2,1)S(1)} %get-tuple-element.59.act_one, bf16[1024,1024]{1,0:T(8,128)(2,1)S(1)} %copy-done), kind=kOutput, calls=%fused_computation.3 | convolution fusion | flops 1076363264 | bytes 6291456 | tf_op jit(solution)/shard_map/dot_general | solution.py:398
  82.9 2.7 %multiply_convert_fusion.gp_one = bf16[512,1024]{1,0:T(8,128)(2,1)} fusion(f32[512,1024]{1,0:T(8,128)S(1)} %get-tuple-element.60, bf16[512,1024]{1,0:T(8,128)(2,1)S(1)} %multiply_convert_fusion.1.gp_two, bf16[1024,1024]{1,0:T(8,128)(2,1)S(1)} %copy-done), kind=kOutput, calls=%fused_computation.1 | convolution fusion | flops 1078460416 | bytes 6291456 | tf_op jit(solution)/shard_map/dot_general | solution.py:407
  85.6 4.8 %shard_map.129 = bf16[1792,512]{1,0:T(8,128)(2,1)} custom-call(s32[1]{0:T(128)} %bitcast.6.half_ref, bf16[512,512]{1,0:T(8,128)(2,1)} %pad_maximum_fusion.joined, bf16[512,1024]{1,0:T(8,128)(2,1)} %copy-done.3, bf16[512,256]{1,0:T(8,128)(2,1)} %cot.3, bf16[512,1024]{1,0:T(8,128)(2,1)} %multiply_convert_fusion.gp_one, bf16[512,1024]{1,0:T(8,128)(2,1)} %copy-done.4, ...), custom_call_target="tpu_custom_call" | custom-call | flops 939524096 | bytes 8388608 | tf_op jit(solution)/shard_map/pallas_call | solution.py:139
  90.8 4.8 %shard_map.128.own = bf16[1792,512]{1,0:T(8,128)(2,1)} custom-call(s32[1]{0:T(128)} %bitcast.5.half_ref, bf16[512,512]{1,0:T(8,128)(2,1)} %pad_maximum_fusion.joined, bf16[512,1024]{1,0:T(8,128)(2,1)} %copy-done.3, bf16[512,256]{1,0:T(8,128)(2,1)} %cot.3, bf16[512,1024]{1,0:T(8,128)(2,1)} %multiply_convert_fusion.gp_one, bf16[512,1024]{1,0:T(8,128)(2,1)} %copy-done.4, ...), custom_call_target="tpu_custom_call" | custom-call | flops 939524096 | bytes 8388608 | tf_op jit(solution)/shard_map/pallas_call | solution.py:139
  95.6 3.7 %chip_sum.1 = bf16[64,112,128]{2,1,0:T(8,128)(2,1)} custom-call(bf16[1792,512]{1,0:T(8,128)(2,1)} %shard_map.128.own, bf16[1792,512]{1,0:T(8,128)(2,1)} %collective-permute-done.26.got), custom_call_target="tpu_custom_call" | custom-call | flops 1048576 | bytes 6291456 | tf_op jit(solution)/shard_map/chip_sum/pallas_call | solution.py:163
  99.3 9.4 %all-to-all-start.1 = ((bf16[64,112,128]{2,1,0:T(8,128)(2,1)}), bf16[64,112,128]{2,1,0:T(8,128)(2,1)}, u32[]{:S(2)}, u32[]{:S(2)}) async-start(bf16[64,112,128]{2,1,0:T(8,128)(2,1)} %chip_sum.1), calls=%async_computation.1 | async-start | bytes 3670016 | tf_op jit(solution)/shard_map/all_to_all | solution.py:336
  108.7 2.9 %fusion.14 = (bf16[512,512]{1,0:T(8,128)(2,1)S(1)}, f32[512,512]{1,0:T(8,128)}) fusion(bf16[512,1024]{1,0:T(8,128)(2,1)S(1)} %copy-done.1, bf16[512,1024]{1,0:T(8,128)(2,1)} %param.14), kind=kOutput, calls=%fused_computation.53 | convolution fusion | flops 537133056 | bytes 3670016 | tf_op jit(solution)/shard_map/dot_general | solution.py:409
  116.2 2.7 %collective-permute-start.14 = (bf16[1024,128]{1,0:T(8,128)(2,1)S(1)}, bf16[1024,128]{1,0:T(8,128)(2,1)S(1)}, u32[]{:S(2)}, u32[]{:S(2)}) collective-permute-start(bf16[1024,128]{1,0:T(8,128)(2,1)S(1)} %pad_maximum_fusion.2.rest_0_), channel_id=1, source_target_pairs={{0,2},{1,3},{2,0},{3,1},{4,6},{5,7},{6,4},{7,5},{8,10},{9,11},{10,... | collective-permute-start | bytes 786440 | tf_op jit(solution)/shard_map/ppermute | solution.py:192
  120.3 15.6 %collective-permute-done.11.rest_1_ = bf16[1024,128]{1,0:T(8,128)(2,1)S(1)} collective-permute-done((bf16[1024,128]{1,0:T(8,128)(2,1)S(1)}, bf16[1024,128]{1,0:T(8,128)(2,1)S(1)}, u32[]{:S(2)}, u32[]{:S(2)}) %collective-permute-start.11) | collective-permute-done | bytes 262176 | tf_op jit(solution)/shard_map/ppermute | solution.py:196
  137.5 2.7 %collective-permute-start.15 = (bf16[1024,128]{1,0:T(8,128)(2,1)S(1)}, bf16[1024,128]{1,0:T(8,128)(2,1)}, u32[]{:S(2)}, u32[]{:S(2)}) collective-permute-start(bf16[1024,128]{1,0:T(8,128)(2,1)S(1)} %collective-permute-done.11.rest_1_), channel_id=1, source_target_pairs={{0,2},{1,3},{2,0},{3,1},{4,6},{5,7},{6,4},{7,5},{8,10},{9,11},{10,... | collective-permute-start | bytes 786440 | tf_op jit(solution)/shard_map/ppermute | solution.py:192
  141.6 2.5 %chunk_sum.1 = bf16[16,112,128]{2,1,0:T(8,128)(2,1)} custom-call(bf16[64,112,128]{2,1,0:T(8,128)(2,1)} %all-to-all-done.1.parts), custom_call_target="tpu_custom_call" | custom-call | flops 1048576 | bytes 1048576 | tf_op jit(solution)/shard_map/chunk_sum/pallas_call | solution.py:181
  144.2 6.8 %all-to-all-start.2 = ((bf16[16,112,128]{2,1,0:T(8,128)(2,1)}), bf16[16,112,128]{2,1,0:T(8,128)(2,1)}, u32[]{:S(2)}, u32[]{:S(2)}) async-start(bf16[16,112,128]{2,1,0:T(8,128)(2,1)} %chunk_sum.1), calls=%async_computation.2 | async-start | bytes 917504 | tf_op jit(solution)/shard_map/all_to_all | solution.py:338
  151.7 2.8 %collective-permute-done.15.rest_5_ = bf16[1024,128]{1,0:T(8,128)(2,1)} collective-permute-done((bf16[1024,128]{1,0:T(8,128)(2,1)S(1)}, bf16[1024,128]{1,0:T(8,128)(2,1)}, u32[]{:S(2)}, u32[]{:S(2)}) %collective-permute-start.15) | collective-permute-done | bytes 262176 | tf_op jit(solution)/shard_map/ppermute | solution.py:192
  154.5 7.4 %cells_back.1 = (bf16[1024,128]{1,0:T(8,128)(2,1)}, bf16[1024,128]{1,0:T(8,128)(2,1)}, bf16[1024,128]{1,0:T(8,128)(2,1)}, bf16[1024,128]{1,0:T(8,128)(2,1)}, bf1...) custom-call(s32[768]{0:T(1024)} %reshape.49.off_ref, ...), custom_call_target="tpu_custom_call" | custom-call | flops 402653184 | bytes 10485760 | tf_op jit(solution)/shard_map/cells_back/pallas_call | solution.py:100
  162.0 4.1 %collective-permute-start.21 = (bf16[1024,128]{1,0:T(8,128)(2,1)}, bf16[1024,128]{1,0:T(8,128)(2,1)}, u32[]{:S(2)}, u32[]{:S(2)}) collective-permute-start(bf16[1024,128]{1,0:T(8,128)(2,1)} %get-tuple-element.28), channel_id=1, source_target_pairs={{0,64},{32,96},{64,0},{96,32},{1,65},{33,97},{65,1},{97,33},{2,66}... | collective-permute-start | bytes 786440 | tf_op jit(solution)/shard_map/ppermute | solution.py:192
  166.1 3.2 %collective-permute-start.23 = (bf16[1024,128]{1,0:T(8,128)(2,1)}, bf16[1024,128]{1,0:T(8,128)(2,1)}, u32[]{:S(2)}, u32[]{:S(2)}) collective-permute-start(bf16[1024,128]{1,0:T(8,128)(2,1)} %get-tuple-element.30), channel_id=1, source_target_pairs={{0,96},{32,0},{64,32},{96,64},{1,97},{33,1},{65,33},{97,65},{2,98}... | collective-permute-start | bytes 786440 | tf_op jit(solution)/shard_map/ppermute | solution.py:192
  170.2 3.4 %collective-permute-done.21.refs_1_ = bf16[1024,128]{1,0:T(8,128)(2,1)} collective-permute-done((bf16[1024,128]{1,0:T(8,128)(2,1)}, bf16[1024,128]{1,0:T(8,128)(2,1)}, u32[]{:S(2)}, u32[]{:S(2)}) %collective-permute-start.21) | collective-permute-done | bytes 262176 | tf_op jit(solution)/shard_map/ppermute | solution.py:192
  173.5 2.6 %collective-permute-start.20 = (bf16[1024,128]{1,0:T(8,128)(2,1)}, bf16[1024,128]{1,0:T(8,128)(2,1)}, u32[]{:S(2)}, u32[]{:S(2)}) collective-permute-start(bf16[1024,128]{1,0:T(8,128)(2,1)} %get-tuple-element.26), channel_id=1, source_target_pairs={{0,96},{32,0},{64,32},{96,64},{1,97},{33,1},{65,33},{97,65},{2,98}... | collective-permute-start | bytes 786440 | tf_op jit(solution)/shard_map/ppermute | solution.py:192
  176.2 6.1 %collective-permute-done.22.refs_2_ = bf16[1024,128]{1,0:T(8,128)(2,1)} collective-permute-done((bf16[1024,128]{1,0:T(8,128)(2,1)}, bf16[1024,128]{1,0:T(8,128)(2,1)}, u32[]{:S(2)}, u32[]{:S(2)}) %collective-permute-start.22) | collective-permute-done | bytes 262176 | tf_op jit(solution)/shard_map/ppermute | solution.py:192
  184.4 4.6 %collective-permute-start.24 = (bf16[1024,128]{1,0:T(8,128)(2,1)}, bf16[1024,128]{1,0:T(8,128)(2,1)}, u32[]{:S(2)}, u32[]{:S(2)}) collective-permute-start(bf16[1024,128]{1,0:T(8,128)(2,1)} %pair_sum.1), channel_id=1, source_target_pairs={{0,16},{16,0},{1,17},{17,1},{2,18},{18,2},{3,19},{19,3},{4,20},{20... | collective-permute-start | bytes 786440 | tf_op jit(solution)/shard_map/ppermute | solution.py:196
  189.2 3.2 %collective-permute-start.31 = (bf16[1792,128]{1,0:T(8,128)(2,1)}, bf16[1792,128]{1,0:T(8,128)(2,1)}, u32[]{:S(2)}, u32[]{:S(2)}) collective-permute-start(bf16[1792,128]{1,0:T(8,128)(2,1)} %bitcast.15.rest_0_), channel_id=1, source_target_pairs={{0,3},{1,0},{2,1},{3,2},{4,7},{5,4},{6,5},{7,6},{8,11},{9,8},{10,9... | collective-permute-start | bytes 1376264 | tf_op jit(solution)/shard_map/ppermute | solution.py:342
  193.1 4.4 %stack.31.lane_ref = s32[6]{0:T(128)} concatenate(s32[1]{0:T(128)} %get-tuple-element.66, s32[1]{0:T(128)} %get-tuple-element.53, s32[1]{0:T(128)} %get-tuple-element.67, s32[1]{0:T(128)} %get-tuple-element.68, s32[1]{0:T(128)} %get-tuple-element.52, s32[1]{0:T(128)} %get-tuple-element.51), dimensions={0} | concatenate | bytes 48 | tf_op jit(solution)/shard_map/stack | solution.py:349
  204.4 5.0 %collective-permute-done.30.rest_2_ = bf16[1792,128]{1,0:T(8,128)(2,1)} collective-permute-done((bf16[1792,128]{1,0:T(8,128)(2,1)}, bf16[1792,128]{1,0:T(8,128)(2,1)}, u32[]{:S(2)}, u32[]{:S(2)}) %collective-permute-start.30) | collective-permute-done | bytes 458784 | tf_op jit(solution)/shard_map/ppermute | solution.py:342
  212.2 4.3 %finish_grads.2 = (f32[512,1024]{1,0:T(8,128)}, f32[1024,1024]{1,0:T(8,128)}, f32[1024,256]{1,0:T(8,128)}) custom-call(s32[6]{0:T(128)} %stack.31.lane_ref, bf16[1792,128]{1,0:T(8,128)(2,1)} %bitcast.15.rest_0_, bf16[1792,128]{1,0:T(8,128)(2,1)} %copy-done.13, bf16[1792,128]{1,0:T(8,128)(2,1)} %collective-permute-done.30.rest_2_, ...), custom_call_target="tpu_custom_call" | custom-call | flops 6291456 | bytes 6291456 | tf_op jit(solution)/shard_map/finish_grads/pallas_call | solution.py:307
  217.3 3.0 %finish_grads.3 = (f32[512,1024]{1,0:T(8,128)}, f32[1024,1024]{1,0:T(8,128)}, f32[1024,256]{1,0:T(8,128)}) custom-call(s32[2]{0:T(128)} %pad_add_fusion.4.lane_ref, bf16[1792,128]{1,0:T(8,128)(2,1)} %collective-permute-done.27.rest_0_, bf16[1792,128]{1,0:T(8,128)(2,1)} %copy-done.12, ...), custom_call_target="tpu_custom_call", output_to_operand_aliasing={{0}: (3, {}), {1}: (4, {}), {2}: (5, {})} | custom-call | flops 2097152 | bytes 2097152 | tf_op jit(solution)/shard_map/finish_grads/pallas_call | solution.py:307
  (137 shorter events, 39.9 us)
Async XLA Ops:
  0.6 26.0 %collective-permute-start.2 = (bf16[64,64,192]{2,1,0:T(8,128)(2,1)}, bf16[64,64,192]{2,1,0:T(8,128)(2,1)}, u32[]{:S(2)}, u32[]{:S(2)}) collective-permute-start(bf16[64,64,192]{2,1,0:T(8,128)(2,1)} %bitcast.35), channel_id=1, source_target_pairs={{0,8},{8,0},{1,9},{9,1},{2,10},{10,2},{3,11},{11,3},{4,12},{12,4},... | collective-permute-start | bytes 4718600 | tf_op jit(solution)/shard_map/ppermute | solution.py:365
  2.3 8.9 %collective-permute-start = (s32[512]{0:T(512)S(1)}, s32[512]{0:T(512)S(1)}, u32[]{:S(2)}, u32[]{:S(2)}) collective-permute-start(s32[512]{0:T(512)S(1)} %pad_add_fusion.3), channel_id=1, source_target_pairs={{0,8},{8,0},{1,9},{9,1},{2,10},{10,2},{3,11},{11,3},{4,12},{12,4},... | collective-permute-start | bytes 6152 | tf_op jit(solution)/shard_map/ppermute | solution.py:364
  5.3 10.7 %collective-permute-start.3 = (bf16[1024,128]{1,0:T(8,128)(2,1)S(1)}, bf16[1024,128]{1,0:T(8,128)(2,1)S(1)}, u32[]{:S(2)}, u32[]{:S(2)}) collective-permute-start(bf16[1024,128]{1,0:T(8,128)(2,1)S(1)} %pad_maximum_fusion.1.rest_0_), channel_id=1, source_target_pairs={{0,16},{16,0},{1,17},{17,1},{2,18},{18,2},{3,19},{19,3},{4,20},{20... | collective-permute-start | bytes 786440 | tf_op jit(solution)/shard_map/ppermute | solution.py:196
  8.7 10.4 %collective-permute-start.4 = (bf16[1024,128]{1,0:T(8,128)(2,1)S(1)}, bf16[1024,128]{1,0:T(8,128)(2,1)S(1)}, u32[]{:S(2)}, u32[]{:S(2)}) collective-permute-start(bf16[1024,128]{1,0:T(8,128)(2,1)S(1)} %pad_maximum_fusion.1.rest_0_), channel_id=1, source_target_pairs={{0,32},{32,64},{64,96},{96,0},{1,33},{33,65},{65,97},{97,1},{2,34}... | collective-permute-start | bytes 786440 | tf_op jit(solution)/shard_map/ppermute | solution.py:192
  11.4 26.3 %collective-permute-start.6 = (bf16[1024,128]{1,0:T(8,128)(2,1)S(1)}, bf16[1024,128]{1,0:T(8,128)(2,1)S(1)}, u32[]{:S(2)}, u32[]{:S(2)}) collective-permute-start(bf16[1024,128]{1,0:T(8,128)(2,1)S(1)} %pad_maximum_fusion.1.rest_0_), channel_id=1, source_target_pairs={{0,64},{32,96},{64,0},{96,32},{1,65},{33,97},{65,1},{97,33},{2,66}... | collective-permute-start | bytes 786440 | tf_op jit(solution)/shard_map/ppermute | solution.py:192
  15.0 22.7 %collective-permute-start.8 = (bf16[1024,128]{1,0:T(8,128)(2,1)S(1)}, bf16[1024,128]{1,0:T(8,128)(2,1)S(1)}, u32[]{:S(2)}, u32[]{:S(2)}) collective-permute-start(bf16[1024,128]{1,0:T(8,128)(2,1)S(1)} %pad_maximum_fusion.1.rest_0_), channel_id=1, source_target_pairs={{0,96},{32,0},{64,32},{96,64},{1,97},{33,1},{65,33},{97,65},{2,98}... | collective-permute-start | bytes 786440 | tf_op jit(solution)/shard_map/ppermute | solution.py:192
  16.0 21.7 %collective-permute-start.5 = (bf16[1024,128]{1,0:T(8,128)(2,1)S(1)}, bf16[1024,128]{1,0:T(8,128)(2,1)}, u32[]{:S(2)}, u32[]{:S(2)}) collective-permute-start(bf16[1024,128]{1,0:T(8,128)(2,1)S(1)} %collective-permute-done.3.rest_1_), channel_id=1, source_target_pairs={{0,32},{32,64},{64,96},{96,0},{1,33},{33,65},{65,97},{97,1},{2,34}... | collective-permute-start | bytes 786440 | tf_op jit(solution)/shard_map/ppermute | solution.py:192
  19.1 18.6 %collective-permute-start.7 = (bf16[1024,128]{1,0:T(8,128)(2,1)S(1)}, bf16[1024,128]{1,0:T(8,128)(2,1)}, u32[]{:S(2)}, u32[]{:S(2)}) collective-permute-start(bf16[1024,128]{1,0:T(8,128)(2,1)S(1)} %collective-permute-done.3.rest_1_), channel_id=1, source_target_pairs={{0,64},{32,96},{64,0},{96,32},{1,65},{33,97},{65,1},{97,33},{2,66}... | collective-permute-start | bytes 786440 | tf_op jit(solution)/shard_map/ppermute | solution.py:192
  26.7 11.1 %collective-permute-start.9 = (bf16[1024,128]{1,0:T(8,128)(2,1)S(1)}, bf16[1024,128]{1,0:T(8,128)(2,1)}, u32[]{:S(2)}, u32[]{:S(2)}) collective-permute-start(bf16[1024,128]{1,0:T(8,128)(2,1)S(1)} %collective-permute-done.3.rest_1_), channel_id=1, source_target_pairs={{0,96},{32,0},{64,32},{96,64},{1,97},{33,1},{65,33},{97,65},{2,98}... | collective-permute-start | bytes 786440 | tf_op jit(solution)/shard_map/ppermute | solution.py:192
  90.4 5.2 %collective-permute-start.26 = (bf16[1792,512]{1,0:T(8,128)(2,1)}, bf16[1792,512]{1,0:T(8,128)(2,1)}, u32[]{:S(2)}, u32[]{:S(2)}) collective-permute-start(bf16[1792,512]{1,0:T(8,128)(2,1)} %shard_map.129), channel_id=1, source_target_pairs={{0,8},{8,0},{1,9},{9,1},{2,10},{10,2},{3,11},{11,3},{4,12},{12,4},... | collective-permute-start | bytes 5505032 | tf_op jit(solution)/shard_map/ppermute | solution.py:334
  99.3 42.3 %all-to-all-start.1 = ((bf16[64,112,128]{2,1,0:T(8,128)(2,1)}), bf16[64,112,128]{2,1,0:T(8,128)(2,1)}, u32[]{:S(2)}, u32[]{:S(2)}) async-start(bf16[64,112,128]{2,1,0:T(8,128)(2,1)} %chip_sum.1), calls=%async_computation.1 | async-start | bytes 3670016 | tf_op jit(solution)/shard_map/all_to_all | solution.py:336
  113.2 22.8 %collective-permute-start.11 = (bf16[1024,128]{1,0:T(8,128)(2,1)S(1)}, bf16[1024,128]{1,0:T(8,128)(2,1)S(1)}, u32[]{:S(2)}, u32[]{:S(2)}) collective-permute-start(bf16[1024,128]{1,0:T(8,128)(2,1)S(1)} %pad_maximum_fusion.2.rest_0_), channel_id=1, source_target_pairs={{0,4},{4,0},{1,5},{5,1},{2,6},{6,2},{3,7},{7,3},{8,12},{12,8},{9,1... | collective-permute-start | bytes 786440 | tf_op jit(solution)/shard_map/ppermute | solution.py:196
  114.8 25.4 %collective-permute-start.12 = (bf16[1024,128]{1,0:T(8,128)(2,1)S(1)}, bf16[1024,128]{1,0:T(8,128)(2,1)S(1)}, u32[]{:S(2)}, u32[]{:S(2)}) collective-permute-start(bf16[1024,128]{1,0:T(8,128)(2,1)S(1)} %pad_maximum_fusion.2.rest_0_), channel_id=1, source_target_pairs={{0,1},{1,2},{2,3},{3,0},{4,5},{5,6},{6,7},{7,4},{8,9},{9,10},{10,1... | collective-permute-start | bytes 786440 | tf_op jit(solution)/shard_map/ppermute | solution.py:192
  116.2 35.5 %collective-permute-start.14 = (bf16[1024,128]{1,0:T(8,128)(2,1)S(1)}, bf16[1024,128]{1,0:T(8,128)(2,1)S(1)}, u32[]{:S(2)}, u32[]{:S(2)}) collective-permute-start(bf16[1024,128]{1,0:T(8,128)(2,1)S(1)} %pad_maximum_fusion.2.rest_0_), channel_id=1, source_target_pairs={{0,2},{1,3},{2,0},{3,1},{4,6},{5,7},{6,4},{7,5},{8,10},{9,11},{10,... | collective-permute-start | bytes 786440 | tf_op jit(solution)/shard_map/ppermute | solution.py:192
  118.9 32.8 %collective-permute-start.16 = (bf16[1024,128]{1,0:T(8,128)(2,1)S(1)}, bf16[1024,128]{1,0:T(8,128)(2,1)S(1)}, u32[]{:S(2)}, u32[]{:S(2)}) collective-permute-start(bf16[1024,128]{1,0:T(8,128)(2,1)S(1)} %pad_maximum_fusion.2.rest_0_), channel_id=1, source_target_pairs={{0,3},{1,0},{2,1},{3,2},{4,7},{5,4},{6,5},{7,6},{8,11},{9,8},{10,9... | collective-permute-start | bytes 786440 | tf_op jit(solution)/shard_map/ppermute | solution.py:192
  136.0 15.7 %collective-permute-start.13 = (bf16[1024,128]{1,0:T(8,128)(2,1)S(1)}, bf16[1024,128]{1,0:T(8,128)(2,1)}, u32[]{:S(2)}, u32[]{:S(2)}) collective-permute-start(bf16[1024,128]{1,0:T(8,128)(2,1)S(1)} %collective-permute-done.11.rest_1_), channel_id=1, source_target_pairs={{0,1},{1,2},{2,3},{3,0},{4,5},{5,6},{6,7},{7,4},{8,9},{9,10},{10,1... | collective-permute-start | bytes 786440 | tf_op jit(solution)/shard_map/ppermute | solution.py:192
  137.5 17.0 %collective-permute-start.15 = (bf16[1024,128]{1,0:T(8,128)(2,1)S(1)}, bf16[1024,128]{1,0:T(8,128)(2,1)}, u32[]{:S(2)}, u32[]{:S(2)}) collective-permute-start(bf16[1024,128]{1,0:T(8,128)(2,1)S(1)} %collective-permute-done.11.rest_1_), channel_id=1, source_target_pairs={{0,2},{1,3},{2,0},{3,1},{4,6},{5,7},{6,4},{7,5},{8,10},{9,11},{10,... | collective-permute-start | bytes 786440 | tf_op jit(solution)/shard_map/ppermute | solution.py:192
  140.1 14.4 %collective-permute-start.17 = (bf16[1024,128]{1,0:T(8,128)(2,1)S(1)}, bf16[1024,128]{1,0:T(8,128)(2,1)}, u32[]{:S(2)}, u32[]{:S(2)}) collective-permute-start(bf16[1024,128]{1,0:T(8,128)(2,1)S(1)} %collective-permute-done.11.rest_1_), channel_id=1, source_target_pairs={{0,3},{1,0},{2,1},{3,2},{4,7},{5,4},{6,5},{7,6},{8,11},{9,8},{10,9... | collective-permute-start | bytes 786440 | tf_op jit(solution)/shard_map/ppermute | solution.py:192
  144.2 44.9 %all-to-all-start.2 = ((bf16[16,112,128]{2,1,0:T(8,128)(2,1)}), bf16[16,112,128]{2,1,0:T(8,128)(2,1)}, u32[]{:S(2)}, u32[]{:S(2)}) async-start(bf16[16,112,128]{2,1,0:T(8,128)(2,1)} %chunk_sum.1), calls=%async_computation.2 | async-start | bytes 917504 | tf_op jit(solution)/shard_map/all_to_all | solution.py:338
  162.0 11.6 %collective-permute-start.21 = (bf16[1024,128]{1,0:T(8,128)(2,1)}, bf16[1024,128]{1,0:T(8,128)(2,1)}, u32[]{:S(2)}, u32[]{:S(2)}) collective-permute-start(bf16[1024,128]{1,0:T(8,128)(2,1)} %get-tuple-element.28), channel_id=1, source_target_pairs={{0,64},{32,96},{64,0},{96,32},{1,65},{33,97},{65,1},{97,33},{2,66}... | collective-permute-start | bytes 786440 | tf_op jit(solution)/shard_map/ppermute | solution.py:192
  166.1 16.3 %collective-permute-start.22 = (bf16[1024,128]{1,0:T(8,128)(2,1)}, bf16[1024,128]{1,0:T(8,128)(2,1)}, u32[]{:S(2)}, u32[]{:S(2)}) collective-permute-start(bf16[1024,128]{1,0:T(8,128)(2,1)} %get-tuple-element.29), channel_id=1, source_target_pairs={{0,32},{32,64},{64,96},{96,0},{1,33},{33,65},{65,97},{97,1},{2,34}... | collective-permute-start | bytes 786440 | tf_op jit(solution)/shard_map/ppermute | solution.py:192
  166.1 16.3 %collective-permute-start.23 = (bf16[1024,128]{1,0:T(8,128)(2,1)}, bf16[1024,128]{1,0:T(8,128)(2,1)}, u32[]{:S(2)}, u32[]{:S(2)}) collective-permute-start(bf16[1024,128]{1,0:T(8,128)(2,1)} %get-tuple-element.30), channel_id=1, source_target_pairs={{0,96},{32,0},{64,32},{96,64},{1,97},{33,1},{65,33},{97,65},{2,98}... | collective-permute-start | bytes 786440 | tf_op jit(solution)/shard_map/ppermute | solution.py:192
  169.3 19.8 %collective-permute-start.18 = (bf16[1024,128]{1,0:T(8,128)(2,1)}, bf16[1024,128]{1,0:T(8,128)(2,1)S(1)}, u32[]{:S(2)}, u32[]{:S(2)}) collective-permute-start(bf16[1024,128]{1,0:T(8,128)(2,1)} %get-tuple-element.24), channel_id=1, source_target_pairs={{0,64},{32,96},{64,0},{96,32},{1,65},{33,97},{65,1},{97,33},{2,66}... | collective-permute-start | bytes 786440 | tf_op jit(solution)/shard_map/ppermute | solution.py:192
  169.3 19.9 %collective-permute-start.19 = (bf16[1024,128]{1,0:T(8,128)(2,1)}, bf16[1024,128]{1,0:T(8,128)(2,1)}, u32[]{:S(2)}, u32[]{:S(2)}) collective-permute-start(bf16[1024,128]{1,0:T(8,128)(2,1)} %get-tuple-element.25), channel_id=1, source_target_pairs={{0,32},{32,64},{64,96},{96,0},{1,33},{33,65},{65,97},{97,1},{2,34}... | collective-permute-start | bytes 786440 | tf_op jit(solution)/shard_map/ppermute | solution.py:192
  173.5 25.8 %collective-permute-start.20 = (bf16[1024,128]{1,0:T(8,128)(2,1)}, bf16[1024,128]{1,0:T(8,128)(2,1)}, u32[]{:S(2)}, u32[]{:S(2)}) collective-permute-start(bf16[1024,128]{1,0:T(8,128)(2,1)} %get-tuple-element.26), channel_id=1, source_target_pairs={{0,96},{32,0},{64,32},{96,64},{1,97},{33,1},{65,33},{97,65},{2,98}... | collective-permute-start | bytes 786440 | tf_op jit(solution)/shard_map/ppermute | solution.py:192
  184.4 15.0 %collective-permute-start.24 = (bf16[1024,128]{1,0:T(8,128)(2,1)}, bf16[1024,128]{1,0:T(8,128)(2,1)}, u32[]{:S(2)}, u32[]{:S(2)}) collective-permute-start(bf16[1024,128]{1,0:T(8,128)(2,1)} %pair_sum.1), channel_id=1, source_target_pairs={{0,16},{16,0},{1,17},{17,1},{2,18},{18,2},{3,19},{19,3},{4,20},{20... | collective-permute-start | bytes 786440 | tf_op jit(solution)/shard_map/ppermute | solution.py:196
  189.0 15.3 %collective-permute-start.27 = (bf16[1792,128]{1,0:T(8,128)(2,1)}, bf16[1792,128]{1,0:T(8,128)(2,1)}, u32[]{:S(2)}, u32[]{:S(2)}) collective-permute-start(bf16[1792,128]{1,0:T(8,128)(2,1)} %bitcast.15.rest_0_), channel_id=1, source_target_pairs={{0,2},{1,3},{2,0},{3,1},{4,6},{5,7},{6,4},{7,5},{8,10},{9,11},{10,... | collective-permute-start | bytes 1376264 | tf_op jit(solution)/shard_map/ppermute | solution.py:342
  189.1 20.2 %collective-permute-start.30 = (bf16[1792,128]{1,0:T(8,128)(2,1)}, bf16[1792,128]{1,0:T(8,128)(2,1)}, u32[]{:S(2)}, u32[]{:S(2)}) collective-permute-start(bf16[1792,128]{1,0:T(8,128)(2,1)} %bitcast.15.rest_0_), channel_id=1, source_target_pairs={{0,1},{1,2},{2,3},{3,0},{4,5},{5,6},{6,7},{7,4},{8,9},{9,10},{10,1... | collective-permute-start | bytes 1376264 | tf_op jit(solution)/shard_map/ppermute | solution.py:342
  189.2 20.1 %collective-permute-start.31 = (bf16[1792,128]{1,0:T(8,128)(2,1)}, bf16[1792,128]{1,0:T(8,128)(2,1)}, u32[]{:S(2)}, u32[]{:S(2)}) collective-permute-start(bf16[1792,128]{1,0:T(8,128)(2,1)} %bitcast.15.rest_0_), channel_id=1, source_target_pairs={{0,3},{1,0},{2,1},{3,2},{4,7},{5,4},{6,5},{7,6},{8,11},{9,8},{10,9... | collective-permute-start | bytes 1376264 | tf_op jit(solution)/shard_map/ppermute | solution.py:342
  201.5 8.4 %collective-permute-start.25 = (bf16[512,128]{1,0:T(8,128)(2,1)}, bf16[512,128]{1,0:T(8,128)(2,1)S(1)}, u32[]{:S(2)}, u32[]{:S(2)}) collective-permute-start(bf16[512,128]{1,0:T(8,128)(2,1)} %get-tuple-element.32), channel_id=1, source_target_pairs={{0,8},{8,0},{1,9},{9,1},{2,10},{10,2},{3,11},{11,3},{4,12},{12,4},... | collective-permute-start | bytes 393224 | tf_op jit(solution)/shard_map/ppermute | solution.py:418
  203.9 6.9 %collective-permute-start.29 = (bf16[1792,128]{1,0:T(8,128)(2,1)}, bf16[1792,128]{1,0:T(8,128)(2,1)S(1)}, u32[]{:S(2)}, u32[]{:S(2)}) collective-permute-start(bf16[1792,128]{1,0:T(8,128)(2,1)} %bitcast.15.rest_0_), channel_id=1, source_target_pairs={{0,8},{8,0},{1,9},{9,1},{2,10},{10,2},{3,11},{11,3},{4,12},{12,4},... | collective-permute-start | bytes 1376264 | tf_op jit(solution)/shard_map/ppermute | solution.py:344
  204.3 12.2 %collective-permute-start.28 = (bf16[1792,128]{1,0:T(8,128)(2,1)}, bf16[1792,128]{1,0:T(8,128)(2,1)S(1)}, u32[]{:S(2)}, u32[]{:S(2)}) collective-permute-start(bf16[1792,128]{1,0:T(8,128)(2,1)} %collective-permute-done.27.rest_0_), channel_id=1, source_target_pairs={{0,8},{8,0},{1,9},{9,1},{2,10},{10,2},{3,11},{11,3},{4,12},{12,4},... | collective-permute-start | bytes 1376264 | tf_op jit(solution)/shard_map/ppermute | solution.py:344
  (30 other events, 348.2 us)

commit v5 on v4

--- a/solution.py
+++ b/solution.py
@@ -16,10 +16,10 @@
 SLOTS = 192
 SIDE = 64
 CHUNK = 32
-UNROLL = 8
+UNROLL = 32
 FINISH = (
-    (("m", 0), ("y", 0), ("m", 1), ("m", 3), ("y", 1), ("y", 3)),
-    (("m", 2), ("y", 2)),
+    (("m", 0), ("y", 0), ("m", 1), ("m", 3)),
+    (("y", 1), ("y", 3), ("m", 2), ("y", 2)),
 )
 VMEM_LIMIT = 60 * 1024 * 1024
 
@@ -149,7 +149,7 @@
 
 
 def chip_kernel(own, got, out_ref):
-    for row in range(16):
+    for row in range(4):
         rows = slice(row * 112, (row + 1) * 112)
         for lane in range(4):
             lanes = slice(lane * 128, (lane + 1) * 128)
@@ -159,12 +159,13 @@
 
 
 def chip_sum(own, got):
-    vm = pl.BlockSpec(memory_space=pltpu.VMEM)
+    rows = pl.BlockSpec((448, 512), lambda i: (i, 0))
     return pl.pallas_call(
         chip_kernel,
+        grid=(4,),
         out_shape=jax.ShapeDtypeStruct((64, 112, 128), BF),
-        in_specs=[vm, vm],
-        out_specs=vm,
+        in_specs=[rows, rows],
+        out_specs=pl.BlockSpec((16, 112, 128), lambda i: (i, 0, 0)),
         cost_estimate=pl.CostEstimate(flops=1 << 20, bytes_accessed=6 << 20, transcendentals=0),
         name="chip_sum",
     )(own, got)
@@ -342,11 +343,11 @@
         mine.append(lax.ppermute(lanes, "x", [(i, (i + k) % 4) for i in range(4)]))
     for k in range(4):
         yours.append(lax.ppermute(mine[k], "core", swap))
-    place = ((x - jnp.arange(4, dtype=jnp.int32)) & 3) * 128
-    at_mine, at_yours = core * 512 + place, (1 - core) * 512 + place
     outs = ()
     for order in FINISH:
-        lanes = jnp.stack([(at_mine if side == "m" else at_yours)[k] for side, k in order])
+        steps = jnp.array([k for _, k in order], jnp.int32)
+        other_core = jnp.array([side == "y" for side, _ in order], jnp.int32)
+        lanes = (core ^ other_core) * 512 + ((x - steps) & 3) * 128
         pieces = [(mine if side == "m" else yours)[k] for side, k in order]
         outs = finish_grads(lanes, pieces, outs)
     return outs
@@ -358,8 +359,10 @@
     yl, x = lax.axis_index("yl"), lax.axis_index("x")
     swap = [(0, 1), (1, 0)]
     blk_own = blocks[0, 0].transpose(1, 2, 0)
+    shard = halves(features, core)
+    slots, _ = lax.optimization_barrier(((block_rows, block_cols, block_count), shard))
     meta = jnp.concatenate(
-        [block_rows[0, 0], block_cols[0, 0], jnp.broadcast_to(block_count[0, 0], (128,))]
+        [slots[0][0, 0], slots[1][0, 0], jnp.broadcast_to(slots[2][0, 0], (128,))]
     )
     meta_other = lax.ppermute(meta, "core", swap)
     blk_other = lax.ppermute(blk_own, "core", swap)
@@ -382,7 +385,6 @@
 
     p = jnp.arange(16, dtype=jnp.int32)
     place = (((z + (p >> 2)) & 3) * 4 + (yh ^ ((p >> 1) & 1)) * 2 + (core ^ (p & 1))) * 512
-    shard = halves(features, core)
     pieces = gather_steps(shard, "z", "yh")
     blk_own, _ = lax.optimization_barrier((blk_own, shard))
     blk_own = with_layout_constraint(blk_own, Layout((0, 1, 2))).transpose(2, 0, 1)

time: 222 us -> 220 us (level)
  waiting for transfers between devices: 38.7 us -> 56.1 us
  starting transfers between devices: 68.9 us -> 56.3 us
  local copies, waits for them, and re-layouts: 19 us -> 13.3 us
    ppermute x18, waiting for transfers between devices: 14.1 us -> 27.5 us  [ring_shift(): return lax.ppermute(value, axis, [(i, (i + k) % 4) for i in range(4)])]
    ppermute x18, starting transfers between devices: 37.4 us -> 32.8 us  [ring_shift(): return lax.ppermute(value, axis, [(i, (i + k) % 4) for i in range(4)])]
    another operation x1 -> x0, local copies, waits for them, and re-layouts: 4.38 us -> none  [sum_grads(): jnp.stack([(at_mine if side == 'm' else at_yours)[k] for side, k in order])]
    ppermute x3, waiting for transfers between devices: 5.02 us -> 9.08 us  [sum_grads(): mine.append(lax.ppermute(lanes, 'x', [(i, (i + k) % 4) for i in range(4)]))]
    all_to_all x1, starting transfers between devices: 9.42 us -> 6.34 us  [sum_grads(): lax.all_to_all(chip_sum(own, got), ('z', 'yh', 'yl', 'x'), 0, 0, tiled=True)]
  transfers between devices with their start and end apart: 36 -> 36, of which waited for: 10 -> 15; matrix products, arithmetic and copies ran while one was open for 12% -> 10% of each run, Pallas kernels for 11% -> 10%
where the time goes in v5:
time: 220 us; the launch traced here: 218 us
  starting transfers between devices  56.3 us (26%)
  waiting for transfers between devices  56.1 us (26%)
  Pallas kernels  40.2 us (18%)
  blocking collectives  31.6 us (14%)
  local copies, waits for them, and re-layouts  13.3 us (6%)
  matrix products  12.4 us (6%)
  other arithmetic  5.95 us (3%)
    ppermute x18, starting transfers between devices, ring_shift(): return lax.ppermute(value, axis, [(i, (i + k) % 4) for i in range(4)])  32.8 us
    all_to_all x1, blocking collectives, shards(): cells = lax.all_to_all(cells, ('core', 'yl', 'x'), 0, 0, tiled=True)  31.6 us
    ppermute x18, waiting for transfers between devices, ring_shift(): return lax.ppermute(value, axis, [(i, (i + k) % 4) for i in range(4)])  27.5 us
    ppermute x3, waiting for transfers between devices, flip(): return lax.ppermute(value, axis, [(0, 1), (1, 0)])  16.6 us
    pallas_call x2, Pallas kernels, cell_products(): pl.pallas_call(functools.partial(cells_kernel, transposed), out_shape=(ja...  12.3 us
    pallas_call x2, Pallas kernels, local_grads(): pl.pallas_call(grads_kernel, out_shape=jax.ShapeDtypeStruct((1792, 512),...  9.63 us
    ppermute x3, waiting for transfers between devices, sum_grads(): mine.append(lax.ppermute(lanes, 'x', [(i, (i + k) % 4) for i in range(4)]))  9.08 us
    ppermute x3, starting transfers between devices, flip(): return lax.ppermute(value, axis, [(0, 1), (1, 0)])  7.75 us
  transfers between devices with their start and end apart: 36, of which 15 were waited for; matrix products, arithmetic and copies ran while one was open for 10% of the time, Pallas kernels for 10%

profile of v5, /device:TPU:0, one launch (start us, length us, event | category | flops | bytes accessed | tf_op | source)
XLA Modules:
  0.0 217.7 jit_solution(8335300248632282478)
XLA Ops:
  5.3 4.2 %collective-permute-start.8 = (bf16[1024,128]{1,0:T(8,128)(2,1)S(1)}, bf16[1024,128]{1,0:T(8,128)(2,1)S(1)}, u32[]{:S(2)}, u32[]{:S(2)}) collective-permute-start(bf16[1024,128]{1,0:T(8,128)(2,1)S(1)} %pad_maximum_fusion.1.rest_0_), channel_id=1, source_target_pairs={{0,96},{32,0},{64,32},{96,64},{1,97},{33,1},{65,33},{97,65},{2,98}... | collective-permute-start | bytes 786440 | tf_op jit(solution)/shard_map/ppermute | solution.py:193
  9.5 3.2 %collective-permute-start.3 = (bf16[1024,128]{1,0:T(8,128)(2,1)S(1)}, bf16[1024,128]{1,0:T(8,128)(2,1)S(1)}, u32[]{:S(2)}, u32[]{:S(2)}) collective-permute-start(bf16[1024,128]{1,0:T(8,128)(2,1)S(1)} %pad_maximum_fusion.1.rest_0_), channel_id=1, source_target_pairs={{0,16},{16,0},{1,17},{17,1},{2,18},{18,2},{3,19},{19,3},{4,20},{20... | collective-permute-start | bytes 786440 | tf_op jit(solution)/shard_map/ppermute | solution.py:197
  13.6 5.1 %copy.30 = bf16[64,64,192]{1,0,2:T(8,128)(2,1)} copy(bf16[64,64,192]{2,1,0:T(8,128)(2,1)} %bitcast.36) | data formatting | bytes 3145728 | tf_op jit(solution)/shard_map/layout_constraint | solution.py:390
  26.3 5.2 %copy.31 = bf16[64,64,192]{1,0,2:T(8,128)(2,1)} copy(bf16[64,64,192]{2,1,0:T(8,128)(2,1)} %collective-permute-done.2) | data formatting | bytes 3145728 | tf_op jit(solution)/shard_map/ppermute | solution.py:368
  35.7 5.1 %collective-permute-done.5.rest_3_ = bf16[1024,128]{1,0:T(8,128)(2,1)} collective-permute-done((bf16[1024,128]{1,0:T(8,128)(2,1)S(1)}, bf16[1024,128]{1,0:T(8,128)(2,1)}, u32[]{:S(2)}, u32[]{:S(2)}) %collective-permute-start.5) | collective-permute-done | bytes 262176 | tf_op jit(solution)/shard_map/ppermute | solution.py:193
  40.8 6.0 %cells_forward.1 = bf16[16,512,128]{2,1,0:T(8,128)(2,1)} custom-call(s32[768]{0:T(1024)} %reshape.47.off_ref, s32[2]{0:T(128)} %copy-done.24, s32[16]{0:T(128)} %add_multiply_fusion.1.place_ref, bf16[192,64,64]{2,1,0:T(8,128)(2,1)} %bitcast.31, bf16[192,64,64]{2,1,0:T(8,128)(2,1)} %bitcast.33, bf16[1024,128]{1,0:T(8,128)(2,1)} %copy-done.9, ...), custom_call_target="tpu_custom_call" | custom-call | flops 402653184 | bytes 10485760 | tf_op jit(solution)/shard_map/cells_forward/pallas_call | solution.py:100
  46.8 31.6 %all_to_all.15 = bf16[16,512,128]{2,1,0:T(8,128)(2,1)S(1)} all-to-all(bf16[16,512,128]{2,1,0:T(8,128)(2,1)} %cells_forward.1), channel_id=1, replica_groups=mesh['z'=4,'yh'=2,'core'=2,'yl'=2,'x'=4] {'core','yl','x'}, dimensions={0} | all-to-all | bytes 4194304 | tf_op jit(solution)/shard_map/all_to_all | solution.py:393
  81.2 2.5 %multiply_convert_fusion.2 = (bf16[512,1024]{1,0:T(8,128)(2,1)}, f32[512,1024]{1,0:T(8,128)S(1)}) fusion(bf16[512,1024]{1,0:T(8,128)(2,1)S(1)} %get-tuple-element.57.act_one, bf16[1024,1024]{1,0:T(8,128)(2,1)S(1)} %copy-done), kind=kOutput, calls=%fused_computation.3 | convolution fusion | flops 1076363264 | bytes 6291456 | tf_op jit(solution)/shard_map/dot_general | solution.py:400
  84.6 2.7 %multiply_convert_fusion.gp_one = bf16[512,1024]{1,0:T(8,128)(2,1)} fusion(f32[512,1024]{1,0:T(8,128)S(1)} %get-tuple-element.58, bf16[512,1024]{1,0:T(8,128)(2,1)S(1)} %multiply_convert_fusion.1.gp_two, bf16[1024,1024]{1,0:T(8,128)(2,1)S(1)} %copy-done), kind=kOutput, calls=%fused_computation.1 | convolution fusion | flops 1078460416 | bytes 6291456 | tf_op jit(solution)/shard_map/dot_general | solution.py:409
  87.4 4.8 %shard_map.165 = bf16[1792,512]{1,0:T(8,128)(2,1)} custom-call(s32[1]{0:T(128)} %bitcast.6.half_ref, bf16[512,512]{1,0:T(8,128)(2,1)} %pad_maximum_fusion.joined, bf16[512,1024]{1,0:T(8,128)(2,1)} %copy-done.3, bf16[512,256]{1,0:T(8,128)(2,1)} %cot.3, bf16[512,1024]{1,0:T(8,128)(2,1)} %multiply_convert_fusion.gp_one, bf16[512,1024]{1,0:T(8,128)(2,1)} %copy-done.4, ...), custom_call_target="tpu_custom_call" | custom-call | flops 939524096 | bytes 8388608 | tf_op jit(solution)/shard_map/pallas_call | solution.py:139
  92.6 4.8 %shard_map.164.own = bf16[1792,512]{1,0:T(8,128)(2,1)} custom-call(s32[1]{0:T(128)} %bitcast.5.half_ref, bf16[512,512]{1,0:T(8,128)(2,1)} %pad_maximum_fusion.joined, bf16[512,1024]{1,0:T(8,128)(2,1)} %copy-done.3, bf16[512,256]{1,0:T(8,128)(2,1)} %cot.3, bf16[512,1024]{1,0:T(8,128)(2,1)} %multiply_convert_fusion.gp_one, bf16[512,1024]{1,0:T(8,128)(2,1)} %copy-done.4, ...), custom_call_target="tpu_custom_call" | custom-call | flops 939524096 | bytes 8388608 | tf_op jit(solution)/shard_map/pallas_call | solution.py:139
  97.4 4.2 %chip_sum.1 = bf16[64,112,128]{2,1,0:T(8,128)(2,1)} custom-call(bf16[1792,512]{1,0:T(8,128)(2,1)} %shard_map.164.own, bf16[1792,512]{1,0:T(8,128)(2,1)} %collective-permute-done.26.got), custom_call_target="tpu_custom_call" | custom-call | flops 1048576 | bytes 6291456 | tf_op jit(solution)/shard_map/chip_sum/pallas_call | solution.py:163
  101.5 6.3 %all-to-all-start.1 = ((bf16[64,112,128]{2,1,0:T(8,128)(2,1)}), bf16[64,112,128]{2,1,0:T(8,128)(2,1)}, u32[]{:S(2)}, u32[]{:S(2)}) async-start(bf16[64,112,128]{2,1,0:T(8,128)(2,1)} %chip_sum.1), calls=%async_computation.1 | async-start | bytes 3670016 | tf_op jit(solution)/shard_map/all_to_all | solution.py:337
  107.9 2.9 %fusion.15 = (bf16[512,512]{1,0:T(8,128)(2,1)S(1)}, f32[512,512]{1,0:T(8,128)}) fusion(bf16[512,1024]{1,0:T(8,128)(2,1)S(1)} %copy-done.1, bf16[512,1024]{1,0:T(8,128)(2,1)} %param.18), kind=kOutput, calls=%fused_computation.53 | convolution fusion | flops 537133056 | bytes 3670016 | tf_op jit(solution)/shard_map/dot_general | solution.py:411
  113.9 2.7 %collective-permute-start.16 = (bf16[1024,128]{1,0:T(8,128)(2,1)S(1)}, bf16[1024,128]{1,0:T(8,128)(2,1)S(1)}, u32[]{:S(2)}, u32[]{:S(2)}) collective-permute-start(bf16[1024,128]{1,0:T(8,128)(2,1)S(1)} %pad_maximum_fusion.2.rest_0_), channel_id=1, source_target_pairs={{0,3},{1,0},{2,1},{3,2},{4,7},{5,4},{6,5},{7,6},{8,11},{9,8},{10,9... | collective-permute-start | bytes 786440 | tf_op jit(solution)/shard_map/ppermute | solution.py:193
  118.3 16.6 %collective-permute-done.11.rest_1_ = bf16[1024,128]{1,0:T(8,128)(2,1)S(1)} collective-permute-done((bf16[1024,128]{1,0:T(8,128)(2,1)S(1)}, bf16[1024,128]{1,0:T(8,128)(2,1)S(1)}, u32[]{:S(2)}, u32[]{:S(2)}) %collective-permute-start.11) | collective-permute-done | bytes 262176 | tf_op jit(solution)/shard_map/ppermute | solution.py:197
  135.0 2.9 %collective-permute-start.17 = (bf16[1024,128]{1,0:T(8,128)(2,1)S(1)}, bf16[1024,128]{1,0:T(8,128)(2,1)}, u32[]{:S(2)}, u32[]{:S(2)}) collective-permute-start(bf16[1024,128]{1,0:T(8,128)(2,1)S(1)} %collective-permute-done.11.rest_1_), channel_id=1, source_target_pairs={{0,3},{1,0},{2,1},{3,2},{4,7},{5,4},{6,5},{7,6},{8,11},{9,8},{10,9... | collective-permute-start | bytes 786440 | tf_op jit(solution)/shard_map/ppermute | solution.py:193
  140.2 2.9 %collective-permute-done.12.rest_2_ = bf16[1024,128]{1,0:T(8,128)(2,1)S(1)} collective-permute-done((bf16[1024,128]{1,0:T(8,128)(2,1)S(1)}, bf16[1024,128]{1,0:T(8,128)(2,1)S(1)}, u32[]{:S(2)}, u32[]{:S(2)}) %collective-permute-start.12) | collective-permute-done | bytes 262176 | tf_op jit(solution)/shard_map/ppermute | solution.py:193
  143.1 4.1 %collective-permute-done.17.rest_7_ = bf16[1024,128]{1,0:T(8,128)(2,1)} collective-permute-done((bf16[1024,128]{1,0:T(8,128)(2,1)S(1)}, bf16[1024,128]{1,0:T(8,128)(2,1)}, u32[]{:S(2)}, u32[]{:S(2)}) %collective-permute-start.17) | collective-permute-done | bytes 262176 | tf_op jit(solution)/shard_map/ppermute | solution.py:193
  148.8 4.5 %collective-permute-done.13.rest_3_ = bf16[1024,128]{1,0:T(8,128)(2,1)} collective-permute-done((bf16[1024,128]{1,0:T(8,128)(2,1)S(1)}, bf16[1024,128]{1,0:T(8,128)(2,1)}, u32[]{:S(2)}, u32[]{:S(2)}) %collective-permute-start.13) | collective-permute-done | bytes 262176 | tf_op jit(solution)/shard_map/ppermute | solution.py:193
  153.4 6.3 %cells_back.1 = (bf16[1024,128]{1,0:T(8,128)(2,1)}, bf16[1024,128]{1,0:T(8,128)(2,1)}, bf16[1024,128]{1,0:T(8,128)(2,1)}, bf16[1024,128]{1,0:T(8,128)(2,1)}, bf1...) custom-call(s32[768]{0:T(1024)} %reshape.49.off_ref, ...), custom_call_target="tpu_custom_call" | custom-call | flops 402653184 | bytes 10485760 | tf_op jit(solution)/shard_map/cells_back/pallas_call | solution.py:100
  159.7 3.1 %collective-permute-start.21 = (bf16[1024,128]{1,0:T(8,128)(2,1)}, bf16[1024,128]{1,0:T(8,128)(2,1)}, u32[]{:S(2)}, u32[]{:S(2)}) collective-permute-start(bf16[1024,128]{1,0:T(8,128)(2,1)} %get-tuple-element.34), channel_id=1, source_target_pairs={{0,64},{32,96},{64,0},{96,32},{1,65},{33,97},{65,1},{97,33},{2,66}... | collective-permute-start | bytes 786440 | tf_op jit(solution)/shard_map/ppermute | solution.py:193
  163.6 2.5 %collective-permute-start.23 = (bf16[1024,128]{1,0:T(8,128)(2,1)}, bf16[1024,128]{1,0:T(8,128)(2,1)}, u32[]{:S(2)}, u32[]{:S(2)}) collective-permute-start(bf16[1024,128]{1,0:T(8,128)(2,1)} %get-tuple-element.36), channel_id=1, source_target_pairs={{0,96},{32,0},{64,32},{96,64},{1,97},{33,1},{65,33},{97,65},{2,98}... | collective-permute-start | bytes 786440 | tf_op jit(solution)/shard_map/ppermute | solution.py:193
  166.1 2.5 %chunk_sum.1 = bf16[16,112,128]{2,1,0:T(8,128)(2,1)} custom-call(bf16[64,112,128]{2,1,0:T(8,128)(2,1)} %all-to-all-done.1.parts), custom_call_target="tpu_custom_call" | custom-call | flops 1048576 | bytes 1048576 | tf_op jit(solution)/shard_map/chunk_sum/pallas_call | solution.py:182
  168.7 5.4 %all-to-all-start.2 = ((bf16[16,112,128]{2,1,0:T(8,128)(2,1)}), bf16[16,112,128]{2,1,0:T(8,128)(2,1)}, u32[]{:S(2)}, u32[]{:S(2)}) async-start(bf16[16,112,128]{2,1,0:T(8,128)(2,1)} %chunk_sum.1), calls=%async_computation.2 | async-start | bytes 917504 | tf_op jit(solution)/shard_map/all_to_all | solution.py:339
  174.0 3.4 %collective-permute-start.18 = (bf16[1024,128]{1,0:T(8,128)(2,1)}, bf16[1024,128]{1,0:T(8,128)(2,1)S(1)}, u32[]{:S(2)}, u32[]{:S(2)}) collective-permute-start(bf16[1024,128]{1,0:T(8,128)(2,1)} %get-tuple-element.30), channel_id=1, source_target_pairs={{0,64},{32,96},{64,0},{96,32},{1,65},{33,97},{65,1},{97,33},{2,66}... | collective-permute-start | bytes 786440 | tf_op jit(solution)/shard_map/ppermute | solution.py:193
  178.0 2.7 %collective-permute-start.20 = (bf16[1024,128]{1,0:T(8,128)(2,1)}, bf16[1024,128]{1,0:T(8,128)(2,1)}, u32[]{:S(2)}, u32[]{:S(2)}) collective-permute-start(bf16[1024,128]{1,0:T(8,128)(2,1)} %get-tuple-element.32), channel_id=1, source_target_pairs={{0,96},{32,0},{64,32},{96,64},{1,97},{33,1},{65,33},{97,65},{2,98}... | collective-permute-start | bytes 786440 | tf_op jit(solution)/shard_map/ppermute | solution.py:193
  182.7 3.0 %collective-permute-start.24 = (bf16[1024,128]{1,0:T(8,128)(2,1)}, bf16[1024,128]{1,0:T(8,128)(2,1)}, u32[]{:S(2)}, u32[]{:S(2)}) collective-permute-start(bf16[1024,128]{1,0:T(8,128)(2,1)} %pair_sum.1), channel_id=1, source_target_pairs={{0,16},{16,0},{1,17},{17,1},{2,18},{18,2},{3,19},{19,3},{4,20},{20... | collective-permute-start | bytes 786440 | tf_op jit(solution)/shard_map/ppermute | solution.py:197
  186.3 3.1 %collective-permute-done.18.refs_1_ = bf16[1024,128]{1,0:T(8,128)(2,1)S(1)} collective-permute-done((bf16[1024,128]{1,0:T(8,128)(2,1)}, bf16[1024,128]{1,0:T(8,128)(2,1)S(1)}, u32[]{:S(2)}, u32[]{:S(2)}) %collective-permute-start.18) | collective-permute-done | bytes 262176 | tf_op jit(solution)/shard_map/ppermute | solution.py:193
  199.8 7.0 %collective-permute-done.29.rest_3_ = bf16[1792,128]{1,0:T(8,128)(2,1)} collective-permute-done((bf16[1792,128]{1,0:T(8,128)(2,1)}, bf16[1792,128]{1,0:T(8,128)(2,1)}, u32[]{:S(2)}, u32[]{:S(2)}) %collective-permute-start.29) | collective-permute-done | bytes 458784 | tf_op jit(solution)/shard_map/ppermute | solution.py:343
  209.2 3.7 %finish_grads.2 = (f32[512,1024]{1,0:T(8,128)}, f32[1024,1024]{1,0:T(8,128)}, f32[1024,256]{1,0:T(8,128)}) custom-call(s32[4]{0:T(128)} %fusion.10.lane_ref, bf16[1792,128]{1,0:T(8,128)(2,1)} %bitcast.15.rest_0_, bf16[1792,128]{1,0:T(8,128)(2,1)} %collective-permute-done.33.rest_1_, bf16[1792,128]{1,0:T(8,128)(2,1)} %collective-permute-done.27.rest_2_, ...), custom_call_target="tpu_custom_call" | custom-call | flops 4194304 | bytes 4194304 | tf_op jit(solution)/shard_map/finish_grads/pallas_call | solution.py:308
  213.8 3.7 %finish_grads.3 = (f32[512,1024]{1,0:T(8,128)}, f32[1024,1024]{1,0:T(8,128)}, f32[1024,256]{1,0:T(8,128)}) custom-call(s32[4]{0:T(128)} %fusion.12.lane_ref, bf16[1792,128]{1,0:T(8,128)(2,1)} %collective-permute-done.28.rest_0_, bf16[1792,128]{1,0:T(8,128)(2,1)} %copy-done.13, ...), custom_call_target="tpu_custom_call", output_to_operand_aliasing={{0}: (5, {}), {1}: (6, {}), {2}: (7, {})} | custom-call | flops 4194304 | bytes 4194304 | tf_op jit(solution)/shard_map/finish_grads/pallas_call | solution.py:308
  (142 shorter events, 47.1 us)
Async XLA Ops:
  0.6 23.9 %collective-permute-start.2 = (bf16[64,64,192]{2,1,0:T(8,128)(2,1)}, bf16[64,64,192]{2,1,0:T(8,128)(2,1)}, u32[]{:S(2)}, u32[]{:S(2)}) collective-permute-start(bf16[64,64,192]{2,1,0:T(8,128)(2,1)} %bitcast.35), channel_id=1, source_target_pairs={{0,8},{8,0},{1,9},{9,1},{2,10},{10,2},{3,11},{11,3},{4,12},{12,4},... | collective-permute-start | bytes 4718600 | tf_op jit(solution)/shard_map/ppermute | solution.py:368
  5.3 17.0 %collective-permute-start.8 = (bf16[1024,128]{1,0:T(8,128)(2,1)S(1)}, bf16[1024,128]{1,0:T(8,128)(2,1)S(1)}, u32[]{:S(2)}, u32[]{:S(2)}) collective-permute-start(bf16[1024,128]{1,0:T(8,128)(2,1)S(1)} %pad_maximum_fusion.1.rest_0_), channel_id=1, source_target_pairs={{0,96},{32,0},{64,32},{96,64},{1,97},{33,1},{65,33},{97,65},{2,98}... | collective-permute-start | bytes 786440 | tf_op jit(solution)/shard_map/ppermute | solution.py:193
  9.5 10.7 %collective-permute-start.3 = (bf16[1024,128]{1,0:T(8,128)(2,1)S(1)}, bf16[1024,128]{1,0:T(8,128)(2,1)S(1)}, u32[]{:S(2)}, u32[]{:S(2)}) collective-permute-start(bf16[1024,128]{1,0:T(8,128)(2,1)S(1)} %pad_maximum_fusion.1.rest_0_), channel_id=1, source_target_pairs={{0,16},{16,0},{1,17},{17,1},{2,18},{18,2},{3,19},{19,3},{4,20},{20... | collective-permute-start | bytes 786440 | tf_op jit(solution)/shard_map/ppermute | solution.py:197
  13.5 5.2 %collective-permute-start.1 = (s32[512]{0:T(512)S(1)}, s32[512]{0:T(512)S(1)}, u32[]{:S(2)}, u32[]{:S(2)}) collective-permute-start(s32[512]{0:T(512)S(1)} %pad_add_fusion.3), channel_id=1, source_target_pairs={{0,8},{8,0},{1,9},{9,1},{2,10},{10,2},{3,11},{11,3},{4,12},{12,4},... | collective-permute-start | bytes 6152 | tf_op jit(solution)/shard_map/ppermute | solution.py:367
  13.6 17.9 %collective-permute-start.6 = (bf16[1024,128]{1,0:T(8,128)(2,1)S(1)}, bf16[1024,128]{1,0:T(8,128)(2,1)S(1)}, u32[]{:S(2)}, u32[]{:S(2)}) collective-permute-start(bf16[1024,128]{1,0:T(8,128)(2,1)S(1)} %pad_maximum_fusion.1.rest_0_), channel_id=1, source_target_pairs={{0,64},{32,96},{64,0},{96,32},{1,65},{33,97},{65,1},{97,33},{2,66}... | collective-permute-start | bytes 786440 | tf_op jit(solution)/shard_map/ppermute | solution.py:193
  18.7 12.8 %collective-permute-start.4 = (bf16[1024,128]{1,0:T(8,128)(2,1)S(1)}, bf16[1024,128]{1,0:T(8,128)(2,1)S(1)}, u32[]{:S(2)}, u32[]{:S(2)}) collective-permute-start(bf16[1024,128]{1,0:T(8,128)(2,1)S(1)} %pad_maximum_fusion.1.rest_0_), channel_id=1, source_target_pairs={{0,32},{32,64},{64,96},{96,0},{1,33},{33,65},{65,97},{97,1},{2,34}... | collective-permute-start | bytes 786440 | tf_op jit(solution)/shard_map/ppermute | solution.py:193
  20.2 13.7 %collective-permute-start.9 = (bf16[1024,128]{1,0:T(8,128)(2,1)S(1)}, bf16[1024,128]{1,0:T(8,128)(2,1)}, u32[]{:S(2)}, u32[]{:S(2)}) collective-permute-start(bf16[1024,128]{1,0:T(8,128)(2,1)S(1)} %collective-permute-done.3.rest_1_), channel_id=1, source_target_pairs={{0,96},{32,0},{64,32},{96,64},{1,97},{33,1},{65,33},{97,65},{2,98}... | collective-permute-start | bytes 786440 | tf_op jit(solution)/shard_map/ppermute | solution.py:193
  22.3 13.4 %collective-permute-start.7 = (bf16[1024,128]{1,0:T(8,128)(2,1)S(1)}, bf16[1024,128]{1,0:T(8,128)(2,1)}, u32[]{:S(2)}, u32[]{:S(2)}) collective-permute-start(bf16[1024,128]{1,0:T(8,128)(2,1)S(1)} %collective-permute-done.3.rest_1_), channel_id=1, source_target_pairs={{0,64},{32,96},{64,0},{96,32},{1,65},{33,97},{65,1},{97,33},{2,66}... | collective-permute-start | bytes 786440 | tf_op jit(solution)/shard_map/ppermute | solution.py:193
  24.6 16.2 %collective-permute-start.5 = (bf16[1024,128]{1,0:T(8,128)(2,1)S(1)}, bf16[1024,128]{1,0:T(8,128)(2,1)}, u32[]{:S(2)}, u32[]{:S(2)}) collective-permute-start(bf16[1024,128]{1,0:T(8,128)(2,1)S(1)} %collective-permute-done.3.rest_1_), channel_id=1, source_target_pairs={{0,32},{32,64},{64,96},{96,0},{1,33},{33,65},{65,97},{97,1},{2,34}... | collective-permute-start | bytes 786440 | tf_op jit(solution)/shard_map/ppermute | solution.py:193
  101.5 64.6 %all-to-all-start.1 = ((bf16[64,112,128]{2,1,0:T(8,128)(2,1)}), bf16[64,112,128]{2,1,0:T(8,128)(2,1)}, u32[]{:S(2)}, u32[]{:S(2)}) async-start(bf16[64,112,128]{2,1,0:T(8,128)(2,1)} %chip_sum.1), calls=%async_computation.1 | async-start | bytes 3670016 | tf_op jit(solution)/shard_map/all_to_all | solution.py:337
  112.3 22.6 %collective-permute-start.11 = (bf16[1024,128]{1,0:T(8,128)(2,1)S(1)}, bf16[1024,128]{1,0:T(8,128)(2,1)S(1)}, u32[]{:S(2)}, u32[]{:S(2)}) collective-permute-start(bf16[1024,128]{1,0:T(8,128)(2,1)S(1)} %pad_maximum_fusion.2.rest_0_), channel_id=1, source_target_pairs={{0,4},{4,0},{1,5},{5,1},{2,6},{6,2},{3,7},{7,3},{8,12},{12,8},{9,1... | collective-permute-start | bytes 786440 | tf_op jit(solution)/shard_map/ppermute | solution.py:197
  113.9 24.8 %collective-permute-start.16 = (bf16[1024,128]{1,0:T(8,128)(2,1)S(1)}, bf16[1024,128]{1,0:T(8,128)(2,1)S(1)}, u32[]{:S(2)}, u32[]{:S(2)}) collective-permute-start(bf16[1024,128]{1,0:T(8,128)(2,1)S(1)} %pad_maximum_fusion.2.rest_0_), channel_id=1, source_target_pairs={{0,3},{1,0},{2,1},{3,2},{4,7},{5,4},{6,5},{7,6},{8,11},{9,8},{10,9... | collective-permute-start | bytes 786440 | tf_op jit(solution)/shard_map/ppermute | solution.py:193
  116.6 23.6 %collective-permute-start.14 = (bf16[1024,128]{1,0:T(8,128)(2,1)S(1)}, bf16[1024,128]{1,0:T(8,128)(2,1)S(1)}, u32[]{:S(2)}, u32[]{:S(2)}) collective-permute-start(bf16[1024,128]{1,0:T(8,128)(2,1)S(1)} %pad_maximum_fusion.2.rest_0_), channel_id=1, source_target_pairs={{0,2},{1,3},{2,0},{3,1},{4,6},{5,7},{6,4},{7,5},{8,10},{9,11},{10,... | collective-permute-start | bytes 786440 | tf_op jit(solution)/shard_map/ppermute | solution.py:193
  117.5 25.6 %collective-permute-start.12 = (bf16[1024,128]{1,0:T(8,128)(2,1)S(1)}, bf16[1024,128]{1,0:T(8,128)(2,1)S(1)}, u32[]{:S(2)}, u32[]{:S(2)}) collective-permute-start(bf16[1024,128]{1,0:T(8,128)(2,1)S(1)} %pad_maximum_fusion.2.rest_0_), channel_id=1, source_target_pairs={{0,1},{1,2},{2,3},{3,0},{4,5},{5,6},{6,7},{7,4},{8,9},{9,10},{10,1... | collective-permute-start | bytes 786440 | tf_op jit(solution)/shard_map/ppermute | solution.py:193
  135.0 12.3 %collective-permute-start.17 = (bf16[1024,128]{1,0:T(8,128)(2,1)S(1)}, bf16[1024,128]{1,0:T(8,128)(2,1)}, u32[]{:S(2)}, u32[]{:S(2)}) collective-permute-start(bf16[1024,128]{1,0:T(8,128)(2,1)S(1)} %collective-permute-done.11.rest_1_), channel_id=1, source_target_pairs={{0,3},{1,0},{2,1},{3,2},{4,7},{5,4},{6,5},{7,6},{8,11},{9,8},{10,9... | collective-permute-start | bytes 786440 | tf_op jit(solution)/shard_map/ppermute | solution.py:193
  137.8 11.0 %collective-permute-start.15 = (bf16[1024,128]{1,0:T(8,128)(2,1)S(1)}, bf16[1024,128]{1,0:T(8,128)(2,1)}, u32[]{:S(2)}, u32[]{:S(2)}) collective-permute-start(bf16[1024,128]{1,0:T(8,128)(2,1)S(1)} %collective-permute-done.11.rest_1_), channel_id=1, source_target_pairs={{0,2},{1,3},{2,0},{3,1},{4,6},{5,7},{6,4},{7,5},{8,10},{9,11},{10,... | collective-permute-start | bytes 786440 | tf_op jit(solution)/shard_map/ppermute | solution.py:193
  138.7 14.6 %collective-permute-start.13 = (bf16[1024,128]{1,0:T(8,128)(2,1)S(1)}, bf16[1024,128]{1,0:T(8,128)(2,1)}, u32[]{:S(2)}, u32[]{:S(2)}) collective-permute-start(bf16[1024,128]{1,0:T(8,128)(2,1)S(1)} %collective-permute-done.11.rest_1_), channel_id=1, source_target_pairs={{0,1},{1,2},{2,3},{3,0},{4,5},{5,6},{6,7},{7,4},{8,9},{9,10},{10,1... | collective-permute-start | bytes 786440 | tf_op jit(solution)/shard_map/ppermute | solution.py:193
  159.7 18.3 %collective-permute-start.21 = (bf16[1024,128]{1,0:T(8,128)(2,1)}, bf16[1024,128]{1,0:T(8,128)(2,1)}, u32[]{:S(2)}, u32[]{:S(2)}) collective-permute-start(bf16[1024,128]{1,0:T(8,128)(2,1)} %get-tuple-element.34), channel_id=1, source_target_pairs={{0,64},{32,96},{64,0},{96,32},{1,65},{33,97},{65,1},{97,33},{2,66}... | collective-permute-start | bytes 786440 | tf_op jit(solution)/shard_map/ppermute | solution.py:193
  162.8 17.9 %collective-permute-start.22 = (bf16[1024,128]{1,0:T(8,128)(2,1)}, bf16[1024,128]{1,0:T(8,128)(2,1)}, u32[]{:S(2)}, u32[]{:S(2)}) collective-permute-start(bf16[1024,128]{1,0:T(8,128)(2,1)} %get-tuple-element.35), channel_id=1, source_target_pairs={{0,32},{32,64},{64,96},{96,0},{1,33},{33,65},{65,97},{97,1},{2,34}... | collective-permute-start | bytes 786440 | tf_op jit(solution)/shard_map/ppermute | solution.py:193
  163.6 17.1 %collective-permute-start.23 = (bf16[1024,128]{1,0:T(8,128)(2,1)}, bf16[1024,128]{1,0:T(8,128)(2,1)}, u32[]{:S(2)}, u32[]{:S(2)}) collective-permute-start(bf16[1024,128]{1,0:T(8,128)(2,1)} %get-tuple-element.36), channel_id=1, source_target_pairs={{0,96},{32,0},{64,32},{96,64},{1,97},{33,1},{65,33},{97,65},{2,98}... | collective-permute-start | bytes 786440 | tf_op jit(solution)/shard_map/ppermute | solution.py:193
  168.7 17.6 %all-to-all-start.2 = ((bf16[16,112,128]{2,1,0:T(8,128)(2,1)}), bf16[16,112,128]{2,1,0:T(8,128)(2,1)}, u32[]{:S(2)}, u32[]{:S(2)}) async-start(bf16[16,112,128]{2,1,0:T(8,128)(2,1)} %chunk_sum.1), calls=%async_computation.2 | async-start | bytes 917504 | tf_op jit(solution)/shard_map/all_to_all | solution.py:339
  174.0 15.3 %collective-permute-start.18 = (bf16[1024,128]{1,0:T(8,128)(2,1)}, bf16[1024,128]{1,0:T(8,128)(2,1)S(1)}, u32[]{:S(2)}, u32[]{:S(2)}) collective-permute-start(bf16[1024,128]{1,0:T(8,128)(2,1)} %get-tuple-element.30), channel_id=1, source_target_pairs={{0,64},{32,96},{64,0},{96,32},{1,65},{33,97},{65,1},{97,33},{2,66}... | collective-permute-start | bytes 786440 | tf_op jit(solution)/shard_map/ppermute | solution.py:193
  177.4 15.7 %collective-permute-start.19 = (bf16[1024,128]{1,0:T(8,128)(2,1)}, bf16[1024,128]{1,0:T(8,128)(2,1)}, u32[]{:S(2)}, u32[]{:S(2)}) collective-permute-start(bf16[1024,128]{1,0:T(8,128)(2,1)} %get-tuple-element.31), channel_id=1, source_target_pairs={{0,32},{32,64},{64,96},{96,0},{1,33},{33,65},{65,97},{97,1},{2,34}... | collective-permute-start | bytes 786440 | tf_op jit(solution)/shard_map/ppermute | solution.py:193
  178.0 16.3 %collective-permute-start.20 = (bf16[1024,128]{1,0:T(8,128)(2,1)}, bf16[1024,128]{1,0:T(8,128)(2,1)}, u32[]{:S(2)}, u32[]{:S(2)}) collective-permute-start(bf16[1024,128]{1,0:T(8,128)(2,1)} %get-tuple-element.32), channel_id=1, source_target_pairs={{0,96},{32,0},{64,32},{96,64},{1,97},{33,1},{65,33},{97,65},{2,98}... | collective-permute-start | bytes 786440 | tf_op jit(solution)/shard_map/ppermute | solution.py:193
  182.7 11.6 %collective-permute-start.24 = (bf16[1024,128]{1,0:T(8,128)(2,1)}, bf16[1024,128]{1,0:T(8,128)(2,1)}, u32[]{:S(2)}, u32[]{:S(2)}) collective-permute-start(bf16[1024,128]{1,0:T(8,128)(2,1)} %pair_sum.1), channel_id=1, source_target_pairs={{0,16},{16,0},{1,17},{17,1},{2,18},{18,2},{3,19},{19,3},{4,20},{20... | collective-permute-start | bytes 786440 | tf_op jit(solution)/shard_map/ppermute | solution.py:197
  186.3 13.6 %collective-permute-start.31 = (bf16[1792,128]{1,0:T(8,128)(2,1)}, bf16[1792,128]{1,0:T(8,128)(2,1)}, u32[]{:S(2)}, u32[]{:S(2)}) collective-permute-start(bf16[1792,128]{1,0:T(8,128)(2,1)} %bitcast.15.rest_0_), channel_id=1, source_target_pairs={{0,2},{1,3},{2,0},{3,1},{4,6},{5,7},{6,4},{7,5},{8,10},{9,11},{10,... | collective-permute-start | bytes 1376264 | tf_op jit(solution)/shard_map/ppermute | solution.py:343
  189.3 17.5 %collective-permute-start.29 = (bf16[1792,128]{1,0:T(8,128)(2,1)}, bf16[1792,128]{1,0:T(8,128)(2,1)}, u32[]{:S(2)}, u32[]{:S(2)}) collective-permute-start(bf16[1792,128]{1,0:T(8,128)(2,1)} %bitcast.15.rest_0_), channel_id=1, source_target_pairs={{0,3},{1,0},{2,1},{3,2},{4,7},{5,4},{6,5},{7,6},{8,11},{9,8},{10,9... | collective-permute-start | bytes 1376264 | tf_op jit(solution)/shard_map/ppermute | solution.py:343
  193.1 15.2 %collective-permute-start.27 = (bf16[1792,128]{1,0:T(8,128)(2,1)}, bf16[1792,128]{1,0:T(8,128)(2,1)}, u32[]{:S(2)}, u32[]{:S(2)}) collective-permute-start(bf16[1792,128]{1,0:T(8,128)(2,1)} %bitcast.15.rest_0_), channel_id=1, source_target_pairs={{0,1},{1,2},{2,3},{3,0},{4,5},{5,6},{6,7},{7,4},{8,9},{9,10},{10,1... | collective-permute-start | bytes 1376264 | tf_op jit(solution)/shard_map/ppermute | solution.py:343
  196.4 11.9 %collective-permute-start.25 = (bf16[512,128]{1,0:T(8,128)(2,1)}, bf16[512,128]{1,0:T(8,128)(2,1)S(1)}, u32[]{:S(2)}, u32[]{:S(2)}) collective-permute-start(bf16[512,128]{1,0:T(8,128)(2,1)} %get-tuple-element.38), channel_id=1, source_target_pairs={{0,8},{8,0},{1,9},{9,1},{2,10},{10,2},{3,11},{11,3},{4,12},{12,4},... | collective-permute-start | bytes 393224 | tf_op jit(solution)/shard_map/ppermute | solution.py:420
  198.8 10.4 %collective-permute-start.33 = (bf16[1792,128]{1,0:T(8,128)(2,1)}, bf16[1792,128]{1,0:T(8,128)(2,1)}, u32[]{:S(2)}, u32[]{:S(2)}) collective-permute-start(bf16[1792,128]{1,0:T(8,128)(2,1)} %bitcast.15.rest_0_), channel_id=1, source_target_pairs={{0,8},{8,0},{1,9},{9,1},{2,10},{10,2},{3,11},{11,3},{4,12},{12,4},... | collective-permute-start | bytes 1376264 | tf_op jit(solution)/shard_map/ppermute | solution.py:345
  199.8 13.1 %collective-permute-start.32 = (bf16[1792,128]{1,0:T(8,128)(2,1)}, bf16[1792,128]{1,0:T(8,128)(2,1)S(1)}, u32[]{:S(2)}, u32[]{:S(2)}) collective-permute-start(bf16[1792,128]{1,0:T(8,128)(2,1)} %collective-permute-done.31.rest_2_), channel_id=1, source_target_pairs={{0,8},{8,0},{1,9},{9,1},{2,10},{10,2},{3,11},{11,3},{4,12},{12,4},... | collective-permute-start | bytes 1376264 | tf_op jit(solution)/shard_map/ppermute | solution.py:345
  206.8 6.1 %collective-permute-start.30 = (bf16[1792,128]{1,0:T(8,128)(2,1)}, bf16[1792,128]{1,0:T(8,128)(2,1)S(1)}, u32[]{:S(2)}, u32[]{:S(2)}) collective-permute-start(bf16[1792,128]{1,0:T(8,128)(2,1)} %collective-permute-done.29.rest_3_), channel_id=1, source_target_pairs={{0,8},{8,0},{1,9},{9,1},{2,10},{10,2},{3,11},{11,3},{4,12},{12,4},... | collective-permute-start | bytes 1376264 | tf_op jit(solution)/shard_map/ppermute | solution.py:345
  (34 other events, 452.7 us)

commit v6 on v4

--- a/solution.py
+++ b/solution.py
@@ -16,12 +16,8 @@
 SLOTS = 192
 SIDE = 64
 CHUNK = 32
-UNROLL = 8
-FINISH = (
-    (("m", 0), ("y", 0), ("m", 1), ("m", 3), ("y", 1), ("y", 3)),
-    (("m", 2), ("y", 2)),
-)
-VMEM_LIMIT = 60 * 1024 * 1024
+UNROLL = 32
+CELL_VMEM = 28 << 20
 
 
 def silu_grad(value):
@@ -113,7 +109,7 @@
             pltpu.SemaphoreType.DMA((2 * n_chunks,)),
             pltpu.SemaphoreType.DMA((8,)),
         ],
-        compiler_params=pltpu.CompilerParams(vmem_limit_bytes=VMEM_LIMIT),
+        compiler_params=pltpu.CompilerParams(vmem_limit_bytes=CELL_VMEM),
         cost_estimate=pl.CostEstimate(
             flops=2 * 2 * SLOTS * SIDE * SIDE * 128, bytes_accessed=10 << 20, transcendentals=0
         ),
@@ -141,7 +137,7 @@
         out_shape=jax.ShapeDtypeStruct((1792, 512), BF),
         in_specs=[pl.BlockSpec(memory_space=pltpu.SMEM)] + [vm] * 6,
         out_specs=vm,
-        compiler_params=pltpu.CompilerParams(vmem_limit_bytes=VMEM_LIMIT),
+        compiler_params=pltpu.CompilerParams(vmem_limit_bytes=16 << 20),
         cost_estimate=pl.CostEstimate(
             flops=512 * 1792 * 1024, bytes_accessed=8 << 20, transcendentals=0
         ),
@@ -166,13 +162,14 @@
         in_specs=[vm, vm],
         out_specs=vm,
         cost_estimate=pl.CostEstimate(flops=1 << 20, bytes_accessed=6 << 20, transcendentals=0),
+        compiler_params=pltpu.CompilerParams(vmem_limit_bytes=12 << 20),
         name="chip_sum",
     )(own, got)
 
 
 def chunk_kernel(parts, out_ref):
     total = jnp.sum(parts[...].astype(F32), axis=0).astype(BF)
-    for k in range(16):
+    for k in range(64):
         out_ref[k] = total
 
 
@@ -180,10 +177,11 @@
     vm = pl.BlockSpec(memory_space=pltpu.VMEM)
     return pl.pallas_call(
         chunk_kernel,
-        out_shape=jax.ShapeDtypeStruct((16, 112, 128), BF),
+        out_shape=jax.ShapeDtypeStruct((64, 112, 128), BF),
         in_specs=[vm],
         out_specs=vm,
         cost_estimate=pl.CostEstimate(flops=1 << 20, bytes_accessed=1 << 20, transcendentals=0),
+        compiler_params=pltpu.CompilerParams(vmem_limit_bytes=12 << 20),
         name="chunk_sum",
     )(parts)
 
@@ -221,6 +219,7 @@
         in_specs=[vm] * len(parts),
         out_specs=vm,
         cost_estimate=pl.CostEstimate(flops=1 << 19, bytes_accessed=5 << 18, transcendentals=0),
+        compiler_params=pltpu.CompilerParams(vmem_limit_bytes=6 << 20),
         name="pair_sum",
     )(*parts)
 
@@ -255,6 +254,7 @@
         in_specs=[vm] * len(parts),
         out_specs=(vm, vm),
         cost_estimate=pl.CostEstimate(flops=1 << 20, bytes_accessed=3 << 20, transcendentals=0),
+        compiler_params=pltpu.CompilerParams(vmem_limit_bytes=8 << 20),
         name="node_sum",
     )(*parts)
 
@@ -268,88 +268,65 @@
     return jnp.concatenate([mine, got], axis=0)
 
 
-def finish_kernel(n, lane_ref, *rest):
-    pieces, rest = rest[:n], rest[-9:]
-    outs = rest[:3]
-    taken, first, second, third, in_sem, out_sem = rest[3:9]
-    reads = [
-        pltpu.make_async_copy(piece, taken.at[k], in_sem.at[k]) for k, piece in enumerate(pieces)
-    ]
-    for read in reads:
-        read.start()
-    writes = []
-    for k in range(n):
-        lane = pl.multiple_of(lane_ref[k], 128)
-        held = (first.at[k], second.at[k], third.at[k])
-        targets = (
-            outs[0].at[:, pl.ds(lane, 128)],
-            outs[1].at[:, pl.ds(lane, 128)],
-            outs[2].at[pl.ds(lane, 128), :],
-        )
-        moves = [
-            pltpu.make_async_copy(held[i], targets[i], out_sem.at[3 * k + i]) for i in range(3)
-        ]
-        reads[k].wait()
-        first[k] = taken[k, :512, :].astype(F32) * (1.0 / 256.0)
-        moves[0].start()
-        second[k] = taken[k, 512:1536, :].astype(F32) * (1.0 / 256.0)
-        moves[1].start()
-        third[k] = (taken[k, 1536:, :].astype(F32) * (1.0 / 256.0)).T
-        moves[2].start()
-        writes += moves
-    for write in writes:
-        write.wait()
-
-
-def finish_grads(lanes, pieces, outs):
+def finish_kernel(half_ref, blocks_ref, *rest):
+    outs, total, turned, sems = rest[-6:-3], rest[-3], rest[-2], rest[-1]
+    lane = pl.multiple_of(half_ref[0] * 512, 512)
+    lanes = pl.ds(lane, 512)
+    moves = (
+        pltpu.make_async_copy(total.at[:512], outs[0].at[:, lanes], sems.at[0]),
+        pltpu.make_async_copy(total.at[512:1536], outs[1].at[:, lanes], sems.at[1]),
+        pltpu.make_async_copy(turned, outs[2].at[lanes, :], sems.at[2]),
+    )
+    for row in range(16):
+        for col in range(4):
+            total[row * 112 : (row + 1) * 112, col * 128 : (col + 1) * 128] = blocks_ref[
+                row * 4 + col
+            ].astype(F32) * (1.0 / 256.0)
+        if row == 4:
+            moves[0].start()
+        if row == 13:
+            moves[1].start()
+    turned[...] = total[1536:, :].T
+    moves[2].start()
+    for move in moves:
+        move.wait()
+
+
+def finish_grads(half, blocks, outs):
+    vm = pl.BlockSpec(memory_space=pltpu.VMEM)
     any_spec = pl.BlockSpec(memory_space=pl.ANY)
-    n = len(pieces)
-    return pl.pallas_call(
-        functools.partial(finish_kernel, n),
+    return pl.pallas_call(
+        finish_kernel,
         out_shape=(
             jax.ShapeDtypeStruct((512, 1024), F32),
             jax.ShapeDtypeStruct((1024, 1024), F32),
             jax.ShapeDtypeStruct((1024, 256), F32),
         ),
-        in_specs=[pl.BlockSpec(memory_space=pltpu.SMEM)] + [any_spec] * (n + len(outs)),
+        in_specs=[pl.BlockSpec(memory_space=pltpu.SMEM), vm] + [any_spec] * len(outs),
         out_specs=(any_spec,) * 3,
         scratch_shapes=[
-            pltpu.VMEM((n, 1792, 128), BF),
-            pltpu.VMEM((n, 512, 128), F32),
-            pltpu.VMEM((n, 1024, 128), F32),
-            pltpu.VMEM((n, 128, 256), F32),
-            pltpu.SemaphoreType.DMA((n,)),
-            pltpu.SemaphoreType.DMA((3 * n,)),
+            pltpu.VMEM((1792, 512), F32),
+            pltpu.VMEM((512, 256), F32),
+            pltpu.SemaphoreType.DMA((3,)),
         ],
-        input_output_aliases={1 + n + k: k for k in range(len(outs))},
-        cost_estimate=pl.CostEstimate(flops=n << 20, bytes_accessed=n << 20, transcendentals=0),
+        input_output_aliases={2 + k: k for k in range(len(outs))},
+        compiler_params=pltpu.CompilerParams(vmem_limit_bytes=16 << 20),
+        cost_estimate=pl.CostEstimate(flops=4 << 20, bytes_accessed=6 << 20, transcendentals=0),
         name="finish_grads",
-    )(lanes, *pieces, *outs)
+    )(half.reshape(1), blocks, *outs)
 
 
 def sum_grads(core, operands):
-    x = lax.axis_index("x")
     swap = [(0, 1), (1, 0)]
     other = local_grads(1 - core, *operands)
     got = lax.ppermute(other, "core", swap)
     own = local_grads(core, *operands)
     parts = lax.all_to_all(chip_sum(own, got), ("z", "yh", "yl", "x"), 0, 0, tiled=True)
     chunk = chunk_sum(parts)
-    lanes = lax.all_to_all(chunk, ("z", "yh", "yl"), 0, 0, tiled=True)
-    lanes = lanes.reshape(1792, 128)
-    mine, yours = [lanes], []
-    for k in range(1, 4):
-        mine.append(lax.ppermute(lanes, "x", [(i, (i + k) % 4) for i in range(4)]))
-    for k in range(4):
-        yours.append(lax.ppermute(mine[k], "core", swap))
-    place = ((x - jnp.arange(4, dtype=jnp.int32)) & 3) * 128
-    at_mine, at_yours = core * 512 + place, (1 - core) * 512 + place
-    outs = ()
-    for order in FINISH:
-        lanes = jnp.stack([(at_mine if side == "m" else at_yours)[k] for side, k in order])
-        pieces = [(mine if side == "m" else yours)[k] for side, k in order]
-        outs = finish_grads(lanes, pieces, outs)
-    return outs
+    mine = lax.all_to_all(chunk, ("z", "yh", "yl", "x"), 0, 0, tiled=True)
+    yours = lax.ppermute(mine, "core", swap)
+    outs = finish_grads(core, mine, ())
+    return finish_grads(1 - core, yours, outs)
 
 
 def shards(features, blocks, block_rows, block_cols, block_count, w_in, w_mid, w_out, cotangent):
@@ -358,8 +335,10 @@
     yl, x = lax.axis_index("yl"), lax.axis_index("x")
     swap = [(0, 1), (1, 0)]
     blk_own = blocks[0, 0].transpose(1, 2, 0)
+    shard = halves(features, core)
+    slots, _ = lax.optimization_barrier(((block_rows, block_cols, block_count), shard))
     meta = jnp.concatenate(
-        [block_rows[0, 0], block_cols[0, 0], jnp.broadcast_to(block_count[0, 0], (128,))]
+        [slots[0][0, 0], slots[1][0, 0], jnp.broadcast_to(slots[2][0, 0], (128,))]
     )
     meta_other = lax.ppermute(meta, "core", swap)
     blk_other = lax.ppermute(blk_own, "core", swap)
@@ -382,7 +361,6 @@
 
     p = jnp.arange(16, dtype=jnp.int32)
     place = (((z + (p >> 2)) & 3) * 4 + (yh ^ ((p >> 1) & 1)) * 2 + (core ^ (p & 1))) * 512
-    shard = halves(features, core)
     pieces = gather_steps(shard, "z", "yh")
     blk_own, _ = lax.optimization_barrier((blk_own, shard))
     blk_own = with_layout_constraint(blk_own, Layout((0, 1, 2))).transpose(2, 0, 1)
@@ -417,7 +395,9 @@
     mine, yours = node_sum(scatter_steps(back, "z", "yh"))
     got = lax.ppermute(yours, "core", swap).astype(F32)
     first = core == 0
-    relaid = jnp.concatenate([jnp.where(first, mine, got), jnp.where(first, got, mine)], axis=1)
+    relaid = jnp.concatenate(
+        [jnp.where(first, mine, got), jnp.where(first, got, mine)], axis=1
+    )
     grad_nodes = (direct + relaid).astype(BF)
     return updated, grad_nodes, grad_in, grad_mid, grad_out
 

time: 222 us -> 228 us (1.027)
  blocking collectives: 31.4 us -> 65 us
  waiting for transfers between devices: 38.7 us -> 66.3 us
  starting transfers between devices: 68.9 us -> 41.7 us
  Pallas kernels: 41.5 us -> 18.6 us
  matrix products: 12.4 us -> 9.23 us
  other arithmetic: 6.53 us -> 3.45 us
    all_to_all x0 -> x1, blocking collectives: none -> 33.6 us  [sum_grads(): lax.all_to_all(chip_sum(own, got), ('z', 'yh', 'yl', 'x'), 0, 0, tiled=True)]
    ppermute x18, waiting for transfers between devices: 14.1 us -> 41.7 us  [ring_shift(): return lax.ppermute(value, axis, [(i, (i + k) % 4) for i in range(4)])]
    all_to_all x2 -> x1, waiting for transfers between devices: 0.01 us -> 18.6 us  [sum_grads(): mine = lax.all_to_all(chunk, ('z', 'yh', 'yl', 'x'), 0, 0, tiled=True)]
    ppermute x3, waiting for transfers between devices: 15.7 us -> 0.01 us  [flip(): return lax.ppermute(value, axis, [(0, 1), (1, 0)])]
    all_to_all x2 -> x1, starting transfers between devices: 16.3 us -> 5.79 us  [sum_grads(): mine = lax.all_to_all(chunk, ('z', 'yh', 'yl', 'x'), 0, 0, tiled=True)]
    ppermute x18, starting transfers between devices: 37.4 us -> 27.3 us  [ring_shift(): return lax.ppermute(value, axis, [(i, (i + k) % 4) for i in range(4)])]
    unnamed x52 -> x30, local copies, waits for them, and re-layouts: 2.28 us -> 9.79 us
    pallas_call x2, Pallas kernels: 9.59 us -> 2.32 us  [local_grads(): pl.pallas_call(grads_kernel, out_shape=jax.ShapeDtypeStruct((1792, 512),...]
  transfers between devices with their start and end apart: 36 -> 29, of which waited for: 10 -> 14; matrix products, arithmetic and copies ran while one was open for 12% -> 8% of each run, Pallas kernels for 11% -> 4%
where the time goes in v6:
time: 228 us; the launch traced here: 226 us
  waiting for transfers between devices  66.3 us (29%)
  blocking collectives  65 us (29%)
  starting transfers between devices  41.7 us (18%)
  local copies, waits for them, and re-layouts  20.3 us (9%)
  Pallas kernels  18.6 us (8%)
  matrix products  9.23 us (4%)
  other arithmetic  3.45 us (2%)
    ppermute x18, waiting for transfers between devices, ring_shift(): return lax.ppermute(value, axis, [(i, (i + k) % 4) for i in range(4)])  41.7 us
    all_to_all x1, blocking collectives, sum_grads(): lax.all_to_all(chip_sum(own, got), ('z', 'yh', 'yl', 'x'), 0, 0, tiled=True)  33.6 us
    all_to_all x1, blocking collectives, shards(): cells = lax.all_to_all(cells, ('core', 'yl', 'x'), 0, 0, tiled=True)  31.4 us
    ppermute x18, starting transfers between devices, ring_shift(): return lax.ppermute(value, axis, [(i, (i + k) % 4) for i in range(4)])  27.3 us
    all_to_all x1, waiting for transfers between devices, sum_grads(): mine = lax.all_to_all(chunk, ('z', 'yh', 'yl', 'x'), 0, 0, tiled=True)  18.6 us
    unnamed x30, local copies, waits for them, and re-layouts  9.79 us
    pallas_call x2, Pallas kernels, cell_products(): pl.pallas_call(functools.partial(cells_kernel, transposed), out_shape=(ja...  8.29 us
    ppermute x3, starting transfers between devices, flip(): return lax.ppermute(value, axis, [(0, 1), (1, 0)])  7.42 us
  transfers between devices with their start and end apart: 29, of which 14 were waited for; matrix products, arithmetic and copies ran while one was open for 8% of the time, Pallas kernels for 4%

profile of v6, /device:TPU:0, one launch (start us, length us, event | category | flops | bytes accessed | tf_op | source)
XLA Modules:
  0.0 226.4 jit_solution(5134470182749182383)
XLA Ops:
  3.0 2.3 %collective-permute-done = bf16[512,128]{1,0:T(8,128)(2,1)S(1)} collective-permute-done((bf16[512,128]{1,0:T(8,128)(2,1)S(1)}, bf16[512,128]{1,0:T(8,128)(2,1)S(1)}, u32[]{:S(2)}, u32[]{:S(2)}) %collective-permute-start) | collective-permute-done | bytes 131104 | tf_op jit(solution)/shard_map/ppermute | solution.py:267
  5.3 4.2 %collective-permute-start.8 = (bf16[1024,128]{1,0:T(8,128)(2,1)S(1)}, bf16[1024,128]{1,0:T(8,128)(2,1)S(1)}, u32[]{:S(2)}, u32[]{:S(2)}) collective-permute-start(bf16[1024,128]{1,0:T(8,128)(2,1)S(1)} %pad_maximum_fusion.1.rest_0_), channel_id=1, source_target_pairs={{0,96},{32,0},{64,32},{96,64},{1,97},{33,1},{65,33},{97,65},{2,98}... | collective-permute-start | bytes 786440 | tf_op jit(solution)/shard_map/ppermute | solution.py:190
  9.5 3.2 %collective-permute-start.3 = (bf16[1024,128]{1,0:T(8,128)(2,1)S(1)}, bf16[1024,128]{1,0:T(8,128)(2,1)S(1)}, u32[]{:S(2)}, u32[]{:S(2)}) collective-permute-start(bf16[1024,128]{1,0:T(8,128)(2,1)S(1)} %pad_maximum_fusion.1.rest_0_), channel_id=1, source_target_pairs={{0,16},{16,0},{1,17},{17,1},{2,18},{18,2},{3,19},{19,3},{4,20},{20... | collective-permute-start | bytes 786440 | tf_op jit(solution)/shard_map/ppermute | solution.py:194
  13.6 5.1 %copy.26 = bf16[64,64,192]{1,0,2:T(8,128)(2,1)} copy(bf16[64,64,192]{2,1,0:T(8,128)(2,1)} %bitcast.35) | data formatting | bytes 3145728 | tf_op jit(solution)/shard_map/layout_constraint | solution.py:366
  20.2 2.1 collective-permute-start.9
  22.2 2.3 %collective-permute-start.7 = (bf16[1024,128]{1,0:T(8,128)(2,1)S(1)}, bf16[1024,128]{1,0:T(8,128)(2,1)}, u32[]{:S(2)}, u32[]{:S(2)}) collective-permute-start(bf16[1024,128]{1,0:T(8,128)(2,1)S(1)} %collective-permute-done.3.rest_1_), channel_id=1, source_target_pairs={{0,64},{32,96},{64,0},{96,32},{1,65},{33,97},{65,1},{97,33},{2,66}... | collective-permute-start | bytes 786440 | tf_op jit(solution)/shard_map/ppermute | solution.py:190
  25.7 5.2 %copy.27 = bf16[64,64,192]{1,0,2:T(8,128)(2,1)} copy(bf16[64,64,192]{2,1,0:T(8,128)(2,1)} %collective-permute-done.2) | data formatting | bytes 3145728 | tf_op jit(solution)/shard_map/ppermute | solution.py:344
  30.9 2.9 %collective-permute-done.9.rest_7_ = bf16[1024,128]{1,0:T(8,128)(2,1)} collective-permute-done((bf16[1024,128]{1,0:T(8,128)(2,1)S(1)}, bf16[1024,128]{1,0:T(8,128)(2,1)}, u32[]{:S(2)}, u32[]{:S(2)}) %collective-permute-start.9) | collective-permute-done | bytes 262176 | tf_op jit(solution)/shard_map/ppermute | solution.py:190
  35.7 5.1 %collective-permute-done.5.rest_3_ = bf16[1024,128]{1,0:T(8,128)(2,1)} collective-permute-done((bf16[1024,128]{1,0:T(8,128)(2,1)S(1)}, bf16[1024,128]{1,0:T(8,128)(2,1)}, u32[]{:S(2)}, u32[]{:S(2)}) %collective-permute-start.5) | collective-permute-done | bytes 262176 | tf_op jit(solution)/shard_map/ppermute | solution.py:190
  40.8 1.9 copy-done.1
  44.6 4.0 %cells_forward.1 = bf16[16,512,128]{2,1,0:T(8,128)(2,1)S(1)} custom-call(s32[768]{0:T(1024)S(1)} %reshape.46.off_ref, s32[2]{0:T(128)S(1)} %fusion.8.cnt_ref, s32[16]{0:T(128)S(1)} %add_multiply_fusion.1.place_ref, bf16[192,64,64]{2,1,0:T(8,128)(2,1)S(1)} %bitcast.30, bf16[192,64,64]{2,1,0:T(8,128)(2,1)S(1)} %bitcast.32, ...), custom_call_target="tpu_custom_call" | custom-call | flops 402653184 | bytes 10485760 | tf_op jit(solution)/shard_map/cells_forward/pallas_call | solution.py:96
  48.6 31.4 %all_to_all.15 = bf16[16,512,128]{2,1,0:T(8,128)(2,1)S(1)} all-to-all(bf16[16,512,128]{2,1,0:T(8,128)(2,1)S(1)} %cells_forward.1), channel_id=1, replica_groups=mesh['z'=4,'yh'=2,'core'=2,'yl'=2,'x'=4] {'core','yl','x'}, dimensions={0} | all-to-all | bytes 4194304 | tf_op jit(solution)/shard_map/all_to_all | solution.py:369
  89.3 2.3 collective-permute-done.26.got
  91.9 33.6 %all_to_all.16.parts = bf16[64,112,128]{2,1,0:T(8,128)(2,1)S(1)} all-to-all(bf16[64,112,128]{2,1,0:T(8,128)(2,1)S(1)} %chip_sum.1), channel_id=1, replica_groups=mesh['z'=4,'yh'=2,'core'=2,'yl'=2,'x'=4] {'z','yh','yl','x'}, dimensions={0} | all-to-all | bytes 3670016 | tf_op jit(solution)/shard_map/all_to_all | solution.py:324
  127.1 5.8 %all-to-all-start.2 = ((bf16[64,112,128]{2,1,0:T(8,128)(2,1)}), bf16[64,112,128]{2,1,0:T(8,128)(2,1)}, u32[]{:S(2)}, u32[]{:S(2)}) async-start(bf16[64,112,128]{2,1,0:T(8,128)(2,1)} %copy-done.5), calls=%async_computation.2 | async-start | bytes 3670016 | tf_op jit(solution)/shard_map/all_to_all | solution.py:326
  132.9 3.0 %fusion.11 = (bf16[512,512]{1,0:T(8,128)(2,1)S(1)}, f32[512,512]{1,0:T(8,128)}) fusion(bf16[512,1024]{1,0:T(8,128)(2,1)S(1)} %multiply_convert_fusion.gp_one, bf16[512,1024]{1,0:T(8,128)(2,1)} %param.14), kind=kOutput, calls=%fused_computation.47 | convolution fusion | flops 537133056 | bytes 3670016 | tf_op jit(solution)/shard_map/dot_general | solution.py:387
  139.0 2.7 %collective-permute-start.16 = (bf16[1024,128]{1,0:T(8,128)(2,1)S(1)}, bf16[1024,128]{1,0:T(8,128)(2,1)S(1)}, u32[]{:S(2)}, u32[]{:S(2)}) collective-permute-start(bf16[1024,128]{1,0:T(8,128)(2,1)S(1)} %pad_maximum_fusion.2.rest_0_), channel_id=1, source_target_pairs={{0,3},{1,0},{2,1},{3,2},{4,7},{5,4},{6,5},{7,6},{8,11},{9,8},{10,9... | collective-permute-start | bytes 786440 | tf_op jit(solution)/shard_map/ppermute | solution.py:190
  142.5 18.6 %all-to-all-done.2.blocks_ref = bf16[64,112,128]{2,1,0:T(8,128)(2,1)} async-done(((bf16[64,112,128]{2,1,0:T(8,128)(2,1)}), bf16[64,112,128]{2,1,0:T(8,128)(2,1)}, u32[]{:S(2)}, u32[]{:S(2)}) %all-to-all-start.2) | async-done | bytes 1835040 | tf_op jit(solution)/shard_map/all_to_all | solution.py:326
  161.6 2.7 %collective-permute-start.17 = (bf16[1024,128]{1,0:T(8,128)(2,1)S(1)}, bf16[1024,128]{1,0:T(8,128)(2,1)}, u32[]{:S(2)}, u32[]{:S(2)}) collective-permute-start(bf16[1024,128]{1,0:T(8,128)(2,1)S(1)} %collective-permute-done.11.rest_1_), channel_id=1, source_target_pairs={{0,3},{1,0},{2,1},{3,2},{4,7},{5,4},{6,5},{7,6},{8,11},{9,8},{10,9... | collective-permute-start | bytes 786440 | tf_op jit(solution)/shard_map/ppermute | solution.py:190
  164.8 3.0 %collective-permute-start.13 = (bf16[1024,128]{1,0:T(8,128)(2,1)S(1)}, bf16[1024,128]{1,0:T(8,128)(2,1)}, u32[]{:S(2)}, u32[]{:S(2)}) collective-permute-start(bf16[1024,128]{1,0:T(8,128)(2,1)S(1)} %collective-permute-done.11.rest_1_), channel_id=1, source_target_pairs={{0,1},{1,2},{2,3},{3,0},{4,5},{5,6},{6,7},{7,4},{8,9},{9,10},{10,1... | collective-permute-start | bytes 786440 | tf_op jit(solution)/shard_map/ppermute | solution.py:190
  167.9 9.2 %collective-permute-done.12.rest_2_ = bf16[1024,128]{1,0:T(8,128)(2,1)} collective-permute-done((bf16[1024,128]{1,0:T(8,128)(2,1)S(1)}, bf16[1024,128]{1,0:T(8,128)(2,1)}, u32[]{:S(2)}, u32[]{:S(2)}) %collective-permute-start.12) | collective-permute-done | bytes 262176 | tf_op jit(solution)/shard_map/ppermute | solution.py:190
  177.2 5.2 %collective-permute-done.13.rest_3_ = bf16[1024,128]{1,0:T(8,128)(2,1)} collective-permute-done((bf16[1024,128]{1,0:T(8,128)(2,1)S(1)}, bf16[1024,128]{1,0:T(8,128)(2,1)}, u32[]{:S(2)}, u32[]{:S(2)}) %collective-permute-start.13) | collective-permute-done | bytes 262176 | tf_op jit(solution)/shard_map/ppermute | solution.py:190
  182.3 1.9 copy-done.2
  186.1 4.3 %cells_back.1 = (bf16[1024,128]{1,0:T(8,128)(2,1)S(1)}, bf16[1024,128]{1,0:T(8,128)(2,1)S(1)}, bf16[1024,128]{1,0:T(8,128)(2,1)S(1)}, bf16[1024,128]{1,0:T(8,128...) custom-call(s32[768]{0:T(1024)S(1)} %reshape.48.off_ref, ...), custom_call_target="tpu_custom_call" | custom-call | flops 402653184 | bytes 10485760 | tf_op jit(solution)/shard_map/cells_back/pallas_call | solution.py:96
  192.8 2.5 %collective-permute-start.23 = (bf16[1024,128]{1,0:T(8,128)(2,1)S(1)}, bf16[1024,128]{1,0:T(8,128)(2,1)S(1)}, u32[]{:S(2)}, u32[]{:S(2)}) collective-permute-start(bf16[1024,128]{1,0:T(8,128)(2,1)S(1)} %get-tuple-element.36), channel_id=1, source_target_pairs={{0,96},{32,0},{64,32},{96,64},{1,97},{33,1},{65,33},{97,65},{2,98}... | collective-permute-start | bytes 786440 | tf_op jit(solution)/shard_map/ppermute | solution.py:190
  196.1 5.2 %collective-permute-done.21.refs_1_ = bf16[1024,128]{1,0:T(8,128)(2,1)S(1)} collective-permute-done((bf16[1024,128]{1,0:T(8,128)(2,1)S(1)}, bf16[1024,128]{1,0:T(8,128)(2,1)S(1)}, u32[]{:S(2)}, u32[]{:S(2)}) %collective-permute-start.21) | collective-permute-done | bytes 262176 | tf_op jit(solution)/shard_map/ppermute | solution.py:190
  201.3 5.7 %collective-permute-done.22.refs_2_ = bf16[1024,128]{1,0:T(8,128)(2,1)S(1)} collective-permute-done((bf16[1024,128]{1,0:T(8,128)(2,1)S(1)}, bf16[1024,128]{1,0:T(8,128)(2,1)S(1)}, u32[]{:S(2)}, u32[]{:S(2)}) %collective-permute-start.22) | collective-permute-done | bytes 262176 | tf_op jit(solution)/shard_map/ppermute | solution.py:190
  207.6 2.6 %collective-permute-start.24 = (bf16[1024,128]{1,0:T(8,128)(2,1)S(1)}, bf16[1024,128]{1,0:T(8,128)(2,1)S(1)}, u32[]{:S(2)}, u32[]{:S(2)}) collective-permute-start(bf16[1024,128]{1,0:T(8,128)(2,1)S(1)} %pair_sum.1), channel_id=1, source_target_pairs={{0,16},{16,0},{1,17},{17,1},{2,18},{18,2},{3,19},{19,3},{4,20},{20... | collective-permute-start | bytes 786440 | tf_op jit(solution)/shard_map/ppermute | solution.py:194
  210.2 2.3 %collective-permute-done.18.refs_1_ = bf16[1024,128]{1,0:T(8,128)(2,1)S(1)} collective-permute-done((bf16[1024,128]{1,0:T(8,128)(2,1)S(1)}, bf16[1024,128]{1,0:T(8,128)(2,1)S(1)}, u32[]{:S(2)}, u32[]{:S(2)}) %collective-permute-start.18) | collective-permute-done | bytes 262176 | tf_op jit(solution)/shard_map/ppermute | solution.py:190
  212.5 4.2 %collective-permute-done.19.refs_2_ = bf16[1024,128]{1,0:T(8,128)(2,1)S(1)} collective-permute-done((bf16[1024,128]{1,0:T(8,128)(2,1)S(1)}, bf16[1024,128]{1,0:T(8,128)(2,1)S(1)}, u32[]{:S(2)}, u32[]{:S(2)}) %collective-permute-start.19) | collective-permute-done | bytes 262176 | tf_op jit(solution)/shard_map/ppermute | solution.py:190
  219.2 3.5 %finish_grads.2 = (f32[512,1024]{1,0:T(8,128)}, f32[1024,1024]{1,0:T(8,128)}, f32[1024,256]{1,0:T(8,128)}) custom-call(s32[1]{0:T(128)} %bitcast.5.half_ref, bf16[64,112,128]{2,1,0:T(8,128)(2,1)} %all-to-all-done.2.blocks_ref), custom_call_target="tpu_custom_call" | custom-call | flops 4194304 | bytes 6291456 | tf_op jit(solution)/shard_map/finish_grads/pallas_call | solution.py:298
  222.7 3.5 %finish_grads.3 = (f32[512,1024]{1,0:T(8,128)}, f32[1024,1024]{1,0:T(8,128)}, f32[1024,256]{1,0:T(8,128)}) custom-call(s32[1]{0:T(128)} %bitcast.6.half_ref, bf16[64,112,128]{2,1,0:T(8,128)(2,1)} %collective-permute-done.27.blocks_ref, f32[512,1024]{1,0:T(8,128)} %get-tuple-element.39.rest_0_, ...), custom_call_target="tpu_custom_call", output_to_operand_aliasing={{0}: (2, {}), {1}: (3, {}), {2}: (4, {})} | custom-call | flops 4194304 | bytes 6291456 | tf_op jit(solution)/shard_map/finish_grads/pallas_call | solution.py:298
  (97 shorter events, 33.2 us)
Async XLA Ops:
  0.6 81.6 %copy-start = (bf16[1024,1024]{1,0:T(8,128)(2,1)S(1)}, bf16[1024,1024]{1,0:T(8,128)(2,1)}, u32[]{:S(2)}) copy-start(bf16[1024,1024]{1,0:T(8,128)(2,1)} %param.15) | copy-start | bytes 6291460
  0.6 23.9 %collective-permute-start.2 = (bf16[64,64,192]{2,1,0:T(8,128)(2,1)}, bf16[64,64,192]{2,1,0:T(8,128)(2,1)}, u32[]{:S(2)}, u32[]{:S(2)}) collective-permute-start(bf16[64,64,192]{2,1,0:T(8,128)(2,1)} %bitcast.34), channel_id=1, source_target_pairs={{0,8},{8,0},{1,9},{9,1},{2,10},{10,2},{3,11},{11,3},{4,12},{12,4},... | collective-permute-start | bytes 4718600 | tf_op jit(solution)/shard_map/ppermute | solution.py:344
  1.9 3.4 %collective-permute-start = (bf16[512,128]{1,0:T(8,128)(2,1)S(1)}, bf16[512,128]{1,0:T(8,128)(2,1)S(1)}, u32[]{:S(2)}, u32[]{:S(2)}) collective-permute-start(bf16[512,128]{1,0:T(8,128)(2,1)S(1)} %get-tuple-element.54), channel_id=1, source_target_pairs={{0,8},{8,0},{1,9},{9,1},{2,10},{10,2},{3,11},{11,3},{4,12},{12,4},... | collective-permute-start | bytes 393224 | tf_op jit(solution)/shard_map/ppermute | solution.py:267
  5.3 16.9 %collective-permute-start.8 = (bf16[1024,128]{1,0:T(8,128)(2,1)S(1)}, bf16[1024,128]{1,0:T(8,128)(2,1)S(1)}, u32[]{:S(2)}, u32[]{:S(2)}) collective-permute-start(bf16[1024,128]{1,0:T(8,128)(2,1)S(1)} %pad_maximum_fusion.1.rest_0_), channel_id=1, source_target_pairs={{0,96},{32,0},{64,32},{96,64},{1,97},{33,1},{65,33},{97,65},{2,98}... | collective-permute-start | bytes 786440 | tf_op jit(solution)/shard_map/ppermute | solution.py:190
  9.5 10.6 %collective-permute-start.3 = (bf16[1024,128]{1,0:T(8,128)(2,1)S(1)}, bf16[1024,128]{1,0:T(8,128)(2,1)S(1)}, u32[]{:S(2)}, u32[]{:S(2)}) collective-permute-start(bf16[1024,128]{1,0:T(8,128)(2,1)S(1)} %pad_maximum_fusion.1.rest_0_), channel_id=1, source_target_pairs={{0,16},{16,0},{1,17},{17,1},{2,18},{18,2},{3,19},{19,3},{4,20},{20... | collective-permute-start | bytes 786440 | tf_op jit(solution)/shard_map/ppermute | solution.py:194
  13.5 5.2 %collective-permute-start.1 = (s32[512]{0:T(512)S(1)}, s32[512]{0:T(512)S(1)}, u32[]{:S(2)}, u32[]{:S(2)}) collective-permute-start(s32[512]{0:T(512)S(1)} %pad_add_fusion.3), channel_id=1, source_target_pairs={{0,8},{8,0},{1,9},{9,1},{2,10},{10,2},{3,11},{11,3},{4,12},{12,4},... | collective-permute-start | bytes 6152 | tf_op jit(solution)/shard_map/ppermute | solution.py:343
  13.6 17.3 %collective-permute-start.6 = (bf16[1024,128]{1,0:T(8,128)(2,1)S(1)}, bf16[1024,128]{1,0:T(8,128)(2,1)S(1)}, u32[]{:S(2)}, u32[]{:S(2)}) collective-permute-start(bf16[1024,128]{1,0:T(8,128)(2,1)S(1)} %pad_maximum_fusion.1.rest_0_), channel_id=1, source_target_pairs={{0,64},{32,96},{64,0},{96,32},{1,65},{33,97},{65,1},{97,33},{2,66}... | collective-permute-start | bytes 786440 | tf_op jit(solution)/shard_map/ppermute | solution.py:190
  18.7 12.2 %collective-permute-start.4 = (bf16[1024,128]{1,0:T(8,128)(2,1)S(1)}, bf16[1024,128]{1,0:T(8,128)(2,1)S(1)}, u32[]{:S(2)}, u32[]{:S(2)}) collective-permute-start(bf16[1024,128]{1,0:T(8,128)(2,1)S(1)} %pad_maximum_fusion.1.rest_0_), channel_id=1, source_target_pairs={{0,32},{32,64},{64,96},{96,0},{1,33},{33,65},{65,97},{97,1},{2,34}... | collective-permute-start | bytes 786440 | tf_op jit(solution)/shard_map/ppermute | solution.py:190
  20.2 13.7 %collective-permute-start.9 = (bf16[1024,128]{1,0:T(8,128)(2,1)S(1)}, bf16[1024,128]{1,0:T(8,128)(2,1)}, u32[]{:S(2)}, u32[]{:S(2)}) collective-permute-start(bf16[1024,128]{1,0:T(8,128)(2,1)S(1)} %collective-permute-done.3.rest_1_), channel_id=1, source_target_pairs={{0,96},{32,0},{64,32},{96,64},{1,97},{33,1},{65,33},{97,65},{2,98}... | collective-permute-start | bytes 786440 | tf_op jit(solution)/shard_map/ppermute | solution.py:190
  22.2 13.4 %collective-permute-start.7 = (bf16[1024,128]{1,0:T(8,128)(2,1)S(1)}, bf16[1024,128]{1,0:T(8,128)(2,1)}, u32[]{:S(2)}, u32[]{:S(2)}) collective-permute-start(bf16[1024,128]{1,0:T(8,128)(2,1)S(1)} %collective-permute-done.3.rest_1_), channel_id=1, source_target_pairs={{0,64},{32,96},{64,0},{96,32},{1,65},{33,97},{65,1},{97,33},{2,66}... | collective-permute-start | bytes 786440 | tf_op jit(solution)/shard_map/ppermute | solution.py:190
  24.5 16.2 %collective-permute-start.5 = (bf16[1024,128]{1,0:T(8,128)(2,1)S(1)}, bf16[1024,128]{1,0:T(8,128)(2,1)}, u32[]{:S(2)}, u32[]{:S(2)}) collective-permute-start(bf16[1024,128]{1,0:T(8,128)(2,1)S(1)} %collective-permute-done.3.rest_1_), channel_id=1, source_target_pairs={{0,32},{32,64},{64,96},{96,0},{1,33},{33,65},{65,97},{97,1},{2,34}... | collective-permute-start | bytes 786440 | tf_op jit(solution)/shard_map/ppermute | solution.py:190
  87.6 3.9 %collective-permute-start.26 = (bf16[1792,512]{1,0:T(8,128)(2,1)S(1)}, bf16[1792,512]{1,0:T(8,128)(2,1)S(1)}, u32[]{:S(2)}, u32[]{:S(2)}) collective-permute-start(bf16[1792,512]{1,0:T(8,128)(2,1)S(1)} %shard_map.129), channel_id=1, source_target_pairs={{0,8},{8,0},{1,9},{9,1},{2,10},{10,2},{3,11},{11,3},{4,12},{12,4},... | collective-permute-start | bytes 5505032 | tf_op jit(solution)/shard_map/ppermute | solution.py:322
  127.1 34.0 %all-to-all-start.2 = ((bf16[64,112,128]{2,1,0:T(8,128)(2,1)}), bf16[64,112,128]{2,1,0:T(8,128)(2,1)}, u32[]{:S(2)}, u32[]{:S(2)}) async-start(bf16[64,112,128]{2,1,0:T(8,128)(2,1)} %copy-done.5), calls=%async_computation.2 | async-start | bytes 3670016 | tf_op jit(solution)/shard_map/all_to_all | solution.py:326
  135.9 1.4 collective-permute-start.10
  137.4 24.2 %collective-permute-start.11 = (bf16[1024,128]{1,0:T(8,128)(2,1)S(1)}, bf16[1024,128]{1,0:T(8,128)(2,1)S(1)}, u32[]{:S(2)}, u32[]{:S(2)}) collective-permute-start(bf16[1024,128]{1,0:T(8,128)(2,1)S(1)} %pad_maximum_fusion.2.rest_0_), channel_id=1, source_target_pairs={{0,4},{4,0},{1,5},{5,1},{2,6},{6,2},{3,7},{7,3},{8,12},{12,8},{9,1... | collective-permute-start | bytes 786440 | tf_op jit(solution)/shard_map/ppermute | solution.py:194
  139.0 25.3 %collective-permute-start.16 = (bf16[1024,128]{1,0:T(8,128)(2,1)S(1)}, bf16[1024,128]{1,0:T(8,128)(2,1)S(1)}, u32[]{:S(2)}, u32[]{:S(2)}) collective-permute-start(bf16[1024,128]{1,0:T(8,128)(2,1)S(1)} %pad_maximum_fusion.2.rest_0_), channel_id=1, source_target_pairs={{0,3},{1,0},{2,1},{3,2},{4,7},{5,4},{6,5},{7,6},{8,11},{9,8},{10,9... | collective-permute-start | bytes 786440 | tf_op jit(solution)/shard_map/ppermute | solution.py:190
  141.7 23.2 %collective-permute-start.14 = (bf16[1024,128]{1,0:T(8,128)(2,1)S(1)}, bf16[1024,128]{1,0:T(8,128)(2,1)S(1)}, u32[]{:S(2)}, u32[]{:S(2)}) collective-permute-start(bf16[1024,128]{1,0:T(8,128)(2,1)S(1)} %pad_maximum_fusion.2.rest_0_), channel_id=1, source_target_pairs={{0,2},{1,3},{2,0},{3,1},{4,6},{5,7},{6,4},{7,5},{8,10},{9,11},{10,... | collective-permute-start | bytes 786440 | tf_op jit(solution)/shard_map/ppermute | solution.py:190
  161.1 61.6 %collective-permute-start.27 = (bf16[64,112,128]{2,1,0:T(8,128)(2,1)}, bf16[64,112,128]{2,1,0:T(8,128)(2,1)}, u32[]{:S(2)}, u32[]{:S(2)}) collective-permute-start(bf16[64,112,128]{2,1,0:T(8,128)(2,1)} %all-to-all-done.2.blocks_ref), channel_id=1, source_target_pairs={{0,8},{8,0},{1,9},{9,1},{2,10},{10,2},{3,11},{11,3},{4,12},{12,4},... | collective-permute-start | bytes 5505032 | tf_op jit(solution)/shard_map/ppermute | solution.py:327
  161.1 16.1 %collective-permute-start.12 = (bf16[1024,128]{1,0:T(8,128)(2,1)S(1)}, bf16[1024,128]{1,0:T(8,128)(2,1)}, u32[]{:S(2)}, u32[]{:S(2)}) collective-permute-start(bf16[1024,128]{1,0:T(8,128)(2,1)S(1)} %pad_maximum_fusion.2.rest_0_), channel_id=1, source_target_pairs={{0,1},{1,2},{2,3},{3,0},{4,5},{5,6},{6,7},{7,4},{8,9},{9,10},{10,1... | collective-permute-start | bytes 786440 | tf_op jit(solution)/shard_map/ppermute | solution.py:190
  161.6 15.5 %collective-permute-start.17 = (bf16[1024,128]{1,0:T(8,128)(2,1)S(1)}, bf16[1024,128]{1,0:T(8,128)(2,1)}, u32[]{:S(2)}, u32[]{:S(2)}) collective-permute-start(bf16[1024,128]{1,0:T(8,128)(2,1)S(1)} %collective-permute-done.11.rest_1_), channel_id=1, source_target_pairs={{0,3},{1,0},{2,1},{3,2},{4,7},{5,4},{6,5},{7,6},{8,11},{9,8},{10,9... | collective-permute-start | bytes 786440 | tf_op jit(solution)/shard_map/ppermute | solution.py:190
  164.3 12.9 %collective-permute-start.15 = (bf16[1024,128]{1,0:T(8,128)(2,1)S(1)}, bf16[1024,128]{1,0:T(8,128)(2,1)}, u32[]{:S(2)}, u32[]{:S(2)}) collective-permute-start(bf16[1024,128]{1,0:T(8,128)(2,1)S(1)} %collective-permute-done.11.rest_1_), channel_id=1, source_target_pairs={{0,2},{1,3},{2,0},{3,1},{4,6},{5,7},{6,4},{7,5},{8,10},{9,11},{10,... | collective-permute-start | bytes 786440 | tf_op jit(solution)/shard_map/ppermute | solution.py:190
  164.8 17.5 %collective-permute-start.13 = (bf16[1024,128]{1,0:T(8,128)(2,1)S(1)}, bf16[1024,128]{1,0:T(8,128)(2,1)}, u32[]{:S(2)}, u32[]{:S(2)}) collective-permute-start(bf16[1024,128]{1,0:T(8,128)(2,1)S(1)} %collective-permute-done.11.rest_1_), channel_id=1, source_target_pairs={{0,1},{1,2},{2,3},{3,0},{4,5},{5,6},{6,7},{7,4},{8,9},{9,10},{10,1... | collective-permute-start | bytes 786440 | tf_op jit(solution)/shard_map/ppermute | solution.py:190
  190.4 26.6 %copy-start.7 = (bf16[512,1024]{1,0:T(8,128)(2,1)S(1)}, bf16[512,1024]{1,0:T(8,128)(2,1)}, u32[]{:S(2)}) copy-start(bf16[512,1024]{1,0:T(8,128)(2,1)} %copy-done.6) | copy-start | bytes 3145732
  190.4 26.6 %copy-start.12 = (bf16[512,256]{1,0:T(8,128)(2,1)S(1)}, bf16[512,256]{1,0:T(8,128)(2,1)}, u32[]{:S(2)}) copy-start(bf16[512,256]{1,0:T(8,128)(2,1)} %param.9) | copy-start | bytes 786436
  190.4 10.8 %collective-permute-start.21 = (bf16[1024,128]{1,0:T(8,128)(2,1)S(1)}, bf16[1024,128]{1,0:T(8,128)(2,1)S(1)}, u32[]{:S(2)}, u32[]{:S(2)}) collective-permute-start(bf16[1024,128]{1,0:T(8,128)(2,1)S(1)} %get-tuple-element.34), channel_id=1, source_target_pairs={{0,64},{32,96},{64,0},{96,32},{1,65},{33,97},{65,1},{97,33},{2,66}... | collective-permute-start | bytes 786440 | tf_op jit(solution)/shard_map/ppermute | solution.py:190
  192.1 14.9 %collective-permute-start.22 = (bf16[1024,128]{1,0:T(8,128)(2,1)S(1)}, bf16[1024,128]{1,0:T(8,128)(2,1)S(1)}, u32[]{:S(2)}, u32[]{:S(2)}) collective-permute-start(bf16[1024,128]{1,0:T(8,128)(2,1)S(1)} %get-tuple-element.35), channel_id=1, source_target_pairs={{0,32},{32,64},{64,96},{96,0},{1,33},{33,65},{65,97},{97,1},{2,34}... | collective-permute-start | bytes 786440 | tf_op jit(solution)/shard_map/ppermute | solution.py:190
  192.8 14.6 %collective-permute-start.23 = (bf16[1024,128]{1,0:T(8,128)(2,1)S(1)}, bf16[1024,128]{1,0:T(8,128)(2,1)S(1)}, u32[]{:S(2)}, u32[]{:S(2)}) collective-permute-start(bf16[1024,128]{1,0:T(8,128)(2,1)S(1)} %get-tuple-element.36), channel_id=1, source_target_pairs={{0,96},{32,0},{64,32},{96,64},{1,97},{33,1},{65,33},{97,65},{2,98}... | collective-permute-start | bytes 786440 | tf_op jit(solution)/shard_map/ppermute | solution.py:190
  195.3 17.2 %collective-permute-start.18 = (bf16[1024,128]{1,0:T(8,128)(2,1)S(1)}, bf16[1024,128]{1,0:T(8,128)(2,1)S(1)}, u32[]{:S(2)}, u32[]{:S(2)}) collective-permute-start(bf16[1024,128]{1,0:T(8,128)(2,1)S(1)} %get-tuple-element.30), channel_id=1, source_target_pairs={{0,64},{32,96},{64,0},{96,32},{1,65},{33,97},{65,1},{97,33},{2,66}... | collective-permute-start | bytes 786440 | tf_op jit(solution)/shard_map/ppermute | solution.py:190
  201.3 15.5 %collective-permute-start.19 = (bf16[1024,128]{1,0:T(8,128)(2,1)S(1)}, bf16[1024,128]{1,0:T(8,128)(2,1)S(1)}, u32[]{:S(2)}, u32[]{:S(2)}) collective-permute-start(bf16[1024,128]{1,0:T(8,128)(2,1)S(1)} %get-tuple-element.31), channel_id=1, source_target_pairs={{0,32},{32,64},{64,96},{96,0},{1,33},{33,65},{65,97},{97,1},{2,34}... | collective-permute-start | bytes 786440 | tf_op jit(solution)/shard_map/ppermute | solution.py:190
  206.9 9.8 %collective-permute-start.20 = (bf16[1024,128]{1,0:T(8,128)(2,1)S(1)}, bf16[1024,128]{1,0:T(8,128)(2,1)S(1)}, u32[]{:S(2)}, u32[]{:S(2)}) collective-permute-start(bf16[1024,128]{1,0:T(8,128)(2,1)S(1)} %get-tuple-element.32), channel_id=1, source_target_pairs={{0,96},{32,0},{64,32},{96,64},{1,97},{33,1},{65,33},{97,65},{2,98}... | collective-permute-start | bytes 786440 | tf_op jit(solution)/shard_map/ppermute | solution.py:190
  207.6 9.2 %collective-permute-start.24 = (bf16[1024,128]{1,0:T(8,128)(2,1)S(1)}, bf16[1024,128]{1,0:T(8,128)(2,1)S(1)}, u32[]{:S(2)}, u32[]{:S(2)}) collective-permute-start(bf16[1024,128]{1,0:T(8,128)(2,1)S(1)} %pair_sum.1), channel_id=1, source_target_pairs={{0,16},{16,0},{1,17},{17,1},{2,18},{18,2},{3,19},{19,3},{4,20},{20... | collective-permute-start | bytes 786440 | tf_op jit(solution)/shard_map/ppermute | solution.py:194
  216.9 1.4 collective-permute-start.25
  (12 other events, 46.7 us)

commit v7 on v6

--- a/solution.py
+++ b/solution.py
@@ -25,10 +25,10 @@
     return sig * (1.0 + value * (1.0 - sig))
 
 
-def cells_kernel(transposed, off_ref, cnt_ref, place_ref, blk0, blk1, *rest):
-    pieces = rest[:8]
-    out_refs = rest[8:-5]
-    src, held, acc, blk_sem, src_sem = rest[-5:]
+def cells_kernel(transposed, spots, off_ref, cnt_ref, place_ref, blk0, blk1, *rest):
+    pieces = rest[: len(spots)]
+    out_refs = rest[len(spots) : -7]
+    src, held, acc, sent, blk_sem, src_sem, out_sem = rest[-7:]
     n_chunks = SLOTS // CHUNK
     blocks = (blk0, blk1)
 
@@ -41,8 +41,8 @@
         )
 
     moves = [
-        pltpu.make_async_copy(piece, src.at[pl.ds(p * 1024, 1024)], src_sem.at[p])
-        for p, piece in enumerate(pieces)
+        pltpu.make_async_copy(piece, src.at[pl.ds(spot, piece.shape[0])], src_sem.at[p])
+        for p, (spot, piece) in enumerate(zip(spots, pieces))
     ]
     for move in moves:
         move.start()
@@ -83,30 +83,43 @@
     if len(out_refs) == 1:
         out_refs[0][...] = acc[: 16 * 512, :].astype(BF).reshape(out_refs[0].shape)
     else:
+        moves = []
         for p, out_ref in enumerate(out_refs):
             for h in range(2):
                 at = pl.multiple_of(place_ref[2 * p + h], 512)
-                out_ref[h * 512 : (h + 1) * 512, :] = acc[pl.ds(at, 512), :].astype(BF)
+                sent[p, h * 512 : (h + 1) * 512, :] = acc[pl.ds(at, 512), :].astype(BF)
+            moves.append(pltpu.make_async_copy(sent.at[p], out_ref, out_sem.at[p]))
+            moves[-1].start()
+        for move in moves:
+            move.wait()
+
+
+def in_hbm(value):
+    return pltpu.with_memory_space_constraint(value, pltpu.HBM)
 
 
 def cell_products(transposed, offsets, counts, place, blk_own, blk_other, pieces):
+    spots = [spot for spot, _ in pieces]
     any_spec = pl.BlockSpec(memory_space=pl.ANY)
+    hbm = pl.BlockSpec(memory_space=pltpu.HBM)
     smem = pl.BlockSpec(memory_space=pltpu.SMEM)
     n_chunks = SLOTS // CHUNK
     return pl.pallas_call(
-        functools.partial(cells_kernel, transposed),
-        out_shape=(jax.ShapeDtypeStruct((1024, 128), BF),) * 8
+        functools.partial(cells_kernel, transposed, spots),
+        out_shape=(pltpu.HBM((1024, 128), BF),) * 8
         if transposed
         else jax.ShapeDtypeStruct((16, 512, 128), BF),
-        in_specs=[smem] * 3 + [any_spec] * 10,
-        out_specs=(pl.BlockSpec(memory_space=pltpu.VMEM),) * 8
+        in_specs=[smem] * 3 + [hbm] * 2 + [any_spec] * len(pieces),
+        out_specs=(hbm,) * 8
         if transposed
         else pl.BlockSpec(memory_space=pltpu.VMEM),
         scratch_shapes=[
             pltpu.VMEM((8192, 128), BF),
             pltpu.VMEM((2, SLOTS, SIDE, SIDE), BF),
             pltpu.VMEM((8192 + SIDE, 128), F32),
+            pltpu.VMEM((8, 1024, 128) if transposed else (8, 16, 128), BF),
             pltpu.SemaphoreType.DMA((2 * n_chunks,)),
+            pltpu.SemaphoreType.DMA((len(pieces),)),
             pltpu.SemaphoreType.DMA((8,)),
         ],
         compiler_params=pltpu.CompilerParams(vmem_limit_bytes=CELL_VMEM),
@@ -114,7 +127,7 @@
             flops=2 * 2 * SLOTS * SIDE * SIDE * 128, bytes_accessed=10 << 20, transcendentals=0
         ),
         name="cells_back" if transposed else "cells_forward",
-    )(offsets, counts, place, blk_own, blk_other, *pieces)
+    )(offsets, counts, place, in_hbm(blk_own), in_hbm(blk_other), *(piece for _, piece in pieces))
 
 
 def grads_kernel(half_ref, joined, act_one, cot, gp_one, gp_two, act_two, sum_ref):
@@ -144,43 +157,58 @@
     )(half.reshape(1), *operands)
 
 
-def chip_kernel(own, got, out_ref):
+def chip_kernel(own, got, out_ref, held, sems):
+    moves = []
     for row in range(16):
         rows = slice(row * 112, (row + 1) * 112)
         for lane in range(4):
             lanes = slice(lane * 128, (lane + 1) * 128)
-            out_ref[row * 4 + lane] = (
-                own[rows, lanes].astype(F32) + got[rows, lanes].astype(F32)
-            ).astype(BF)
+            held[row * 4 + lane] = (own[rows, lanes].astype(F32) + got[rows, lanes].astype(F32)).astype(
+                BF
+            )
+        if row % 4 == 3:
+            part = slice((row - 3) * 4, (row + 1) * 4)
+            moves.append(pltpu.make_async_copy(held.at[part], out_ref.at[part], sems.at[row // 4]))
+            moves[-1].start()
+    for move in moves:
+        move.wait()
 
 
 def chip_sum(own, got):
     vm = pl.BlockSpec(memory_space=pltpu.VMEM)
     return pl.pallas_call(
         chip_kernel,
-        out_shape=jax.ShapeDtypeStruct((64, 112, 128), BF),
+        out_shape=pltpu.HBM((64, 112, 128), BF),
         in_specs=[vm, vm],
-        out_specs=vm,
+        out_specs=pl.BlockSpec(memory_space=pltpu.HBM),
+        scratch_shapes=[pltpu.VMEM((64, 112, 128), BF), pltpu.SemaphoreType.DMA((4,))],
         cost_estimate=pl.CostEstimate(flops=1 << 20, bytes_accessed=6 << 20, transcendentals=0),
         compiler_params=pltpu.CompilerParams(vmem_limit_bytes=12 << 20),
         name="chip_sum",
     )(own, got)
 
 
-def chunk_kernel(parts, out_ref):
+def chunk_kernel(parts, out_ref, held, sems):
     total = jnp.sum(parts[...].astype(F32), axis=0).astype(BF)
-    for k in range(64):
-        out_ref[k] = total
+    for k in range(8):
+        held[k] = total
+    moves = [
+        pltpu.make_async_copy(held, out_ref.at[8 * k : 8 * k + 8], sems.at[k]) for k in range(8)
+    ]
+    for move in moves:
+        move.start()
+    for move in moves:
+        move.wait()
 
 
 def chunk_sum(parts):
-    vm = pl.BlockSpec(memory_space=pltpu.VMEM)
     return pl.pallas_call(
         chunk_kernel,
-        out_shape=jax.ShapeDtypeStruct((64, 112, 128), BF),
-        in_specs=[vm],
-        out_specs=vm,
-        cost_estimate=pl.CostEstimate(flops=1 << 20, bytes_accessed=1 << 20, transcendentals=0),
+        out_shape=pltpu.HBM((64, 112, 128), BF),
+        in_specs=[pl.BlockSpec(memory_space=pltpu.VMEM)],
+        out_specs=pl.BlockSpec(memory_space=pltpu.HBM),
+        scratch_shapes=[pltpu.VMEM((8, 112, 128), BF), pltpu.SemaphoreType.DMA((8,))],
+        cost_estimate=pl.CostEstimate(flops=1 << 20, bytes_accessed=3 << 20, transcendentals=0),
         compiler_params=pltpu.CompilerParams(vmem_limit_bytes=12 << 20),
         name="chunk_sum",
     )(parts)
@@ -195,13 +223,37 @@
 
 
 def gather_steps(value, ring, pair):
+    over = flip(value, pair)
+    below = ring_shift(value, ring, 1)
+    above = ring_shift(value, ring, 3)
+    low = ring_shift(above[:512], ring, 3)
+    high = ring_shift(below[512:], ring, 1)
+    over_below = ring_shift(over, ring, 1)
+    over_above = ring_shift(over, ring, 3)
+    over_low = flip(low, pair)
+    over_high = flip(high, pair)
+    return [
+        (0, value),
+        (1024, over),
+        (2048, below),
+        (3072, over_below),
+        (4096, low),
+        (4608, high),
+        (5120, over_low),
+        (5632, over_high),
+        (6144, above),
+        (7168, over_above),
+    ]
+
+
+def gather_direct(value, ring, pair):
     got = [value] * 8
     got[1] = flip(value, pair)
     for small in range(2):
         for big in (2, 1, 3):
             p = 2 * big + small
             got[p] = ring_shift(got[small], ring, big)
-    return got
+    return [(1024 * p, block) for p, block in enumerate(got)]
 
 
 def pair_kernel(*refs):
@@ -388,7 +440,7 @@
     direct = cotangent.astype(F32) + grad_joined[:, :256]
     grad_agg = grad_joined[:, 256:].astype(BF)
 
-    pieces = gather_steps(halves(grad_agg, core), "x", "yl")
+    pieces = gather_direct(halves(grad_agg, core), "x", "yl")
     operands = (joined, act_one, cotangent, grad_pre_one, grad_pre_two, act_two)
     grad_in, grad_mid, grad_out = sum_grads(core, operands)
     back = cell_products(True, bwd_off, count, place, blk_own, blk_other, pieces)

time: 228 us -> 222 us (0.974)
  local copies, waits for them, and re-layouts: 20.3 us -> 13.4 us
  waiting for transfers between devices: 66.3 us -> 60.7 us
  Pallas kernels: 18.6 us -> 22.5 us
    ppermute x18, waiting for transfers between devices: 41.7 us -> 33.7 us  [ring_shift(): return lax.ppermute(value, axis, [(i, (i + k) % 4) for i in range(4)])]
    unnamed x30 -> x28, local copies, waits for them, and re-layouts: 9.79 us -> 2.91 us
    pallas_call x4, Pallas kernels: 9.03 us -> 12.9 us  [the longest x2 10 us: cell_products(): pl.pallas_call(functools.partial(cells_kernel, transposed, spots), out_sh...]
    ppermute x3 -> x5, starting transfers between devices: 7.42 us -> 8.39 us  [flip(): return lax.ppermute(value, axis, [(0, 1), (1, 0)])]
  transfers between devices with their start and end apart: 29 -> 31, of which waited for: 14 -> 14; matrix products, arithmetic and copies ran while one was open for 8% -> 8% of each run, Pallas kernels for 4% -> 5%
where the time goes in v7:
time: 222 us; the launch traced here: 220 us
  blocking collectives  65.9 us (30%)
  waiting for transfers between devices  60.7 us (27%)
  starting transfers between devices  42.6 us (19%)
  Pallas kernels  22.5 us (10%)
  local copies, waits for them, and re-layouts  13.4 us (6%)
  matrix products  9.23 us (4%)
  other arithmetic  4.04 us (2%)
    all_to_all x1, blocking collectives, sum_grads(): lax.all_to_all(chip_sum(own, got), ('z', 'yh', 'yl', 'x'), 0, 0, tiled=True)  34.5 us
    ppermute x18, waiting for transfers between devices, ring_shift(): return lax.ppermute(value, axis, [(i, (i + k) % 4) for i in range(4)])  33.7 us
    all_to_all x1, blocking collectives, shards(): cells = lax.all_to_all(cells, ('core', 'yl', 'x'), 0, 0, tiled=True)  31.4 us
    ppermute x18, starting transfers between devices, ring_shift(): return lax.ppermute(value, axis, [(i, (i + k) % 4) for i in range(4)])  27.3 us
    all_to_all x1, waiting for transfers between devices, sum_grads(): mine = lax.all_to_all(chunk, ('z', 'yh', 'yl', 'x'), 0, 0, tiled=True)  18.5 us
    pallas_call x2, Pallas kernels, cell_products(): pl.pallas_call(functools.partial(cells_kernel, transposed, spots), out_sh...  10 us
    ppermute x5, starting transfers between devices, flip(): return lax.ppermute(value, axis, [(0, 1), (1, 0)])  8.39 us
    pallas_call x2, Pallas kernels, finish_grads(): pl.pallas_call(finish_kernel, out_shape=(jax.ShapeDtypeStruct((512, 1024)...  6.92 us
  transfers between devices with their start and end apart: 31, of which 14 were waited for; matrix products, arithmetic and copies ran while one was open for 8% of the time, Pallas kernels for 5%

profile of v7, /device:TPU:0, one launch (start us, length us, event | category | flops | bytes accessed | tf_op | source)
XLA Modules:
  0.0 220.2 jit_solution(17713543479109016604)
XLA Ops:
  2.3 3.0 %collective-permute-done = bf16[512,128]{1,0:T(8,128)(2,1)S(1)} collective-permute-done((bf16[512,128]{1,0:T(8,128)(2,1)S(1)}, bf16[512,128]{1,0:T(8,128)(2,1)S(1)}, u32[]{:S(2)}, u32[]{:S(2)}) %collective-permute-start) | collective-permute-done | bytes 131104 | tf_op jit(solution)/shard_map/ppermute | solution.py:319
  5.3 4.2 %collective-permute-start.6 = (bf16[1024,128]{1,0:T(8,128)(2,1)S(1)}, bf16[1024,128]{1,0:T(8,128)(2,1)S(1)}, u32[]{:S(2)}, u32[]{:S(2)}) collective-permute-start(bf16[1024,128]{1,0:T(8,128)(2,1)S(1)} %pad_maximum_fusion.1.rest_0_), channel_id=1, source_target_pairs={{0,96},{32,0},{64,32},{96,64},{1,97},{33,1},{65,33},{97,65},{2,98}... | collective-permute-start | bytes 786440 | tf_op jit(solution)/shard_map/ppermute | solution.py:218
  10.2 3.3 %collective-permute-start.3 = (bf16[1024,128]{1,0:T(8,128)(2,1)S(1)}, bf16[1024,128]{1,0:T(8,128)(2,1)S(1)}, u32[]{:S(2)}, u32[]{:S(2)}) collective-permute-start(bf16[1024,128]{1,0:T(8,128)(2,1)S(1)} %pad_maximum_fusion.1.rest_0_), channel_id=1, source_target_pairs={{0,16},{16,0},{1,17},{17,1},{2,18},{18,2},{3,19},{19,3},{4,20},{20... | collective-permute-start | bytes 786440 | tf_op jit(solution)/shard_map/ppermute | solution.py:222
  14.3 5.1 %copy.26 = bf16[64,64,192]{1,0,2:T(8,128)(2,1)} copy(bf16[64,64,192]{2,1,0:T(8,128)(2,1)} %bitcast.35) | data formatting | bytes 3145728 | tf_op jit(solution)/shard_map/layout_constraint | solution.py:418
  19.6 3.3 %collective-permute-start.7 = (bf16[512,128]{1,0:T(8,128)(2,1)S(1)}, bf16[512,128]{1,0:T(8,128)(2,1)S(1)}, u32[]{:S(2)}, u32[]{:S(2)}) collective-permute-start(bf16[512,128]{1,0:T(8,128)(2,1)S(1)} %slice.56), channel_id=1, source_target_pairs={{0,96},{32,0},{64,32},{96,64},{1,97},{33,1},{65,33},{97,65},{2,98}... | collective-permute-start | bytes 393224 | tf_op jit(solution)/shard_map/ppermute | solution.py:218
  23.6 3.2 %collective-permute-start.11 = (bf16[1024,128]{1,0:T(8,128)(2,1)S(1)}, bf16[1024,128]{1,0:T(8,128)(2,1)S(1)}, u32[]{:S(2)}, u32[]{:S(2)}) collective-permute-start(bf16[1024,128]{1,0:T(8,128)(2,1)S(1)} %collective-permute-done.3.rest_1_), channel_id=1, source_target_pairs={{0,96},{32,0},{64,32},{96,64},{1,97},{33,1},{65,33},{97,65},{2,98}... | collective-permute-start | bytes 786440 | tf_op jit(solution)/shard_map/ppermute | solution.py:218
  27.2 2.7 %collective-permute-done.8.rest_5_ = bf16[512,128]{1,0:T(8,128)(2,1)} collective-permute-done((bf16[512,128]{1,0:T(8,128)(2,1)S(1)}, bf16[512,128]{1,0:T(8,128)(2,1)}, u32[]{:S(2)}, u32[]{:S(2)}) %collective-permute-start.8) | collective-permute-done | bytes 131104 | tf_op jit(solution)/shard_map/ppermute | solution.py:218
  30.5 5.2 %copy.27 = bf16[64,64,192]{1,0,2:T(8,128)(2,1)} copy(bf16[64,64,192]{2,1,0:T(8,128)(2,1)} %collective-permute-done.2) | data formatting | bytes 3145728 | tf_op jit(solution)/shard_map/ppermute | solution.py:396
  36.7 4.4 %cells_forward.1 = bf16[16,512,128]{2,1,0:T(8,128)(2,1)S(1)} custom-call(s32[768]{0:T(1024)S(1)} %reshape.46.off_ref, s32[2]{0:T(128)S(1)} %fusion.8.cnt_ref, s32[16]{0:T(128)S(1)} %add_multiply_fusion.1.place_ref, bf16[192,64,64]{2,1,0:T(8,128)(2,1)} %bitcast.30, bf16[192,64,64]{2,1,0:T(8,128)(2,1)} %bitcast.32, ...), custom_call_target="tpu_custom_call" | custom-call | flops 402653184 | bytes 10485760 | tf_op jit(solution)/shard_map/cells_forward/pallas_call | solution.py:107
  41.1 31.4 %all_to_all.15 = bf16[16,512,128]{2,1,0:T(8,128)(2,1)S(1)} all-to-all(bf16[16,512,128]{2,1,0:T(8,128)(2,1)S(1)} %cells_forward.1), channel_id=1, replica_groups=mesh['z'=4,'yh'=2,'core'=2,'yl'=2,'x'=4] {'core','yl','x'}, dimensions={0} | all-to-all | bytes 4194304 | tf_op jit(solution)/shard_map/all_to_all | solution.py:421
  77.3 1.7 multiply_convert_fusion.gp_one
  81.8 2.3 %collective-permute-done.28.got = bf16[1792,512]{1,0:T(8,128)(2,1)S(1)} collective-permute-done((bf16[1792,512]{1,0:T(8,128)(2,1)S(1)}, bf16[1792,512]{1,0:T(8,128)(2,1)S(1)}, u32[]{:S(2)}, u32[]{:S(2)}) %collective-permute-start.28) | collective-permute-done | bytes 1835040 | tf_op jit(solution)/shard_map/ppermute | solution.py:374
  85.4 34.5 %all_to_all.16.parts = bf16[64,112,128]{2,1,0:T(8,128)(2,1)S(1)} all-to-all(bf16[64,112,128]{2,1,0:T(8,128)(2,1)} %chip_sum.1), channel_id=1, replica_groups=mesh['z'=4,'yh'=2,'core'=2,'yl'=2,'x'=4] {'z','yh','yl','x'}, dimensions={0} | all-to-all | bytes 3670016 | tf_op jit(solution)/shard_map/all_to_all | solution.py:376
  119.9 1.6 chunk_sum.1
  121.4 5.8 %all-to-all-start.2 = ((bf16[64,112,128]{2,1,0:T(8,128)(2,1)}), bf16[64,112,128]{2,1,0:T(8,128)(2,1)}, u32[]{:S(2)}, u32[]{:S(2)}) async-start(bf16[64,112,128]{2,1,0:T(8,128)(2,1)} %chunk_sum.1), calls=%async_computation.2 | async-start | bytes 3670016 | tf_op jit(solution)/shard_map/all_to_all | solution.py:378
  127.3 3.0 %fusion.11 = (bf16[512,512]{1,0:T(8,128)(2,1)S(1)}, f32[512,512]{1,0:T(8,128)}) fusion(bf16[512,1024]{1,0:T(8,128)(2,1)S(1)} %multiply_convert_fusion.gp_one, bf16[512,1024]{1,0:T(8,128)(2,1)} %param.14), kind=kOutput, calls=%fused_computation.47 | convolution fusion | flops 537133056 | bytes 3670016 | tf_op jit(solution)/shard_map/dot_general | solution.py:439
  131.8 1.6 collective-permute-start.13
  133.3 2.7 %collective-permute-start.18 = (bf16[1024,128]{1,0:T(8,128)(2,1)S(1)}, bf16[1024,128]{1,0:T(8,128)(2,1)S(1)}, u32[]{:S(2)}, u32[]{:S(2)}) collective-permute-start(bf16[1024,128]{1,0:T(8,128)(2,1)S(1)} %pad_maximum_fusion.2.rest_0_), channel_id=1, source_target_pairs={{0,3},{1,0},{2,1},{3,2},{4,7},{5,4},{6,5},{7,6},{8,11},{9,8},{10,9... | collective-permute-start | bytes 786440 | tf_op jit(solution)/shard_map/ppermute | solution.py:218
  136.9 18.5 %all-to-all-done.2.blocks_ref = bf16[64,112,128]{2,1,0:T(8,128)(2,1)} async-done(((bf16[64,112,128]{2,1,0:T(8,128)(2,1)}), bf16[64,112,128]{2,1,0:T(8,128)(2,1)}, u32[]{:S(2)}, u32[]{:S(2)}) %all-to-all-start.2) | async-done | bytes 1835040 | tf_op jit(solution)/shard_map/all_to_all | solution.py:378
  156.0 2.7 %collective-permute-start.19 = (bf16[1024,128]{1,0:T(8,128)(2,1)S(1)}, bf16[1024,128]{1,0:T(8,128)(2,1)}, u32[]{:S(2)}, u32[]{:S(2)}) collective-permute-start(bf16[1024,128]{1,0:T(8,128)(2,1)S(1)} %collective-permute-done.13.rest_1_), channel_id=1, source_target_pairs={{0,3},{1,0},{2,1},{3,2},{4,7},{5,4},{6,5},{7,6},{8,11},{9,8},{10,9... | collective-permute-start | bytes 786440 | tf_op jit(solution)/shard_map/ppermute | solution.py:218
  159.1 3.0 %collective-permute-start.15 = (bf16[1024,128]{1,0:T(8,128)(2,1)S(1)}, bf16[1024,128]{1,0:T(8,128)(2,1)}, u32[]{:S(2)}, u32[]{:S(2)}) collective-permute-start(bf16[1024,128]{1,0:T(8,128)(2,1)S(1)} %collective-permute-done.13.rest_1_), channel_id=1, source_target_pairs={{0,1},{1,2},{2,3},{3,0},{4,5},{5,6},{6,7},{7,4},{8,9},{9,10},{10,1... | collective-permute-start | bytes 786440 | tf_op jit(solution)/shard_map/ppermute | solution.py:218
  162.3 9.2 %collective-permute-done.14.rest_2_ = bf16[1024,128]{1,0:T(8,128)(2,1)} collective-permute-done((bf16[1024,128]{1,0:T(8,128)(2,1)S(1)}, bf16[1024,128]{1,0:T(8,128)(2,1)}, u32[]{:S(2)}, u32[]{:S(2)}) %collective-permute-start.14) | collective-permute-done | bytes 262176 | tf_op jit(solution)/shard_map/ppermute | solution.py:218
  171.5 5.2 %collective-permute-done.15.rest_3_ = bf16[1024,128]{1,0:T(8,128)(2,1)} collective-permute-done((bf16[1024,128]{1,0:T(8,128)(2,1)S(1)}, bf16[1024,128]{1,0:T(8,128)(2,1)}, u32[]{:S(2)}, u32[]{:S(2)}) %collective-permute-start.15) | collective-permute-done | bytes 262176 | tf_op jit(solution)/shard_map/ppermute | solution.py:218
  176.7 5.6 %cells_back.1 = (bf16[1024,128]{1,0:T(8,128)(2,1)}, bf16[1024,128]{1,0:T(8,128)(2,1)}, bf16[1024,128]{1,0:T(8,128)(2,1)}, bf16[1024,128]{1,0:T(8,128)(2,1)}, bf1...) custom-call(s32[768]{0:T(1024)S(1)} %reshape.48.off_ref, ...), custom_call_target="tpu_custom_call" | custom-call | flops 402653184 | bytes 10485760 | tf_op jit(solution)/shard_map/cells_back/pallas_call | solution.py:107
  182.3 1.6 collective-permute-start.23
  184.7 2.5 %collective-permute-start.25 = (bf16[1024,128]{1,0:T(8,128)(2,1)}, bf16[1024,128]{1,0:T(8,128)(2,1)S(1)}, u32[]{:S(2)}, u32[]{:S(2)}) collective-permute-start(bf16[1024,128]{1,0:T(8,128)(2,1)} %get-tuple-element.36), channel_id=1, source_target_pairs={{0,96},{32,0},{64,32},{96,64},{1,97},{33,1},{65,33},{97,65},{2,98}... | collective-permute-start | bytes 786440 | tf_op jit(solution)/shard_map/ppermute | solution.py:218
  188.0 5.4 %collective-permute-done.23.refs_1_ = bf16[1024,128]{1,0:T(8,128)(2,1)S(1)} collective-permute-done((bf16[1024,128]{1,0:T(8,128)(2,1)}, bf16[1024,128]{1,0:T(8,128)(2,1)S(1)}, u32[]{:S(2)}, u32[]{:S(2)}) %collective-permute-start.23) | collective-permute-done | bytes 262176 | tf_op jit(solution)/shard_map/ppermute | solution.py:218
  193.3 5.7 %collective-permute-done.24.refs_2_ = bf16[1024,128]{1,0:T(8,128)(2,1)S(1)} collective-permute-done((bf16[1024,128]{1,0:T(8,128)(2,1)}, bf16[1024,128]{1,0:T(8,128)(2,1)S(1)}, u32[]{:S(2)}, u32[]{:S(2)}) %collective-permute-start.24) | collective-permute-done | bytes 262176 | tf_op jit(solution)/shard_map/ppermute | solution.py:218
  200.6 2.7 %collective-permute-start.26 = (bf16[1024,128]{1,0:T(8,128)(2,1)S(1)}, bf16[1024,128]{1,0:T(8,128)(2,1)S(1)}, u32[]{:S(2)}, u32[]{:S(2)}) collective-permute-start(bf16[1024,128]{1,0:T(8,128)(2,1)S(1)} %pair_sum.1), channel_id=1, source_target_pairs={{0,16},{16,0},{1,17},{17,1},{2,18},{18,2},{3,19},{19,3},{4,20},{20... | collective-permute-start | bytes 786440 | tf_op jit(solution)/shard_map/ppermute | solution.py:222
  204.6 4.2 %collective-permute-done.21.refs_2_ = bf16[1024,128]{1,0:T(8,128)(2,1)S(1)} collective-permute-done((bf16[1024,128]{1,0:T(8,128)(2,1)}, bf16[1024,128]{1,0:T(8,128)(2,1)S(1)}, u32[]{:S(2)}, u32[]{:S(2)}) %collective-permute-start.21) | collective-permute-done | bytes 262176 | tf_op jit(solution)/shard_map/ppermute | solution.py:218
  213.1 3.5 %finish_grads.2 = (f32[512,1024]{1,0:T(8,128)}, f32[1024,1024]{1,0:T(8,128)}, f32[1024,256]{1,0:T(8,128)}) custom-call(s32[1]{0:T(128)} %bitcast.5.half_ref, bf16[64,112,128]{2,1,0:T(8,128)(2,1)} %all-to-all-done.2.blocks_ref), custom_call_target="tpu_custom_call" | custom-call | flops 4194304 | bytes 6291456 | tf_op jit(solution)/shard_map/finish_grads/pallas_call | solution.py:350
  216.6 3.5 %finish_grads.3 = (f32[512,1024]{1,0:T(8,128)}, f32[1024,1024]{1,0:T(8,128)}, f32[1024,256]{1,0:T(8,128)}) custom-call(s32[1]{0:T(128)} %bitcast.6.half_ref, bf16[64,112,128]{2,1,0:T(8,128)(2,1)} %collective-permute-done.29.blocks_ref, f32[512,1024]{1,0:T(8,128)} %get-tuple-element.39.rest_0_, ...), custom_call_target="tpu_custom_call", output_to_operand_aliasing={{0}: (2, {}), {1}: (3, {}), {2}: (4, {})} | custom-call | flops 4194304 | bytes 6291456 | tf_op jit(solution)/shard_map/finish_grads/pallas_call | solution.py:350
  (101 shorter events, 26.4 us)
Async XLA Ops:
  0.6 74.2 %copy-start = (bf16[1024,1024]{1,0:T(8,128)(2,1)S(1)}, bf16[1024,1024]{1,0:T(8,128)(2,1)}, u32[]{:S(2)}) copy-start(bf16[1024,1024]{1,0:T(8,128)(2,1)} %param.15) | copy-start | bytes 6291460
  0.6 29.9 %collective-permute-start.2 = (bf16[64,64,192]{2,1,0:T(8,128)(2,1)}, bf16[64,64,192]{2,1,0:T(8,128)(2,1)}, u32[]{:S(2)}, u32[]{:S(2)}) collective-permute-start(bf16[64,64,192]{2,1,0:T(8,128)(2,1)} %bitcast.34), channel_id=1, source_target_pairs={{0,8},{8,0},{1,9},{9,1},{2,10},{10,2},{3,11},{11,3},{4,12},{12,4},... | collective-permute-start | bytes 4718600 | tf_op jit(solution)/shard_map/ppermute | solution.py:396
  1.9 3.4 %collective-permute-start = (bf16[512,128]{1,0:T(8,128)(2,1)S(1)}, bf16[512,128]{1,0:T(8,128)(2,1)S(1)}, u32[]{:S(2)}, u32[]{:S(2)}) collective-permute-start(bf16[512,128]{1,0:T(8,128)(2,1)S(1)} %get-tuple-element.54), channel_id=1, source_target_pairs={{0,8},{8,0},{1,9},{9,1},{2,10},{10,2},{3,11},{11,3},{4,12},{12,4},... | collective-permute-start | bytes 393224 | tf_op jit(solution)/shard_map/ppermute | solution.py:319
  5.3 14.2 %collective-permute-start.6 = (bf16[1024,128]{1,0:T(8,128)(2,1)S(1)}, bf16[1024,128]{1,0:T(8,128)(2,1)S(1)}, u32[]{:S(2)}, u32[]{:S(2)}) collective-permute-start(bf16[1024,128]{1,0:T(8,128)(2,1)S(1)} %pad_maximum_fusion.1.rest_0_), channel_id=1, source_target_pairs={{0,96},{32,0},{64,32},{96,64},{1,97},{33,1},{65,33},{97,65},{2,98}... | collective-permute-start | bytes 786440 | tf_op jit(solution)/shard_map/ppermute | solution.py:218
  9.5 13.3 %collective-permute-start.4 = (bf16[1024,128]{1,0:T(8,128)(2,1)S(1)}, bf16[1024,128]{1,0:T(8,128)(2,1)S(1)}, u32[]{:S(2)}, u32[]{:S(2)}) collective-permute-start(bf16[1024,128]{1,0:T(8,128)(2,1)S(1)} %pad_maximum_fusion.1.rest_0_), channel_id=1, source_target_pairs={{0,32},{32,64},{64,96},{96,0},{1,33},{33,65},{65,97},{97,1},{2,34}... | collective-permute-start | bytes 786440 | tf_op jit(solution)/shard_map/ppermute | solution.py:218
  10.2 13.4 %collective-permute-start.3 = (bf16[1024,128]{1,0:T(8,128)(2,1)S(1)}, bf16[1024,128]{1,0:T(8,128)(2,1)S(1)}, u32[]{:S(2)}, u32[]{:S(2)}) collective-permute-start(bf16[1024,128]{1,0:T(8,128)(2,1)S(1)} %pad_maximum_fusion.1.rest_0_), channel_id=1, source_target_pairs={{0,16},{16,0},{1,17},{17,1},{2,18},{18,2},{3,19},{19,3},{4,20},{20... | collective-permute-start | bytes 786440 | tf_op jit(solution)/shard_map/ppermute | solution.py:222
  14.2 5.2 %collective-permute-start.1 = (s32[512]{0:T(512)S(1)}, s32[512]{0:T(512)S(1)}, u32[]{:S(2)}, u32[]{:S(2)}) collective-permute-start(s32[512]{0:T(512)S(1)} %pad_add_fusion.3), channel_id=1, source_target_pairs={{0,8},{8,0},{1,9},{9,1},{2,10},{10,2},{3,11},{11,3},{4,12},{12,4},... | collective-permute-start | bytes 6152 | tf_op jit(solution)/shard_map/ppermute | solution.py:395
  19.6 7.3 %collective-permute-start.7 = (bf16[512,128]{1,0:T(8,128)(2,1)S(1)}, bf16[512,128]{1,0:T(8,128)(2,1)S(1)}, u32[]{:S(2)}, u32[]{:S(2)}) collective-permute-start(bf16[512,128]{1,0:T(8,128)(2,1)S(1)} %slice.56), channel_id=1, source_target_pairs={{0,96},{32,0},{64,32},{96,64},{1,97},{33,1},{65,33},{97,65},{2,98}... | collective-permute-start | bytes 393224 | tf_op jit(solution)/shard_map/ppermute | solution.py:218
  22.9 7.0 %collective-permute-start.8 = (bf16[512,128]{1,0:T(8,128)(2,1)S(1)}, bf16[512,128]{1,0:T(8,128)(2,1)}, u32[]{:S(2)}, u32[]{:S(2)}) collective-permute-start(bf16[512,128]{1,0:T(8,128)(2,1)S(1)} %slice.57), channel_id=1, source_target_pairs={{0,32},{32,64},{64,96},{96,0},{1,33},{33,65},{65,97},{97,1},{2,34}... | collective-permute-start | bytes 393224 | tf_op jit(solution)/shard_map/ppermute | solution.py:218
  23.6 13.0 %collective-permute-start.11 = (bf16[1024,128]{1,0:T(8,128)(2,1)S(1)}, bf16[1024,128]{1,0:T(8,128)(2,1)S(1)}, u32[]{:S(2)}, u32[]{:S(2)}) collective-permute-start(bf16[1024,128]{1,0:T(8,128)(2,1)S(1)} %collective-permute-done.3.rest_1_), channel_id=1, source_target_pairs={{0,96},{32,0},{64,32},{96,64},{1,97},{33,1},{65,33},{97,65},{2,98}... | collective-permute-start | bytes 786440 | tf_op jit(solution)/shard_map/ppermute | solution.py:218
  26.9 9.8 %collective-permute-start.5 = (bf16[1024,128]{1,0:T(8,128)(2,1)S(1)}, bf16[1024,128]{1,0:T(8,128)(2,1)}, u32[]{:S(2)}, u32[]{:S(2)}) collective-permute-start(bf16[1024,128]{1,0:T(8,128)(2,1)S(1)} %collective-permute-done.3.rest_1_), channel_id=1, source_target_pairs={{0,32},{32,64},{64,96},{96,0},{1,33},{33,65},{65,97},{97,1},{2,34}... | collective-permute-start | bytes 786440 | tf_op jit(solution)/shard_map/ppermute | solution.py:218
  26.9 8.9 %collective-permute-start.9 = (bf16[512,128]{1,0:T(8,128)(2,1)S(1)}, bf16[512,128]{1,0:T(8,128)(2,1)}, u32[]{:S(2)}, u32[]{:S(2)}) collective-permute-start(bf16[512,128]{1,0:T(8,128)(2,1)S(1)} %collective-permute-done.7.rest_4_), channel_id=1, source_target_pairs={{0,16},{16,0},{1,17},{17,1},{2,18},{18,2},{3,19},{19,3},{4,20},{20... | collective-permute-start | bytes 393224 | tf_op jit(solution)/shard_map/ppermute | solution.py:222
  29.9 6.8 %collective-permute-start.10 = (bf16[512,128]{1,0:T(8,128)(2,1)}, bf16[512,128]{1,0:T(8,128)(2,1)}, u32[]{:S(2)}, u32[]{:S(2)}) collective-permute-start(bf16[512,128]{1,0:T(8,128)(2,1)} %collective-permute-done.8.rest_5_), channel_id=1, source_target_pairs={{0,16},{16,0},{1,17},{17,1},{2,18},{18,2},{3,19},{19,3},{4,20},{20... | collective-permute-start | bytes 393224 | tf_op jit(solution)/shard_map/ppermute | solution.py:222
  80.2 3.9 %collective-permute-start.28 = (bf16[1792,512]{1,0:T(8,128)(2,1)S(1)}, bf16[1792,512]{1,0:T(8,128)(2,1)S(1)}, u32[]{:S(2)}, u32[]{:S(2)}) collective-permute-start(bf16[1792,512]{1,0:T(8,128)(2,1)S(1)} %shard_map.129), channel_id=1, source_target_pairs={{0,8},{8,0},{1,9},{9,1},{2,10},{10,2},{3,11},{11,3},{4,12},{12,4},... | collective-permute-start | bytes 5505032 | tf_op jit(solution)/shard_map/ppermute | solution.py:374
  121.4 34.0 %all-to-all-start.2 = ((bf16[64,112,128]{2,1,0:T(8,128)(2,1)}), bf16[64,112,128]{2,1,0:T(8,128)(2,1)}, u32[]{:S(2)}, u32[]{:S(2)}) async-start(bf16[64,112,128]{2,1,0:T(8,128)(2,1)} %chunk_sum.1), calls=%async_computation.2 | async-start | bytes 3670016 | tf_op jit(solution)/shard_map/all_to_all | solution.py:378
  130.3 1.4 collective-permute-start.12
  131.8 24.2 %collective-permute-start.13 = (bf16[1024,128]{1,0:T(8,128)(2,1)S(1)}, bf16[1024,128]{1,0:T(8,128)(2,1)S(1)}, u32[]{:S(2)}, u32[]{:S(2)}) collective-permute-start(bf16[1024,128]{1,0:T(8,128)(2,1)S(1)} %pad_maximum_fusion.2.rest_0_), channel_id=1, source_target_pairs={{0,4},{4,0},{1,5},{5,1},{2,6},{6,2},{3,7},{7,3},{8,12},{12,8},{9,1... | collective-permute-start | bytes 786440 | tf_op jit(solution)/shard_map/ppermute | solution.py:222
  133.3 25.3 %collective-permute-start.18 = (bf16[1024,128]{1,0:T(8,128)(2,1)S(1)}, bf16[1024,128]{1,0:T(8,128)(2,1)S(1)}, u32[]{:S(2)}, u32[]{:S(2)}) collective-permute-start(bf16[1024,128]{1,0:T(8,128)(2,1)S(1)} %pad_maximum_fusion.2.rest_0_), channel_id=1, source_target_pairs={{0,3},{1,0},{2,1},{3,2},{4,7},{5,4},{6,5},{7,6},{8,11},{9,8},{10,9... | collective-permute-start | bytes 786440 | tf_op jit(solution)/shard_map/ppermute | solution.py:218
  136.0 23.1 %collective-permute-start.16 = (bf16[1024,128]{1,0:T(8,128)(2,1)S(1)}, bf16[1024,128]{1,0:T(8,128)(2,1)S(1)}, u32[]{:S(2)}, u32[]{:S(2)}) collective-permute-start(bf16[1024,128]{1,0:T(8,128)(2,1)S(1)} %pad_maximum_fusion.2.rest_0_), channel_id=1, source_target_pairs={{0,2},{1,3},{2,0},{3,1},{4,6},{5,7},{6,4},{7,5},{8,10},{9,11},{10,... | collective-permute-start | bytes 786440 | tf_op jit(solution)/shard_map/ppermute | solution.py:218
  155.4 61.2 %collective-permute-start.29 = (bf16[64,112,128]{2,1,0:T(8,128)(2,1)}, bf16[64,112,128]{2,1,0:T(8,128)(2,1)}, u32[]{:S(2)}, u32[]{:S(2)}) collective-permute-start(bf16[64,112,128]{2,1,0:T(8,128)(2,1)} %all-to-all-done.2.blocks_ref), channel_id=1, source_target_pairs={{0,8},{8,0},{1,9},{9,1},{2,10},{10,2},{3,11},{11,3},{4,12},{12,4},... | collective-permute-start | bytes 5505032 | tf_op jit(solution)/shard_map/ppermute | solution.py:379
  155.4 16.1 %collective-permute-start.14 = (bf16[1024,128]{1,0:T(8,128)(2,1)S(1)}, bf16[1024,128]{1,0:T(8,128)(2,1)}, u32[]{:S(2)}, u32[]{:S(2)}) collective-permute-start(bf16[1024,128]{1,0:T(8,128)(2,1)S(1)} %pad_maximum_fusion.2.rest_0_), channel_id=1, source_target_pairs={{0,1},{1,2},{2,3},{3,0},{4,5},{5,6},{6,7},{7,4},{8,9},{9,10},{10,1... | collective-permute-start | bytes 786440 | tf_op jit(solution)/shard_map/ppermute | solution.py:218
  156.0 15.5 %collective-permute-start.19 = (bf16[1024,128]{1,0:T(8,128)(2,1)S(1)}, bf16[1024,128]{1,0:T(8,128)(2,1)}, u32[]{:S(2)}, u32[]{:S(2)}) collective-permute-start(bf16[1024,128]{1,0:T(8,128)(2,1)S(1)} %collective-permute-done.13.rest_1_), channel_id=1, source_target_pairs={{0,3},{1,0},{2,1},{3,2},{4,7},{5,4},{6,5},{7,6},{8,11},{9,8},{10,9... | collective-permute-start | bytes 786440 | tf_op jit(solution)/shard_map/ppermute | solution.py:218
  158.7 12.9 %collective-permute-start.17 = (bf16[1024,128]{1,0:T(8,128)(2,1)S(1)}, bf16[1024,128]{1,0:T(8,128)(2,1)}, u32[]{:S(2)}, u32[]{:S(2)}) collective-permute-start(bf16[1024,128]{1,0:T(8,128)(2,1)S(1)} %collective-permute-done.13.rest_1_), channel_id=1, source_target_pairs={{0,2},{1,3},{2,0},{3,1},{4,6},{5,7},{6,4},{7,5},{8,10},{9,11},{10,... | collective-permute-start | bytes 786440 | tf_op jit(solution)/shard_map/ppermute | solution.py:218
  159.1 17.5 %collective-permute-start.15 = (bf16[1024,128]{1,0:T(8,128)(2,1)S(1)}, bf16[1024,128]{1,0:T(8,128)(2,1)}, u32[]{:S(2)}, u32[]{:S(2)}) collective-permute-start(bf16[1024,128]{1,0:T(8,128)(2,1)S(1)} %collective-permute-done.13.rest_1_), channel_id=1, source_target_pairs={{0,1},{1,2},{2,3},{3,0},{4,5},{5,6},{6,7},{7,4},{8,9},{9,10},{10,1... | collective-permute-start | bytes 786440 | tf_op jit(solution)/shard_map/ppermute | solution.py:218
  182.3 11.0 %collective-permute-start.23 = (bf16[1024,128]{1,0:T(8,128)(2,1)}, bf16[1024,128]{1,0:T(8,128)(2,1)S(1)}, u32[]{:S(2)}, u32[]{:S(2)}) collective-permute-start(bf16[1024,128]{1,0:T(8,128)(2,1)} %get-tuple-element.34), channel_id=1, source_target_pairs={{0,64},{32,96},{64,0},{96,32},{1,65},{33,97},{65,1},{97,33},{2,66}... | collective-permute-start | bytes 786440 | tf_op jit(solution)/shard_map/ppermute | solution.py:218
  183.9 15.1 %collective-permute-start.24 = (bf16[1024,128]{1,0:T(8,128)(2,1)}, bf16[1024,128]{1,0:T(8,128)(2,1)S(1)}, u32[]{:S(2)}, u32[]{:S(2)}) collective-permute-start(bf16[1024,128]{1,0:T(8,128)(2,1)} %get-tuple-element.35), channel_id=1, source_target_pairs={{0,32},{32,64},{64,96},{96,0},{1,33},{33,65},{65,97},{97,1},{2,34}... | collective-permute-start | bytes 786440 | tf_op jit(solution)/shard_map/ppermute | solution.py:218
  184.7 14.8 %collective-permute-start.25 = (bf16[1024,128]{1,0:T(8,128)(2,1)}, bf16[1024,128]{1,0:T(8,128)(2,1)S(1)}, u32[]{:S(2)}, u32[]{:S(2)}) collective-permute-start(bf16[1024,128]{1,0:T(8,128)(2,1)} %get-tuple-element.36), channel_id=1, source_target_pairs={{0,96},{32,0},{64,32},{96,64},{1,97},{33,1},{65,33},{97,65},{2,98}... | collective-permute-start | bytes 786440 | tf_op jit(solution)/shard_map/ppermute | solution.py:218
  187.2 17.4 %collective-permute-start.20 = (bf16[1024,128]{1,0:T(8,128)(2,1)}, bf16[1024,128]{1,0:T(8,128)(2,1)S(1)}, u32[]{:S(2)}, u32[]{:S(2)}) collective-permute-start(bf16[1024,128]{1,0:T(8,128)(2,1)} %get-tuple-element.30), channel_id=1, source_target_pairs={{0,64},{32,96},{64,0},{96,32},{1,65},{33,97},{65,1},{97,33},{2,66}... | collective-permute-start | bytes 786440 | tf_op jit(solution)/shard_map/ppermute | solution.py:218
  193.3 15.5 %collective-permute-start.21 = (bf16[1024,128]{1,0:T(8,128)(2,1)}, bf16[1024,128]{1,0:T(8,128)(2,1)S(1)}, u32[]{:S(2)}, u32[]{:S(2)}) collective-permute-start(bf16[1024,128]{1,0:T(8,128)(2,1)} %get-tuple-element.31), channel_id=1, source_target_pairs={{0,32},{32,64},{64,96},{96,0},{1,33},{33,65},{65,97},{97,1},{2,34}... | collective-permute-start | bytes 786440 | tf_op jit(solution)/shard_map/ppermute | solution.py:218
  199.0 9.8 %collective-permute-start.22 = (bf16[1024,128]{1,0:T(8,128)(2,1)}, bf16[1024,128]{1,0:T(8,128)(2,1)S(1)}, u32[]{:S(2)}, u32[]{:S(2)}) collective-permute-start(bf16[1024,128]{1,0:T(8,128)(2,1)} %get-tuple-element.32), channel_id=1, source_target_pairs={{0,96},{32,0},{64,32},{96,64},{1,97},{33,1},{65,33},{97,65},{2,98}... | collective-permute-start | bytes 786440 | tf_op jit(solution)/shard_map/ppermute | solution.py:218
  200.6 9.1 %collective-permute-start.26 = (bf16[1024,128]{1,0:T(8,128)(2,1)S(1)}, bf16[1024,128]{1,0:T(8,128)(2,1)S(1)}, u32[]{:S(2)}, u32[]{:S(2)}) collective-permute-start(bf16[1024,128]{1,0:T(8,128)(2,1)S(1)} %pair_sum.1), channel_id=1, source_target_pairs={{0,16},{16,0},{1,17},{17,1},{2,18},{18,2},{3,19},{19,3},{4,20},{20... | collective-permute-start | bytes 786440 | tf_op jit(solution)/shard_map/ppermute | solution.py:222
  210.8 1.4 collective-permute-start.27
  (13 other events, 180.2 us)

commit v8 on v7

--- a/solution.py
+++ b/solution.py
@@ -5,7 +5,6 @@
 from jax import lax
 from jax.experimental import pallas as pl
 from jax.experimental.pallas import tpu as pltpu
-from jax.experimental.layout import Layout, with_layout_constraint
 from jax.sharding import Mesh, PartitionSpec as P
 
 
@@ -272,16 +271,18 @@
         out_specs=vm,
         cost_estimate=pl.CostEstimate(flops=1 << 19, bytes_accessed=5 << 18, transcendentals=0),
         compiler_params=pltpu.CompilerParams(vmem_limit_bytes=6 << 20),
-        name="pair_sum",
     )(*parts)
 
 
 def scatter_steps(pieces, ring, pair):
+    cross = flip(pieces[5], pair)
     far, near = [pieces[1]], [pieces[0]]
     for small, got in ((1, far), (0, near)):
-        for big in (2, 1, 3):
+        for big in (1, 3):
             p = 2 * big + small
             got.append(ring_shift(pieces[p], ring, big))
+    cross = pair_sum([pieces[4], cross])
+    near.append(ring_shift(cross, ring, 2))
     far = pair_sum(far)
     return near + [flip(far, pair)]
 
@@ -316,7 +317,7 @@
     first = core == 0
     mine = jnp.where(first, left, right)
     yours = jnp.where(first, right, left)
-    got = lax.ppermute(yours, "core", [(0, 1), (1, 0)])
+    got = flip(yours, "core")
     return jnp.concatenate([mine, got], axis=0)
 
 
@@ -386,14 +387,14 @@
     z, yh = lax.axis_index("z"), lax.axis_index("yh")
     yl, x = lax.axis_index("yl"), lax.axis_index("x")
     swap = [(0, 1), (1, 0)]
-    blk_own = blocks[0, 0].transpose(1, 2, 0)
     shard = halves(features, core)
+    blk_own = blocks[0, 0]
     slots, _ = lax.optimization_barrier(((block_rows, block_cols, block_count), shard))
     meta = jnp.concatenate(
         [slots[0][0, 0], slots[1][0, 0], jnp.broadcast_to(slots[2][0, 0], (128,))]
     )
     meta_other = lax.ppermute(meta, "core", swap)
-    blk_other = lax.ppermute(blk_own, "core", swap)
+    blk_other = flip(blk_own, "core")
 
     both = jnp.stack([meta, meta_other])
     rows, cols, count = both[:, :SLOTS], both[:, SLOTS : 2 * SLOTS], both[:, 2 * SLOTS]
@@ -414,9 +415,6 @@
     p = jnp.arange(16, dtype=jnp.int32)
     place = (((z + (p >> 2)) & 3) * 4 + (yh ^ ((p >> 1) & 1)) * 2 + (core ^ (p & 1))) * 512
     pieces = gather_steps(shard, "z", "yh")
-    blk_own, _ = lax.optimization_barrier((blk_own, shard))
-    blk_own = with_layout_constraint(blk_own, Layout((0, 1, 2))).transpose(2, 0, 1)
-    blk_other = blk_other.transpose(2, 0, 1)
     cells = cell_products(False, fwd_off, count, place, blk_own, blk_other, pieces)
     cells = lax.all_to_all(cells, ("core", "yl", "x"), 0, 0, tiled=True)
     sums = jnp.sum(cells.reshape(2, 8, 512, 128).astype(F32), axis=1).astype(BF)

time: 222 us -> 217 us (0.977)
  waiting for transfers between devices: 60.7 us -> 55.7 us
    ppermute x18 -> x17, waiting for transfers between devices: 33.7 us -> 22.3 us  [ring_shift(): return lax.ppermute(value, axis, [(i, (i + k) % 4) for i in range(4)])]
    ppermute x5 -> x9, waiting for transfers between devices: 1.77 us -> 12.6 us  [flip(): return lax.ppermute(value, axis, [(0, 1), (1, 0)])]
    unnamed x28 -> x31, local copies, waits for them, and re-layouts: 2.91 us -> 8.95 us
    another operation x1 -> x0, local copies, waits for them, and re-layouts: 5.09 us -> none  [shards(): with_layout_constraint(blk_own, Layout((0, 1, 2))).transpose(2, 0, 1)]
    ppermute x3 -> x0, waiting for transfers between devices: 4.31 us -> none  [the longest x2 4.31 us: halves(): got = lax.ppermute(yours, 'core', [(0, 1), (1, 0)])]
    ppermute x5 -> x9, starting transfers between devices: 8.39 us -> 7.96 us  [flip(): return lax.ppermute(value, axis, [(0, 1), (1, 0)])]
    ppermute x18 -> x17, starting transfers between devices: 27.3 us -> 27 us  [ring_shift(): return lax.ppermute(value, axis, [(i, (i + k) % 4) for i in range(4)])]
  transfers between devices with their start and end apart: 31 -> 31, of which waited for: 14 -> 14; matrix products, arithmetic and copies ran while one was open for 8% -> 9% of each run, Pallas kernels for 5% -> 5%
where the time goes in v8:
time: 217 us; the launch traced here: 215 us
  blocking collectives  65.9 us (30%)
  waiting for transfers between devices  55.7 us (26%)
  starting transfers between devices  41.3 us (19%)
  Pallas kernels  22.5 us (10%)
  local copies, waits for them, and re-layouts  14.4 us (7%)
  matrix products  9.21 us (4%)
  other arithmetic  4.04 us (2%)
    all_to_all x1, blocking collectives, sum_grads(): lax.all_to_all(chip_sum(own, got), ('z', 'yh', 'yl', 'x'), 0, 0, tiled=True)  34.4 us
    all_to_all x1, blocking collectives, shards(): cells = lax.all_to_all(cells, ('core', 'yl', 'x'), 0, 0, tiled=True)  31.4 us
    ppermute x17, starting transfers between devices, ring_shift(): return lax.ppermute(value, axis, [(i, (i + k) % 4) for i in range(4)])  27 us
    ppermute x17, waiting for transfers between devices, ring_shift(): return lax.ppermute(value, axis, [(i, (i + k) % 4) for i in range(4)])  22.3 us
    all_to_all x1, waiting for transfers between devices, sum_grads(): mine = lax.all_to_all(chunk, ('z', 'yh', 'yl', 'x'), 0, 0, tiled=True)  18.5 us
    ppermute x9, waiting for transfers between devices, flip(): return lax.ppermute(value, axis, [(0, 1), (1, 0)])  12.6 us
    pallas_call x2, Pallas kernels, cell_products(): pl.pallas_call(functools.partial(cells_kernel, transposed, spots), out_sh...  10.1 us
    unnamed x31, local copies, waits for them, and re-layouts  8.95 us
  transfers between devices with their start and end apart: 31, of which 14 were waited for; matrix products, arithmetic and copies ran while one was open for 9% of the time, Pallas kernels for 5%

profile of v8, /device:TPU:0, one launch (start us, length us, event | category | flops | bytes accessed | tf_op | source)
XLA Modules:
  0.0 214.9 jit_solution(3249628052349836177)
XLA Ops:
  2.3 3.0 %collective-permute-done = bf16[512,128]{1,0:T(8,128)(2,1)S(1)} collective-permute-done((bf16[512,128]{1,0:T(8,128)(2,1)S(1)}, bf16[512,128]{1,0:T(8,128)(2,1)S(1)}, u32[]{:S(2)}, u32[]{:S(2)}) %collective-permute-start) | collective-permute-done | bytes 131104 | tf_op jit(solution)/shard_map/ppermute | solution.py:221
  5.3 4.2 %collective-permute-start.6 = (bf16[1024,128]{1,0:T(8,128)(2,1)S(1)}, bf16[1024,128]{1,0:T(8,128)(2,1)S(1)}, u32[]{:S(2)}, u32[]{:S(2)}) collective-permute-start(bf16[1024,128]{1,0:T(8,128)(2,1)S(1)} %pad_maximum_fusion.1.rest_0_), channel_id=1, source_target_pairs={{0,96},{32,0},{64,32},{96,64},{1,97},{33,1},{65,33},{97,65},{2,98}... | collective-permute-start | bytes 786440 | tf_op jit(solution)/shard_map/ppermute | solution.py:217
  10.2 3.3 %collective-permute-start.3 = (bf16[1024,128]{1,0:T(8,128)(2,1)S(1)}, bf16[1024,128]{1,0:T(8,128)(2,1)S(1)}, u32[]{:S(2)}, u32[]{:S(2)}) collective-permute-start(bf16[1024,128]{1,0:T(8,128)(2,1)S(1)} %pad_maximum_fusion.1.rest_0_), channel_id=1, source_target_pairs={{0,16},{16,0},{1,17},{17,1},{2,18},{18,2},{3,19},{19,3},{4,20},{20... | collective-permute-start | bytes 786440 | tf_op jit(solution)/shard_map/ppermute | solution.py:221
  14.3 5.1 %copy.20 = bf16[1,1,192,64,64]{4,3,2,1,0:T(8,128)(2,1)} copy(bf16[1,1,192,64,64]{2,4,3,1,0:T(8,128)(2,1)} %param.10) | data formatting | bytes 3145728 | tf_op args[1]
  19.6 3.3 %collective-permute-start.7 = (bf16[512,128]{1,0:T(8,128)(2,1)S(1)}, bf16[512,128]{1,0:T(8,128)(2,1)S(1)}, u32[]{:S(2)}, u32[]{:S(2)}) collective-permute-start(bf16[512,128]{1,0:T(8,128)(2,1)S(1)} %slice.56), channel_id=1, source_target_pairs={{0,96},{32,0},{64,32},{96,64},{1,97},{33,1},{65,33},{97,65},{2,98}... | collective-permute-start | bytes 393224 | tf_op jit(solution)/shard_map/ppermute | solution.py:217
  23.6 3.2 %collective-permute-start.11 = (bf16[1024,128]{1,0:T(8,128)(2,1)S(1)}, bf16[1024,128]{1,0:T(8,128)(2,1)S(1)}, u32[]{:S(2)}, u32[]{:S(2)}) collective-permute-start(bf16[1024,128]{1,0:T(8,128)(2,1)S(1)} %collective-permute-done.3.rest_1_), channel_id=1, source_target_pairs={{0,96},{32,0},{64,32},{96,64},{1,97},{33,1},{65,33},{97,65},{2,98}... | collective-permute-start | bytes 786440 | tf_op jit(solution)/shard_map/ppermute | solution.py:217
  27.2 2.7 %collective-permute-done.8.rest_5_ = bf16[512,128]{1,0:T(8,128)(2,1)} collective-permute-done((bf16[512,128]{1,0:T(8,128)(2,1)S(1)}, bf16[512,128]{1,0:T(8,128)(2,1)}, u32[]{:S(2)}, u32[]{:S(2)}) %collective-permute-start.8) | collective-permute-done | bytes 131104 | tf_op jit(solution)/shard_map/ppermute | solution.py:217
  30.5 5.2 %copy.22.blk1 = bf16[192,64,64]{2,1,0:T(8,128)(2,1)} copy(bf16[192,64,64]{0,2,1:T(8,128)(2,1)} %collective-permute-done.2) | data formatting | bytes 3145728 | tf_op jit(solution)/shard_map/ppermute | solution.py:221
  36.7 4.4 %cells_forward.1 = bf16[16,512,128]{2,1,0:T(8,128)(2,1)S(1)} custom-call(s32[768]{0:T(1024)S(1)} %reshape.46.off_ref, s32[2]{0:T(128)S(1)} %fusion.8.cnt_ref, s32[16]{0:T(128)S(1)} %add_multiply_fusion.1.place_ref, bf16[192,64,64]{2,1,0:T(8,128)(2,1)} %bitcast.27, bf16[192,64,64]{2,1,0:T(8,128)(2,1)} %copy.22.blk1, ...), custom_call_target="tpu_custom_call" | custom-call | flops 402653184 | bytes 10485760 | tf_op jit(solution)/shard_map/cells_forward/pallas_call | solution.py:106
  41.1 31.4 %all_to_all.15 = bf16[16,512,128]{2,1,0:T(8,128)(2,1)S(1)} all-to-all(bf16[16,512,128]{2,1,0:T(8,128)(2,1)S(1)} %cells_forward.1), channel_id=1, replica_groups=mesh['z'=4,'yh'=2,'core'=2,'yl'=2,'x'=4] {'core','yl','x'}, dimensions={0} | all-to-all | bytes 4194304 | tf_op jit(solution)/shard_map/all_to_all | solution.py:419
  77.3 1.6 multiply_convert_fusion.gp_one
  81.7 2.3 %collective-permute-done.28.got = bf16[1792,512]{1,0:T(8,128)(2,1)S(1)} collective-permute-done((bf16[1792,512]{1,0:T(8,128)(2,1)S(1)}, bf16[1792,512]{1,0:T(8,128)(2,1)S(1)}, u32[]{:S(2)}, u32[]{:S(2)}) %collective-permute-start.28) | collective-permute-done | bytes 1835040 | tf_op jit(solution)/shard_map/ppermute | solution.py:375
  85.3 34.4 %all_to_all.16.parts = bf16[64,112,128]{2,1,0:T(8,128)(2,1)S(1)} all-to-all(bf16[64,112,128]{2,1,0:T(8,128)(2,1)} %chip_sum.1), channel_id=1, replica_groups=mesh['z'=4,'yh'=2,'core'=2,'yl'=2,'x'=4] {'z','yh','yl','x'}, dimensions={0} | all-to-all | bytes 3670016 | tf_op jit(solution)/shard_map/all_to_all | solution.py:377
  119.8 1.6 chunk_sum.1
  121.3 5.8 %all-to-all-start.2 = ((bf16[64,112,128]{2,1,0:T(8,128)(2,1)}), bf16[64,112,128]{2,1,0:T(8,128)(2,1)}, u32[]{:S(2)}, u32[]{:S(2)}) async-start(bf16[64,112,128]{2,1,0:T(8,128)(2,1)} %chunk_sum.1), calls=%async_computation.2 | async-start | bytes 3670016 | tf_op jit(solution)/shard_map/all_to_all | solution.py:379
  127.2 3.1 %fusion.11 = (bf16[512,512]{1,0:T(8,128)(2,1)S(1)}, f32[512,512]{1,0:T(8,128)}) fusion(bf16[512,1024]{1,0:T(8,128)(2,1)S(1)} %multiply_convert_fusion.gp_one, bf16[512,1024]{1,0:T(8,128)(2,1)} %param.14), kind=kOutput, calls=%fused_computation.47 | convolution fusion | flops 537133056 | bytes 3670016 | tf_op jit(solution)/shard_map/dot_general | solution.py:437
  131.7 1.6 collective-permute-start.13
  133.3 2.7 %collective-permute-start.18 = (bf16[1024,128]{1,0:T(8,128)(2,1)S(1)}, bf16[1024,128]{1,0:T(8,128)(2,1)S(1)}, u32[]{:S(2)}, u32[]{:S(2)}) collective-permute-start(bf16[1024,128]{1,0:T(8,128)(2,1)S(1)} %pad_maximum_fusion.2.rest_0_), channel_id=1, source_target_pairs={{0,3},{1,0},{2,1},{3,2},{4,7},{5,4},{6,5},{7,6},{8,11},{9,8},{10,9... | collective-permute-start | bytes 786440 | tf_op jit(solution)/shard_map/ppermute | solution.py:217
  136.8 18.5 %all-to-all-done.2.blocks_ref = bf16[64,112,128]{2,1,0:T(8,128)(2,1)} async-done(((bf16[64,112,128]{2,1,0:T(8,128)(2,1)}), bf16[64,112,128]{2,1,0:T(8,128)(2,1)}, u32[]{:S(2)}, u32[]{:S(2)}) %all-to-all-start.2) | async-done | bytes 1835040 | tf_op jit(solution)/shard_map/all_to_all | solution.py:379
  155.9 2.7 %collective-permute-start.19 = (bf16[1024,128]{1,0:T(8,128)(2,1)S(1)}, bf16[1024,128]{1,0:T(8,128)(2,1)}, u32[]{:S(2)}, u32[]{:S(2)}) collective-permute-start(bf16[1024,128]{1,0:T(8,128)(2,1)S(1)} %collective-permute-done.13.rest_1_), channel_id=1, source_target_pairs={{0,3},{1,0},{2,1},{3,2},{4,7},{5,4},{6,5},{7,6},{8,11},{9,8},{10,9... | collective-permute-start | bytes 786440 | tf_op jit(solution)/shard_map/ppermute | solution.py:217
  159.1 3.0 %collective-permute-start.15 = (bf16[1024,128]{1,0:T(8,128)(2,1)S(1)}, bf16[1024,128]{1,0:T(8,128)(2,1)}, u32[]{:S(2)}, u32[]{:S(2)}) collective-permute-start(bf16[1024,128]{1,0:T(8,128)(2,1)S(1)} %collective-permute-done.13.rest_1_), channel_id=1, source_target_pairs={{0,1},{1,2},{2,3},{3,0},{4,5},{5,6},{6,7},{7,4},{8,9},{9,10},{10,1... | collective-permute-start | bytes 786440 | tf_op jit(solution)/shard_map/ppermute | solution.py:217
  162.2 9.2 %collective-permute-done.14.rest_2_ = bf16[1024,128]{1,0:T(8,128)(2,1)} collective-permute-done((bf16[1024,128]{1,0:T(8,128)(2,1)S(1)}, bf16[1024,128]{1,0:T(8,128)(2,1)}, u32[]{:S(2)}, u32[]{:S(2)}) %collective-permute-start.14) | collective-permute-done | bytes 262176 | tf_op jit(solution)/shard_map/ppermute | solution.py:217
  171.5 5.2 %collective-permute-done.15.rest_3_ = bf16[1024,128]{1,0:T(8,128)(2,1)} collective-permute-done((bf16[1024,128]{1,0:T(8,128)(2,1)S(1)}, bf16[1024,128]{1,0:T(8,128)(2,1)}, u32[]{:S(2)}, u32[]{:S(2)}) %collective-permute-start.15) | collective-permute-done | bytes 262176 | tf_op jit(solution)/shard_map/ppermute | solution.py:217
  176.6 5.6 %cells_back.1 = (bf16[1024,128]{1,0:T(8,128)(2,1)}, bf16[1024,128]{1,0:T(8,128)(2,1)}, bf16[1024,128]{1,0:T(8,128)(2,1)}, bf16[1024,128]{1,0:T(8,128)(2,1)}, bf1...) custom-call(s32[768]{0:T(1024)S(1)} %reshape.48.off_ref, ...), custom_call_target="tpu_custom_call" | custom-call | flops 402653184 | bytes 10485760 | tf_op jit(solution)/shard_map/cells_back/pallas_call | solution.py:106
  183.8 1.9 collective-permute-start.25
  185.9 6.1 %collective-permute-done.22.refs_1_ = bf16[1024,128]{1,0:T(8,128)(2,1)S(1)} collective-permute-done((bf16[1024,128]{1,0:T(8,128)(2,1)}, bf16[1024,128]{1,0:T(8,128)(2,1)S(1)}, u32[]{:S(2)}, u32[]{:S(2)}) %collective-permute-start.22) | collective-permute-done | bytes 262176 | tf_op jit(solution)/shard_map/ppermute | solution.py:221
  193.5 1.8 collective-permute-start.23
  196.4 1.6 collective-permute-start.26
  198.7 2.7 %collective-permute-done.21.refs_2_ = bf16[1024,128]{1,0:T(8,128)(2,1)S(1)} collective-permute-done((bf16[1024,128]{1,0:T(8,128)(2,1)}, bf16[1024,128]{1,0:T(8,128)(2,1)S(1)}, u32[]{:S(2)}, u32[]{:S(2)}) %collective-permute-start.21) | collective-permute-done | bytes 262176 | tf_op jit(solution)/shard_map/ppermute | solution.py:217
  201.3 1.7 collective-permute-done.23.refs_3_
  207.7 3.5 %finish_grads.2 = (f32[512,1024]{1,0:T(8,128)}, f32[1024,1024]{1,0:T(8,128)}, f32[1024,256]{1,0:T(8,128)}) custom-call(s32[1]{0:T(128)} %bitcast.5.half_ref, bf16[64,112,128]{2,1,0:T(8,128)(2,1)} %all-to-all-done.2.blocks_ref), custom_call_target="tpu_custom_call" | custom-call | flops 4194304 | bytes 6291456 | tf_op jit(solution)/shard_map/finish_grads/pallas_call | solution.py:351
  211.2 3.5 %finish_grads.3 = (f32[512,1024]{1,0:T(8,128)}, f32[1024,1024]{1,0:T(8,128)}, f32[1024,256]{1,0:T(8,128)}) custom-call(s32[1]{0:T(128)} %bitcast.6.half_ref, bf16[64,112,128]{2,1,0:T(8,128)(2,1)} %collective-permute-done.29.blocks_ref, f32[512,1024]{1,0:T(8,128)} %get-tuple-element.37.rest_0_, ...), custom_call_target="tpu_custom_call", output_to_operand_aliasing={{0}: (2, {}), {1}: (3, {}), {2}: (4, {})} | custom-call | flops 4194304 | bytes 6291456 | tf_op jit(solution)/shard_map/finish_grads/pallas_call | solution.py:351
  (104 shorter events, 27.3 us)
Async XLA Ops:
  0.6 74.2 %copy-start = (bf16[1024,1024]{1,0:T(8,128)(2,1)S(1)}, bf16[1024,1024]{1,0:T(8,128)(2,1)}, u32[]{:S(2)}) copy-start(bf16[1024,1024]{1,0:T(8,128)(2,1)} %param.15) | copy-start | bytes 6291460
  0.6 29.9 %collective-permute-start.2 = (bf16[192,64,64]{0,2,1:T(8,128)(2,1)}, bf16[192,64,64]{0,2,1:T(8,128)(2,1)}, u32[]{:S(2)}, u32[]{:S(2)}) collective-permute-start(bf16[192,64,64]{0,2,1:T(8,128)(2,1)} %bitcast.29), channel_id=1, source_target_pairs={{0,8},{8,0},{1,9},{9,1},{2,10},{10,2},{3,11},{11,3},{4,12},{12,4},... | collective-permute-start | bytes 4718600 | tf_op jit(solution)/shard_map/ppermute | solution.py:221
  1.9 3.4 %collective-permute-start = (bf16[512,128]{1,0:T(8,128)(2,1)S(1)}, bf16[512,128]{1,0:T(8,128)(2,1)S(1)}, u32[]{:S(2)}, u32[]{:S(2)}) collective-permute-start(bf16[512,128]{1,0:T(8,128)(2,1)S(1)} %get-tuple-element.52), channel_id=1, source_target_pairs={{0,8},{8,0},{1,9},{9,1},{2,10},{10,2},{3,11},{11,3},{4,12},{12,4},... | collective-permute-start | bytes 393224 | tf_op jit(solution)/shard_map/ppermute | solution.py:221
  5.3 14.2 %collective-permute-start.6 = (bf16[1024,128]{1,0:T(8,128)(2,1)S(1)}, bf16[1024,128]{1,0:T(8,128)(2,1)S(1)}, u32[]{:S(2)}, u32[]{:S(2)}) collective-permute-start(bf16[1024,128]{1,0:T(8,128)(2,1)S(1)} %pad_maximum_fusion.1.rest_0_), channel_id=1, source_target_pairs={{0,96},{32,0},{64,32},{96,64},{1,97},{33,1},{65,33},{97,65},{2,98}... | collective-permute-start | bytes 786440 | tf_op jit(solution)/shard_map/ppermute | solution.py:217
  9.5 13.3 %collective-permute-start.4 = (bf16[1024,128]{1,0:T(8,128)(2,1)S(1)}, bf16[1024,128]{1,0:T(8,128)(2,1)S(1)}, u32[]{:S(2)}, u32[]{:S(2)}) collective-permute-start(bf16[1024,128]{1,0:T(8,128)(2,1)S(1)} %pad_maximum_fusion.1.rest_0_), channel_id=1, source_target_pairs={{0,32},{32,64},{64,96},{96,0},{1,33},{33,65},{65,97},{97,1},{2,34}... | collective-permute-start | bytes 786440 | tf_op jit(solution)/shard_map/ppermute | solution.py:217
  10.2 13.4 %collective-permute-start.3 = (bf16[1024,128]{1,0:T(8,128)(2,1)S(1)}, bf16[1024,128]{1,0:T(8,128)(2,1)S(1)}, u32[]{:S(2)}, u32[]{:S(2)}) collective-permute-start(bf16[1024,128]{1,0:T(8,128)(2,1)S(1)} %pad_maximum_fusion.1.rest_0_), channel_id=1, source_target_pairs={{0,16},{16,0},{1,17},{17,1},{2,18},{18,2},{3,19},{19,3},{4,20},{20... | collective-permute-start | bytes 786440 | tf_op jit(solution)/shard_map/ppermute | solution.py:221
  14.2 5.2 %collective-permute-start.1 = (s32[512]{0:T(512)S(1)}, s32[512]{0:T(512)S(1)}, u32[]{:S(2)}, u32[]{:S(2)}) collective-permute-start(s32[512]{0:T(512)S(1)} %pad_add_fusion.3), channel_id=1, source_target_pairs={{0,8},{8,0},{1,9},{9,1},{2,10},{10,2},{3,11},{11,3},{4,12},{12,4},... | collective-permute-start | bytes 6152 | tf_op jit(solution)/shard_map/ppermute | solution.py:396
  19.6 7.3 %collective-permute-start.7 = (bf16[512,128]{1,0:T(8,128)(2,1)S(1)}, bf16[512,128]{1,0:T(8,128)(2,1)S(1)}, u32[]{:S(2)}, u32[]{:S(2)}) collective-permute-start(bf16[512,128]{1,0:T(8,128)(2,1)S(1)} %slice.56), channel_id=1, source_target_pairs={{0,96},{32,0},{64,32},{96,64},{1,97},{33,1},{65,33},{97,65},{2,98}... | collective-permute-start | bytes 393224 | tf_op jit(solution)/shard_map/ppermute | solution.py:217
  22.9 7.0 %collective-permute-start.8 = (bf16[512,128]{1,0:T(8,128)(2,1)S(1)}, bf16[512,128]{1,0:T(8,128)(2,1)}, u32[]{:S(2)}, u32[]{:S(2)}) collective-permute-start(bf16[512,128]{1,0:T(8,128)(2,1)S(1)} %slice.57), channel_id=1, source_target_pairs={{0,32},{32,64},{64,96},{96,0},{1,33},{33,65},{65,97},{97,1},{2,34}... | collective-permute-start | bytes 393224 | tf_op jit(solution)/shard_map/ppermute | solution.py:217
  23.6 13.0 %collective-permute-start.11 = (bf16[1024,128]{1,0:T(8,128)(2,1)S(1)}, bf16[1024,128]{1,0:T(8,128)(2,1)S(1)}, u32[]{:S(2)}, u32[]{:S(2)}) collective-permute-start(bf16[1024,128]{1,0:T(8,128)(2,1)S(1)} %collective-permute-done.3.rest_1_), channel_id=1, source_target_pairs={{0,96},{32,0},{64,32},{96,64},{1,97},{33,1},{65,33},{97,65},{2,98}... | collective-permute-start | bytes 786440 | tf_op jit(solution)/shard_map/ppermute | solution.py:217
  26.9 9.8 %collective-permute-start.5 = (bf16[1024,128]{1,0:T(8,128)(2,1)S(1)}, bf16[1024,128]{1,0:T(8,128)(2,1)}, u32[]{:S(2)}, u32[]{:S(2)}) collective-permute-start(bf16[1024,128]{1,0:T(8,128)(2,1)S(1)} %collective-permute-done.3.rest_1_), channel_id=1, source_target_pairs={{0,32},{32,64},{64,96},{96,0},{1,33},{33,65},{65,97},{97,1},{2,34}... | collective-permute-start | bytes 786440 | tf_op jit(solution)/shard_map/ppermute | solution.py:217
  26.9 8.8 %collective-permute-start.9 = (bf16[512,128]{1,0:T(8,128)(2,1)S(1)}, bf16[512,128]{1,0:T(8,128)(2,1)}, u32[]{:S(2)}, u32[]{:S(2)}) collective-permute-start(bf16[512,128]{1,0:T(8,128)(2,1)S(1)} %collective-permute-done.7.rest_4_), channel_id=1, source_target_pairs={{0,16},{16,0},{1,17},{17,1},{2,18},{18,2},{3,19},{19,3},{4,20},{20... | collective-permute-start | bytes 393224 | tf_op jit(solution)/shard_map/ppermute | solution.py:221
  29.9 6.8 %collective-permute-start.10 = (bf16[512,128]{1,0:T(8,128)(2,1)}, bf16[512,128]{1,0:T(8,128)(2,1)}, u32[]{:S(2)}, u32[]{:S(2)}) collective-permute-start(bf16[512,128]{1,0:T(8,128)(2,1)} %collective-permute-done.8.rest_5_), channel_id=1, source_target_pairs={{0,16},{16,0},{1,17},{17,1},{2,18},{18,2},{3,19},{19,3},{4,20},{20... | collective-permute-start | bytes 393224 | tf_op jit(solution)/shard_map/ppermute | solution.py:221
  80.1 3.9 %collective-permute-start.28 = (bf16[1792,512]{1,0:T(8,128)(2,1)S(1)}, bf16[1792,512]{1,0:T(8,128)(2,1)S(1)}, u32[]{:S(2)}, u32[]{:S(2)}) collective-permute-start(bf16[1792,512]{1,0:T(8,128)(2,1)S(1)} %shard_map.131), channel_id=1, source_target_pairs={{0,8},{8,0},{1,9},{9,1},{2,10},{10,2},{3,11},{11,3},{4,12},{12,4},... | collective-permute-start | bytes 5505032 | tf_op jit(solution)/shard_map/ppermute | solution.py:375
  121.3 34.0 %all-to-all-start.2 = ((bf16[64,112,128]{2,1,0:T(8,128)(2,1)}), bf16[64,112,128]{2,1,0:T(8,128)(2,1)}, u32[]{:S(2)}, u32[]{:S(2)}) async-start(bf16[64,112,128]{2,1,0:T(8,128)(2,1)} %chunk_sum.1), calls=%async_computation.2 | async-start | bytes 3670016 | tf_op jit(solution)/shard_map/all_to_all | solution.py:379
  130.3 1.4 collective-permute-start.12
  131.7 24.2 %collective-permute-start.13 = (bf16[1024,128]{1,0:T(8,128)(2,1)S(1)}, bf16[1024,128]{1,0:T(8,128)(2,1)S(1)}, u32[]{:S(2)}, u32[]{:S(2)}) collective-permute-start(bf16[1024,128]{1,0:T(8,128)(2,1)S(1)} %pad_maximum_fusion.2.rest_0_), channel_id=1, source_target_pairs={{0,4},{4,0},{1,5},{5,1},{2,6},{6,2},{3,7},{7,3},{8,12},{12,8},{9,1... | collective-permute-start | bytes 786440 | tf_op jit(solution)/shard_map/ppermute | solution.py:221
  133.3 25.3 %collective-permute-start.18 = (bf16[1024,128]{1,0:T(8,128)(2,1)S(1)}, bf16[1024,128]{1,0:T(8,128)(2,1)S(1)}, u32[]{:S(2)}, u32[]{:S(2)}) collective-permute-start(bf16[1024,128]{1,0:T(8,128)(2,1)S(1)} %pad_maximum_fusion.2.rest_0_), channel_id=1, source_target_pairs={{0,3},{1,0},{2,1},{3,2},{4,7},{5,4},{6,5},{7,6},{8,11},{9,8},{10,9... | collective-permute-start | bytes 786440 | tf_op jit(solution)/shard_map/ppermute | solution.py:217
  136.0 23.1 %collective-permute-start.16 = (bf16[1024,128]{1,0:T(8,128)(2,1)S(1)}, bf16[1024,128]{1,0:T(8,128)(2,1)S(1)}, u32[]{:S(2)}, u32[]{:S(2)}) collective-permute-start(bf16[1024,128]{1,0:T(8,128)(2,1)S(1)} %pad_maximum_fusion.2.rest_0_), channel_id=1, source_target_pairs={{0,2},{1,3},{2,0},{3,1},{4,6},{5,7},{6,4},{7,5},{8,10},{9,11},{10,... | collective-permute-start | bytes 786440 | tf_op jit(solution)/shard_map/ppermute | solution.py:217
  155.3 55.9 %collective-permute-start.29 = (bf16[64,112,128]{2,1,0:T(8,128)(2,1)}, bf16[64,112,128]{2,1,0:T(8,128)(2,1)}, u32[]{:S(2)}, u32[]{:S(2)}) collective-permute-start(bf16[64,112,128]{2,1,0:T(8,128)(2,1)} %all-to-all-done.2.blocks_ref), channel_id=1, source_target_pairs={{0,8},{8,0},{1,9},{9,1},{2,10},{10,2},{3,11},{11,3},{4,12},{12,4},... | collective-permute-start | bytes 5505032 | tf_op jit(solution)/shard_map/ppermute | solution.py:380
  155.3 16.1 %collective-permute-start.14 = (bf16[1024,128]{1,0:T(8,128)(2,1)S(1)}, bf16[1024,128]{1,0:T(8,128)(2,1)}, u32[]{:S(2)}, u32[]{:S(2)}) collective-permute-start(bf16[1024,128]{1,0:T(8,128)(2,1)S(1)} %pad_maximum_fusion.2.rest_0_), channel_id=1, source_target_pairs={{0,1},{1,2},{2,3},{3,0},{4,5},{5,6},{6,7},{7,4},{8,9},{9,10},{10,1... | collective-permute-start | bytes 786440 | tf_op jit(solution)/shard_map/ppermute | solution.py:217
  155.9 15.5 %collective-permute-start.19 = (bf16[1024,128]{1,0:T(8,128)(2,1)S(1)}, bf16[1024,128]{1,0:T(8,128)(2,1)}, u32[]{:S(2)}, u32[]{:S(2)}) collective-permute-start(bf16[1024,128]{1,0:T(8,128)(2,1)S(1)} %collective-permute-done.13.rest_1_), channel_id=1, source_target_pairs={{0,3},{1,0},{2,1},{3,2},{4,7},{5,4},{6,5},{7,6},{8,11},{9,8},{10,9... | collective-permute-start | bytes 786440 | tf_op jit(solution)/shard_map/ppermute | solution.py:217
  158.6 12.9 %collective-permute-start.17 = (bf16[1024,128]{1,0:T(8,128)(2,1)S(1)}, bf16[1024,128]{1,0:T(8,128)(2,1)}, u32[]{:S(2)}, u32[]{:S(2)}) collective-permute-start(bf16[1024,128]{1,0:T(8,128)(2,1)S(1)} %collective-permute-done.13.rest_1_), channel_id=1, source_target_pairs={{0,2},{1,3},{2,0},{3,1},{4,6},{5,7},{6,4},{7,5},{8,10},{9,11},{10,... | collective-permute-start | bytes 786440 | tf_op jit(solution)/shard_map/ppermute | solution.py:217
  159.1 17.5 %collective-permute-start.15 = (bf16[1024,128]{1,0:T(8,128)(2,1)S(1)}, bf16[1024,128]{1,0:T(8,128)(2,1)}, u32[]{:S(2)}, u32[]{:S(2)}) collective-permute-start(bf16[1024,128]{1,0:T(8,128)(2,1)S(1)} %collective-permute-done.13.rest_1_), channel_id=1, source_target_pairs={{0,1},{1,2},{2,3},{3,0},{4,5},{5,6},{6,7},{7,4},{8,9},{9,10},{10,1... | collective-permute-start | bytes 786440 | tf_op jit(solution)/shard_map/ppermute | solution.py:217
  182.3 9.7 %collective-permute-start.22 = (bf16[1024,128]{1,0:T(8,128)(2,1)}, bf16[1024,128]{1,0:T(8,128)(2,1)S(1)}, u32[]{:S(2)}, u32[]{:S(2)}) collective-permute-start(bf16[1024,128]{1,0:T(8,128)(2,1)} %get-tuple-element.31), channel_id=1, source_target_pairs={{0,16},{16,0},{1,17},{17,1},{2,18},{18,2},{3,19},{19,3},{4,20},{20... | collective-permute-start | bytes 786440 | tf_op jit(solution)/shard_map/ppermute | solution.py:221
  182.4 11.1 %collective-permute-start.24 = (bf16[1024,128]{1,0:T(8,128)(2,1)}, bf16[1024,128]{1,0:T(8,128)(2,1)S(1)}, u32[]{:S(2)}, u32[]{:S(2)}) collective-permute-start(bf16[1024,128]{1,0:T(8,128)(2,1)} %get-tuple-element.33), channel_id=1, source_target_pairs={{0,32},{32,64},{64,96},{96,0},{1,33},{33,65},{65,97},{97,1},{2,34}... | collective-permute-start | bytes 786440 | tf_op jit(solution)/shard_map/ppermute | solution.py:217
  183.8 11.5 %collective-permute-start.25 = (bf16[1024,128]{1,0:T(8,128)(2,1)}, bf16[1024,128]{1,0:T(8,128)(2,1)S(1)}, u32[]{:S(2)}, u32[]{:S(2)}) collective-permute-start(bf16[1024,128]{1,0:T(8,128)(2,1)} %get-tuple-element.34), channel_id=1, source_target_pairs={{0,96},{32,0},{64,32},{96,64},{1,97},{33,1},{65,33},{97,65},{2,98}... | collective-permute-start | bytes 786440 | tf_op jit(solution)/shard_map/ppermute | solution.py:217
  185.7 13.0 %collective-permute-start.20 = (bf16[1024,128]{1,0:T(8,128)(2,1)}, bf16[1024,128]{1,0:T(8,128)(2,1)S(1)}, u32[]{:S(2)}, u32[]{:S(2)}) collective-permute-start(bf16[1024,128]{1,0:T(8,128)(2,1)} %get-tuple-element.28), channel_id=1, source_target_pairs={{0,32},{32,64},{64,96},{96,0},{1,33},{33,65},{65,97},{97,1},{2,34}... | collective-permute-start | bytes 786440 | tf_op jit(solution)/shard_map/ppermute | solution.py:217
  191.9 9.4 %collective-permute-start.21 = (bf16[1024,128]{1,0:T(8,128)(2,1)}, bf16[1024,128]{1,0:T(8,128)(2,1)S(1)}, u32[]{:S(2)}, u32[]{:S(2)}) collective-permute-start(bf16[1024,128]{1,0:T(8,128)(2,1)} %get-tuple-element.29), channel_id=1, source_target_pairs={{0,96},{32,0},{64,32},{96,64},{1,97},{33,1},{65,33},{97,65},{2,98}... | collective-permute-start | bytes 786440 | tf_op jit(solution)/shard_map/ppermute | solution.py:217
  193.5 9.6 %collective-permute-start.23 = (bf16[1024,128]{1,0:T(8,128)(2,1)S(1)}, bf16[1024,128]{1,0:T(8,128)(2,1)S(1)}, u32[]{:S(2)}, u32[]{:S(2)}) collective-permute-start(bf16[1024,128]{1,0:T(8,128)(2,1)S(1)} %shard_map.128), channel_id=1, source_target_pairs={{0,64},{32,96},{64,0},{96,32},{1,65},{33,97},{65,1},{97,33},{2,66}... | collective-permute-start | bytes 786440 | tf_op jit(solution)/shard_map/ppermute | solution.py:217
  196.4 8.0 %collective-permute-start.26 = (bf16[1024,128]{1,0:T(8,128)(2,1)S(1)}, bf16[1024,128]{1,0:T(8,128)(2,1)S(1)}, u32[]{:S(2)}, u32[]{:S(2)}) collective-permute-start(bf16[1024,128]{1,0:T(8,128)(2,1)S(1)} %shard_map.129), channel_id=1, source_target_pairs={{0,16},{16,0},{1,17},{17,1},{2,18},{18,2},{3,19},{19,3},{4,20},{20... | collective-permute-start | bytes 786440 | tf_op jit(solution)/shard_map/ppermute | solution.py:221
  205.4 1.4 collective-permute-start.27
  (14 other events, 165.2 us)

commit v9 on v8

--- a/solution.py
+++ b/solution.py
@@ -187,26 +187,43 @@
     )(own, got)
 
 
-def chunk_kernel(parts, out_ref, held, sems):
-    total = jnp.sum(parts[...].astype(F32), axis=0).astype(BF)
+def chunk_kernel(parts, out_ref, taken, held, in_sem, out_sem):
+    reads = [
+        pltpu.make_async_copy(parts.at[8 * k : 8 * k + 8], taken.at[k], in_sem.at[k])
+        for k in range(8)
+    ]
+    for read in reads:
+        read.start()
+    total = None
+    for k, read in enumerate(reads):
+        read.wait()
+        part = jnp.sum(taken[k].astype(F32), axis=0)
+        total = part if total is None else total + part
+    total = total.astype(BF)
     for k in range(8):
         held[k] = total
-    moves = [
-        pltpu.make_async_copy(held, out_ref.at[8 * k : 8 * k + 8], sems.at[k]) for k in range(8)
+    writes = [
+        pltpu.make_async_copy(held, out_ref.at[8 * k : 8 * k + 8], out_sem.at[k])
+        for k in range(8)
     ]
-    for move in moves:
-        move.start()
-    for move in moves:
-        move.wait()
+    for write in writes:
+        write.start()
+    for write in writes:
+        write.wait()
 
 
 def chunk_sum(parts):
     return pl.pallas_call(
         chunk_kernel,
         out_shape=pltpu.HBM((64, 112, 128), BF),
-        in_specs=[pl.BlockSpec(memory_space=pltpu.VMEM)],
+        in_specs=[pl.BlockSpec(memory_space=pl.ANY)],
         out_specs=pl.BlockSpec(memory_space=pltpu.HBM),
-        scratch_shapes=[pltpu.VMEM((8, 112, 128), BF), pltpu.SemaphoreType.DMA((8,))],
+        scratch_shapes=[
+            pltpu.VMEM((8, 8, 112, 128), BF),
+            pltpu.VMEM((8, 112, 128), BF),
+            pltpu.SemaphoreType.DMA((8,)),
+            pltpu.SemaphoreType.DMA((8,)),
+        ],
         cost_estimate=pl.CostEstimate(flops=1 << 20, bytes_accessed=3 << 20, transcendentals=0),
         compiler_params=pltpu.CompilerParams(vmem_limit_bytes=12 << 20),
         name="chunk_sum",
@@ -322,7 +339,13 @@
 
 
 def finish_kernel(half_ref, blocks_ref, *rest):
-    outs, total, turned, sems = rest[-6:-3], rest[-3], rest[-2], rest[-1]
+    outs, taken, total, turned, sems, in_sem = rest[-8:-5], *rest[-5:]
+    reads = [
+        pltpu.make_async_copy(blocks_ref.at[16 * k : 16 * k + 16], taken.at[k], in_sem.at[k])
+        for k in range(4)
+    ]
+    for read in reads:
+        read.start()
     lane = pl.multiple_of(half_ref[0] * 512, 512)
     lanes = pl.ds(lane, 512)
     moves = (
@@ -331,9 +354,11 @@
         pltpu.make_async_copy(turned, outs[2].at[lanes, :], sems.at[2]),
     )
     for row in range(16):
+        if row % 4 == 0:
+            reads[row // 4].wait()
         for col in range(4):
-            total[row * 112 : (row + 1) * 112, col * 128 : (col + 1) * 128] = blocks_ref[
-                row * 4 + col
+            total[row * 112 : (row + 1) * 112, col * 128 : (col + 1) * 128] = taken[
+                row // 4, (row % 4) * 4 + col
             ].astype(F32) * (1.0 / 256.0)
         if row == 4:
             moves[0].start()
@@ -346,7 +371,6 @@
 
 
 def finish_grads(half, blocks, outs):
-    vm = pl.BlockSpec(memory_space=pltpu.VMEM)
     any_spec = pl.BlockSpec(memory_space=pl.ANY)
     return pl.pallas_call(
         finish_kernel,
@@ -355,12 +379,14 @@
             jax.ShapeDtypeStruct((1024, 1024), F32),
             jax.ShapeDtypeStruct((1024, 256), F32),
         ),
-        in_specs=[pl.BlockSpec(memory_space=pltpu.SMEM), vm] + [any_spec] * len(outs),
+        in_specs=[pl.BlockSpec(memory_space=pltpu.SMEM)] + [any_spec] * (1 + len(outs)),
         out_specs=(any_spec,) * 3,
         scratch_shapes=[
+            pltpu.VMEM((4, 16, 112, 128), BF),
             pltpu.VMEM((1792, 512), F32),
             pltpu.VMEM((512, 256), F32),
             pltpu.SemaphoreType.DMA((3,)),
+            pltpu.SemaphoreType.DMA((4,)),
         ],
         input_output_aliases={2 + k: k for k in range(len(outs))},
         compiler_params=pltpu.CompilerParams(vmem_limit_bytes=16 << 20),

time: 217 us -> 218 us (level)
    pallas_call x1, Pallas kernels: 1.55 us -> 3.98 us  [chunk_sum(): pl.pallas_call(chunk_kernel, out_shape=pltpu.HBM((64, 112, 128), BF), in_...]
  transfers between devices with their start and end apart: 31 -> 31, of which waited for: 14 -> 14; matrix products, arithmetic and copies ran while one was open for 9% -> 8% of each run, Pallas kernels for 5% -> 5%
where the time goes in v9:
time: 218 us; the launch traced here: 216 us
  blocking collectives  65.9 us (30%)
  waiting for transfers between devices  55.7 us (26%)
  starting transfers between devices  41.2 us (19%)
  Pallas kernels  24.2 us (11%)
  local copies, waits for them, and re-layouts  14.3 us (7%)
  matrix products  9.21 us (4%)
  other arithmetic  4.04 us (2%)
    all_to_all x1, blocking collectives, sum_grads(): lax.all_to_all(chip_sum(own, got), ('z', 'yh', 'yl', 'x'), 0, 0, tiled=True)  34.4 us
    all_to_all x1, blocking collectives, shards(): cells = lax.all_to_all(cells, ('core', 'yl', 'x'), 0, 0, tiled=True)  31.4 us
    ppermute x17, starting transfers between devices, ring_shift(): return lax.ppermute(value, axis, [(i, (i + k) % 4) for i in range(4)])  26.9 us
    ppermute x17, waiting for transfers between devices, ring_shift(): return lax.ppermute(value, axis, [(i, (i + k) % 4) for i in range(4)])  22.3 us
    all_to_all x1, waiting for transfers between devices, sum_grads(): mine = lax.all_to_all(chunk, ('z', 'yh', 'yl', 'x'), 0, 0, tiled=True)  18.5 us
    ppermute x9, waiting for transfers between devices, flip(): return lax.ppermute(value, axis, [(0, 1), (1, 0)])  12.6 us
    pallas_call x2, Pallas kernels, cell_products(): pl.pallas_call(functools.partial(cells_kernel, transposed, spots), out_sh...  10.1 us
    unnamed x31, local copies, waits for them, and re-layouts  8.95 us
  transfers between devices with their start and end apart: 31, of which 14 were waited for; matrix products, arithmetic and copies ran while one was open for 8% of the time, Pallas kernels for 5%

profile of v9, /device:TPU:0, one launch (start us, length us, event | category | flops | bytes accessed | tf_op | source)
XLA Modules:
  0.0 216.5 jit_solution(58577772049481326)
XLA Ops:
  2.3 3.0 %collective-permute-done = bf16[512,128]{1,0:T(8,128)(2,1)S(1)} collective-permute-done((bf16[512,128]{1,0:T(8,128)(2,1)S(1)}, bf16[512,128]{1,0:T(8,128)(2,1)S(1)}, u32[]{:S(2)}, u32[]{:S(2)}) %collective-permute-start) | collective-permute-done | bytes 131104 | tf_op jit(solution)/shard_map/ppermute | solution.py:238
  5.3 4.2 %collective-permute-start.6 = (bf16[1024,128]{1,0:T(8,128)(2,1)S(1)}, bf16[1024,128]{1,0:T(8,128)(2,1)S(1)}, u32[]{:S(2)}, u32[]{:S(2)}) collective-permute-start(bf16[1024,128]{1,0:T(8,128)(2,1)S(1)} %pad_maximum_fusion.1.rest_0_), channel_id=1, source_target_pairs={{0,96},{32,0},{64,32},{96,64},{1,97},{33,1},{65,33},{97,65},{2,98}... | collective-permute-start | bytes 786440 | tf_op jit(solution)/shard_map/ppermute | solution.py:234
  10.2 3.3 %collective-permute-start.3 = (bf16[1024,128]{1,0:T(8,128)(2,1)S(1)}, bf16[1024,128]{1,0:T(8,128)(2,1)S(1)}, u32[]{:S(2)}, u32[]{:S(2)}) collective-permute-start(bf16[1024,128]{1,0:T(8,128)(2,1)S(1)} %pad_maximum_fusion.1.rest_0_), channel_id=1, source_target_pairs={{0,16},{16,0},{1,17},{17,1},{2,18},{18,2},{3,19},{19,3},{4,20},{20... | collective-permute-start | bytes 786440 | tf_op jit(solution)/shard_map/ppermute | solution.py:238
  14.3 5.1 %copy.20 = bf16[1,1,192,64,64]{4,3,2,1,0:T(8,128)(2,1)} copy(bf16[1,1,192,64,64]{2,4,3,1,0:T(8,128)(2,1)} %param.10) | data formatting | bytes 3145728 | tf_op args[1]
  19.6 3.3 %collective-permute-start.7 = (bf16[512,128]{1,0:T(8,128)(2,1)S(1)}, bf16[512,128]{1,0:T(8,128)(2,1)S(1)}, u32[]{:S(2)}, u32[]{:S(2)}) collective-permute-start(bf16[512,128]{1,0:T(8,128)(2,1)S(1)} %slice.56), channel_id=1, source_target_pairs={{0,96},{32,0},{64,32},{96,64},{1,97},{33,1},{65,33},{97,65},{2,98}... | collective-permute-start | bytes 393224 | tf_op jit(solution)/shard_map/ppermute | solution.py:234
  23.6 3.2 %collective-permute-start.11 = (bf16[1024,128]{1,0:T(8,128)(2,1)S(1)}, bf16[1024,128]{1,0:T(8,128)(2,1)S(1)}, u32[]{:S(2)}, u32[]{:S(2)}) collective-permute-start(bf16[1024,128]{1,0:T(8,128)(2,1)S(1)} %collective-permute-done.3.rest_1_), channel_id=1, source_target_pairs={{0,96},{32,0},{64,32},{96,64},{1,97},{33,1},{65,33},{97,65},{2,98}... | collective-permute-start | bytes 786440 | tf_op jit(solution)/shard_map/ppermute | solution.py:234
  27.2 2.7 %collective-permute-done.8.rest_5_ = bf16[512,128]{1,0:T(8,128)(2,1)} collective-permute-done((bf16[512,128]{1,0:T(8,128)(2,1)S(1)}, bf16[512,128]{1,0:T(8,128)(2,1)}, u32[]{:S(2)}, u32[]{:S(2)}) %collective-permute-start.8) | collective-permute-done | bytes 131104 | tf_op jit(solution)/shard_map/ppermute | solution.py:234
  30.5 5.2 %copy.22.blk1 = bf16[192,64,64]{2,1,0:T(8,128)(2,1)} copy(bf16[192,64,64]{0,2,1:T(8,128)(2,1)} %collective-permute-done.2) | data formatting | bytes 3145728 | tf_op jit(solution)/shard_map/ppermute | solution.py:238
  36.7 4.4 %cells_forward.1 = bf16[16,512,128]{2,1,0:T(8,128)(2,1)S(1)} custom-call(s32[768]{0:T(1024)S(1)} %reshape.46.off_ref, s32[2]{0:T(128)S(1)} %fusion.8.cnt_ref, s32[16]{0:T(128)S(1)} %add_multiply_fusion.1.place_ref, bf16[192,64,64]{2,1,0:T(8,128)(2,1)} %bitcast.27, bf16[192,64,64]{2,1,0:T(8,128)(2,1)} %copy.22.blk1, ...), custom_call_target="tpu_custom_call" | custom-call | flops 402653184 | bytes 10485760 | tf_op jit(solution)/shard_map/cells_forward/pallas_call | solution.py:106
  41.1 31.4 %all_to_all.15 = bf16[16,512,128]{2,1,0:T(8,128)(2,1)S(1)} all-to-all(bf16[16,512,128]{2,1,0:T(8,128)(2,1)S(1)} %cells_forward.1), channel_id=1, replica_groups=mesh['z'=4,'yh'=2,'core'=2,'yl'=2,'x'=4] {'core','yl','x'}, dimensions={0} | all-to-all | bytes 4194304 | tf_op jit(solution)/shard_map/all_to_all | solution.py:445
  77.3 1.6 multiply_convert_fusion.gp_one
  81.7 2.3 %collective-permute-done.28.got = bf16[1792,512]{1,0:T(8,128)(2,1)S(1)} collective-permute-done((bf16[1792,512]{1,0:T(8,128)(2,1)S(1)}, bf16[1792,512]{1,0:T(8,128)(2,1)S(1)}, u32[]{:S(2)}, u32[]{:S(2)}) %collective-permute-start.28) | collective-permute-done | bytes 1835040 | tf_op jit(solution)/shard_map/ppermute | solution.py:401
  85.3 34.4 %all_to_all.16.parts = bf16[64,112,128]{2,1,0:T(8,128)(2,1)S(1)} all-to-all(bf16[64,112,128]{2,1,0:T(8,128)(2,1)} %chip_sum.1), channel_id=1, replica_groups=mesh['z'=4,'yh'=2,'core'=2,'yl'=2,'x'=4] {'z','yh','yl','x'}, dimensions={0} | all-to-all | bytes 3670016 | tf_op jit(solution)/shard_map/all_to_all | solution.py:403
  119.8 4.0 %chunk_sum.1 = bf16[64,112,128]{2,1,0:T(8,128)(2,1)} custom-call(bf16[64,112,128]{2,1,0:T(8,128)(2,1)S(1)} %all_to_all.16.parts), custom_call_target="tpu_custom_call" | custom-call | flops 1048576 | bytes 3145728 | tf_op jit(solution)/shard_map/chunk_sum/pallas_call | solution.py:216
  123.8 5.8 %all-to-all-start.2 = ((bf16[64,112,128]{2,1,0:T(8,128)(2,1)}), bf16[64,112,128]{2,1,0:T(8,128)(2,1)}, u32[]{:S(2)}, u32[]{:S(2)}) async-start(bf16[64,112,128]{2,1,0:T(8,128)(2,1)} %chunk_sum.1), calls=%async_computation.2 | async-start | bytes 3670016 | tf_op jit(solution)/shard_map/all_to_all | solution.py:405
  129.6 3.1 %fusion.11 = (bf16[512,512]{1,0:T(8,128)(2,1)S(1)}, f32[512,512]{1,0:T(8,128)}) fusion(bf16[512,1024]{1,0:T(8,128)(2,1)S(1)} %multiply_convert_fusion.gp_one, bf16[512,1024]{1,0:T(8,128)(2,1)} %param.14), kind=kOutput, calls=%fused_computation.47 | convolution fusion | flops 537133056 | bytes 3670016 | tf_op jit(solution)/shard_map/dot_general | solution.py:463
  134.2 1.6 collective-permute-start.13
  135.7 2.7 %collective-permute-start.18 = (bf16[1024,128]{1,0:T(8,128)(2,1)S(1)}, bf16[1024,128]{1,0:T(8,128)(2,1)S(1)}, u32[]{:S(2)}, u32[]{:S(2)}) collective-permute-start(bf16[1024,128]{1,0:T(8,128)(2,1)S(1)} %pad_maximum_fusion.2.rest_0_), channel_id=1, source_target_pairs={{0,3},{1,0},{2,1},{3,2},{4,7},{5,4},{6,5},{7,6},{8,11},{9,8},{10,9... | collective-permute-start | bytes 786440 | tf_op jit(solution)/shard_map/ppermute | solution.py:234
  139.3 18.5 %all-to-all-done.2.blocks_ref = bf16[64,112,128]{2,1,0:T(8,128)(2,1)} async-done(((bf16[64,112,128]{2,1,0:T(8,128)(2,1)}), bf16[64,112,128]{2,1,0:T(8,128)(2,1)}, u32[]{:S(2)}, u32[]{:S(2)}) %all-to-all-start.2) | async-done | bytes 1835040 | tf_op jit(solution)/shard_map/all_to_all | solution.py:405
  158.3 2.7 %collective-permute-start.19 = (bf16[1024,128]{1,0:T(8,128)(2,1)S(1)}, bf16[1024,128]{1,0:T(8,128)(2,1)}, u32[]{:S(2)}, u32[]{:S(2)}) collective-permute-start(bf16[1024,128]{1,0:T(8,128)(2,1)S(1)} %collective-permute-done.13.rest_1_), channel_id=1, source_target_pairs={{0,3},{1,0},{2,1},{3,2},{4,7},{5,4},{6,5},{7,6},{8,11},{9,8},{10,9... | collective-permute-start | bytes 786440 | tf_op jit(solution)/shard_map/ppermute | solution.py:234
  161.5 3.0 %collective-permute-start.15 = (bf16[1024,128]{1,0:T(8,128)(2,1)S(1)}, bf16[1024,128]{1,0:T(8,128)(2,1)}, u32[]{:S(2)}, u32[]{:S(2)}) collective-permute-start(bf16[1024,128]{1,0:T(8,128)(2,1)S(1)} %collective-permute-done.13.rest_1_), channel_id=1, source_target_pairs={{0,1},{1,2},{2,3},{3,0},{4,5},{5,6},{6,7},{7,4},{8,9},{9,10},{10,1... | collective-permute-start | bytes 786440 | tf_op jit(solution)/shard_map/ppermute | solution.py:234
  164.6 9.2 %collective-permute-done.14.rest_2_ = bf16[1024,128]{1,0:T(8,128)(2,1)} collective-permute-done((bf16[1024,128]{1,0:T(8,128)(2,1)S(1)}, bf16[1024,128]{1,0:T(8,128)(2,1)}, u32[]{:S(2)}, u32[]{:S(2)}) %collective-permute-start.14) | collective-permute-done | bytes 262176 | tf_op jit(solution)/shard_map/ppermute | solution.py:234
  173.9 5.2 %collective-permute-done.15.rest_3_ = bf16[1024,128]{1,0:T(8,128)(2,1)} collective-permute-done((bf16[1024,128]{1,0:T(8,128)(2,1)S(1)}, bf16[1024,128]{1,0:T(8,128)(2,1)}, u32[]{:S(2)}, u32[]{:S(2)}) %collective-permute-start.15) | collective-permute-done | bytes 262176 | tf_op jit(solution)/shard_map/ppermute | solution.py:234
  179.0 5.7 %cells_back.1 = (bf16[1024,128]{1,0:T(8,128)(2,1)}, bf16[1024,128]{1,0:T(8,128)(2,1)}, bf16[1024,128]{1,0:T(8,128)(2,1)}, bf16[1024,128]{1,0:T(8,128)(2,1)}, bf1...) custom-call(s32[768]{0:T(1024)S(1)} %reshape.48.off_ref, ...), custom_call_target="tpu_custom_call" | custom-call | flops 402653184 | bytes 10485760 | tf_op jit(solution)/shard_map/cells_back/pallas_call | solution.py:106
  186.2 1.9 collective-permute-start.25
  188.3 6.1 %collective-permute-done.22.refs_1_ = bf16[1024,128]{1,0:T(8,128)(2,1)S(1)} collective-permute-done((bf16[1024,128]{1,0:T(8,128)(2,1)}, bf16[1024,128]{1,0:T(8,128)(2,1)S(1)}, u32[]{:S(2)}, u32[]{:S(2)}) %collective-permute-start.22) | collective-permute-done | bytes 262176 | tf_op jit(solution)/shard_map/ppermute | solution.py:238
  196.0 1.8 collective-permute-start.23
  198.8 1.6 collective-permute-start.26
  201.1 2.7 %collective-permute-done.21.refs_2_ = bf16[1024,128]{1,0:T(8,128)(2,1)S(1)} collective-permute-done((bf16[1024,128]{1,0:T(8,128)(2,1)}, bf16[1024,128]{1,0:T(8,128)(2,1)S(1)}, u32[]{:S(2)}, u32[]{:S(2)}) %collective-permute-start.21) | collective-permute-done | bytes 262176 | tf_op jit(solution)/shard_map/ppermute | solution.py:234
  203.8 1.8 collective-permute-done.23.refs_3_
  210.1 3.1 %finish_grads.2 = (f32[512,1024]{1,0:T(8,128)}, f32[1024,1024]{1,0:T(8,128)}, f32[1024,256]{1,0:T(8,128)}) custom-call(s32[1]{0:T(128)} %bitcast.5.half_ref, bf16[64,112,128]{2,1,0:T(8,128)(2,1)} %all-to-all-done.2.blocks_ref), custom_call_target="tpu_custom_call" | custom-call | flops 4194304 | bytes 6291456 | tf_op jit(solution)/shard_map/finish_grads/pallas_call | solution.py:375
  213.2 3.1 %finish_grads.3 = (f32[512,1024]{1,0:T(8,128)}, f32[1024,1024]{1,0:T(8,128)}, f32[1024,256]{1,0:T(8,128)}) custom-call(s32[1]{0:T(128)} %bitcast.6.half_ref, bf16[64,112,128]{2,1,0:T(8,128)(2,1)} %collective-permute-done.29.blocks_ref, f32[512,1024]{1,0:T(8,128)} %get-tuple-element.37.rest_0_, ...), custom_call_target="tpu_custom_call", output_to_operand_aliasing={{0}: (2, {}), {1}: (3, {}), {2}: (4, {})} | custom-call | flops 4194304 | bytes 6291456 | tf_op jit(solution)/shard_map/finish_grads/pallas_call | solution.py:375
  (104 shorter events, 27.2 us)
Async XLA Ops:
  0.6 74.2 %copy-start = (bf16[1024,1024]{1,0:T(8,128)(2,1)S(1)}, bf16[1024,1024]{1,0:T(8,128)(2,1)}, u32[]{:S(2)}) copy-start(bf16[1024,1024]{1,0:T(8,128)(2,1)} %param.15) | copy-start | bytes 6291460
  0.6 29.9 %collective-permute-start.2 = (bf16[192,64,64]{0,2,1:T(8,128)(2,1)}, bf16[192,64,64]{0,2,1:T(8,128)(2,1)}, u32[]{:S(2)}, u32[]{:S(2)}) collective-permute-start(bf16[192,64,64]{0,2,1:T(8,128)(2,1)} %bitcast.29), channel_id=1, source_target_pairs={{0,8},{8,0},{1,9},{9,1},{2,10},{10,2},{3,11},{11,3},{4,12},{12,4},... | collective-permute-start | bytes 4718600 | tf_op jit(solution)/shard_map/ppermute | solution.py:238
  1.9 3.4 %collective-permute-start = (bf16[512,128]{1,0:T(8,128)(2,1)S(1)}, bf16[512,128]{1,0:T(8,128)(2,1)S(1)}, u32[]{:S(2)}, u32[]{:S(2)}) collective-permute-start(bf16[512,128]{1,0:T(8,128)(2,1)S(1)} %get-tuple-element.52), channel_id=1, source_target_pairs={{0,8},{8,0},{1,9},{9,1},{2,10},{10,2},{3,11},{11,3},{4,12},{12,4},... | collective-permute-start | bytes 393224 | tf_op jit(solution)/shard_map/ppermute | solution.py:238
  5.3 14.2 %collective-permute-start.6 = (bf16[1024,128]{1,0:T(8,128)(2,1)S(1)}, bf16[1024,128]{1,0:T(8,128)(2,1)S(1)}, u32[]{:S(2)}, u32[]{:S(2)}) collective-permute-start(bf16[1024,128]{1,0:T(8,128)(2,1)S(1)} %pad_maximum_fusion.1.rest_0_), channel_id=1, source_target_pairs={{0,96},{32,0},{64,32},{96,64},{1,97},{33,1},{65,33},{97,65},{2,98}... | collective-permute-start | bytes 786440 | tf_op jit(solution)/shard_map/ppermute | solution.py:234
  9.5 13.3 %collective-permute-start.4 = (bf16[1024,128]{1,0:T(8,128)(2,1)S(1)}, bf16[1024,128]{1,0:T(8,128)(2,1)S(1)}, u32[]{:S(2)}, u32[]{:S(2)}) collective-permute-start(bf16[1024,128]{1,0:T(8,128)(2,1)S(1)} %pad_maximum_fusion.1.rest_0_), channel_id=1, source_target_pairs={{0,32},{32,64},{64,96},{96,0},{1,33},{33,65},{65,97},{97,1},{2,34}... | collective-permute-start | bytes 786440 | tf_op jit(solution)/shard_map/ppermute | solution.py:234
  10.2 13.4 %collective-permute-start.3 = (bf16[1024,128]{1,0:T(8,128)(2,1)S(1)}, bf16[1024,128]{1,0:T(8,128)(2,1)S(1)}, u32[]{:S(2)}, u32[]{:S(2)}) collective-permute-start(bf16[1024,128]{1,0:T(8,128)(2,1)S(1)} %pad_maximum_fusion.1.rest_0_), channel_id=1, source_target_pairs={{0,16},{16,0},{1,17},{17,1},{2,18},{18,2},{3,19},{19,3},{4,20},{20... | collective-permute-start | bytes 786440 | tf_op jit(solution)/shard_map/ppermute | solution.py:238
  14.2 5.2 %collective-permute-start.1 = (s32[512]{0:T(512)S(1)}, s32[512]{0:T(512)S(1)}, u32[]{:S(2)}, u32[]{:S(2)}) collective-permute-start(s32[512]{0:T(512)S(1)} %pad_add_fusion.3), channel_id=1, source_target_pairs={{0,8},{8,0},{1,9},{9,1},{2,10},{10,2},{3,11},{11,3},{4,12},{12,4},... | collective-permute-start | bytes 6152 | tf_op jit(solution)/shard_map/ppermute | solution.py:422
  19.6 7.3 %collective-permute-start.7 = (bf16[512,128]{1,0:T(8,128)(2,1)S(1)}, bf16[512,128]{1,0:T(8,128)(2,1)S(1)}, u32[]{:S(2)}, u32[]{:S(2)}) collective-permute-start(bf16[512,128]{1,0:T(8,128)(2,1)S(1)} %slice.56), channel_id=1, source_target_pairs={{0,96},{32,0},{64,32},{96,64},{1,97},{33,1},{65,33},{97,65},{2,98}... | collective-permute-start | bytes 393224 | tf_op jit(solution)/shard_map/ppermute | solution.py:234
  22.9 7.0 %collective-permute-start.8 = (bf16[512,128]{1,0:T(8,128)(2,1)S(1)}, bf16[512,128]{1,0:T(8,128)(2,1)}, u32[]{:S(2)}, u32[]{:S(2)}) collective-permute-start(bf16[512,128]{1,0:T(8,128)(2,1)S(1)} %slice.57), channel_id=1, source_target_pairs={{0,32},{32,64},{64,96},{96,0},{1,33},{33,65},{65,97},{97,1},{2,34}... | collective-permute-start | bytes 393224 | tf_op jit(solution)/shard_map/ppermute | solution.py:234
  23.6 13.0 %collective-permute-start.11 = (bf16[1024,128]{1,0:T(8,128)(2,1)S(1)}, bf16[1024,128]{1,0:T(8,128)(2,1)S(1)}, u32[]{:S(2)}, u32[]{:S(2)}) collective-permute-start(bf16[1024,128]{1,0:T(8,128)(2,1)S(1)} %collective-permute-done.3.rest_1_), channel_id=1, source_target_pairs={{0,96},{32,0},{64,32},{96,64},{1,97},{33,1},{65,33},{97,65},{2,98}... | collective-permute-start | bytes 786440 | tf_op jit(solution)/shard_map/ppermute | solution.py:234
  26.9 9.8 %collective-permute-start.5 = (bf16[1024,128]{1,0:T(8,128)(2,1)S(1)}, bf16[1024,128]{1,0:T(8,128)(2,1)}, u32[]{:S(2)}, u32[]{:S(2)}) collective-permute-start(bf16[1024,128]{1,0:T(8,128)(2,1)S(1)} %collective-permute-done.3.rest_1_), channel_id=1, source_target_pairs={{0,32},{32,64},{64,96},{96,0},{1,33},{33,65},{65,97},{97,1},{2,34}... | collective-permute-start | bytes 786440 | tf_op jit(solution)/shard_map/ppermute | solution.py:234
  26.9 8.8 %collective-permute-start.9 = (bf16[512,128]{1,0:T(8,128)(2,1)S(1)}, bf16[512,128]{1,0:T(8,128)(2,1)}, u32[]{:S(2)}, u32[]{:S(2)}) collective-permute-start(bf16[512,128]{1,0:T(8,128)(2,1)S(1)} %collective-permute-done.7.rest_4_), channel_id=1, source_target_pairs={{0,16},{16,0},{1,17},{17,1},{2,18},{18,2},{3,19},{19,3},{4,20},{20... | collective-permute-start | bytes 393224 | tf_op jit(solution)/shard_map/ppermute | solution.py:238
  29.9 6.8 %collective-permute-start.10 = (bf16[512,128]{1,0:T(8,128)(2,1)}, bf16[512,128]{1,0:T(8,128)(2,1)}, u32[]{:S(2)}, u32[]{:S(2)}) collective-permute-start(bf16[512,128]{1,0:T(8,128)(2,1)} %collective-permute-done.8.rest_5_), channel_id=1, source_target_pairs={{0,16},{16,0},{1,17},{17,1},{2,18},{18,2},{3,19},{19,3},{4,20},{20... | collective-permute-start | bytes 393224 | tf_op jit(solution)/shard_map/ppermute | solution.py:238
  80.1 3.9 %collective-permute-start.28 = (bf16[1792,512]{1,0:T(8,128)(2,1)S(1)}, bf16[1792,512]{1,0:T(8,128)(2,1)S(1)}, u32[]{:S(2)}, u32[]{:S(2)}) collective-permute-start(bf16[1792,512]{1,0:T(8,128)(2,1)S(1)} %shard_map.131), channel_id=1, source_target_pairs={{0,8},{8,0},{1,9},{9,1},{2,10},{10,2},{3,11},{11,3},{4,12},{12,4},... | collective-permute-start | bytes 5505032 | tf_op jit(solution)/shard_map/ppermute | solution.py:401
  123.8 34.0 %all-to-all-start.2 = ((bf16[64,112,128]{2,1,0:T(8,128)(2,1)}), bf16[64,112,128]{2,1,0:T(8,128)(2,1)}, u32[]{:S(2)}, u32[]{:S(2)}) async-start(bf16[64,112,128]{2,1,0:T(8,128)(2,1)} %chunk_sum.1), calls=%async_computation.2 | async-start | bytes 3670016 | tf_op jit(solution)/shard_map/all_to_all | solution.py:405
  132.7 1.4 collective-permute-start.12
  134.2 24.2 %collective-permute-start.13 = (bf16[1024,128]{1,0:T(8,128)(2,1)S(1)}, bf16[1024,128]{1,0:T(8,128)(2,1)S(1)}, u32[]{:S(2)}, u32[]{:S(2)}) collective-permute-start(bf16[1024,128]{1,0:T(8,128)(2,1)S(1)} %pad_maximum_fusion.2.rest_0_), channel_id=1, source_target_pairs={{0,4},{4,0},{1,5},{5,1},{2,6},{6,2},{3,7},{7,3},{8,12},{12,8},{9,1... | collective-permute-start | bytes 786440 | tf_op jit(solution)/shard_map/ppermute | solution.py:238
  135.7 25.3 %collective-permute-start.18 = (bf16[1024,128]{1,0:T(8,128)(2,1)S(1)}, bf16[1024,128]{1,0:T(8,128)(2,1)S(1)}, u32[]{:S(2)}, u32[]{:S(2)}) collective-permute-start(bf16[1024,128]{1,0:T(8,128)(2,1)S(1)} %pad_maximum_fusion.2.rest_0_), channel_id=1, source_target_pairs={{0,3},{1,0},{2,1},{3,2},{4,7},{5,4},{6,5},{7,6},{8,11},{9,8},{10,9... | collective-permute-start | bytes 786440 | tf_op jit(solution)/shard_map/ppermute | solution.py:234
  138.4 23.1 %collective-permute-start.16 = (bf16[1024,128]{1,0:T(8,128)(2,1)S(1)}, bf16[1024,128]{1,0:T(8,128)(2,1)S(1)}, u32[]{:S(2)}, u32[]{:S(2)}) collective-permute-start(bf16[1024,128]{1,0:T(8,128)(2,1)S(1)} %pad_maximum_fusion.2.rest_0_), channel_id=1, source_target_pairs={{0,2},{1,3},{2,0},{3,1},{4,6},{5,7},{6,4},{7,5},{8,10},{9,11},{10,... | collective-permute-start | bytes 786440 | tf_op jit(solution)/shard_map/ppermute | solution.py:234
  157.8 55.5 %collective-permute-start.29 = (bf16[64,112,128]{2,1,0:T(8,128)(2,1)}, bf16[64,112,128]{2,1,0:T(8,128)(2,1)}, u32[]{:S(2)}, u32[]{:S(2)}) collective-permute-start(bf16[64,112,128]{2,1,0:T(8,128)(2,1)} %all-to-all-done.2.blocks_ref), channel_id=1, source_target_pairs={{0,8},{8,0},{1,9},{9,1},{2,10},{10,2},{3,11},{11,3},{4,12},{12,4},... | collective-permute-start | bytes 5505032 | tf_op jit(solution)/shard_map/ppermute | solution.py:406
  157.8 16.1 %collective-permute-start.14 = (bf16[1024,128]{1,0:T(8,128)(2,1)S(1)}, bf16[1024,128]{1,0:T(8,128)(2,1)}, u32[]{:S(2)}, u32[]{:S(2)}) collective-permute-start(bf16[1024,128]{1,0:T(8,128)(2,1)S(1)} %pad_maximum_fusion.2.rest_0_), channel_id=1, source_target_pairs={{0,1},{1,2},{2,3},{3,0},{4,5},{5,6},{6,7},{7,4},{8,9},{9,10},{10,1... | collective-permute-start | bytes 786440 | tf_op jit(solution)/shard_map/ppermute | solution.py:234
  158.3 15.5 %collective-permute-start.19 = (bf16[1024,128]{1,0:T(8,128)(2,1)S(1)}, bf16[1024,128]{1,0:T(8,128)(2,1)}, u32[]{:S(2)}, u32[]{:S(2)}) collective-permute-start(bf16[1024,128]{1,0:T(8,128)(2,1)S(1)} %collective-permute-done.13.rest_1_), channel_id=1, source_target_pairs={{0,3},{1,0},{2,1},{3,2},{4,7},{5,4},{6,5},{7,6},{8,11},{9,8},{10,9... | collective-permute-start | bytes 786440 | tf_op jit(solution)/shard_map/ppermute | solution.py:234
  161.0 12.9 %collective-permute-start.17 = (bf16[1024,128]{1,0:T(8,128)(2,1)S(1)}, bf16[1024,128]{1,0:T(8,128)(2,1)}, u32[]{:S(2)}, u32[]{:S(2)}) collective-permute-start(bf16[1024,128]{1,0:T(8,128)(2,1)S(1)} %collective-permute-done.13.rest_1_), channel_id=1, source_target_pairs={{0,2},{1,3},{2,0},{3,1},{4,6},{5,7},{6,4},{7,5},{8,10},{9,11},{10,... | collective-permute-start | bytes 786440 | tf_op jit(solution)/shard_map/ppermute | solution.py:234
  161.5 17.5 %collective-permute-start.15 = (bf16[1024,128]{1,0:T(8,128)(2,1)S(1)}, bf16[1024,128]{1,0:T(8,128)(2,1)}, u32[]{:S(2)}, u32[]{:S(2)}) collective-permute-start(bf16[1024,128]{1,0:T(8,128)(2,1)S(1)} %collective-permute-done.13.rest_1_), channel_id=1, source_target_pairs={{0,1},{1,2},{2,3},{3,0},{4,5},{5,6},{6,7},{7,4},{8,9},{9,10},{10,1... | collective-permute-start | bytes 786440 | tf_op jit(solution)/shard_map/ppermute | solution.py:234
  184.7 9.7 %collective-permute-start.22 = (bf16[1024,128]{1,0:T(8,128)(2,1)}, bf16[1024,128]{1,0:T(8,128)(2,1)S(1)}, u32[]{:S(2)}, u32[]{:S(2)}) collective-permute-start(bf16[1024,128]{1,0:T(8,128)(2,1)} %get-tuple-element.31), channel_id=1, source_target_pairs={{0,16},{16,0},{1,17},{17,1},{2,18},{18,2},{3,19},{19,3},{4,20},{20... | collective-permute-start | bytes 786440 | tf_op jit(solution)/shard_map/ppermute | solution.py:238
  184.8 11.1 %collective-permute-start.24 = (bf16[1024,128]{1,0:T(8,128)(2,1)}, bf16[1024,128]{1,0:T(8,128)(2,1)S(1)}, u32[]{:S(2)}, u32[]{:S(2)}) collective-permute-start(bf16[1024,128]{1,0:T(8,128)(2,1)} %get-tuple-element.33), channel_id=1, source_target_pairs={{0,32},{32,64},{64,96},{96,0},{1,33},{33,65},{65,97},{97,1},{2,34}... | collective-permute-start | bytes 786440 | tf_op jit(solution)/shard_map/ppermute | solution.py:234
  186.2 11.5 %collective-permute-start.25 = (bf16[1024,128]{1,0:T(8,128)(2,1)}, bf16[1024,128]{1,0:T(8,128)(2,1)S(1)}, u32[]{:S(2)}, u32[]{:S(2)}) collective-permute-start(bf16[1024,128]{1,0:T(8,128)(2,1)} %get-tuple-element.34), channel_id=1, source_target_pairs={{0,96},{32,0},{64,32},{96,64},{1,97},{33,1},{65,33},{97,65},{2,98}... | collective-permute-start | bytes 786440 | tf_op jit(solution)/shard_map/ppermute | solution.py:234
  188.1 13.0 %collective-permute-start.20 = (bf16[1024,128]{1,0:T(8,128)(2,1)}, bf16[1024,128]{1,0:T(8,128)(2,1)S(1)}, u32[]{:S(2)}, u32[]{:S(2)}) collective-permute-start(bf16[1024,128]{1,0:T(8,128)(2,1)} %get-tuple-element.28), channel_id=1, source_target_pairs={{0,32},{32,64},{64,96},{96,0},{1,33},{33,65},{65,97},{97,1},{2,34}... | collective-permute-start | bytes 786440 | tf_op jit(solution)/shard_map/ppermute | solution.py:234
  194.4 9.4 %collective-permute-start.21 = (bf16[1024,128]{1,0:T(8,128)(2,1)}, bf16[1024,128]{1,0:T(8,128)(2,1)S(1)}, u32[]{:S(2)}, u32[]{:S(2)}) collective-permute-start(bf16[1024,128]{1,0:T(8,128)(2,1)} %get-tuple-element.29), channel_id=1, source_target_pairs={{0,96},{32,0},{64,32},{96,64},{1,97},{33,1},{65,33},{97,65},{2,98}... | collective-permute-start | bytes 786440 | tf_op jit(solution)/shard_map/ppermute | solution.py:234
  196.0 9.6 %collective-permute-start.23 = (bf16[1024,128]{1,0:T(8,128)(2,1)S(1)}, bf16[1024,128]{1,0:T(8,128)(2,1)S(1)}, u32[]{:S(2)}, u32[]{:S(2)}) collective-permute-start(bf16[1024,128]{1,0:T(8,128)(2,1)S(1)} %shard_map.128), channel_id=1, source_target_pairs={{0,64},{32,96},{64,0},{96,32},{1,65},{33,97},{65,1},{97,33},{2,66}... | collective-permute-start | bytes 786440 | tf_op jit(solution)/shard_map/ppermute | solution.py:234
  198.8 8.0 %collective-permute-start.26 = (bf16[1024,128]{1,0:T(8,128)(2,1)S(1)}, bf16[1024,128]{1,0:T(8,128)(2,1)S(1)}, u32[]{:S(2)}, u32[]{:S(2)}) collective-permute-start(bf16[1024,128]{1,0:T(8,128)(2,1)S(1)} %shard_map.129), channel_id=1, source_target_pairs={{0,16},{16,0},{1,17},{17,1},{2,18},{18,2},{3,19},{19,3},{4,20},{20... | collective-permute-start | bytes 786440 | tf_op jit(solution)/shard_map/ppermute | solution.py:238
  207.8 1.4 collective-permute-start.27
  (14 other events, 165.1 us)

commit v10 on v9

--- a/solution.py
+++ b/solution.py
@@ -272,23 +272,39 @@
     return [(1024 * p, block) for p, block in enumerate(got)]
 
 
+def taken_sum(parts, taken, sems):
+    reads = [pltpu.make_async_copy(part, taken.at[k], sems.at[k]) for k, part in enumerate(parts)]
+    for read in reads:
+        read.start()
+    total = None
+    for k, read in enumerate(reads):
+        read.wait()
+        part = taken[k].astype(F32)
+        total = part if total is None else total + part
+    return total
+
+
 def pair_kernel(*refs):
-    total = refs[0][...].astype(F32)
-    for ref in refs[1:-1]:
-        total = total + ref[...].astype(F32)
-    refs[-1][...] = total.astype(BF)
+    refs[-3][...] = taken_sum(refs[:-3], refs[-2], refs[-1]).astype(BF)
+
+
+def sum_scratch(parts):
+    return [
+        pltpu.VMEM((len(parts), 1024, 128), BF),
+        pltpu.SemaphoreType.DMA((len(parts),)),
+    ]
 
 
 def pair_sum(parts):
-    vm = pl.BlockSpec(memory_space=pltpu.VMEM)
     return pl.pallas_call(
         pair_kernel,
         out_shape=jax.ShapeDtypeStruct((1024, 128), BF),
-        in_specs=[vm] * len(parts),
-        out_specs=vm,
+        in_specs=[pl.BlockSpec(memory_space=pl.ANY)] * len(parts),
+        out_specs=pl.BlockSpec(memory_space=pltpu.VMEM),
+        scratch_shapes=sum_scratch(parts),
         cost_estimate=pl.CostEstimate(flops=1 << 19, bytes_accessed=5 << 18, transcendentals=0),
         compiler_params=pltpu.CompilerParams(vmem_limit_bytes=6 << 20),
-    )(*parts)
+    )(in_hbm(parts[0]), *parts[1:])
 
 
 def scatter_steps(pieces, ring, pair):
@@ -305,12 +321,10 @@
 
 
 def node_kernel(*refs):
-    mine_ref, yours_ref = refs[-2:]
-    for rows, out_ref in ((slice(0, 512), mine_ref), (slice(512, 1024), yours_ref)):
-        total = refs[0][rows, :].astype(F32)
-        for ref in refs[1:-2]:
-            total = total + ref[rows, :].astype(F32)
-        out_ref[...] = total.astype(out_ref.dtype)
+    mine_ref, yours_ref = refs[-4:-2]
+    total = taken_sum(refs[:-4], refs[-2], refs[-1])
+    mine_ref[...] = total[:512]
+    yours_ref[...] = total[512:].astype(BF)
 
 
 def node_sum(parts):
@@ -321,12 +335,13 @@
             jax.ShapeDtypeStruct((512, 128), F32),
             jax.ShapeDtypeStruct((512, 128), BF),
         ),
-        in_specs=[vm] * len(parts),
+        in_specs=[pl.BlockSpec(memory_space=pl.ANY)] * len(parts),
         out_specs=(vm, vm),
+        scratch_shapes=sum_scratch(parts),
         cost_estimate=pl.CostEstimate(flops=1 << 20, bytes_accessed=3 << 20, transcendentals=0),
         compiler_params=pltpu.CompilerParams(vmem_limit_bytes=8 << 20),
         name="node_sum",
-    )(*parts)
+    )(in_hbm(parts[0]), *parts[1:])
 
 
 def halves(value, core):

time: 218 us -> 219 us (level)
  Pallas kernels: 24.2 us -> 27.4 us
  local copies, waits for them, and re-layouts: 14.3 us -> 11.5 us
    unnamed x31 -> x25, local copies, waits for them, and re-layouts: 8.95 us -> 6.11 us
  transfers between devices with their start and end apart: 31 -> 31, of which waited for: 14 -> 14; matrix products, arithmetic and copies ran while one was open for 8% -> 8% of each run, Pallas kernels for 5% -> 6%
where the time goes in v10:
time: 219 us; the launch traced here: 217 us
  blocking collectives  65.9 us (30%)
  waiting for transfers between devices  55.7 us (25%)
  starting transfers between devices  41.2 us (19%)
  Pallas kernels  27.4 us (13%)
  local copies, waits for them, and re-layouts  11.5 us (5%)
  matrix products  9.19 us (4%)
  other arithmetic  4.04 us (2%)
    all_to_all x1, blocking collectives, sum_grads(): lax.all_to_all(chip_sum(own, got), ('z', 'yh', 'yl', 'x'), 0, 0, tiled=True)  34.4 us
    all_to_all x1, blocking collectives, shards(): cells = lax.all_to_all(cells, ('core', 'yl', 'x'), 0, 0, tiled=True)  31.4 us
    ppermute x17, starting transfers between devices, ring_shift(): return lax.ppermute(value, axis, [(i, (i + k) % 4) for i in range(4)])  26.9 us
    ppermute x17, waiting for transfers between devices, ring_shift(): return lax.ppermute(value, axis, [(i, (i + k) % 4) for i in range(4)])  22.1 us
    all_to_all x1, waiting for transfers between devices, sum_grads(): mine = lax.all_to_all(chunk, ('z', 'yh', 'yl', 'x'), 0, 0, tiled=True)  18.5 us
    ppermute x9, waiting for transfers between devices, flip(): return lax.ppermute(value, axis, [(0, 1), (1, 0)])  12.7 us
    pallas_call x2, Pallas kernels, cell_products(): pl.pallas_call(functools.partial(cells_kernel, transposed, spots), out_sh...  10.1 us
    ppermute x9, starting transfers between devices, flip(): return lax.ppermute(value, axis, [(0, 1), (1, 0)])  8.01 us
  transfers between devices with their start and end apart: 31, of which 14 were waited for; matrix products, arithmetic and copies ran while one was open for 8% of the time, Pallas kernels for 6%

profile of v10, /device:TPU:0, one launch (start us, length us, event | category | flops | bytes accessed | tf_op | source)
XLA Modules:
  0.0 216.9 jit_solution(6823846610886912498)
XLA Ops:
  2.3 3.0 %collective-permute-done = bf16[512,128]{1,0:T(8,128)(2,1)S(1)} collective-permute-done((bf16[512,128]{1,0:T(8,128)(2,1)S(1)}, bf16[512,128]{1,0:T(8,128)(2,1)S(1)}, u32[]{:S(2)}, u32[]{:S(2)}) %collective-permute-start) | collective-permute-done | bytes 131104 | tf_op jit(solution)/shard_map/ppermute | solution.py:238
  5.3 4.2 %collective-permute-start.6 = (bf16[1024,128]{1,0:T(8,128)(2,1)S(1)}, bf16[1024,128]{1,0:T(8,128)(2,1)S(1)}, u32[]{:S(2)}, u32[]{:S(2)}) collective-permute-start(bf16[1024,128]{1,0:T(8,128)(2,1)S(1)} %pad_maximum_fusion.1.rest_0_), channel_id=1, source_target_pairs={{0,96},{32,0},{64,32},{96,64},{1,97},{33,1},{65,33},{97,65},{2,98}... | collective-permute-start | bytes 786440 | tf_op jit(solution)/shard_map/ppermute | solution.py:234
  10.2 3.3 %collective-permute-start.3 = (bf16[1024,128]{1,0:T(8,128)(2,1)S(1)}, bf16[1024,128]{1,0:T(8,128)(2,1)S(1)}, u32[]{:S(2)}, u32[]{:S(2)}) collective-permute-start(bf16[1024,128]{1,0:T(8,128)(2,1)S(1)} %pad_maximum_fusion.1.rest_0_), channel_id=1, source_target_pairs={{0,16},{16,0},{1,17},{17,1},{2,18},{18,2},{3,19},{19,3},{4,20},{20... | collective-permute-start | bytes 786440 | tf_op jit(solution)/shard_map/ppermute | solution.py:238
  14.3 5.1 %copy.20 = bf16[1,1,192,64,64]{4,3,2,1,0:T(8,128)(2,1)} copy(bf16[1,1,192,64,64]{2,4,3,1,0:T(8,128)(2,1)} %param.10) | data formatting | bytes 3145728 | tf_op args[1]
  19.6 3.3 %collective-permute-start.7 = (bf16[512,128]{1,0:T(8,128)(2,1)S(1)}, bf16[512,128]{1,0:T(8,128)(2,1)S(1)}, u32[]{:S(2)}, u32[]{:S(2)}) collective-permute-start(bf16[512,128]{1,0:T(8,128)(2,1)S(1)} %slice.56), channel_id=1, source_target_pairs={{0,96},{32,0},{64,32},{96,64},{1,97},{33,1},{65,33},{97,65},{2,98}... | collective-permute-start | bytes 393224 | tf_op jit(solution)/shard_map/ppermute | solution.py:234
  23.6 3.2 %collective-permute-start.11 = (bf16[1024,128]{1,0:T(8,128)(2,1)S(1)}, bf16[1024,128]{1,0:T(8,128)(2,1)S(1)}, u32[]{:S(2)}, u32[]{:S(2)}) collective-permute-start(bf16[1024,128]{1,0:T(8,128)(2,1)S(1)} %collective-permute-done.3.rest_1_), channel_id=1, source_target_pairs={{0,96},{32,0},{64,32},{96,64},{1,97},{33,1},{65,33},{97,65},{2,98}... | collective-permute-start | bytes 786440 | tf_op jit(solution)/shard_map/ppermute | solution.py:234
  27.2 2.7 %collective-permute-done.8.rest_5_ = bf16[512,128]{1,0:T(8,128)(2,1)} collective-permute-done((bf16[512,128]{1,0:T(8,128)(2,1)S(1)}, bf16[512,128]{1,0:T(8,128)(2,1)}, u32[]{:S(2)}, u32[]{:S(2)}) %collective-permute-start.8) | collective-permute-done | bytes 131104 | tf_op jit(solution)/shard_map/ppermute | solution.py:234
  30.5 5.2 %copy.22.blk1 = bf16[192,64,64]{2,1,0:T(8,128)(2,1)} copy(bf16[192,64,64]{0,2,1:T(8,128)(2,1)} %collective-permute-done.2) | data formatting | bytes 3145728 | tf_op jit(solution)/shard_map/ppermute | solution.py:238
  36.7 4.4 %cells_forward.1 = bf16[16,512,128]{2,1,0:T(8,128)(2,1)S(1)} custom-call(s32[768]{0:T(1024)S(1)} %reshape.46.off_ref, s32[2]{0:T(128)S(1)} %fusion.8.cnt_ref, s32[16]{0:T(128)S(1)} %add_multiply_fusion.1.place_ref, bf16[192,64,64]{2,1,0:T(8,128)(2,1)} %bitcast.27, bf16[192,64,64]{2,1,0:T(8,128)(2,1)} %copy.22.blk1, ...), custom_call_target="tpu_custom_call" | custom-call | flops 402653184 | bytes 10485760 | tf_op jit(solution)/shard_map/cells_forward/pallas_call | solution.py:106
  41.1 31.4 %all_to_all.15 = bf16[16,512,128]{2,1,0:T(8,128)(2,1)S(1)} all-to-all(bf16[16,512,128]{2,1,0:T(8,128)(2,1)S(1)} %cells_forward.1), channel_id=1, replica_groups=mesh['z'=4,'yh'=2,'core'=2,'yl'=2,'x'=4] {'core','yl','x'}, dimensions={0} | all-to-all | bytes 4194304 | tf_op jit(solution)/shard_map/all_to_all | solution.py:460
  77.3 1.6 multiply_convert_fusion.gp_one
  81.7 2.3 %collective-permute-done.28.got = bf16[1792,512]{1,0:T(8,128)(2,1)S(1)} collective-permute-done((bf16[1792,512]{1,0:T(8,128)(2,1)S(1)}, bf16[1792,512]{1,0:T(8,128)(2,1)S(1)}, u32[]{:S(2)}, u32[]{:S(2)}) %collective-permute-start.28) | collective-permute-done | bytes 1835040 | tf_op jit(solution)/shard_map/ppermute | solution.py:416
  85.3 34.4 %all_to_all.16.parts = bf16[64,112,128]{2,1,0:T(8,128)(2,1)S(1)} all-to-all(bf16[64,112,128]{2,1,0:T(8,128)(2,1)} %chip_sum.1), channel_id=1, replica_groups=mesh['z'=4,'yh'=2,'core'=2,'yl'=2,'x'=4] {'z','yh','yl','x'}, dimensions={0} | all-to-all | bytes 3670016 | tf_op jit(solution)/shard_map/all_to_all | solution.py:418
  119.8 4.0 %chunk_sum.1 = bf16[64,112,128]{2,1,0:T(8,128)(2,1)} custom-call(bf16[64,112,128]{2,1,0:T(8,128)(2,1)S(1)} %all_to_all.16.parts), custom_call_target="tpu_custom_call" | custom-call | flops 1048576 | bytes 3145728 | tf_op jit(solution)/shard_map/chunk_sum/pallas_call | solution.py:216
  123.8 5.8 %all-to-all-start.2 = ((bf16[64,112,128]{2,1,0:T(8,128)(2,1)}), bf16[64,112,128]{2,1,0:T(8,128)(2,1)}, u32[]{:S(2)}, u32[]{:S(2)}) async-start(bf16[64,112,128]{2,1,0:T(8,128)(2,1)} %chunk_sum.1), calls=%async_computation.2 | async-start | bytes 3670016 | tf_op jit(solution)/shard_map/all_to_all | solution.py:420
  129.6 3.1 %fusion.11 = (bf16[512,512]{1,0:T(8,128)(2,1)S(1)}, f32[512,512]{1,0:T(8,128)}) fusion(bf16[512,1024]{1,0:T(8,128)(2,1)S(1)} %multiply_convert_fusion.gp_one, bf16[512,1024]{1,0:T(8,128)(2,1)} %param.14), kind=kOutput, calls=%fused_computation.47 | convolution fusion | flops 537133056 | bytes 3670016 | tf_op jit(solution)/shard_map/dot_general | solution.py:478
  134.1 1.6 collective-permute-start.13
  135.7 2.7 %collective-permute-start.18 = (bf16[1024,128]{1,0:T(8,128)(2,1)S(1)}, bf16[1024,128]{1,0:T(8,128)(2,1)S(1)}, u32[]{:S(2)}, u32[]{:S(2)}) collective-permute-start(bf16[1024,128]{1,0:T(8,128)(2,1)S(1)} %pad_maximum_fusion.2.rest_0_), channel_id=1, source_target_pairs={{0,3},{1,0},{2,1},{3,2},{4,7},{5,4},{6,5},{7,6},{8,11},{9,8},{10,9... | collective-permute-start | bytes 786440 | tf_op jit(solution)/shard_map/ppermute | solution.py:234
  139.3 18.5 %all-to-all-done.2.blocks_ref = bf16[64,112,128]{2,1,0:T(8,128)(2,1)} async-done(((bf16[64,112,128]{2,1,0:T(8,128)(2,1)}), bf16[64,112,128]{2,1,0:T(8,128)(2,1)}, u32[]{:S(2)}, u32[]{:S(2)}) %all-to-all-start.2) | async-done | bytes 1835040 | tf_op jit(solution)/shard_map/all_to_all | solution.py:420
  158.3 2.7 %collective-permute-start.19 = (bf16[1024,128]{1,0:T(8,128)(2,1)S(1)}, bf16[1024,128]{1,0:T(8,128)(2,1)}, u32[]{:S(2)}, u32[]{:S(2)}) collective-permute-start(bf16[1024,128]{1,0:T(8,128)(2,1)S(1)} %collective-permute-done.13.rest_1_), channel_id=1, source_target_pairs={{0,3},{1,0},{2,1},{3,2},{4,7},{5,4},{6,5},{7,6},{8,11},{9,8},{10,9... | collective-permute-start | bytes 786440 | tf_op jit(solution)/shard_map/ppermute | solution.py:234
  161.5 3.0 %collective-permute-start.15 = (bf16[1024,128]{1,0:T(8,128)(2,1)S(1)}, bf16[1024,128]{1,0:T(8,128)(2,1)}, u32[]{:S(2)}, u32[]{:S(2)}) collective-permute-start(bf16[1024,128]{1,0:T(8,128)(2,1)S(1)} %collective-permute-done.13.rest_1_), channel_id=1, source_target_pairs={{0,1},{1,2},{2,3},{3,0},{4,5},{5,6},{6,7},{7,4},{8,9},{9,10},{10,1... | collective-permute-start | bytes 786440 | tf_op jit(solution)/shard_map/ppermute | solution.py:234
  164.6 9.2 %collective-permute-done.14.rest_2_ = bf16[1024,128]{1,0:T(8,128)(2,1)} collective-permute-done((bf16[1024,128]{1,0:T(8,128)(2,1)S(1)}, bf16[1024,128]{1,0:T(8,128)(2,1)}, u32[]{:S(2)}, u32[]{:S(2)}) %collective-permute-start.14) | collective-permute-done | bytes 262176 | tf_op jit(solution)/shard_map/ppermute | solution.py:234
  173.9 5.2 %collective-permute-done.15.rest_3_ = bf16[1024,128]{1,0:T(8,128)(2,1)} collective-permute-done((bf16[1024,128]{1,0:T(8,128)(2,1)S(1)}, bf16[1024,128]{1,0:T(8,128)(2,1)}, u32[]{:S(2)}, u32[]{:S(2)}) %collective-permute-start.15) | collective-permute-done | bytes 262176 | tf_op jit(solution)/shard_map/ppermute | solution.py:234
  179.0 5.7 %cells_back.1 = (bf16[1024,128]{1,0:T(8,128)(2,1)}, bf16[1024,128]{1,0:T(8,128)(2,1)}, bf16[1024,128]{1,0:T(8,128)(2,1)}, bf16[1024,128]{1,0:T(8,128)(2,1)}, bf1...) custom-call(s32[768]{0:T(1024)S(1)} %reshape.48.off_ref, ...), custom_call_target="tpu_custom_call" | custom-call | flops 402653184 | bytes 10485760 | tf_op jit(solution)/shard_map/cells_back/pallas_call | solution.py:106
  186.3 1.9 collective-permute-start.25
  188.3 6.1 %collective-permute-done.22.refs_1_ = bf16[1024,128]{1,0:T(8,128)(2,1)S(1)} collective-permute-done((bf16[1024,128]{1,0:T(8,128)(2,1)}, bf16[1024,128]{1,0:T(8,128)(2,1)S(1)}, u32[]{:S(2)}, u32[]{:S(2)}) %collective-permute-start.22) | collective-permute-done | bytes 262176 | tf_op jit(solution)/shard_map/ppermute | solution.py:238
  196.0 1.7 collective-permute-start.23
  198.9 1.6 collective-permute-start.26
  201.2 2.6 %collective-permute-done.21.refs_2_ = bf16[1024,128]{1,0:T(8,128)(2,1)S(1)} collective-permute-done((bf16[1024,128]{1,0:T(8,128)(2,1)}, bf16[1024,128]{1,0:T(8,128)(2,1)S(1)}, u32[]{:S(2)}, u32[]{:S(2)}) %collective-permute-start.21) | collective-permute-done | bytes 262176 | tf_op jit(solution)/shard_map/ppermute | solution.py:234
  203.8 1.7 collective-permute-done.23.refs_3_
  210.5 3.1 %finish_grads.2 = (f32[512,1024]{1,0:T(8,128)}, f32[1024,1024]{1,0:T(8,128)}, f32[1024,256]{1,0:T(8,128)}) custom-call(s32[1]{0:T(128)} %bitcast.5.half_ref, bf16[64,112,128]{2,1,0:T(8,128)(2,1)} %all-to-all-done.2.blocks_ref), custom_call_target="tpu_custom_call" | custom-call | flops 4194304 | bytes 6291456 | tf_op jit(solution)/shard_map/finish_grads/pallas_call | solution.py:390
  213.6 3.1 %finish_grads.3 = (f32[512,1024]{1,0:T(8,128)}, f32[1024,1024]{1,0:T(8,128)}, f32[1024,256]{1,0:T(8,128)}) custom-call(s32[1]{0:T(128)} %bitcast.6.half_ref, bf16[64,112,128]{2,1,0:T(8,128)(2,1)} %collective-permute-done.29.blocks_ref, f32[512,1024]{1,0:T(8,128)} %get-tuple-element.37.rest_0_, ...), custom_call_target="tpu_custom_call", output_to_operand_aliasing={{0}: (2, {}), {1}: (3, {}), {2}: (4, {})} | custom-call | flops 4194304 | bytes 6291456 | tf_op jit(solution)/shard_map/finish_grads/pallas_call | solution.py:390
  (98 shorter events, 27.7 us)
Async XLA Ops:
  0.6 74.2 %copy-start = (bf16[1024,1024]{1,0:T(8,128)(2,1)S(1)}, bf16[1024,1024]{1,0:T(8,128)(2,1)}, u32[]{:S(2)}) copy-start(bf16[1024,1024]{1,0:T(8,128)(2,1)} %param.15) | copy-start | bytes 6291460
  0.6 29.9 %collective-permute-start.2 = (bf16[192,64,64]{0,2,1:T(8,128)(2,1)}, bf16[192,64,64]{0,2,1:T(8,128)(2,1)}, u32[]{:S(2)}, u32[]{:S(2)}) collective-permute-start(bf16[192,64,64]{0,2,1:T(8,128)(2,1)} %bitcast.29), channel_id=1, source_target_pairs={{0,8},{8,0},{1,9},{9,1},{2,10},{10,2},{3,11},{11,3},{4,12},{12,4},... | collective-permute-start | bytes 4718600 | tf_op jit(solution)/shard_map/ppermute | solution.py:238
  1.9 3.4 %collective-permute-start = (bf16[512,128]{1,0:T(8,128)(2,1)S(1)}, bf16[512,128]{1,0:T(8,128)(2,1)S(1)}, u32[]{:S(2)}, u32[]{:S(2)}) collective-permute-start(bf16[512,128]{1,0:T(8,128)(2,1)S(1)} %get-tuple-element.52), channel_id=1, source_target_pairs={{0,8},{8,0},{1,9},{9,1},{2,10},{10,2},{3,11},{11,3},{4,12},{12,4},... | collective-permute-start | bytes 393224 | tf_op jit(solution)/shard_map/ppermute | solution.py:238
  5.3 14.2 %collective-permute-start.6 = (bf16[1024,128]{1,0:T(8,128)(2,1)S(1)}, bf16[1024,128]{1,0:T(8,128)(2,1)S(1)}, u32[]{:S(2)}, u32[]{:S(2)}) collective-permute-start(bf16[1024,128]{1,0:T(8,128)(2,1)S(1)} %pad_maximum_fusion.1.rest_0_), channel_id=1, source_target_pairs={{0,96},{32,0},{64,32},{96,64},{1,97},{33,1},{65,33},{97,65},{2,98}... | collective-permute-start | bytes 786440 | tf_op jit(solution)/shard_map/ppermute | solution.py:234
  9.5 13.3 %collective-permute-start.4 = (bf16[1024,128]{1,0:T(8,128)(2,1)S(1)}, bf16[1024,128]{1,0:T(8,128)(2,1)S(1)}, u32[]{:S(2)}, u32[]{:S(2)}) collective-permute-start(bf16[1024,128]{1,0:T(8,128)(2,1)S(1)} %pad_maximum_fusion.1.rest_0_), channel_id=1, source_target_pairs={{0,32},{32,64},{64,96},{96,0},{1,33},{33,65},{65,97},{97,1},{2,34}... | collective-permute-start | bytes 786440 | tf_op jit(solution)/shard_map/ppermute | solution.py:234
  10.2 13.4 %collective-permute-start.3 = (bf16[1024,128]{1,0:T(8,128)(2,1)S(1)}, bf16[1024,128]{1,0:T(8,128)(2,1)S(1)}, u32[]{:S(2)}, u32[]{:S(2)}) collective-permute-start(bf16[1024,128]{1,0:T(8,128)(2,1)S(1)} %pad_maximum_fusion.1.rest_0_), channel_id=1, source_target_pairs={{0,16},{16,0},{1,17},{17,1},{2,18},{18,2},{3,19},{19,3},{4,20},{20... | collective-permute-start | bytes 786440 | tf_op jit(solution)/shard_map/ppermute | solution.py:238
  14.2 5.2 %collective-permute-start.1 = (s32[512]{0:T(512)S(1)}, s32[512]{0:T(512)S(1)}, u32[]{:S(2)}, u32[]{:S(2)}) collective-permute-start(s32[512]{0:T(512)S(1)} %pad_add_fusion.3), channel_id=1, source_target_pairs={{0,8},{8,0},{1,9},{9,1},{2,10},{10,2},{3,11},{11,3},{4,12},{12,4},... | collective-permute-start | bytes 6152 | tf_op jit(solution)/shard_map/ppermute | solution.py:437
  19.6 7.3 %collective-permute-start.7 = (bf16[512,128]{1,0:T(8,128)(2,1)S(1)}, bf16[512,128]{1,0:T(8,128)(2,1)S(1)}, u32[]{:S(2)}, u32[]{:S(2)}) collective-permute-start(bf16[512,128]{1,0:T(8,128)(2,1)S(1)} %slice.56), channel_id=1, source_target_pairs={{0,96},{32,0},{64,32},{96,64},{1,97},{33,1},{65,33},{97,65},{2,98}... | collective-permute-start | bytes 393224 | tf_op jit(solution)/shard_map/ppermute | solution.py:234
  22.9 7.0 %collective-permute-start.8 = (bf16[512,128]{1,0:T(8,128)(2,1)S(1)}, bf16[512,128]{1,0:T(8,128)(2,1)}, u32[]{:S(2)}, u32[]{:S(2)}) collective-permute-start(bf16[512,128]{1,0:T(8,128)(2,1)S(1)} %slice.57), channel_id=1, source_target_pairs={{0,32},{32,64},{64,96},{96,0},{1,33},{33,65},{65,97},{97,1},{2,34}... | collective-permute-start | bytes 393224 | tf_op jit(solution)/shard_map/ppermute | solution.py:234
  23.6 13.0 %collective-permute-start.11 = (bf16[1024,128]{1,0:T(8,128)(2,1)S(1)}, bf16[1024,128]{1,0:T(8,128)(2,1)S(1)}, u32[]{:S(2)}, u32[]{:S(2)}) collective-permute-start(bf16[1024,128]{1,0:T(8,128)(2,1)S(1)} %collective-permute-done.3.rest_1_), channel_id=1, source_target_pairs={{0,96},{32,0},{64,32},{96,64},{1,97},{33,1},{65,33},{97,65},{2,98}... | collective-permute-start | bytes 786440 | tf_op jit(solution)/shard_map/ppermute | solution.py:234
  26.9 9.8 %collective-permute-start.5 = (bf16[1024,128]{1,0:T(8,128)(2,1)S(1)}, bf16[1024,128]{1,0:T(8,128)(2,1)}, u32[]{:S(2)}, u32[]{:S(2)}) collective-permute-start(bf16[1024,128]{1,0:T(8,128)(2,1)S(1)} %collective-permute-done.3.rest_1_), channel_id=1, source_target_pairs={{0,32},{32,64},{64,96},{96,0},{1,33},{33,65},{65,97},{97,1},{2,34}... | collective-permute-start | bytes 786440 | tf_op jit(solution)/shard_map/ppermute | solution.py:234
  26.9 8.9 %collective-permute-start.9 = (bf16[512,128]{1,0:T(8,128)(2,1)S(1)}, bf16[512,128]{1,0:T(8,128)(2,1)}, u32[]{:S(2)}, u32[]{:S(2)}) collective-permute-start(bf16[512,128]{1,0:T(8,128)(2,1)S(1)} %collective-permute-done.7.rest_4_), channel_id=1, source_target_pairs={{0,16},{16,0},{1,17},{17,1},{2,18},{18,2},{3,19},{19,3},{4,20},{20... | collective-permute-start | bytes 393224 | tf_op jit(solution)/shard_map/ppermute | solution.py:238
  29.9 6.8 %collective-permute-start.10 = (bf16[512,128]{1,0:T(8,128)(2,1)}, bf16[512,128]{1,0:T(8,128)(2,1)}, u32[]{:S(2)}, u32[]{:S(2)}) collective-permute-start(bf16[512,128]{1,0:T(8,128)(2,1)} %collective-permute-done.8.rest_5_), channel_id=1, source_target_pairs={{0,16},{16,0},{1,17},{17,1},{2,18},{18,2},{3,19},{19,3},{4,20},{20... | collective-permute-start | bytes 393224 | tf_op jit(solution)/shard_map/ppermute | solution.py:238
  80.1 3.9 %collective-permute-start.28 = (bf16[1792,512]{1,0:T(8,128)(2,1)S(1)}, bf16[1792,512]{1,0:T(8,128)(2,1)S(1)}, u32[]{:S(2)}, u32[]{:S(2)}) collective-permute-start(bf16[1792,512]{1,0:T(8,128)(2,1)S(1)} %shard_map.131), channel_id=1, source_target_pairs={{0,8},{8,0},{1,9},{9,1},{2,10},{10,2},{3,11},{11,3},{4,12},{12,4},... | collective-permute-start | bytes 5505032 | tf_op jit(solution)/shard_map/ppermute | solution.py:416
  123.8 34.0 %all-to-all-start.2 = ((bf16[64,112,128]{2,1,0:T(8,128)(2,1)}), bf16[64,112,128]{2,1,0:T(8,128)(2,1)}, u32[]{:S(2)}, u32[]{:S(2)}) async-start(bf16[64,112,128]{2,1,0:T(8,128)(2,1)} %chunk_sum.1), calls=%async_computation.2 | async-start | bytes 3670016 | tf_op jit(solution)/shard_map/all_to_all | solution.py:420
  132.7 1.4 collective-permute-start.12
  134.1 24.2 %collective-permute-start.13 = (bf16[1024,128]{1,0:T(8,128)(2,1)S(1)}, bf16[1024,128]{1,0:T(8,128)(2,1)S(1)}, u32[]{:S(2)}, u32[]{:S(2)}) collective-permute-start(bf16[1024,128]{1,0:T(8,128)(2,1)S(1)} %pad_maximum_fusion.2.rest_0_), channel_id=1, source_target_pairs={{0,4},{4,0},{1,5},{5,1},{2,6},{6,2},{3,7},{7,3},{8,12},{12,8},{9,1... | collective-permute-start | bytes 786440 | tf_op jit(solution)/shard_map/ppermute | solution.py:238
  135.7 25.3 %collective-permute-start.18 = (bf16[1024,128]{1,0:T(8,128)(2,1)S(1)}, bf16[1024,128]{1,0:T(8,128)(2,1)S(1)}, u32[]{:S(2)}, u32[]{:S(2)}) collective-permute-start(bf16[1024,128]{1,0:T(8,128)(2,1)S(1)} %pad_maximum_fusion.2.rest_0_), channel_id=1, source_target_pairs={{0,3},{1,0},{2,1},{3,2},{4,7},{5,4},{6,5},{7,6},{8,11},{9,8},{10,9... | collective-permute-start | bytes 786440 | tf_op jit(solution)/shard_map/ppermute | solution.py:234
  138.4 23.1 %collective-permute-start.16 = (bf16[1024,128]{1,0:T(8,128)(2,1)S(1)}, bf16[1024,128]{1,0:T(8,128)(2,1)S(1)}, u32[]{:S(2)}, u32[]{:S(2)}) collective-permute-start(bf16[1024,128]{1,0:T(8,128)(2,1)S(1)} %pad_maximum_fusion.2.rest_0_), channel_id=1, source_target_pairs={{0,2},{1,3},{2,0},{3,1},{4,6},{5,7},{6,4},{7,5},{8,10},{9,11},{10,... | collective-permute-start | bytes 786440 | tf_op jit(solution)/shard_map/ppermute | solution.py:234
  157.8 55.8 %collective-permute-start.29 = (bf16[64,112,128]{2,1,0:T(8,128)(2,1)}, bf16[64,112,128]{2,1,0:T(8,128)(2,1)}, u32[]{:S(2)}, u32[]{:S(2)}) collective-permute-start(bf16[64,112,128]{2,1,0:T(8,128)(2,1)} %all-to-all-done.2.blocks_ref), channel_id=1, source_target_pairs={{0,8},{8,0},{1,9},{9,1},{2,10},{10,2},{3,11},{11,3},{4,12},{12,4},... | collective-permute-start | bytes 5505032 | tf_op jit(solution)/shard_map/ppermute | solution.py:421
  157.8 16.1 %collective-permute-start.14 = (bf16[1024,128]{1,0:T(8,128)(2,1)S(1)}, bf16[1024,128]{1,0:T(8,128)(2,1)}, u32[]{:S(2)}, u32[]{:S(2)}) collective-permute-start(bf16[1024,128]{1,0:T(8,128)(2,1)S(1)} %pad_maximum_fusion.2.rest_0_), channel_id=1, source_target_pairs={{0,1},{1,2},{2,3},{3,0},{4,5},{5,6},{6,7},{7,4},{8,9},{9,10},{10,1... | collective-permute-start | bytes 786440 | tf_op jit(solution)/shard_map/ppermute | solution.py:234
  158.3 15.5 %collective-permute-start.19 = (bf16[1024,128]{1,0:T(8,128)(2,1)S(1)}, bf16[1024,128]{1,0:T(8,128)(2,1)}, u32[]{:S(2)}, u32[]{:S(2)}) collective-permute-start(bf16[1024,128]{1,0:T(8,128)(2,1)S(1)} %collective-permute-done.13.rest_1_), channel_id=1, source_target_pairs={{0,3},{1,0},{2,1},{3,2},{4,7},{5,4},{6,5},{7,6},{8,11},{9,8},{10,9... | collective-permute-start | bytes 786440 | tf_op jit(solution)/shard_map/ppermute | solution.py:234
  161.0 12.9 %collective-permute-start.17 = (bf16[1024,128]{1,0:T(8,128)(2,1)S(1)}, bf16[1024,128]{1,0:T(8,128)(2,1)}, u32[]{:S(2)}, u32[]{:S(2)}) collective-permute-start(bf16[1024,128]{1,0:T(8,128)(2,1)S(1)} %collective-permute-done.13.rest_1_), channel_id=1, source_target_pairs={{0,2},{1,3},{2,0},{3,1},{4,6},{5,7},{6,4},{7,5},{8,10},{9,11},{10,... | collective-permute-start | bytes 786440 | tf_op jit(solution)/shard_map/ppermute | solution.py:234
  161.5 17.5 %collective-permute-start.15 = (bf16[1024,128]{1,0:T(8,128)(2,1)S(1)}, bf16[1024,128]{1,0:T(8,128)(2,1)}, u32[]{:S(2)}, u32[]{:S(2)}) collective-permute-start(bf16[1024,128]{1,0:T(8,128)(2,1)S(1)} %collective-permute-done.13.rest_1_), channel_id=1, source_target_pairs={{0,1},{1,2},{2,3},{3,0},{4,5},{5,6},{6,7},{7,4},{8,9},{9,10},{10,1... | collective-permute-start | bytes 786440 | tf_op jit(solution)/shard_map/ppermute | solution.py:234
  184.7 9.7 %collective-permute-start.22 = (bf16[1024,128]{1,0:T(8,128)(2,1)}, bf16[1024,128]{1,0:T(8,128)(2,1)S(1)}, u32[]{:S(2)}, u32[]{:S(2)}) collective-permute-start(bf16[1024,128]{1,0:T(8,128)(2,1)} %get-tuple-element.31), channel_id=1, source_target_pairs={{0,16},{16,0},{1,17},{17,1},{2,18},{18,2},{3,19},{19,3},{4,20},{20... | collective-permute-start | bytes 786440 | tf_op jit(solution)/shard_map/ppermute | solution.py:238
  184.8 11.2 %collective-permute-start.24 = (bf16[1024,128]{1,0:T(8,128)(2,1)}, bf16[1024,128]{1,0:T(8,128)(2,1)S(1)}, u32[]{:S(2)}, u32[]{:S(2)}) collective-permute-start(bf16[1024,128]{1,0:T(8,128)(2,1)} %get-tuple-element.33), channel_id=1, source_target_pairs={{0,32},{32,64},{64,96},{96,0},{1,33},{33,65},{65,97},{97,1},{2,34}... | collective-permute-start | bytes 786440 | tf_op jit(solution)/shard_map/ppermute | solution.py:234
  186.3 11.5 %collective-permute-start.25 = (bf16[1024,128]{1,0:T(8,128)(2,1)}, bf16[1024,128]{1,0:T(8,128)(2,1)S(1)}, u32[]{:S(2)}, u32[]{:S(2)}) collective-permute-start(bf16[1024,128]{1,0:T(8,128)(2,1)} %get-tuple-element.34), channel_id=1, source_target_pairs={{0,96},{32,0},{64,32},{96,64},{1,97},{33,1},{65,33},{97,65},{2,98}... | collective-permute-start | bytes 786440 | tf_op jit(solution)/shard_map/ppermute | solution.py:234
  188.1 13.0 %collective-permute-start.20 = (bf16[1024,128]{1,0:T(8,128)(2,1)}, bf16[1024,128]{1,0:T(8,128)(2,1)S(1)}, u32[]{:S(2)}, u32[]{:S(2)}) collective-permute-start(bf16[1024,128]{1,0:T(8,128)(2,1)} %get-tuple-element.28), channel_id=1, source_target_pairs={{0,32},{32,64},{64,96},{96,0},{1,33},{33,65},{65,97},{97,1},{2,34}... | collective-permute-start | bytes 786440 | tf_op jit(solution)/shard_map/ppermute | solution.py:234
  194.4 9.4 %collective-permute-start.21 = (bf16[1024,128]{1,0:T(8,128)(2,1)}, bf16[1024,128]{1,0:T(8,128)(2,1)S(1)}, u32[]{:S(2)}, u32[]{:S(2)}) collective-permute-start(bf16[1024,128]{1,0:T(8,128)(2,1)} %get-tuple-element.29), channel_id=1, source_target_pairs={{0,96},{32,0},{64,32},{96,64},{1,97},{33,1},{65,33},{97,65},{2,98}... | collective-permute-start | bytes 786440 | tf_op jit(solution)/shard_map/ppermute | solution.py:234
  196.0 9.5 %collective-permute-start.23 = (bf16[1024,128]{1,0:T(8,128)(2,1)S(1)}, bf16[1024,128]{1,0:T(8,128)(2,1)S(1)}, u32[]{:S(2)}, u32[]{:S(2)}) collective-permute-start(bf16[1024,128]{1,0:T(8,128)(2,1)S(1)} %shard_map.128), channel_id=1, source_target_pairs={{0,64},{32,96},{64,0},{96,32},{1,65},{33,97},{65,1},{97,33},{2,66}... | collective-permute-start | bytes 786440 | tf_op jit(solution)/shard_map/ppermute | solution.py:234
  198.9 8.0 %collective-permute-start.26 = (bf16[1024,128]{1,0:T(8,128)(2,1)S(1)}, bf16[1024,128]{1,0:T(8,128)(2,1)S(1)}, u32[]{:S(2)}, u32[]{:S(2)}) collective-permute-start(bf16[1024,128]{1,0:T(8,128)(2,1)S(1)} %shard_map.129), channel_id=1, source_target_pairs={{0,16},{16,0},{1,17},{17,1},{2,18},{18,2},{3,19},{19,3},{4,20},{20... | collective-permute-start | bytes 786440 | tf_op jit(solution)/shard_map/ppermute | solution.py:238
  208.2 1.4 collective-permute-start.27
  (11 other events, 153.1 us)

commit v11 on v10

--- a/solution.py
+++ b/solution.py
@@ -353,9 +353,9 @@
     return jnp.concatenate([mine, got], axis=0)
 
 
-def finish_kernel(half_ref, blocks_ref, *rest):
+def finish_kernel(near, half_ref, blocks_ref, *rest):
     outs, taken, total, turned, sems, in_sem = rest[-8:-5], *rest[-5:]
-    reads = [
+    reads = [] if near else [
         pltpu.make_async_copy(blocks_ref.at[16 * k : 16 * k + 16], taken.at[k], in_sem.at[k])
         for k in range(4)
     ]
@@ -369,12 +369,15 @@
         pltpu.make_async_copy(turned, outs[2].at[lanes, :], sems.at[2]),
     )
     for row in range(16):
-        if row % 4 == 0:
+        if row % 4 == 0 and not near:
             reads[row // 4].wait()
         for col in range(4):
-            total[row * 112 : (row + 1) * 112, col * 128 : (col + 1) * 128] = taken[
-                row // 4, (row % 4) * 4 + col
-            ].astype(F32) * (1.0 / 256.0)
+            block = (
+                blocks_ref[row * 4 + col] if near else taken[row // 4, (row % 4) * 4 + col]
+            )
+            total[row * 112 : (row + 1) * 112, col * 128 : (col + 1) * 128] = block.astype(
+                F32
+            ) * (1.0 / 256.0)
         if row == 4:
             moves[0].start()
         if row == 13:
@@ -385,19 +388,20 @@
         move.wait()
 
 
-def finish_grads(half, blocks, outs):
+def finish_grads(half, blocks, outs, near):
     any_spec = pl.BlockSpec(memory_space=pl.ANY)
-    return pl.pallas_call(
-        finish_kernel,
+    own_spec = pl.BlockSpec(memory_space=pltpu.VMEM) if near else any_spec
+    return pl.pallas_call(
+        functools.partial(finish_kernel, near),
         out_shape=(
             jax.ShapeDtypeStruct((512, 1024), F32),
             jax.ShapeDtypeStruct((1024, 1024), F32),
             jax.ShapeDtypeStruct((1024, 256), F32),
         ),
-        in_specs=[pl.BlockSpec(memory_space=pltpu.SMEM)] + [any_spec] * (1 + len(outs)),
+        in_specs=[pl.BlockSpec(memory_space=pltpu.SMEM), own_spec] + [any_spec] * len(outs),
         out_specs=(any_spec,) * 3,
         scratch_shapes=[
-            pltpu.VMEM((4, 16, 112, 128), BF),
+            pltpu.VMEM((1, 16, 16, 128) if near else (4, 16, 112, 128), BF),
             pltpu.VMEM((1792, 512), F32),
             pltpu.VMEM((512, 256), F32),
             pltpu.SemaphoreType.DMA((3,)),
@@ -419,8 +423,8 @@
     chunk = chunk_sum(parts)
     mine = lax.all_to_all(chunk, ("z", "yh", "yl", "x"), 0, 0, tiled=True)
     yours = lax.ppermute(mine, "core", swap)
-    outs = finish_grads(core, mine, ())
-    return finish_grads(1 - core, yours, outs)
+    outs = finish_grads(core, mine, (), False)
+    return finish_grads(1 - core, yours, outs, True)
 
 
 def shards(features, blocks, block_rows, block_cols, block_count, w_in, w_mid, w_out, cotangent):

time: 219 us -> 219 us (level)
  no operation moved by 1% of the time
where the time goes in v11:
time: 219 us; the launch traced here: 217 us
  blocking collectives  65.9 us (30%)
  waiting for transfers between devices  55.7 us (25%)
  starting transfers between devices  41.2 us (19%)
  Pallas kernels  27.8 us (13%)
  local copies, waits for them, and re-layouts  11.5 us (5%)
  matrix products  9.19 us (4%)
  other arithmetic  4.04 us (2%)
    all_to_all x1, blocking collectives, sum_grads(): lax.all_to_all(chip_sum(own, got), ('z', 'yh', 'yl', 'x'), 0, 0, tiled=True)  34.4 us
    all_to_all x1, blocking collectives, shards(): cells = lax.all_to_all(cells, ('core', 'yl', 'x'), 0, 0, tiled=True)  31.4 us
    ppermute x17, starting transfers between devices, ring_shift(): return lax.ppermute(value, axis, [(i, (i + k) % 4) for i in range(4)])  26.9 us
    ppermute x17, waiting for transfers between devices, ring_shift(): return lax.ppermute(value, axis, [(i, (i + k) % 4) for i in range(4)])  22.1 us
    all_to_all x1, waiting for transfers between devices, sum_grads(): mine = lax.all_to_all(chunk, ('z', 'yh', 'yl', 'x'), 0, 0, tiled=True)  18.5 us
    ppermute x9, waiting for transfers between devices, flip(): return lax.ppermute(value, axis, [(0, 1), (1, 0)])  12.7 us
    pallas_call x2, Pallas kernels, cell_products(): pl.pallas_call(functools.partial(cells_kernel, transposed, spots), out_sh...  10.1 us
    ppermute x9, starting transfers between devices, flip(): return lax.ppermute(value, axis, [(0, 1), (1, 0)])  8.01 us
  transfers between devices with their start and end apart: 31, of which 14 were waited for; matrix products, arithmetic and copies ran while one was open for 8% of the time, Pallas kernels for 6%

profile of v11, /device:TPU:0, one launch (start us, length us, event | category | flops | bytes accessed | tf_op | source)
XLA Modules:
  0.0 217.3 jit_solution(4096928675991619674)
XLA Ops:
  2.3 3.0 %collective-permute-done = bf16[512,128]{1,0:T(8,128)(2,1)S(1)} collective-permute-done((bf16[512,128]{1,0:T(8,128)(2,1)S(1)}, bf16[512,128]{1,0:T(8,128)(2,1)S(1)}, u32[]{:S(2)}, u32[]{:S(2)}) %collective-permute-start) | collective-permute-done | bytes 131104 | tf_op jit(solution)/shard_map/ppermute | solution.py:238
  5.3 4.2 %collective-permute-start.6 = (bf16[1024,128]{1,0:T(8,128)(2,1)S(1)}, bf16[1024,128]{1,0:T(8,128)(2,1)S(1)}, u32[]{:S(2)}, u32[]{:S(2)}) collective-permute-start(bf16[1024,128]{1,0:T(8,128)(2,1)S(1)} %pad_maximum_fusion.1.rest_0_), channel_id=1, source_target_pairs={{0,96},{32,0},{64,32},{96,64},{1,97},{33,1},{65,33},{97,65},{2,98}... | collective-permute-start | bytes 786440 | tf_op jit(solution)/shard_map/ppermute | solution.py:234
  10.2 3.3 %collective-permute-start.3 = (bf16[1024,128]{1,0:T(8,128)(2,1)S(1)}, bf16[1024,128]{1,0:T(8,128)(2,1)S(1)}, u32[]{:S(2)}, u32[]{:S(2)}) collective-permute-start(bf16[1024,128]{1,0:T(8,128)(2,1)S(1)} %pad_maximum_fusion.1.rest_0_), channel_id=1, source_target_pairs={{0,16},{16,0},{1,17},{17,1},{2,18},{18,2},{3,19},{19,3},{4,20},{20... | collective-permute-start | bytes 786440 | tf_op jit(solution)/shard_map/ppermute | solution.py:238
  14.3 5.1 %copy.20 = bf16[1,1,192,64,64]{4,3,2,1,0:T(8,128)(2,1)} copy(bf16[1,1,192,64,64]{2,4,3,1,0:T(8,128)(2,1)} %param.10) | data formatting | bytes 3145728 | tf_op args[1]
  19.6 3.3 %collective-permute-start.7 = (bf16[512,128]{1,0:T(8,128)(2,1)S(1)}, bf16[512,128]{1,0:T(8,128)(2,1)S(1)}, u32[]{:S(2)}, u32[]{:S(2)}) collective-permute-start(bf16[512,128]{1,0:T(8,128)(2,1)S(1)} %slice.56), channel_id=1, source_target_pairs={{0,96},{32,0},{64,32},{96,64},{1,97},{33,1},{65,33},{97,65},{2,98}... | collective-permute-start | bytes 393224 | tf_op jit(solution)/shard_map/ppermute | solution.py:234
  23.6 3.2 %collective-permute-start.11 = (bf16[1024,128]{1,0:T(8,128)(2,1)S(1)}, bf16[1024,128]{1,0:T(8,128)(2,1)S(1)}, u32[]{:S(2)}, u32[]{:S(2)}) collective-permute-start(bf16[1024,128]{1,0:T(8,128)(2,1)S(1)} %collective-permute-done.3.rest_1_), channel_id=1, source_target_pairs={{0,96},{32,0},{64,32},{96,64},{1,97},{33,1},{65,33},{97,65},{2,98}... | collective-permute-start | bytes 786440 | tf_op jit(solution)/shard_map/ppermute | solution.py:234
  27.2 2.7 %collective-permute-done.8.rest_5_ = bf16[512,128]{1,0:T(8,128)(2,1)} collective-permute-done((bf16[512,128]{1,0:T(8,128)(2,1)S(1)}, bf16[512,128]{1,0:T(8,128)(2,1)}, u32[]{:S(2)}, u32[]{:S(2)}) %collective-permute-start.8) | collective-permute-done | bytes 131104 | tf_op jit(solution)/shard_map/ppermute | solution.py:234
  30.5 5.2 %copy.22.blk1 = bf16[192,64,64]{2,1,0:T(8,128)(2,1)} copy(bf16[192,64,64]{0,2,1:T(8,128)(2,1)} %collective-permute-done.2) | data formatting | bytes 3145728 | tf_op jit(solution)/shard_map/ppermute | solution.py:238
  36.7 4.4 %cells_forward.1 = bf16[16,512,128]{2,1,0:T(8,128)(2,1)S(1)} custom-call(s32[768]{0:T(1024)S(1)} %reshape.46.off_ref, s32[2]{0:T(128)S(1)} %fusion.8.cnt_ref, s32[16]{0:T(128)S(1)} %add_multiply_fusion.1.place_ref, bf16[192,64,64]{2,1,0:T(8,128)(2,1)} %bitcast.27, bf16[192,64,64]{2,1,0:T(8,128)(2,1)} %copy.22.blk1, ...), custom_call_target="tpu_custom_call" | custom-call | flops 402653184 | bytes 10485760 | tf_op jit(solution)/shard_map/cells_forward/pallas_call | solution.py:106
  41.1 31.4 %all_to_all.15 = bf16[16,512,128]{2,1,0:T(8,128)(2,1)S(1)} all-to-all(bf16[16,512,128]{2,1,0:T(8,128)(2,1)S(1)} %cells_forward.1), channel_id=1, replica_groups=mesh['z'=4,'yh'=2,'core'=2,'yl'=2,'x'=4] {'core','yl','x'}, dimensions={0} | all-to-all | bytes 4194304 | tf_op jit(solution)/shard_map/all_to_all | solution.py:464
  77.3 1.6 multiply_convert_fusion.gp_one
  81.7 2.3 %collective-permute-done.28.got = bf16[1792,512]{1,0:T(8,128)(2,1)S(1)} collective-permute-done((bf16[1792,512]{1,0:T(8,128)(2,1)S(1)}, bf16[1792,512]{1,0:T(8,128)(2,1)S(1)}, u32[]{:S(2)}, u32[]{:S(2)}) %collective-permute-start.28) | collective-permute-done | bytes 1835040 | tf_op jit(solution)/shard_map/ppermute | solution.py:420
  85.3 34.4 %all_to_all.16.parts = bf16[64,112,128]{2,1,0:T(8,128)(2,1)S(1)} all-to-all(bf16[64,112,128]{2,1,0:T(8,128)(2,1)} %chip_sum.1), channel_id=1, replica_groups=mesh['z'=4,'yh'=2,'core'=2,'yl'=2,'x'=4] {'z','yh','yl','x'}, dimensions={0} | all-to-all | bytes 3670016 | tf_op jit(solution)/shard_map/all_to_all | solution.py:422
  119.8 4.0 %chunk_sum.1 = bf16[64,112,128]{2,1,0:T(8,128)(2,1)} custom-call(bf16[64,112,128]{2,1,0:T(8,128)(2,1)S(1)} %all_to_all.16.parts), custom_call_target="tpu_custom_call" | custom-call | flops 1048576 | bytes 3145728 | tf_op jit(solution)/shard_map/chunk_sum/pallas_call | solution.py:216
  123.8 5.8 %all-to-all-start.2 = ((bf16[64,112,128]{2,1,0:T(8,128)(2,1)}), bf16[64,112,128]{2,1,0:T(8,128)(2,1)}, u32[]{:S(2)}, u32[]{:S(2)}) async-start(bf16[64,112,128]{2,1,0:T(8,128)(2,1)} %chunk_sum.1), calls=%async_computation.2 | async-start | bytes 3670016 | tf_op jit(solution)/shard_map/all_to_all | solution.py:424
  129.6 3.1 %fusion.11 = (bf16[512,512]{1,0:T(8,128)(2,1)S(1)}, f32[512,512]{1,0:T(8,128)}) fusion(bf16[512,1024]{1,0:T(8,128)(2,1)S(1)} %multiply_convert_fusion.gp_one, bf16[512,1024]{1,0:T(8,128)(2,1)} %param.14), kind=kOutput, calls=%fused_computation.47 | convolution fusion | flops 537133056 | bytes 3670016 | tf_op jit(solution)/shard_map/dot_general | solution.py:482
  134.1 1.6 collective-permute-start.13
  135.7 2.7 %collective-permute-start.18 = (bf16[1024,128]{1,0:T(8,128)(2,1)S(1)}, bf16[1024,128]{1,0:T(8,128)(2,1)S(1)}, u32[]{:S(2)}, u32[]{:S(2)}) collective-permute-start(bf16[1024,128]{1,0:T(8,128)(2,1)S(1)} %pad_maximum_fusion.2.rest_0_), channel_id=1, source_target_pairs={{0,3},{1,0},{2,1},{3,2},{4,7},{5,4},{6,5},{7,6},{8,11},{9,8},{10,9... | collective-permute-start | bytes 786440 | tf_op jit(solution)/shard_map/ppermute | solution.py:234
  139.3 18.5 %all-to-all-done.2.blocks_ref = bf16[64,112,128]{2,1,0:T(8,128)(2,1)} async-done(((bf16[64,112,128]{2,1,0:T(8,128)(2,1)}), bf16[64,112,128]{2,1,0:T(8,128)(2,1)}, u32[]{:S(2)}, u32[]{:S(2)}) %all-to-all-start.2) | async-done | bytes 1835040 | tf_op jit(solution)/shard_map/all_to_all | solution.py:424
  158.3 2.7 %collective-permute-start.19 = (bf16[1024,128]{1,0:T(8,128)(2,1)S(1)}, bf16[1024,128]{1,0:T(8,128)(2,1)}, u32[]{:S(2)}, u32[]{:S(2)}) collective-permute-start(bf16[1024,128]{1,0:T(8,128)(2,1)S(1)} %collective-permute-done.13.rest_1_), channel_id=1, source_target_pairs={{0,3},{1,0},{2,1},{3,2},{4,7},{5,4},{6,5},{7,6},{8,11},{9,8},{10,9... | collective-permute-start | bytes 786440 | tf_op jit(solution)/shard_map/ppermute | solution.py:234
  161.5 3.0 %collective-permute-start.15 = (bf16[1024,128]{1,0:T(8,128)(2,1)S(1)}, bf16[1024,128]{1,0:T(8,128)(2,1)}, u32[]{:S(2)}, u32[]{:S(2)}) collective-permute-start(bf16[1024,128]{1,0:T(8,128)(2,1)S(1)} %collective-permute-done.13.rest_1_), channel_id=1, source_target_pairs={{0,1},{1,2},{2,3},{3,0},{4,5},{5,6},{6,7},{7,4},{8,9},{9,10},{10,1... | collective-permute-start | bytes 786440 | tf_op jit(solution)/shard_map/ppermute | solution.py:234
  164.6 9.2 %collective-permute-done.14.rest_2_ = bf16[1024,128]{1,0:T(8,128)(2,1)} collective-permute-done((bf16[1024,128]{1,0:T(8,128)(2,1)S(1)}, bf16[1024,128]{1,0:T(8,128)(2,1)}, u32[]{:S(2)}, u32[]{:S(2)}) %collective-permute-start.14) | collective-permute-done | bytes 262176 | tf_op jit(solution)/shard_map/ppermute | solution.py:234
  173.9 5.2 %collective-permute-done.15.rest_3_ = bf16[1024,128]{1,0:T(8,128)(2,1)} collective-permute-done((bf16[1024,128]{1,0:T(8,128)(2,1)S(1)}, bf16[1024,128]{1,0:T(8,128)(2,1)}, u32[]{:S(2)}, u32[]{:S(2)}) %collective-permute-start.15) | collective-permute-done | bytes 262176 | tf_op jit(solution)/shard_map/ppermute | solution.py:234
  179.0 5.7 %cells_back.1 = (bf16[1024,128]{1,0:T(8,128)(2,1)}, bf16[1024,128]{1,0:T(8,128)(2,1)}, bf16[1024,128]{1,0:T(8,128)(2,1)}, bf16[1024,128]{1,0:T(8,128)(2,1)}, bf1...) custom-call(s32[768]{0:T(1024)S(1)} %reshape.48.off_ref, ...), custom_call_target="tpu_custom_call" | custom-call | flops 402653184 | bytes 10485760 | tf_op jit(solution)/shard_map/cells_back/pallas_call | solution.py:106
  186.3 1.9 collective-permute-start.25
  188.3 6.1 %collective-permute-done.22.refs_1_ = bf16[1024,128]{1,0:T(8,128)(2,1)S(1)} collective-permute-done((bf16[1024,128]{1,0:T(8,128)(2,1)}, bf16[1024,128]{1,0:T(8,128)(2,1)S(1)}, u32[]{:S(2)}, u32[]{:S(2)}) %collective-permute-start.22) | collective-permute-done | bytes 262176 | tf_op jit(solution)/shard_map/ppermute | solution.py:238
  196.0 1.7 collective-permute-start.23
  198.9 1.6 collective-permute-start.26
  201.2 2.6 %collective-permute-done.21.refs_2_ = bf16[1024,128]{1,0:T(8,128)(2,1)S(1)} collective-permute-done((bf16[1024,128]{1,0:T(8,128)(2,1)}, bf16[1024,128]{1,0:T(8,128)(2,1)S(1)}, u32[]{:S(2)}, u32[]{:S(2)}) %collective-permute-start.21) | collective-permute-done | bytes 262176 | tf_op jit(solution)/shard_map/ppermute | solution.py:234
  203.8 1.7 collective-permute-done.23.refs_3_
  210.5 3.1 %finish_grads.2 = (f32[512,1024]{1,0:T(8,128)}, f32[1024,1024]{1,0:T(8,128)}, f32[1024,256]{1,0:T(8,128)}) custom-call(s32[1]{0:T(128)} %bitcast.5.half_ref, bf16[64,112,128]{2,1,0:T(8,128)(2,1)} %all-to-all-done.2.blocks_ref), custom_call_target="tpu_custom_call" | custom-call | flops 4194304 | bytes 6291456 | tf_op jit(solution)/shard_map/finish_grads/pallas_call | solution.py:394
  213.6 3.5 %finish_grads.3 = (f32[512,1024]{1,0:T(8,128)}, f32[1024,1024]{1,0:T(8,128)}, f32[1024,256]{1,0:T(8,128)}) custom-call(s32[1]{0:T(128)} %bitcast.6.half_ref, bf16[64,112,128]{2,1,0:T(8,128)(2,1)} %collective-permute-done.29.blocks_ref, f32[512,1024]{1,0:T(8,128)} %get-tuple-element.37.rest_0_, ...), custom_call_target="tpu_custom_call", output_to_operand_aliasing={{0}: (2, {}), {1}: (3, {}), {2}: (4, {})} | custom-call | flops 4194304 | bytes 6291456 | tf_op jit(solution)/shard_map/finish_grads/pallas_call | solution.py:394
  (98 shorter events, 27.7 us)
Async XLA Ops:
  0.6 74.2 %copy-start = (bf16[1024,1024]{1,0:T(8,128)(2,1)S(1)}, bf16[1024,1024]{1,0:T(8,128)(2,1)}, u32[]{:S(2)}) copy-start(bf16[1024,1024]{1,0:T(8,128)(2,1)} %param.15) | copy-start | bytes 6291460
  0.6 29.9 %collective-permute-start.2 = (bf16[192,64,64]{0,2,1:T(8,128)(2,1)}, bf16[192,64,64]{0,2,1:T(8,128)(2,1)}, u32[]{:S(2)}, u32[]{:S(2)}) collective-permute-start(bf16[192,64,64]{0,2,1:T(8,128)(2,1)} %bitcast.29), channel_id=1, source_target_pairs={{0,8},{8,0},{1,9},{9,1},{2,10},{10,2},{3,11},{11,3},{4,12},{12,4},... | collective-permute-start | bytes 4718600 | tf_op jit(solution)/shard_map/ppermute | solution.py:238
  1.9 3.4 %collective-permute-start = (bf16[512,128]{1,0:T(8,128)(2,1)S(1)}, bf16[512,128]{1,0:T(8,128)(2,1)S(1)}, u32[]{:S(2)}, u32[]{:S(2)}) collective-permute-start(bf16[512,128]{1,0:T(8,128)(2,1)S(1)} %get-tuple-element.52), channel_id=1, source_target_pairs={{0,8},{8,0},{1,9},{9,1},{2,10},{10,2},{3,11},{11,3},{4,12},{12,4},... | collective-permute-start | bytes 393224 | tf_op jit(solution)/shard_map/ppermute | solution.py:238
  5.3 14.2 %collective-permute-start.6 = (bf16[1024,128]{1,0:T(8,128)(2,1)S(1)}, bf16[1024,128]{1,0:T(8,128)(2,1)S(1)}, u32[]{:S(2)}, u32[]{:S(2)}) collective-permute-start(bf16[1024,128]{1,0:T(8,128)(2,1)S(1)} %pad_maximum_fusion.1.rest_0_), channel_id=1, source_target_pairs={{0,96},{32,0},{64,32},{96,64},{1,97},{33,1},{65,33},{97,65},{2,98}... | collective-permute-start | bytes 786440 | tf_op jit(solution)/shard_map/ppermute | solution.py:234
  9.5 13.3 %collective-permute-start.4 = (bf16[1024,128]{1,0:T(8,128)(2,1)S(1)}, bf16[1024,128]{1,0:T(8,128)(2,1)S(1)}, u32[]{:S(2)}, u32[]{:S(2)}) collective-permute-start(bf16[1024,128]{1,0:T(8,128)(2,1)S(1)} %pad_maximum_fusion.1.rest_0_), channel_id=1, source_target_pairs={{0,32},{32,64},{64,96},{96,0},{1,33},{33,65},{65,97},{97,1},{2,34}... | collective-permute-start | bytes 786440 | tf_op jit(solution)/shard_map/ppermute | solution.py:234
  10.2 13.4 %collective-permute-start.3 = (bf16[1024,128]{1,0:T(8,128)(2,1)S(1)}, bf16[1024,128]{1,0:T(8,128)(2,1)S(1)}, u32[]{:S(2)}, u32[]{:S(2)}) collective-permute-start(bf16[1024,128]{1,0:T(8,128)(2,1)S(1)} %pad_maximum_fusion.1.rest_0_), channel_id=1, source_target_pairs={{0,16},{16,0},{1,17},{17,1},{2,18},{18,2},{3,19},{19,3},{4,20},{20... | collective-permute-start | bytes 786440 | tf_op jit(solution)/shard_map/ppermute | solution.py:238
  14.2 5.2 %collective-permute-start.1 = (s32[512]{0:T(512)S(1)}, s32[512]{0:T(512)S(1)}, u32[]{:S(2)}, u32[]{:S(2)}) collective-permute-start(s32[512]{0:T(512)S(1)} %pad_add_fusion.3), channel_id=1, source_target_pairs={{0,8},{8,0},{1,9},{9,1},{2,10},{10,2},{3,11},{11,3},{4,12},{12,4},... | collective-permute-start | bytes 6152 | tf_op jit(solution)/shard_map/ppermute | solution.py:441
  19.6 7.3 %collective-permute-start.7 = (bf16[512,128]{1,0:T(8,128)(2,1)S(1)}, bf16[512,128]{1,0:T(8,128)(2,1)S(1)}, u32[]{:S(2)}, u32[]{:S(2)}) collective-permute-start(bf16[512,128]{1,0:T(8,128)(2,1)S(1)} %slice.56), channel_id=1, source_target_pairs={{0,96},{32,0},{64,32},{96,64},{1,97},{33,1},{65,33},{97,65},{2,98}... | collective-permute-start | bytes 393224 | tf_op jit(solution)/shard_map/ppermute | solution.py:234
  22.9 7.0 %collective-permute-start.8 = (bf16[512,128]{1,0:T(8,128)(2,1)S(1)}, bf16[512,128]{1,0:T(8,128)(2,1)}, u32[]{:S(2)}, u32[]{:S(2)}) collective-permute-start(bf16[512,128]{1,0:T(8,128)(2,1)S(1)} %slice.57), channel_id=1, source_target_pairs={{0,32},{32,64},{64,96},{96,0},{1,33},{33,65},{65,97},{97,1},{2,34}... | collective-permute-start | bytes 393224 | tf_op jit(solution)/shard_map/ppermute | solution.py:234
  23.6 13.0 %collective-permute-start.11 = (bf16[1024,128]{1,0:T(8,128)(2,1)S(1)}, bf16[1024,128]{1,0:T(8,128)(2,1)S(1)}, u32[]{:S(2)}, u32[]{:S(2)}) collective-permute-start(bf16[1024,128]{1,0:T(8,128)(2,1)S(1)} %collective-permute-done.3.rest_1_), channel_id=1, source_target_pairs={{0,96},{32,0},{64,32},{96,64},{1,97},{33,1},{65,33},{97,65},{2,98}... | collective-permute-start | bytes 786440 | tf_op jit(solution)/shard_map/ppermute | solution.py:234
  26.9 9.8 %collective-permute-start.5 = (bf16[1024,128]{1,0:T(8,128)(2,1)S(1)}, bf16[1024,128]{1,0:T(8,128)(2,1)}, u32[]{:S(2)}, u32[]{:S(2)}) collective-permute-start(bf16[1024,128]{1,0:T(8,128)(2,1)S(1)} %collective-permute-done.3.rest_1_), channel_id=1, source_target_pairs={{0,32},{32,64},{64,96},{96,0},{1,33},{33,65},{65,97},{97,1},{2,34}... | collective-permute-start | bytes 786440 | tf_op jit(solution)/shard_map/ppermute | solution.py:234
  26.9 8.9 %collective-permute-start.9 = (bf16[512,128]{1,0:T(8,128)(2,1)S(1)}, bf16[512,128]{1,0:T(8,128)(2,1)}, u32[]{:S(2)}, u32[]{:S(2)}) collective-permute-start(bf16[512,128]{1,0:T(8,128)(2,1)S(1)} %collective-permute-done.7.rest_4_), channel_id=1, source_target_pairs={{0,16},{16,0},{1,17},{17,1},{2,18},{18,2},{3,19},{19,3},{4,20},{20... | collective-permute-start | bytes 393224 | tf_op jit(solution)/shard_map/ppermute | solution.py:238
  29.9 6.8 %collective-permute-start.10 = (bf16[512,128]{1,0:T(8,128)(2,1)}, bf16[512,128]{1,0:T(8,128)(2,1)}, u32[]{:S(2)}, u32[]{:S(2)}) collective-permute-start(bf16[512,128]{1,0:T(8,128)(2,1)} %collective-permute-done.8.rest_5_), channel_id=1, source_target_pairs={{0,16},{16,0},{1,17},{17,1},{2,18},{18,2},{3,19},{19,3},{4,20},{20... | collective-permute-start | bytes 393224 | tf_op jit(solution)/shard_map/ppermute | solution.py:238
  80.1 3.9 %collective-permute-start.28 = (bf16[1792,512]{1,0:T(8,128)(2,1)S(1)}, bf16[1792,512]{1,0:T(8,128)(2,1)S(1)}, u32[]{:S(2)}, u32[]{:S(2)}) collective-permute-start(bf16[1792,512]{1,0:T(8,128)(2,1)S(1)} %shard_map.131), channel_id=1, source_target_pairs={{0,8},{8,0},{1,9},{9,1},{2,10},{10,2},{3,11},{11,3},{4,12},{12,4},... | collective-permute-start | bytes 5505032 | tf_op jit(solution)/shard_map/ppermute | solution.py:420
  123.8 34.0 %all-to-all-start.2 = ((bf16[64,112,128]{2,1,0:T(8,128)(2,1)}), bf16[64,112,128]{2,1,0:T(8,128)(2,1)}, u32[]{:S(2)}, u32[]{:S(2)}) async-start(bf16[64,112,128]{2,1,0:T(8,128)(2,1)} %chunk_sum.1), calls=%async_computation.2 | async-start | bytes 3670016 | tf_op jit(solution)/shard_map/all_to_all | solution.py:424
  132.7 1.4 collective-permute-start.12
  134.1 24.2 %collective-permute-start.13 = (bf16[1024,128]{1,0:T(8,128)(2,1)S(1)}, bf16[1024,128]{1,0:T(8,128)(2,1)S(1)}, u32[]{:S(2)}, u32[]{:S(2)}) collective-permute-start(bf16[1024,128]{1,0:T(8,128)(2,1)S(1)} %pad_maximum_fusion.2.rest_0_), channel_id=1, source_target_pairs={{0,4},{4,0},{1,5},{5,1},{2,6},{6,2},{3,7},{7,3},{8,12},{12,8},{9,1... | collective-permute-start | bytes 786440 | tf_op jit(solution)/shard_map/ppermute | solution.py:238
  135.7 25.3 %collective-permute-start.18 = (bf16[1024,128]{1,0:T(8,128)(2,1)S(1)}, bf16[1024,128]{1,0:T(8,128)(2,1)S(1)}, u32[]{:S(2)}, u32[]{:S(2)}) collective-permute-start(bf16[1024,128]{1,0:T(8,128)(2,1)S(1)} %pad_maximum_fusion.2.rest_0_), channel_id=1, source_target_pairs={{0,3},{1,0},{2,1},{3,2},{4,7},{5,4},{6,5},{7,6},{8,11},{9,8},{10,9... | collective-permute-start | bytes 786440 | tf_op jit(solution)/shard_map/ppermute | solution.py:234
  138.4 23.1 %collective-permute-start.16 = (bf16[1024,128]{1,0:T(8,128)(2,1)S(1)}, bf16[1024,128]{1,0:T(8,128)(2,1)S(1)}, u32[]{:S(2)}, u32[]{:S(2)}) collective-permute-start(bf16[1024,128]{1,0:T(8,128)(2,1)S(1)} %pad_maximum_fusion.2.rest_0_), channel_id=1, source_target_pairs={{0,2},{1,3},{2,0},{3,1},{4,6},{5,7},{6,4},{7,5},{8,10},{9,11},{10,... | collective-permute-start | bytes 786440 | tf_op jit(solution)/shard_map/ppermute | solution.py:234
  157.8 55.8 %collective-permute-start.29 = (bf16[64,112,128]{2,1,0:T(8,128)(2,1)}, bf16[64,112,128]{2,1,0:T(8,128)(2,1)}, u32[]{:S(2)}, u32[]{:S(2)}) collective-permute-start(bf16[64,112,128]{2,1,0:T(8,128)(2,1)} %all-to-all-done.2.blocks_ref), channel_id=1, source_target_pairs={{0,8},{8,0},{1,9},{9,1},{2,10},{10,2},{3,11},{11,3},{4,12},{12,4},... | collective-permute-start | bytes 5505032 | tf_op jit(solution)/shard_map/ppermute | solution.py:425
  157.8 16.1 %collective-permute-start.14 = (bf16[1024,128]{1,0:T(8,128)(2,1)S(1)}, bf16[1024,128]{1,0:T(8,128)(2,1)}, u32[]{:S(2)}, u32[]{:S(2)}) collective-permute-start(bf16[1024,128]{1,0:T(8,128)(2,1)S(1)} %pad_maximum_fusion.2.rest_0_), channel_id=1, source_target_pairs={{0,1},{1,2},{2,3},{3,0},{4,5},{5,6},{6,7},{7,4},{8,9},{9,10},{10,1... | collective-permute-start | bytes 786440 | tf_op jit(solution)/shard_map/ppermute | solution.py:234
  158.3 15.5 %collective-permute-start.19 = (bf16[1024,128]{1,0:T(8,128)(2,1)S(1)}, bf16[1024,128]{1,0:T(8,128)(2,1)}, u32[]{:S(2)}, u32[]{:S(2)}) collective-permute-start(bf16[1024,128]{1,0:T(8,128)(2,1)S(1)} %collective-permute-done.13.rest_1_), channel_id=1, source_target_pairs={{0,3},{1,0},{2,1},{3,2},{4,7},{5,4},{6,5},{7,6},{8,11},{9,8},{10,9... | collective-permute-start | bytes 786440 | tf_op jit(solution)/shard_map/ppermute | solution.py:234
  161.0 12.9 %collective-permute-start.17 = (bf16[1024,128]{1,0:T(8,128)(2,1)S(1)}, bf16[1024,128]{1,0:T(8,128)(2,1)}, u32[]{:S(2)}, u32[]{:S(2)}) collective-permute-start(bf16[1024,128]{1,0:T(8,128)(2,1)S(1)} %collective-permute-done.13.rest_1_), channel_id=1, source_target_pairs={{0,2},{1,3},{2,0},{3,1},{4,6},{5,7},{6,4},{7,5},{8,10},{9,11},{10,... | collective-permute-start | bytes 786440 | tf_op jit(solution)/shard_map/ppermute | solution.py:234
  161.5 17.5 %collective-permute-start.15 = (bf16[1024,128]{1,0:T(8,128)(2,1)S(1)}, bf16[1024,128]{1,0:T(8,128)(2,1)}, u32[]{:S(2)}, u32[]{:S(2)}) collective-permute-start(bf16[1024,128]{1,0:T(8,128)(2,1)S(1)} %collective-permute-done.13.rest_1_), channel_id=1, source_target_pairs={{0,1},{1,2},{2,3},{3,0},{4,5},{5,6},{6,7},{7,4},{8,9},{9,10},{10,1... | collective-permute-start | bytes 786440 | tf_op jit(solution)/shard_map/ppermute | solution.py:234
  184.7 9.7 %collective-permute-start.22 = (bf16[1024,128]{1,0:T(8,128)(2,1)}, bf16[1024,128]{1,0:T(8,128)(2,1)S(1)}, u32[]{:S(2)}, u32[]{:S(2)}) collective-permute-start(bf16[1024,128]{1,0:T(8,128)(2,1)} %get-tuple-element.31), channel_id=1, source_target_pairs={{0,16},{16,0},{1,17},{17,1},{2,18},{18,2},{3,19},{19,3},{4,20},{20... | collective-permute-start | bytes 786440 | tf_op jit(solution)/shard_map/ppermute | solution.py:238
  184.8 11.2 %collective-permute-start.24 = (bf16[1024,128]{1,0:T(8,128)(2,1)}, bf16[1024,128]{1,0:T(8,128)(2,1)S(1)}, u32[]{:S(2)}, u32[]{:S(2)}) collective-permute-start(bf16[1024,128]{1,0:T(8,128)(2,1)} %get-tuple-element.33), channel_id=1, source_target_pairs={{0,32},{32,64},{64,96},{96,0},{1,33},{33,65},{65,97},{97,1},{2,34}... | collective-permute-start | bytes 786440 | tf_op jit(solution)/shard_map/ppermute | solution.py:234
  186.3 11.5 %collective-permute-start.25 = (bf16[1024,128]{1,0:T(8,128)(2,1)}, bf16[1024,128]{1,0:T(8,128)(2,1)S(1)}, u32[]{:S(2)}, u32[]{:S(2)}) collective-permute-start(bf16[1024,128]{1,0:T(8,128)(2,1)} %get-tuple-element.34), channel_id=1, source_target_pairs={{0,96},{32,0},{64,32},{96,64},{1,97},{33,1},{65,33},{97,65},{2,98}... | collective-permute-start | bytes 786440 | tf_op jit(solution)/shard_map/ppermute | solution.py:234
  188.1 13.0 %collective-permute-start.20 = (bf16[1024,128]{1,0:T(8,128)(2,1)}, bf16[1024,128]{1,0:T(8,128)(2,1)S(1)}, u32[]{:S(2)}, u32[]{:S(2)}) collective-permute-start(bf16[1024,128]{1,0:T(8,128)(2,1)} %get-tuple-element.28), channel_id=1, source_target_pairs={{0,32},{32,64},{64,96},{96,0},{1,33},{33,65},{65,97},{97,1},{2,34}... | collective-permute-start | bytes 786440 | tf_op jit(solution)/shard_map/ppermute | solution.py:234
  194.4 9.4 %collective-permute-start.21 = (bf16[1024,128]{1,0:T(8,128)(2,1)}, bf16[1024,128]{1,0:T(8,128)(2,1)S(1)}, u32[]{:S(2)}, u32[]{:S(2)}) collective-permute-start(bf16[1024,128]{1,0:T(8,128)(2,1)} %get-tuple-element.29), channel_id=1, source_target_pairs={{0,96},{32,0},{64,32},{96,64},{1,97},{33,1},{65,33},{97,65},{2,98}... | collective-permute-start | bytes 786440 | tf_op jit(solution)/shard_map/ppermute | solution.py:234
  196.0 9.5 %collective-permute-start.23 = (bf16[1024,128]{1,0:T(8,128)(2,1)S(1)}, bf16[1024,128]{1,0:T(8,128)(2,1)S(1)}, u32[]{:S(2)}, u32[]{:S(2)}) collective-permute-start(bf16[1024,128]{1,0:T(8,128)(2,1)S(1)} %shard_map.128), channel_id=1, source_target_pairs={{0,64},{32,96},{64,0},{96,32},{1,65},{33,97},{65,1},{97,33},{2,66}... | collective-permute-start | bytes 786440 | tf_op jit(solution)/shard_map/ppermute | solution.py:234
  198.9 8.0 %collective-permute-start.26 = (bf16[1024,128]{1,0:T(8,128)(2,1)S(1)}, bf16[1024,128]{1,0:T(8,128)(2,1)S(1)}, u32[]{:S(2)}, u32[]{:S(2)}) collective-permute-start(bf16[1024,128]{1,0:T(8,128)(2,1)S(1)} %shard_map.129), channel_id=1, source_target_pairs={{0,16},{16,0},{1,17},{17,1},{2,18},{18,2},{3,19},{19,3},{4,20},{20... | collective-permute-start | bytes 786440 | tf_op jit(solution)/shard_map/ppermute | solution.py:238
  208.2 1.4 collective-permute-start.27
  (11 other events, 153.1 us)
